TPU v7x, 512 devices: a whole 4x4x16 slice. The times are simulated.
512 devices in a mesh: replica: 64 (over z_hi, y, x, core), tensor: 8 (over z_lo).
Axes of the slice: x: 4, y: 4, z: 16 (z_hi: 2, z_lo: 8; z = z_hi * 8 + z_lo), core: 2. Of those that a mesh axis runs over, the one named last changes fastest.
Arguments:
- tokens: bfloat16 [32768, 8192], P(('replica', 'tensor')), may hold values from -6 to 6
- norm_gain: bfloat16 [8192], replicated, may hold values from 0.099609375 to 1.8984375
- key_weight: bfloat16 [64, 8192, 1024], P('replica', None, 'tensor'), may hold values from -0.0625 to 0.0625
- inner_params: bfloat16 [64, 8, 1024, 512], P('replica', 'tensor'), may hold values from -16 to 16
- outer_params: float32 [8, 1024, 512], P('tensor', 'replica'), may hold values from -6 to 6
- outer_momentum: float32 [8, 1024, 512], P('tensor', 'replica'), may hold values from -3 to 3
Outputs:
- key_rows: bfloat16 [32768, 1024], P('replica', 'tensor')
- new_outer: float32 [8, 1024, 512], P('tensor', 'replica')
- new_momentum: float32 [8, 1024, 512], P('tensor', 'replica')
- synced_params: bfloat16 [8, 1024, 512], P('tensor')
All inputs are finite; a program needn't handle non-finite values.
Results may differ from a plain program's by a relative error of at most 0.0049.
Values may be sent and summed in bfloat16 or wider, within the bound.
No kernel may reach another device: no remote copies, remote signals or barrier semaphores. Data moves between devices by JAX's collectives and lax.ppermute only.
A program may use at most 64 MiB of HBM per device.

v0:
```python
import math

import jax
import jax.numpy as jnp
from jax import lax
from jax.sharding import PartitionSpec as P

HD = 128


EPSILON = 1e-05
ROPE_BASE = 500000.0
LR_OUTER = 0.7
MOMENTUM_OUTER = 0.9


def rotate(keys_f32, positions):
    rows = keys_f32.shape[0]
    cols = keys_f32.shape[1]
    half = HD // 2
    shaped = keys_f32.reshape(rows, cols // HD, HD)
    index = jnp.arange(half).astype(jnp.float32)
    inverse = jnp.exp(-(2.0 * index / HD) * math.log(ROPE_BASE))
    angles = positions[:, None] * inverse[None, :]
    cosine = jnp.cos(angles)[:, None, :]
    sine = jnp.sin(angles)[:, None, :]
    first = shaped[:, :, :half]
    second = shaped[:, :, half:]
    joined = jnp.concatenate(
        [first * cosine - second * sine, second * cosine + first * sine], axis=-1
    )
    return joined.reshape(rows, cols)


def forward_keys(tokens, norm_gain, key_weight):
    block_f32 = tokens.astype(jnp.float32)
    scale = lax.rsqrt(jnp.mean(block_f32 * block_f32, axis=-1, keepdims=True) + EPSILON)
    normed = (block_f32 * scale * norm_gain.astype(jnp.float32)).astype(jnp.bfloat16)
    weight = key_weight[0]
    piece = lax.all_gather(normed, "tensor", axis=0, tiled=True)
    projected = jnp.dot(piece, weight, preferred_element_type=jnp.float32)
    positions = jnp.arange(piece.shape[0], dtype=jnp.int32).astype(jnp.float32)
    return rotate(projected, positions).astype(jnp.bfloat16)


def nesterov(outer_rows, moment_rows, summed, replicas):
    delta = outer_rows - summed / replicas
    moment_next = MOMENTUM_OUTER * moment_rows + delta
    outer_next = outer_rows - LR_OUTER * (delta + MOMENTUM_OUTER * moment_next)
    return (outer_next, moment_next)


def owned_sum(local_params):
    return lax.psum_scatter(
        local_params.astype(jnp.float32), "replica", scatter_dimension=0, tiled=True
    )


def sync_fragment(inner_params, outer_params, outer_momentum):
    replicas = lax.axis_size("replica")
    local_params = inner_params[0, 0]
    summed = owned_sum(local_params)
    outer_next, moment_next = nesterov(outer_params[0], outer_momentum[0], summed, replicas)
    synced = lax.all_gather(outer_next.astype(jnp.bfloat16), "replica", axis=0, tiled=True)
    return (outer_next[None], moment_next[None], synced[None])


def body(tokens, norm_gain, key_weight, inner_params, outer_params, outer_momentum):
    key_rows = forward_keys(tokens, norm_gain, key_weight)
    new_outer, new_momentum, synced_params = sync_fragment(
        inner_params, outer_params, outer_momentum
    )
    return (key_rows, new_outer, new_momentum, synced_params)


def solution(mesh):
    in_specs = (
        P(("replica", "tensor"), None),
        P(),
        P("replica", None, "tensor"),
        P("replica", "tensor", None, None),
        P("tensor", "replica", None),
        P("tensor", "replica", None),
    )
    out_specs = (
        P("replica", "tensor"),
        P("tensor", "replica", None),
        P("tensor", "replica", None),
        P("tensor", None, None),
    )
    return jax.shard_map(body, mesh=mesh, in_specs=in_specs, out_specs=out_specs, check_vma=False)
```

profile of v0, /device:TPU:6, one launch (start us, length us, event | category | flops | bytes accessed | tf_op | source)
XLA Modules:
  0.0 875.0 jit_solution(4072510112862424039)
XLA Ops:
  7.2 0.0 copy-start
  7.2 0.0 copy-start.5
  7.2 0.0 copy-start.1
  7.2 0.0 reduce-scatter.2.cloned.1.call-start
  7.2 3.0 bitcast_convert_fusion
  10.2 0.0 copy-start.3
  10.2 0.0 copy-start.4
  10.2 0.0 reduce-scatter.2.cloned.1.call-update
  10.3 0.0 all-gather.5.cloned.1.call-start
  10.3 0.0 copy-done.5
  10.3 0.0 copy-done.1
  10.4 0.3 fusion
  10.7 535.4 %reduce-scatter.2.cloned.1.call-done = f32[16,512]{1,0:T(8,128)} async-done(((f32[1024,512]{1,0:T(8,128)}), f32[16,512]{1,0:T(8,128)}) %reduce-scatter.2.cloned.1.call-update) | async-done | bytes 32784 | tf_op jit(solution)/shard_map/reduce_scatter | solution.py:54
  546.1 0.0 copy-done.3
  546.1 0.0 copy-done.4
  546.1 1.4 fusion.17
  547.5 0.0 all-gather.5.cloned.1.call-update
  547.5 0.0 all-gather.3.cloned.1.call-start
  547.6 1.3 fusion.2
  548.9 0.0 all-gather.3.cloned.1.call-update
  548.9 135.5 %all-gather.5.cloned.1.call-done = bf16[1024,512]{1,0:T(8,128)(2,1)} async-done(((bf16[16,512]{1,0:T(8,128)(2,1)}), bf16[1024,512]{1,0:T(8,128)(2,1)}) %all-gather.5.cloned.1.call-update) | async-done | bytes 1048592 | tf_op jit(solution)/shard_map/all_gather | solution.py:64
  684.4 0.0 copy-start.2
  684.4 175.5 %all-gather.3.cloned.1.call-done = bf16[512,8192]{1,0:T(8,128)(2,1)} async-done(((bf16[64,8192]{1,0:T(8,128)(2,1)}), bf16[512,8192]{1,0:T(8,128)(2,1)}) %all-gather.3.cloned.1.call-update) | async-done | bytes 8388624 | tf_op jit(solution)/shard_map/all_gather | solution.py:40
  859.9 0.0 copy-done
  859.9 6.3 fusion.5
  866.2 0.6 fusion.13
  866.8 0.8 copy.10
  867.5 0.0 copy-done.2
  867.5 1.0 copy.12
  (5 shorter events, 0.0 us)
Async XLA Ops:
  7.2 852.7 %copy-start = (bf16[1,8192,128]{2,1,0:T(8,128)(2,1)S(1)}, bf16[1,8192,128]{2,1,0:T(8,128)(2,1)}, u32[]{:S(2)}) copy-start(bf16[1,8192,128]{2,1,0:T(8,128)(2,1)} %param.8) | copy-start | bytes 6291460
  7.2 3.1 copy-start.5
  7.2 3.2 copy-start.1
  7.2 538.9 %reduce-scatter.2.cloned.1.call-start = ((), (), s32[]{:S(2)}) async-start(), calls=%async_computation.2 | async-start | bytes 2129920 | tf_op jit(solution)/shard_map/reduce_scatter | solution.py:54
  10.2 535.9 %copy-start.3 = (f32[1,16,512]{2,1,0:T(8,128)S(1)}, f32[1,16,512]{2,1,0:T(8,128)}, u32[]{:S(2)}) copy-start(f32[1,16,512]{2,1,0:T(8,128)} %param.11) | copy-start | bytes 98308
  10.2 535.9 %copy-start.4 = (f32[1,16,512]{2,1,0:T(8,128)S(1)}, f32[1,16,512]{2,1,0:T(8,128)}, u32[]{:S(2)}) copy-start(f32[1,16,512]{2,1,0:T(8,128)} %param.10) | copy-start | bytes 98308
  10.3 674.1 %all-gather.5.cloned.1.call-start = ((), (), s32[]{:S(2)}) async-start(), calls=%async_computation.3 | async-start | bytes 1064960 | tf_op jit(solution)/shard_map/all_gather | solution.py:64
  547.5 312.4 %all-gather.3.cloned.1.call-start = ((), (), s32[]{:S(2)}) async-start(), calls=%async_computation.1 | async-start | bytes 9437184 | tf_op jit(solution)/shard_map/all_gather | solution.py:40
  684.4 183.1 %copy-start.2 = (bf16[1024,512]{1,0:T(8,128)(2,1)S(1)}, bf16[1024,512]{1,0:T(8,128)(2,1)}, u32[]{:S(2)}) copy-start(bf16[1024,512]{1,0:T(8,128)(2,1)} %all-gather.5.cloned.1.call-done) | copy-start | bytes 3145732
Sparse Core Ops, SparseCore 0:
  10.8 535.2 reduce-scatter.1
  551.9 132.4 all-gather.4
  687.2 172.6 all-gather.2
where the time goes:
time: 876 us; the launch traced here: 875 us
  waiting for transfers between devices  846 us (97%)
  between operations  13.8 us (2%)
    reduce_scatter x1, waiting for transfers between devices, owned_sum(): lax.psum_scatter(local_params.astype(jnp.float32), 'replica', scatter_dim...  535 us
    all_gather x1, waiting for transfers between devices, forward_keys(): piece = lax.all_gather(normed, 'tensor', axis=0, tiled=True)  176 us
    all_gather x1, waiting for transfers between devices, sync_fragment(): lax.all_gather(outer_next.astype(jnp.bfloat16), 'replica', axis=0, tiled=...  135 us
  transfers between devices with their start and end apart: 3, of which 3 were waited for; matrix products, arithmetic and copies ran while one was open for 0% of the time, Pallas kernels for 0%

commit v1 on v0

--- a/solution.py
+++ b/solution.py
@@ -3,6 +3,7 @@
 import jax
 import jax.numpy as jnp
 from jax import lax
+from jax.sharding import Mesh
 from jax.sharding import PartitionSpec as P
 
 HD = 128
@@ -12,6 +13,9 @@
 ROPE_BASE = 500000.0
 LR_OUTER = 0.7
 MOMENTUM_OUTER = 0.9
+
+PLANE = ("y", "x", "core")
+REPLICA = ("zh",) + PLANE
 
 
 def rotate(keys_f32, positions):
@@ -50,18 +54,20 @@
     return (outer_next, moment_next)
 
 
-def owned_sum(local_params):
-    return lax.psum_scatter(
-        local_params.astype(jnp.float32), "replica", scatter_dimension=0, tiled=True
-    )
-
-
 def sync_fragment(inner_params, outer_params, outer_momentum):
-    replicas = lax.axis_size("replica")
-    local_params = inner_params[0, 0]
-    summed = owned_sum(local_params)
-    outer_next, moment_next = nesterov(outer_params[0], outer_momentum[0], summed, replicas)
-    synced = lax.all_gather(outer_next.astype(jnp.bfloat16), "replica", axis=0, tiled=True)
+    params = inner_params[0, 0].reshape(2, 32, 16, 512).transpose(1, 0, 2, 3)
+    pieces = lax.all_to_all(params, PLANE, 0, 0, tiled=True)
+    partial = jnp.sum(pieces.astype(jnp.float32), axis=0)
+    zh = lax.axis_index("zh")
+    other = lax.dynamic_index_in_dim(partial, 1 - zh, 0, keepdims=False)
+    own = lax.dynamic_index_in_dim(partial, zh, 0, keepdims=False)
+    summed = own + lax.ppermute(other, "zh", [(0, 1), (1, 0)])
+    outer_next, moment_next = nesterov(outer_params[0], outer_momentum[0], summed, 64)
+    mine = outer_next.astype(jnp.bfloat16)
+    theirs = lax.ppermute(mine, "zh", [(0, 1), (1, 0)])
+    pair = jnp.where(zh == 0, jnp.stack([mine, theirs]), jnp.stack([theirs, mine]))
+    synced = lax.all_to_all(jnp.broadcast_to(pair[None], (32, 2, 16, 512)), PLANE, 0, 0, tiled=True)
+    synced = synced.transpose(1, 0, 2, 3).reshape(1024, 512)
     return (outer_next[None], moment_next[None], synced[None])
 
 
@@ -74,18 +80,19 @@
 
 
 def solution(mesh):
+    fine = Mesh(mesh.devices.reshape(2, 4, 4, 2, 8), REPLICA + ("tensor",))
     in_specs = (
-        P(("replica", "tensor"), None),
+        P(REPLICA + ("tensor",), None),
         P(),
-        P("replica", None, "tensor"),
-        P("replica", "tensor", None, None),
-        P("tensor", "replica", None),
-        P("tensor", "replica", None),
+        P(REPLICA, None, "tensor"),
+        P(REPLICA, "tensor", None, None),
+        P("tensor", REPLICA, None),
+        P("tensor", REPLICA, None),
     )
     out_specs = (
-        P("replica", "tensor"),
-        P("tensor", "replica", None),
-        P("tensor", "replica", None),
+        P(REPLICA, "tensor"),
+        P("tensor", REPLICA, None),
+        P("tensor", REPLICA, None),
         P("tensor", None, None),
     )
-    return jax.shard_map(body, mesh=mesh, in_specs=in_specs, out_specs=out_specs, check_vma=False)
+    return jax.shard_map(body, mesh=fine, in_specs=in_specs, out_specs=out_specs, check_vma=False)

time: 876 us -> 219 us (0.25)
  waiting for transfers between devices: 846 us -> 142 us
  starting transfers between devices: 0.12 us -> 44.1 us
    reduce_scatter x1 -> x0, waiting for transfers between devices: 535 us -> none  [owned_sum(): lax.psum_scatter(local_params.astype(jnp.float32), 'replica', scatter_dim...]
    all_gather x1 -> x0, waiting for transfers between devices: 135 us -> none  [sync_fragment(): lax.all_gather(outer_next.astype(jnp.bfloat16), 'replica', axis=0, tiled=...]
    all_gather x1, waiting for transfers between devices: 176 us -> 108 us  [forward_keys(): piece = lax.all_gather(normed, 'tensor', axis=0, tiled=True)]
    all_to_all x0 -> x2, waiting for transfers between devices: none -> 29.4 us  [the longest x1 14.7 us: sync_fragment(): pieces = lax.all_to_all(params, PLANE, 0, 0, tiled=True)]
    ppermute x0 -> x2, starting transfers between devices: none -> 26.3 us  [the longest x1 13.7 us: sync_fragment(): summed = own + lax.ppermute(other, 'zh', [(0, 1), (1, 0)])]
    all_to_all x0 -> x2, starting transfers between devices: none -> 17.8 us  [the longest x1 9.6 us: sync_fragment(): pieces = lax.all_to_all(params, PLANE, 0, 0, tiled=True)]
  transfers between devices with their start and end apart: 3 -> 5, of which waited for: 3 -> 5; matrix products, arithmetic and copies ran while one was open for 0% -> 2% of each run, Pallas kernels for 0% -> 0%
where the time goes in v1:
time: 219 us; the launch traced here: 217 us
  waiting for transfers between devices  142 us (65%)
  starting transfers between devices  44.1 us (20%)
  between operations  14.1 us (6%)
  other arithmetic  6.47 us (3%)
  matrix products  6.25 us (3%)
  local copies, waits for them, and re-layouts  4.01 us (2%)
    all_gather x1, waiting for transfers between devices, forward_keys(): piece = lax.all_gather(normed, 'tensor', axis=0, tiled=True)  108 us
    all_to_all x1, waiting for transfers between devices, sync_fragment(): pieces = lax.all_to_all(params, PLANE, 0, 0, tiled=True)  14.7 us
    all_to_all x1, waiting for transfers between devices, sync_fragment(): lax.all_to_all(jnp.broadcast_to(pair[None], (32, 2, 16, 512)), PLANE, 0,...  14.7 us
    ppermute x1, starting transfers between devices, sync_fragment(): summed = own + lax.ppermute(other, 'zh', [(0, 1), (1, 0)])  13.7 us
    ppermute x1, starting transfers between devices, sync_fragment(): theirs = lax.ppermute(mine, 'zh', [(0, 1), (1, 0)])  12.6 us
    all_to_all x1, starting transfers between devices, sync_fragment(): pieces = lax.all_to_all(params, PLANE, 0, 0, tiled=True)  9.6 us
    all_to_all x1, starting transfers between devices, sync_fragment(): lax.all_to_all(jnp.broadcast_to(pair[None], (32, 2, 16, 512)), PLANE, 0,...  8.21 us
    dot_general x1, matrix products, forward_keys(): projected = jnp.dot(piece, weight, preferred_element_type=jnp.float32)  6.25 us
  transfers between devices with their start and end apart: 5, of which 5 were waited for; matrix products, arithmetic and copies ran while one was open for 2% of the time, Pallas kernels for 0%

profile of v1, /device:TPU:6, one launch (start us, length us, event | category | flops | bytes accessed | tf_op | source)
XLA Modules:
  0.0 217.5 jit_solution(10720558171822153706)
XLA Ops:
  7.2 0.0 copy-start
  7.2 0.0 all-gather.2.cloned.1.call-start
  7.2 0.9 convert_element_type.46
  8.1 0.0 copy-start.1
  8.1 1.6 fusion
  9.7 2.6 %fusion.2 = bf16[64,8192]{1,0:T(8,128)(2,1)} fusion(bf16[64,8192]{1,0:T(8,128)(2,1)} %param.6, f32[8192]{0:T(1024)S(1)} %convert_element_type.46, f32[64]{0:T(128)S(1)} %add_rsqrt_fusion), kind=kLoop, calls=%fused_computation.4 | loop fusion | flops 2097152 | bytes 2130176 | tf_op jit(solution)/shard_map/convert_element_type | solution.py:42
  12.3 0.0 all-gather.2.cloned.1.call-update
  12.3 0.0 copy-done.1
  12.4 1.1 copy.12
  13.4 0.0 copy-start.2
  13.4 0.0 copy-start.3
  13.4 9.6 %all-to-all-start = ((bf16[32,2,16,512]{3,2,1,0:T(8,128)(2,1)}), bf16[32,2,16,512]{3,2,1,0:T(8,128)(2,1)S(1)}, u32[]{:S(2)}, u32[]{:S(2)}) async-start(bf16[32,2,16,512]{3,2,1,0:T(8,128)(2,1)} %copy.12), calls=%async_computation | async-start | bytes 2097152 | tf_op jit(solution)/shard_map/all_to_all | solution.py:59
  23.0 14.7 %all-to-all-done = bf16[32,2,16,512]{3,2,1,0:T(8,128)(2,1)S(1)} async-done(((bf16[32,2,16,512]{3,2,1,0:T(8,128)(2,1)}), bf16[32,2,16,512]{3,2,1,0:T(8,128)(2,1)S(1)}, u32[]{:S(2)}, u32[]{:S(2)}) %all-to-all-start) | async-done | bytes 1048608 | tf_op jit(solution)/shard_map/all_to_all | solution.py:59
  37.7 0.2 convert_reduce_fusion
  37.9 13.7 %collective-permute-start = (f32[16,512]{1,0:T(8,128)S(1)}, f32[16,512]{1,0:T(8,128)S(1)}, u32[]{:S(2)}, u32[]{:S(2)}) collective-permute-start(f32[16,512]{1,0:T(8,128)S(1)} %dynamic-slice_bitcast_fusion), channel_id=1, source_target_pairs={{0,256},{256,0},{1,257},{257,1},{2,258},{258,2},{3,259},{259,3},{4... | collective-permute-start | bytes 98312 | tf_op jit(solution)/shard_map/ppermute | solution.py:64
  51.7 2.9 %collective-permute-done = f32[16,512]{1,0:T(8,128)S(1)} collective-permute-done((f32[16,512]{1,0:T(8,128)S(1)}, f32[16,512]{1,0:T(8,128)S(1)}, u32[]{:S(2)}, u32[]{:S(2)}) %collective-permute-start) | collective-permute-done | bytes 32800 | tf_op jit(solution)/shard_map/ppermute | solution.py:64
  54.5 0.0 copy-done.2
  54.5 0.0 copy-done.3
  54.6 0.6 fusion.19
  55.2 12.6 %collective-permute-start.1 = (bf16[16,512]{1,0:T(8,128)(2,1)S(1)}, bf16[16,512]{1,0:T(8,128)(2,1)S(1)}, u32[]{:S(2)}, u32[]{:S(2)}) collective-permute-start(bf16[16,512]{1,0:T(8,128)(2,1)S(1)} %get-tuple-element.16), channel_id=1, source_target_pairs={{0,256},{256,0},{1,257},{257,1},{2,258},{258,2},{3,259},{259,3},{4... | collective-permute-start | bytes 49160 | tf_op jit(solution)/shard_map/ppermute | solution.py:67
  67.8 2.4 %collective-permute-done.1 = bf16[16,512]{1,0:T(8,128)(2,1)S(1)} collective-permute-done((bf16[16,512]{1,0:T(8,128)(2,1)S(1)}, bf16[16,512]{1,0:T(8,128)(2,1)S(1)}, u32[]{:S(2)}, u32[]{:S(2)}) %collective-permute-start.1) | collective-permute-done | bytes 16416 | tf_op jit(solution)/shard_map/ppermute | solution.py:67
  70.2 1.1 broadcast_in_dim.8
  71.3 8.2 %all-to-all-start.1 = ((bf16[32,2,16,512]{3,2,1,0:T(8,128)(2,1)}), bf16[32,2,16,512]{3,2,1,0:T(8,128)(2,1)S(1)}, u32[]{:S(2)}, u32[]{:S(2)}) async-start(bf16[32,2,16,512]{3,2,1,0:T(8,128)(2,1)} %broadcast_in_dim.8), calls=%async_computation.1 | async-start | bytes 2097152 | tf_op jit(solution)/shard_map/all_to_all | solution.py:69
  79.5 14.7 %all-to-all-done.1 = bf16[32,2,16,512]{3,2,1,0:T(8,128)(2,1)S(1)} async-done(((bf16[32,2,16,512]{3,2,1,0:T(8,128)(2,1)}), bf16[32,2,16,512]{3,2,1,0:T(8,128)(2,1)S(1)}, u32[]{:S(2)}, u32[]{:S(2)}) %all-to-all-start.1) | async-done | bytes 1048608 | tf_op jit(solution)/shard_map/all_to_all | solution.py:69
  94.2 1.1 copy.13
  95.3 107.8 %all-gather.2.cloned.1.call-done = bf16[512,8192]{1,0:T(8,128)(2,1)} async-done(((bf16[64,8192]{1,0:T(8,128)(2,1)}), bf16[512,8192]{1,0:T(8,128)(2,1)}) %all-gather.2.cloned.1.call-update) | async-done | bytes 8388624 | tf_op jit(solution)/shard_map/all_gather | solution.py:44
  203.0 0.0 copy-done
  203.0 6.3 %fusion.5 = f32[512,1,128]{0,2,1:T(8,128)S(1)} fusion(bf16[512,8192]{1,0:T(8,128)(2,1)} %all-gather.2.cloned.1.call-done, bf16[1,8192,128]{2,1,0:T(8,128)(2,1)S(1)} %copy-done), kind=kOutput, calls=%fused_computation.8 | convolution fusion | flops 1073741824 | bytes 10747904 | tf_op jit(solution)/shard_map/dot_general | solution.py:45
  209.3 0.6 fusion.13
  209.9 0.8 copy.14
  (6 shorter events, 0.0 us)
Async XLA Ops:
  7.2 195.9 %copy-start = (bf16[1,8192,128]{2,1,0:T(8,128)(2,1)S(1)}, bf16[1,8192,128]{2,1,0:T(8,128)(2,1)}, u32[]{:S(2)}) copy-start(bf16[1,8192,128]{2,1,0:T(8,128)(2,1)} %param.8) | copy-start | bytes 6291460
  7.2 195.8 %all-gather.2.cloned.1.call-start = ((), (), s32[]{:S(2)}) async-start(), calls=%async_computation.2 | async-start | bytes 9437184 | tf_op jit(solution)/shard_map/all_gather | solution.py:44
  8.1 4.3 %copy-start.1 = (bf16[1,1,1024,512]{3,2,1,0:T(8,128)(2,1)S(1)}, bf16[1,1,1024,512]{3,2,1,0:T(8,128)(2,1)}, u32[]{:S(2)}) copy-start(bf16[1,1,1024,512]{3,2,1,0:T(8,128)(2,1)} %param.9) | copy-start | bytes 3145732
  13.4 41.1 %copy-start.2 = (f32[1,16,512]{2,1,0:T(8,128)S(1)}, f32[1,16,512]{2,1,0:T(8,128)}, u32[]{:S(2)}) copy-start(f32[1,16,512]{2,1,0:T(8,128)} %param.11) | copy-start | bytes 98308
  13.4 41.1 %copy-start.3 = (f32[1,16,512]{2,1,0:T(8,128)S(1)}, f32[1,16,512]{2,1,0:T(8,128)}, u32[]{:S(2)}) copy-start(f32[1,16,512]{2,1,0:T(8,128)} %param.10) | copy-start | bytes 98308
  13.4 24.3 %all-to-all-start = ((bf16[32,2,16,512]{3,2,1,0:T(8,128)(2,1)}), bf16[32,2,16,512]{3,2,1,0:T(8,128)(2,1)S(1)}, u32[]{:S(2)}, u32[]{:S(2)}) async-start(bf16[32,2,16,512]{3,2,1,0:T(8,128)(2,1)} %copy.12), calls=%async_computation | async-start | bytes 2097152 | tf_op jit(solution)/shard_map/all_to_all | solution.py:59
  37.9 16.6 %collective-permute-start = (f32[16,512]{1,0:T(8,128)S(1)}, f32[16,512]{1,0:T(8,128)S(1)}, u32[]{:S(2)}, u32[]{:S(2)}) collective-permute-start(f32[16,512]{1,0:T(8,128)S(1)} %dynamic-slice_bitcast_fusion), channel_id=1, source_target_pairs={{0,256},{256,0},{1,257},{257,1},{2,258},{258,2},{3,259},{259,3},{4... | collective-permute-start | bytes 98312 | tf_op jit(solution)/shard_map/ppermute | solution.py:64
  55.2 15.0 %collective-permute-start.1 = (bf16[16,512]{1,0:T(8,128)(2,1)S(1)}, bf16[16,512]{1,0:T(8,128)(2,1)S(1)}, u32[]{:S(2)}, u32[]{:S(2)}) collective-permute-start(bf16[16,512]{1,0:T(8,128)(2,1)S(1)} %get-tuple-element.16), channel_id=1, source_target_pairs={{0,256},{256,0},{1,257},{257,1},{2,258},{258,2},{3,259},{259,3},{4... | collective-permute-start | bytes 49160 | tf_op jit(solution)/shard_map/ppermute | solution.py:67
  71.3 22.9 %all-to-all-start.1 = ((bf16[32,2,16,512]{3,2,1,0:T(8,128)(2,1)}), bf16[32,2,16,512]{3,2,1,0:T(8,128)(2,1)S(1)}, u32[]{:S(2)}, u32[]{:S(2)}) async-start(bf16[32,2,16,512]{3,2,1,0:T(8,128)(2,1)} %broadcast_in_dim.8), calls=%async_computation.1 | async-start | bytes 2097152 | tf_op jit(solution)/shard_map/all_to_all | solution.py:69
Sparse Core Ops, SparseCore 0:
  12.5 190.5 all-gather.1

commit v2 on v1

v2 whole, which is shorter than its diff:
```python
import math

import jax
import jax.numpy as jnp
from jax import lax
from jax.sharding import Mesh
from jax.sharding import PartitionSpec as P

HD = 128


EPSILON = 1e-05
ROPE_BASE = 500000.0
LR_OUTER = 0.7
MOMENTUM_OUTER = 0.9

PLANE = ("y", "x", "core")
REPLICA = ("zh",) + PLANE

K_LINE = 6144


def rotary_tables(rows):
    half = HD // 2
    index = jnp.arange(half).astype(jnp.float32)
    inverse = jnp.exp(-(2.0 * index / HD) * math.log(ROPE_BASE))
    angles = jnp.arange(rows).astype(jnp.float32)[:, None] * inverse[None, :]
    return jnp.cos(angles), jnp.sin(angles)


def dot(a, b):
    return jnp.dot(a, b, preferred_element_type=jnp.float32)


def after(mark, *values):
    return lax.optimization_barrier(values + (mark[:8, :128],))[: len(values)]


def nesterov(outer_rows, moment_rows, summed, replicas):
    delta = outer_rows - summed / replicas
    moment_next = MOMENTUM_OUTER * moment_rows + delta
    outer_next = outer_rows - LR_OUTER * (delta + MOMENTUM_OUTER * moment_next)
    return (outer_next, moment_next)


def body(tokens, norm_gain, key_weight, inner_params, outer_params, outer_momentum):
    me = lax.axis_index("tensor")
    zh = lax.axis_index("zh")
    low = me < 4
    params = inner_params[0, 0].reshape(2, 32, 16, 512).transpose(1, 0, 2, 3)
    pieces = lax.all_to_all(params, PLANE, 0, 0, tiled=True)

    block_f32 = tokens.astype(jnp.float32)
    scale = lax.rsqrt(jnp.mean(block_f32 * block_f32, axis=-1, keepdims=True) + EPSILON)
    normed = (block_f32 * scale * norm_gain.astype(jnp.float32)).astype(jnp.bfloat16)
    weight = key_weight[0]
    shard, rest = normed[:, :K_LINE], normed[:, K_LINE:]
    w_line, w_rest = weight[:K_LINE], weight[K_LINE:]

    rows = jnp.zeros((22, 64, HD), jnp.float32)

    def put(rows, block, at):
        return lax.dynamic_update_slice(rows, dot(block, w_line)[None], (7 + at, 0, 0))

    def hop(a, b, s):
        a = lax.ppermute(a, "tensor", [(j, j + 1) for j in range(s, 7)])
        b = lax.ppermute(b, "tensor", [(j + 1, j) for j in range(7 - s)])
        return a, b

    rows = put(rows, shard, me)
    a, b = hop(shard, shard, 0)
    rows = put(put(rows, a, me - 1), b, me + 1)

    (pieces,) = after(a, pieces)
    partial = jnp.sum(pieces.astype(jnp.float32), axis=0)
    other = lax.dynamic_index_in_dim(partial, 1 - zh, 0, keepdims=False)
    own = lax.dynamic_index_in_dim(partial, zh, 0, keepdims=False)
    came = lax.ppermute(other, "zh", [(0, 1), (1, 0)])

    a, b = hop(a, b, 1)
    rows = put(put(rows, a, me - 2), b, me + 2)

    (came,) = after(a, came)
    outer_next, moment_next = nesterov(outer_params[0], outer_momentum[0], own + came, 64)
    mine = outer_next.astype(jnp.bfloat16)
    theirs = lax.ppermute(mine, "zh", [(0, 1), (1, 0)])

    a, b = hop(a, b, 2)
    rows = put(put(rows, a, me - 3), b, me + 3)

    (theirs,) = after(a, theirs)
    pair = jnp.where(zh == 0, jnp.stack([mine, theirs]), jnp.stack([theirs, mine]))
    synced = lax.all_to_all(jnp.broadcast_to(pair[None], (32, 2, 16, 512)), PLANE, 0, 0, tiled=True)

    rest, w_rest = after(a, rest, w_rest)
    inward = {d: [(3 - d, 3), (4 + d, 4)] for d in (1, 2, 3)}
    held = [lax.ppermute(rest, "tensor", inward[d]) for d in (1, 2, 3)]
    wide = [lax.ppermute(w_rest, "tensor", inward[d]) for d in (1, 2, 3)]

    a, b = hop(a, b, 3)
    x = jnp.where(low, b, a)
    rows = put(rows, x, jnp.where(low, me + 4, me - 4))

    held = after(x, *held)
    near = jnp.concatenate((rest,) + tuple(held))
    far = lax.ppermute(near, "tensor", [(3, 4), (4, 3)])

    def hop_out(x, s):
        pairs = [(j, j + 1) for j in range(s, 7)] + [(j + 1, j) for j in range(7 - s)]
        return lax.ppermute(x, "tensor", pairs)

    x = hop_out(x, 4)
    rows = put(rows, x, jnp.where(low, me + 5, me - 5))
    x = hop_out(x, 5)
    rows = put(rows, x, jnp.where(low, me + 6, me - 6))

    far, synced, *wide = after(x, far, synced, *wide)
    synced = synced.transpose(1, 0, 2, 3).reshape(1024, 512)
    wide = jnp.concatenate([w_rest] + wide, axis=1)
    near, far = dot(near, wide), dot(far, wide)
    first = jnp.where(low, near, far).reshape(4, 64, 512)[::-1].reshape(256, 512)
    both = jnp.concatenate([first, jnp.where(low, far, near)])
    middle = jnp.where((me == 3) | (me == 4), both[:, :HD], 0.0)
    for d in (1, 2, 3):
        block = both[:, HD * d : HD * d + HD].astype(jnp.bfloat16)
        middle += lax.ppermute(block, "tensor", [(3, 3 - d), (4, 4 + d)]).astype(jnp.float32)

    x = hop_out(x, 6)
    rows = put(rows, x, jnp.where(low, me + 7, me - 7))
    projected = rows[7:15].reshape(512, HD) + middle
    cosine, sine = rotary_tables(512)
    first, second = projected[:, : HD // 2], projected[:, HD // 2 :]
    key_rows = jnp.concatenate(
        [first * cosine - second * sine, second * cosine + first * sine], axis=-1
    ).astype(jnp.bfloat16)
    return (key_rows, outer_next[None], moment_next[None], synced[None])


def solution(mesh):
    fine = Mesh(mesh.devices.reshape(2, 4, 4, 2, 8), REPLICA + ("tensor",))
    in_specs = (
        P(REPLICA + ("tensor",), None),
        P(),
        P(REPLICA, None, "tensor"),
        P(REPLICA, "tensor", None, None),
        P("tensor", REPLICA, None),
        P("tensor", REPLICA, None),
    )
    out_specs = (
        P(REPLICA, "tensor"),
        P("tensor", REPLICA, None),
        P("tensor", REPLICA, None),
        P("tensor", None, None),
    )
    return jax.shard_map(body, mesh=fine, in_specs=in_specs, out_specs=out_specs, check_vma=False)
```

time: 219 us -> 199 us (0.909)
  waiting for transfers between devices: 142 us -> 54.6 us
  starting transfers between devices: 44.1 us -> 93.7 us
  matrix products: 6.25 us -> 22.8 us
  local copies, waits for them, and re-layouts: 4.01 us -> 18 us
  between operations: 14.1 us -> 1.28 us
    all_gather x1 -> x0, waiting for transfers between devices: 108 us -> none  [forward_keys(): piece = lax.all_gather(normed, 'tensor', axis=0, tiled=True)]
    ppermute x2 -> x23, starting transfers between devices: 26.3 us -> 78.6 us  [the longest x3 20.2 us: body(): held = [lax.ppermute(rest, 'tensor', inward[d]) for d in (1, 2, 3)]]
    ppermute x2 -> x23, waiting for transfers between devices: 5.31 us -> 54.2 us  [the longest x3 41.7 us: hop_out(): return lax.ppermute(x, 'tensor', pairs)]
    all_to_all x2, waiting for transfers between devices: 29.4 us -> 0.48 us  [the longest x1 0.48 us: body(): pieces = lax.all_to_all(params, PLANE, 0, 0, tiled=True)]
    dot_general x1 -> x13, matrix products: 6.25 us -> 22.8 us  [dot(): return jnp.dot(a, b, preferred_element_type=jnp.float32)]
    unnamed x9 -> x33, local copies, waits for them, and re-layouts: 0.78 us -> 9.46 us
    concatenate x0 -> x2, local copies, waits for them, and re-layouts: none -> 2.84 us  [the longest x1 1.67 us: body(): near = jnp.concatenate((rest,) + tuple(held))]
    all_to_all x2, starting transfers between devices: 17.8 us -> 15.1 us  [the longest x1 7.56 us: body(): lax.all_to_all(jnp.broadcast_to(pair[None], (32, 2, 16, 512)), PLANE, 0,...]
  transfers between devices with their start and end apart: 5 -> 25, of which waited for: 5 -> 7; matrix products, arithmetic and copies ran while one was open for 2% -> 19% of each run, Pallas kernels for 0% -> 0%
where the time goes in v2:
time: 199 us; the launch traced here: 197 us
  starting transfers between devices  93.7 us (47%)
  waiting for transfers between devices  54.6 us (27%)
  matrix products  22.8 us (11%)
  local copies, waits for them, and re-layouts  18 us (9%)
  other arithmetic  6.41 us (3%)
    ppermute x3, waiting for transfers between devices, hop_out(): return lax.ppermute(x, 'tensor', pairs)  41.7 us
    dot_general x13, matrix products, dot(): return jnp.dot(a, b, preferred_element_type=jnp.float32)  22.8 us
    ppermute x3, starting transfers between devices, body(): held = [lax.ppermute(rest, 'tensor', inward[d]) for d in (1, 2, 3)]  20.2 us
    ppermute x1, starting transfers between devices, body(): theirs = lax.ppermute(mine, 'zh', [(0, 1), (1, 0)])  15.2 us
    ppermute x1, starting transfers between devices, body(): came = lax.ppermute(other, 'zh', [(0, 1), (1, 0)])  15 us
    unnamed x33, local copies, waits for them, and re-layouts  9.46 us
    ppermute x4, waiting for transfers between devices, hop(): b = lax.ppermute(b, 'tensor', [(j + 1, j) for j in range(7 - s)])  9.09 us
    ppermute x4, starting transfers between devices, hop(): a = lax.ppermute(a, 'tensor', [(j, j + 1) for j in range(s, 7)])  7.82 us
  transfers between devices with their start and end apart: 25, of which 7 were waited for; matrix products, arithmetic and copies ran while one was open for 19% of the time, Pallas kernels for 0%

profile of v2, /device:TPU:6, one launch (start us, length us, event | category | flops | bytes accessed | tf_op | source)
XLA Modules:
  0.0 196.9 jit_solution(12302673729509379265)
XLA Ops:
  1.4 1.5 fusion
  2.9 1.6 fusion.2
  4.5 1.0 slice.64
  5.5 4.7 %collective-permute-start = (bf16[64,6144]{1,0:T(8,128)(2,1)}, bf16[64,6144]{1,0:T(8,128)(2,1)}, u32[]{:S(2)}, u32[]{:S(2)}) collective-permute-start(bf16[64,6144]{1,0:T(8,128)(2,1)} %slice.64), channel_id=1, source_target_pairs={{0,1},{1,2},{2,3},{3,4},{4,5},{5,6},{6,7},{8,9},{9,10},{10,11},{11... | collective-permute-start | bytes 2359304 | tf_op jit(solution)/shard_map/ppermute | solution.py:66
  10.2 1.3 collective-permute-start.1
  11.5 1.0 copy.30
  12.5 7.6 %all-to-all-start = ((bf16[32,2,16,512]{3,2,1,0:T(8,128)(2,1)}), bf16[32,2,16,512]{3,2,1,0:T(8,128)(2,1)S(1)}, u32[]{:S(2)}, u32[]{:S(2)}) async-start(bf16[32,2,16,512]{3,2,1,0:T(8,128)(2,1)} %copy.30), calls=%async_computation | async-start | bytes 2097152 | tf_op jit(solution)/shard_map/all_to_all | solution.py:51
  20.3 1.9 fusion.28
  23.1 3.3 %collective-permute-done = bf16[64,6144]{1,0:T(8,128)(2,1)} collective-permute-done((bf16[64,6144]{1,0:T(8,128)(2,1)}, bf16[64,6144]{1,0:T(8,128)(2,1)}, u32[]{:S(2)}, u32[]{:S(2)}) %collective-permute-start) | collective-permute-done | bytes 786464 | tf_op jit(solution)/shard_map/ppermute | solution.py:66
  26.4 1.6 collective-permute-start.2
  28.0 3.4 %collective-permute-done.1 = bf16[64,6144]{1,0:T(8,128)(2,1)} collective-permute-done((bf16[64,6144]{1,0:T(8,128)(2,1)}, bf16[64,6144]{1,0:T(8,128)(2,1)}, u32[]{:S(2)}, u32[]{:S(2)}) %collective-permute-start.1) | collective-permute-done | bytes 786464 | tf_op jit(solution)/shard_map/ppermute | solution.py:67
  31.4 1.3 collective-permute-start.3
  32.7 1.5 fusion.34
  34.9 15.0 %collective-permute-start.15 = (f32[16,512]{1,0:T(8,128)S(1)}, f32[16,512]{1,0:T(8,128)S(1)}, u32[]{:S(2)}, u32[]{:S(2)}) collective-permute-start(f32[16,512]{1,0:T(8,128)S(1)} %dynamic-slice_bitcast_fusion), channel_id=1, source_target_pairs={{0,256},{256,0},{1,257},{257,1},{2,258},{258,2},{3,259},{259,3},{4... | collective-permute-start | bytes 98312 | tf_op jit(solution)/shard_map/ppermute | solution.py:78
  49.9 2.1 %fusion.40 = f32[22,64,128]{2,1,0:T(8,128)S(1)} fusion(f32[22,64,128]{2,1,0:T(8,128)S(1)} %fusion.34, s32[]{:T(128)S(6)} %select_n.95, bf16[64,6144]{1,0:T(8,128)(2,1)} %collective-permute-done.1, bf16[1,8192,128]{2,1,0:T(8,128)(2,1)} %param.8), kind=kOutput, calls=%fused_computation.36 | convolution fusion | flops 100663296 | bytes 2392068 | tf_op jit(solution)/shard_map/dot_general | solution.py:32
  52.7 1.3 collective-permute-start.5
  54.7 15.2 %collective-permute-start.16 = (bf16[16,512]{1,0:T(8,128)(2,1)S(1)}, bf16[16,512]{1,0:T(8,128)(2,1)S(1)}, u32[]{:S(2)}, u32[]{:S(2)}) collective-permute-start(bf16[16,512]{1,0:T(8,128)(2,1)S(1)} %get-tuple-element.34), channel_id=1, source_target_pairs={{0,256},{256,0},{1,257},{257,1},{2,258},{258,2},{3,259},{259,3},{4... | collective-permute-start | bytes 49160 | tf_op jit(solution)/shard_map/ppermute | solution.py:86
  69.9 1.5 fusion.46
  71.4 1.5 fusion.52
  74.4 18.8 %collective-permute-start.13 = (bf16[64,2048]{1,0:T(8,128)(2,1)S(1)}, bf16[64,2048]{1,0:T(8,128)(2,1)}, u32[]{:S(2)}, u32[]{:S(2)}) collective-permute-start(bf16[64,2048]{1,0:T(8,128)(2,1)S(1)} %slice.66), channel_id=1, source_target_pairs={{0,3},{7,4},{8,11},{15,12},{16,19},{23,20},{24,27},{31,28},{32,35}... | collective-permute-start | bytes 786440 | tf_op jit(solution)/shard_map/ppermute | solution.py:97
  93.2 1.1 broadcast_in_dim.68
  94.3 7.6 %all-to-all-start.1 = ((bf16[32,2,16,512]{3,2,1,0:T(8,128)(2,1)}), bf16[32,2,16,512]{3,2,1,0:T(8,128)(2,1)S(1)}, u32[]{:S(2)}, u32[]{:S(2)}) async-start(bf16[32,2,16,512]{3,2,1,0:T(8,128)(2,1)} %broadcast_in_dim.68), calls=%async_computation.1 | async-start | bytes 2097152 | tf_op jit(solution)/shard_map/all_to_all | solution.py:93
  102.8 1.3 collective-permute-start.6
  104.1 2.1 %fusion.58 = f32[22,64,128]{2,1,0:T(8,128)S(1)} fusion(f32[22,64,128]{2,1,0:T(8,128)S(1)} %fusion.52, s32[]{:T(128)S(6)} %select_n.98, bf16[64,6144]{1,0:T(8,128)(2,1)} %copy-done.12, bf16[1,8192,128]{2,1,0:T(8,128)(2,1)} %param.8), kind=kOutput, calls=%fused_computation.42 | convolution fusion | flops 100663296 | bytes 2392068 | tf_op jit(solution)/shard_map/dot_general | solution.py:32
  106.2 1.5 fusion.64
  109.9 5.8 %collective-permute-start.19 = (bf16[2048,128]{1,0:T(8,128)(2,1)}, bf16[2048,128]{1,0:T(8,128)(2,1)}, u32[]{:S(2)}, u32[]{:S(2)}) collective-permute-start(bf16[2048,128]{1,0:T(8,128)(2,1)} %slice_bitcast_fusion), channel_id=1, source_target_pairs={{0,3},{7,4},{8,11},{15,12},{16,19},{23,20},{24,27},{31,28},{32,35}... | collective-permute-start | bytes 1572872 | tf_op jit(solution)/shard_map/ppermute | solution.py:98
  117.2 1.7 constant_dynamic-update-slice_fusion
  118.8 5.7 %collective-permute-done.6 = bf16[64,6144]{1,0:T(8,128)(2,1)S(1)} collective-permute-done((bf16[64,6144]{1,0:T(8,128)(2,1)}, bf16[64,6144]{1,0:T(8,128)(2,1)S(1)}, u32[]{:S(2)}, u32[]{:S(2)}) %collective-permute-start.6) | collective-permute-done | bytes 786464 | tf_op jit(solution)/shard_map/ppermute | solution.py:67
  124.5 1.6 collective-permute-start.14
  126.1 1.0 broadcast_select_fusion
  127.1 1.3 collective-permute-start.8
  128.4 1.1 constant_dynamic-update-slice_fusion.7
  129.5 2.2 %fusion.70 = f32[22,64,128]{2,1,0:T(8,128)} fusion(f32[22,64,128]{2,1,0:T(8,128)} %copy-done.1, s32[]{:T(128)S(6)} %select_n.103, bf16[64,6144]{1,0:T(8,128)(2,1)} %broadcast_select_fusion, bf16[1,8192,128]{2,1,0:T(8,128)(2,1)S(1)} %copy-done.8), kind=kOutput, calls=%fused_computation.46 | convolution fusion | flops 100663296 | bytes 2392068 | tf_op jit(solution)/shard_map/dot_general | solution.py:32
  133.3 1.2 constant_dynamic-update-slice_fusion.6
  134.5 1.2 constant_dynamic-update-slice_fusion.5
  135.7 12.4 %collective-permute-done.8 = bf16[64,6144]{1,0:T(8,128)(2,1)} collective-permute-done((bf16[64,6144]{1,0:T(8,128)(2,1)}, bf16[64,6144]{1,0:T(8,128)(2,1)}, u32[]{:S(2)}, u32[]{:S(2)}) %collective-permute-start.8) | collective-permute-done | bytes 786464 | tf_op jit(solution)/shard_map/ppermute | solution.py:110
  148.1 1.3 collective-permute-start.9
  149.4 1.2 constant_dynamic-update-slice_fusion.4
  150.5 1.3 copy-done
  151.9 2.1 %fusion.123 = f32[256,512]{0,1:T(8,128)S(1)} fusion(bf16[256,2048]{1,0:T(8,128)(2,1)} %constant_dynamic-update-slice_fusion, bf16[2048,512]{1,0:T(8,128)(2,1)S(1)} %constant_dynamic-update-slice_fusion.4), kind=kOutput, calls=%fused_computation.108 | convolution fusion | flops 536870912 | bytes 3670016 | tf_op jit(solution)/shard_map/dot_general | solution.py:32
  154.0 2.9 %broadcast_select_fusion.1 = (f32[256,512]{0,1:T(8,128)S(1)}, f32[256,512]{0,1:T(8,128)S(1)}) fusion(f32[256,512]{0,1:T(8,128)S(1)} %fusion.123, pred[]{:T(512)S(6)} %lt.50, bf16[256,2048]{1,0:T(8,128)(2,1)} %collective-permute-done.14, bf16[2048,512]{1,0:T(8,128)(2,1)} %copy-done), kind=kOutput, calls=%fused_computation.62 | convolution fusion | flops 537133056 | bytes 4718593 | tf_op jit(solution)/shard_map/dot_general | solution.py:32
  157.4 10.7 %collective-permute-done.9 = bf16[64,6144]{1,0:T(8,128)(2,1)} collective-permute-done((bf16[64,6144]{1,0:T(8,128)(2,1)}, bf16[64,6144]{1,0:T(8,128)(2,1)}, u32[]{:S(2)}, u32[]{:S(2)}) %collective-permute-start.9) | collective-permute-done | bytes 786464 | tf_op jit(solution)/shard_map/ppermute | solution.py:110
  168.1 1.3 collective-permute-start.10
  169.4 1.3 collective-permute-start.22
  172.1 1.1 copy.38
  173.2 1.5 fusion.76
  174.7 1.5 fusion.82
  176.2 18.6 %collective-permute-done.10 = bf16[64,6144]{1,0:T(8,128)(2,1)S(1)} collective-permute-done((bf16[64,6144]{1,0:T(8,128)(2,1)}, bf16[64,6144]{1,0:T(8,128)(2,1)S(1)}, u32[]{:S(2)}, u32[]{:S(2)}) %collective-permute-start.10) | collective-permute-done | bytes 786464 | tf_op jit(solution)/shard_map/ppermute | solution.py:110
  (78 shorter events, 15.0 us)
Async XLA Ops:
  2.9 8.6 %copy-start.3 = (bf16[1,1,1024,512]{3,2,1,0:T(8,128)(2,1)S(1)}, bf16[1,1,1024,512]{3,2,1,0:T(8,128)(2,1)}, u32[]{:S(2)}) copy-start(bf16[1,1,1024,512]{3,2,1,0:T(8,128)(2,1)} %param.9) | copy-start | bytes 3145732
  5.5 20.9 %collective-permute-start = (bf16[64,6144]{1,0:T(8,128)(2,1)}, bf16[64,6144]{1,0:T(8,128)(2,1)}, u32[]{:S(2)}, u32[]{:S(2)}) collective-permute-start(bf16[64,6144]{1,0:T(8,128)(2,1)} %slice.64), channel_id=1, source_target_pairs={{0,1},{1,2},{2,3},{3,4},{4,5},{5,6},{6,7},{8,9},{9,10},{10,11},{11... | collective-permute-start | bytes 2359304 | tf_op jit(solution)/shard_map/ppermute | solution.py:66
  10.2 21.2 %collective-permute-start.1 = (bf16[64,6144]{1,0:T(8,128)(2,1)}, bf16[64,6144]{1,0:T(8,128)(2,1)}, u32[]{:S(2)}, u32[]{:S(2)}) collective-permute-start(bf16[64,6144]{1,0:T(8,128)(2,1)} %slice.64), channel_id=1, source_target_pairs={{1,0},{2,1},{3,2},{4,3},{5,4},{6,5},{7,6},{9,8},{10,9},{11,10},{12... | collective-permute-start | bytes 2359304 | tf_op jit(solution)/shard_map/ppermute | solution.py:67
  12.5 22.2 %all-to-all-start = ((bf16[32,2,16,512]{3,2,1,0:T(8,128)(2,1)}), bf16[32,2,16,512]{3,2,1,0:T(8,128)(2,1)S(1)}, u32[]{:S(2)}, u32[]{:S(2)}) async-start(bf16[32,2,16,512]{3,2,1,0:T(8,128)(2,1)} %copy.30), calls=%async_computation | async-start | bytes 2097152 | tf_op jit(solution)/shard_map/all_to_all | solution.py:51
  20.2 2.1 %copy-start.6 = (bf16[1,8192,128]{2,1,0:T(8,128)(2,1)S(1)}, bf16[1,8192,128]{2,1,0:T(8,128)(2,1)}, u32[]{:S(2)}) copy-start(bf16[1,8192,128]{2,1,0:T(8,128)(2,1)} %param.8) | copy-start | bytes 6291460
  26.4 25.6 %collective-permute-start.2 = (bf16[64,6144]{1,0:T(8,128)(2,1)}, bf16[64,6144]{1,0:T(8,128)(2,1)}, u32[]{:S(2)}, u32[]{:S(2)}) collective-permute-start(bf16[64,6144]{1,0:T(8,128)(2,1)} %collective-permute-done), channel_id=1, source_target_pairs={{1,2},{2,3},{3,4},{4,5},{5,6},{6,7},{9,10},{10,11},{11,12},{12,13}... | collective-permute-start | bytes 2359304 | tf_op jit(solution)/shard_map/ppermute | solution.py:66
  31.4 21.3 %collective-permute-start.3 = (bf16[64,6144]{1,0:T(8,128)(2,1)}, bf16[64,6144]{1,0:T(8,128)(2,1)}, u32[]{:S(2)}, u32[]{:S(2)}) collective-permute-start(bf16[64,6144]{1,0:T(8,128)(2,1)} %collective-permute-done.1), channel_id=1, source_target_pairs={{1,0},{2,1},{3,2},{4,3},{5,4},{6,5},{9,8},{10,9},{11,10},{12,11},{... | collective-permute-start | bytes 2359304 | tf_op jit(solution)/shard_map/ppermute | solution.py:67
  34.2 19.8 %copy-start.10 = (f32[1,16,512]{2,1,0:T(8,128)S(1)}, f32[1,16,512]{2,1,0:T(8,128)}, u32[]{:S(2)}) copy-start(f32[1,16,512]{2,1,0:T(8,128)} %param.11) | copy-start | bytes 98308
  34.2 19.8 %copy-start.11 = (f32[1,16,512]{2,1,0:T(8,128)S(1)}, f32[1,16,512]{2,1,0:T(8,128)}, u32[]{:S(2)}) copy-start(f32[1,16,512]{2,1,0:T(8,128)} %param.10) | copy-start | bytes 98308
  34.7 35.1 %copy-start.7 = (bf16[1,8192,128]{2,1,0:T(8,128)(2,1)S(1)}, bf16[1,8192,128]{2,1,0:T(8,128)(2,1)}, u32[]{:S(2)}) copy-start(bf16[1,8192,128]{2,1,0:T(8,128)(2,1)} %param.8) | copy-start | bytes 6291460
  34.9 17.0 %collective-permute-start.15 = (f32[16,512]{1,0:T(8,128)S(1)}, f32[16,512]{1,0:T(8,128)S(1)}, u32[]{:S(2)}, u32[]{:S(2)}) collective-permute-start(f32[16,512]{1,0:T(8,128)S(1)} %dynamic-slice_bitcast_fusion), channel_id=1, source_target_pairs={{0,256},{256,0},{1,257},{257,1},{2,258},{258,2},{3,259},{259,3},{4... | collective-permute-start | bytes 98312 | tf_op jit(solution)/shard_map/ppermute | solution.py:78
  52.0 21.0 %collective-permute-start.4 = (bf16[64,6144]{1,0:T(8,128)(2,1)}, bf16[64,6144]{1,0:T(8,128)(2,1)S(1)}, u32[]{:S(2)}, u32[]{:S(2)}) collective-permute-start(bf16[64,6144]{1,0:T(8,128)(2,1)} %collective-permute-done.2), channel_id=1, source_target_pairs={{2,3},{3,4},{4,5},{5,6},{6,7},{10,11},{11,12},{12,13},{13,14},{14,... | collective-permute-start | bytes 2359304 | tf_op jit(solution)/shard_map/ppermute | solution.py:66
  52.7 50.1 %collective-permute-start.5 = (bf16[64,6144]{1,0:T(8,128)(2,1)}, bf16[64,6144]{1,0:T(8,128)(2,1)}, u32[]{:S(2)}, u32[]{:S(2)}) collective-permute-start(bf16[64,6144]{1,0:T(8,128)(2,1)} %collective-permute-done.3), channel_id=1, source_target_pairs={{1,0},{2,1},{3,2},{4,3},{5,4},{9,8},{10,9},{11,10},{12,11},{13,12}... | collective-permute-start | bytes 2359304 | tf_op jit(solution)/shard_map/ppermute | solution.py:67
  54.7 38.5 %collective-permute-start.16 = (bf16[16,512]{1,0:T(8,128)(2,1)S(1)}, bf16[16,512]{1,0:T(8,128)(2,1)S(1)}, u32[]{:S(2)}, u32[]{:S(2)}) collective-permute-start(bf16[16,512]{1,0:T(8,128)(2,1)S(1)} %get-tuple-element.34), channel_id=1, source_target_pairs={{0,256},{256,0},{1,257},{257,1},{2,258},{258,2},{3,259},{259,3},{4... | collective-permute-start | bytes 49160 | tf_op jit(solution)/shard_map/ppermute | solution.py:86
  73.0 21.3 %copy-start.12 = (bf16[64,6144]{1,0:T(8,128)(2,1)}, bf16[64,6144]{1,0:T(8,128)(2,1)S(1)}, u32[]{:S(2)}) copy-start(bf16[64,6144]{1,0:T(8,128)(2,1)S(1)} %collective-permute-done.4) | copy-start | bytes 2359300
  73.0 35.5 %collective-permute-start.11 = (bf16[64,2048]{1,0:T(8,128)(2,1)S(1)}, bf16[64,2048]{1,0:T(8,128)(2,1)S(1)}, u32[]{:S(2)}, u32[]{:S(2)}) collective-permute-start(bf16[64,2048]{1,0:T(8,128)(2,1)S(1)} %slice.66), channel_id=1, source_target_pairs={{2,3},{5,4},{10,11},{13,12},{18,19},{21,20},{26,27},{29,28},{34,35... | collective-permute-start | bytes 786440 | tf_op jit(solution)/shard_map/ppermute | solution.py:97
  73.7 35.5 %collective-permute-start.12 = (bf16[64,2048]{1,0:T(8,128)(2,1)S(1)}, bf16[64,2048]{1,0:T(8,128)(2,1)S(1)}, u32[]{:S(2)}, u32[]{:S(2)}) collective-permute-start(bf16[64,2048]{1,0:T(8,128)(2,1)S(1)} %slice.66), channel_id=1, source_target_pairs={{1,3},{6,4},{9,11},{14,12},{17,19},{22,20},{25,27},{30,28},{33,35}... | collective-permute-start | bytes 786440 | tf_op jit(solution)/shard_map/ppermute | solution.py:97
  74.4 35.5 %collective-permute-start.13 = (bf16[64,2048]{1,0:T(8,128)(2,1)S(1)}, bf16[64,2048]{1,0:T(8,128)(2,1)}, u32[]{:S(2)}, u32[]{:S(2)}) collective-permute-start(bf16[64,2048]{1,0:T(8,128)(2,1)S(1)} %slice.66), channel_id=1, source_target_pairs={{0,3},{7,4},{8,11},{15,12},{16,19},{23,20},{24,27},{31,28},{32,35}... | collective-permute-start | bytes 786440 | tf_op jit(solution)/shard_map/ppermute | solution.py:97
  94.3 39.0 %all-to-all-start.1 = ((bf16[32,2,16,512]{3,2,1,0:T(8,128)(2,1)}), bf16[32,2,16,512]{3,2,1,0:T(8,128)(2,1)S(1)}, u32[]{:S(2)}, u32[]{:S(2)}) async-start(bf16[32,2,16,512]{3,2,1,0:T(8,128)(2,1)} %broadcast_in_dim.68), calls=%async_computation.1 | async-start | bytes 2097152 | tf_op jit(solution)/shard_map/all_to_all | solution.py:93
  101.9 4.2 %copy-start.8 = (bf16[1,8192,128]{2,1,0:T(8,128)(2,1)S(1)}, bf16[1,8192,128]{2,1,0:T(8,128)(2,1)}, u32[]{:S(2)}) copy-start(bf16[1,8192,128]{2,1,0:T(8,128)(2,1)} %param.8) | copy-start | bytes 6291460
  101.9 24.2 %collective-permute-start.7 = (bf16[64,6144]{1,0:T(8,128)(2,1)}, bf16[64,6144]{1,0:T(8,128)(2,1)S(1)}, u32[]{:S(2)}, u32[]{:S(2)}) collective-permute-start(bf16[64,6144]{1,0:T(8,128)(2,1)} %copy-done.12), channel_id=1, source_target_pairs={{3,4},{4,5},{5,6},{6,7},{11,12},{12,13},{13,14},{14,15},{19,20},{2... | collective-permute-start | bytes 2359304 | tf_op jit(solution)/shard_map/ppermute | solution.py:66
  102.8 21.7 %collective-permute-start.6 = (bf16[64,6144]{1,0:T(8,128)(2,1)}, bf16[64,6144]{1,0:T(8,128)(2,1)S(1)}, u32[]{:S(2)}, u32[]{:S(2)}) collective-permute-start(bf16[64,6144]{1,0:T(8,128)(2,1)} %collective-permute-done.5), channel_id=1, source_target_pairs={{1,0},{2,1},{3,2},{4,3},{9,8},{10,9},{11,10},{12,11},{17,16},{18,1... | collective-permute-start | bytes 2359304 | tf_op jit(solution)/shard_map/ppermute | solution.py:67
  107.7 19.4 %copy-start.1 = (f32[22,64,128]{2,1,0:T(8,128)}, f32[22,64,128]{2,1,0:T(8,128)S(1)}, u32[]{:S(2)}) copy-start(f32[22,64,128]{2,1,0:T(8,128)S(1)} %fusion.64) | copy-start | bytes 2162692
  108.5 23.2 %collective-permute-start.17 = (bf16[2048,128]{1,0:T(8,128)(2,1)}, bf16[2048,128]{1,0:T(8,128)(2,1)S(1)}, u32[]{:S(2)}, u32[]{:S(2)}) collective-permute-start(bf16[2048,128]{1,0:T(8,128)(2,1)} %slice_bitcast_fusion), channel_id=1, source_target_pairs={{2,3},{5,4},{10,11},{13,12},{18,19},{21,20},{26,27},{29,28},{34,35... | collective-permute-start | bytes 1572872 | tf_op jit(solution)/shard_map/ppermute | solution.py:98
  109.2 22.5 %collective-permute-start.18 = (bf16[2048,128]{1,0:T(8,128)(2,1)}, bf16[2048,128]{1,0:T(8,128)(2,1)S(1)}, u32[]{:S(2)}, u32[]{:S(2)}) collective-permute-start(bf16[2048,128]{1,0:T(8,128)(2,1)} %slice_bitcast_fusion), channel_id=1, source_target_pairs={{1,3},{6,4},{9,11},{14,12},{17,19},{22,20},{25,27},{30,28},{33,35}... | collective-permute-start | bytes 1572872 | tf_op jit(solution)/shard_map/ppermute | solution.py:98
  109.9 23.4 %collective-permute-start.19 = (bf16[2048,128]{1,0:T(8,128)(2,1)}, bf16[2048,128]{1,0:T(8,128)(2,1)}, u32[]{:S(2)}, u32[]{:S(2)}) collective-permute-start(bf16[2048,128]{1,0:T(8,128)(2,1)} %slice_bitcast_fusion), channel_id=1, source_target_pairs={{0,3},{7,4},{8,11},{15,12},{16,19},{23,20},{24,27},{31,28},{32,35}... | collective-permute-start | bytes 1572872 | tf_op jit(solution)/shard_map/ppermute | solution.py:98
  124.5 8.8 %collective-permute-start.14 = (bf16[256,2048]{1,0:T(8,128)(2,1)}, bf16[256,2048]{1,0:T(8,128)(2,1)}, u32[]{:S(2)}, u32[]{:S(2)}) collective-permute-start(bf16[256,2048]{1,0:T(8,128)(2,1)} %constant_dynamic-update-slice_fusion), channel_id=1, source_target_pairs={{3,4},{4,3},{11,12},{12,11},{19,20},{20,19},{27,28},{28,27},{35,36... | collective-permute-start | bytes 3145736 | tf_op jit(solution)/shard_map/ppermute | solution.py:106
  127.1 21.0 %collective-permute-start.8 = (bf16[64,6144]{1,0:T(8,128)(2,1)}, bf16[64,6144]{1,0:T(8,128)(2,1)}, u32[]{:S(2)}, u32[]{:S(2)}) collective-permute-start(bf16[64,6144]{1,0:T(8,128)(2,1)} %broadcast_select_fusion), channel_id=1, source_target_pairs={{4,5},{5,6},{6,7},{1,0},{2,1},{3,2},{12,13},{13,14},{14,15},{9,8},... | collective-permute-start | bytes 2359304 | tf_op jit(solution)/shard_map/ppermute | solution.py:110
  131.7 0.8 copy-start.4
  132.5 0.8 copy-start.5
  148.1 20.0 %collective-permute-start.9 = (bf16[64,6144]{1,0:T(8,128)(2,1)}, bf16[64,6144]{1,0:T(8,128)(2,1)}, u32[]{:S(2)}, u32[]{:S(2)}) collective-permute-start(bf16[64,6144]{1,0:T(8,128)(2,1)} %collective-permute-done.8), channel_id=1, source_target_pairs={{5,6},{6,7},{1,0},{2,1},{13,14},{14,15},{9,8},{10,9},{21,22},{22,2... | collective-permute-start | bytes 2359304 | tf_op jit(solution)/shard_map/ppermute | solution.py:110
  150.5 1.4 copy-start
  157.4 15.8 %copy-start.2 = (f32[22,64,128]{2,1,0:T(8,128)S(1)}, f32[22,64,128]{2,1,0:T(8,128)}, u32[]{:S(2)}) copy-start(f32[22,64,128]{2,1,0:T(8,128)} %fusion.70) | copy-start | bytes 2162692
  157.4 15.8 %copy-start.9 = (bf16[1,8192,128]{2,1,0:T(8,128)(2,1)S(1)}, bf16[1,8192,128]{2,1,0:T(8,128)(2,1)}, u32[]{:S(2)}) copy-start(bf16[1,8192,128]{2,1,0:T(8,128)(2,1)} %param.8) | copy-start | bytes 6291460
  168.1 26.7 %collective-permute-start.10 = (bf16[64,6144]{1,0:T(8,128)(2,1)}, bf16[64,6144]{1,0:T(8,128)(2,1)S(1)}, u32[]{:S(2)}, u32[]{:S(2)}) collective-permute-start(bf16[64,6144]{1,0:T(8,128)(2,1)} %collective-permute-done.9), channel_id=1, source_target_pairs={{6,7},{1,0},{14,15},{9,8},{22,23},{17,16},{30,31},{25,24},{38,39},... | collective-permute-start | bytes 2359304 | tf_op jit(solution)/shard_map/ppermute | solution.py:110
  169.4 26.0 %collective-permute-start.22 = (bf16[512,128]{0,1:T(8,128)(2,1)S(1)}, bf16[512,128]{0,1:T(8,128)(2,1)S(1)}, u32[]{:S(2)}, u32[]{:S(2)}) collective-permute-start(bf16[512,128]{0,1:T(8,128)(2,1)S(1)} %get-tuple-element.39), channel_id=1, source_target_pairs={{3,0},{4,7},{11,8},{12,15},{19,16},{20,23},{27,24},{28,31},{35,32}... | collective-permute-start | bytes 393224 | tf_op jit(solution)/shard_map/ppermute | solution.py:126
  170.7 24.7 %collective-permute-start.21 = (bf16[512,128]{0,1:T(8,128)(2,1)S(1)}, bf16[512,128]{0,1:T(8,128)(2,1)S(1)}, u32[]{:S(2)}, u32[]{:S(2)}) collective-permute-start(bf16[512,128]{0,1:T(8,128)(2,1)S(1)} %get-tuple-element.40), channel_id=1, source_target_pairs={{3,1},{4,6},{11,9},{12,14},{19,17},{20,22},{27,25},{28,30},{35,33}... | collective-permute-start | bytes 393224 | tf_op jit(solution)/shard_map/ppermute | solution.py:126
  171.4 24.0 %collective-permute-start.20 = (bf16[512,128]{0,1:T(8,128)(2,1)S(1)}, bf16[512,128]{0,1:T(8,128)(2,1)S(1)}, u32[]{:S(2)}, u32[]{:S(2)}) collective-permute-start(bf16[512,128]{0,1:T(8,128)(2,1)S(1)} %get-tuple-element.38), channel_id=1, source_target_pairs={{3,2},{4,5},{11,10},{12,13},{19,18},{20,21},{27,26},{28,29},{35,34... | collective-permute-start | bytes 393224 | tf_op jit(solution)/shard_map/ppermute | solution.py:126

commit v3 on v2

--- a/solution.py
+++ b/solution.py
@@ -88,20 +88,16 @@
     a, b = hop(a, b, 2)
     rows = put(put(rows, a, me - 3), b, me + 3)
 
-    (theirs,) = after(a, theirs)
-    pair = jnp.where(zh == 0, jnp.stack([mine, theirs]), jnp.stack([theirs, mine]))
-    synced = lax.all_to_all(jnp.broadcast_to(pair[None], (32, 2, 16, 512)), PLANE, 0, 0, tiled=True)
-
-    rest, w_rest = after(a, rest, w_rest)
+    rows, rest, w_rest, theirs = lax.optimization_barrier((rows, rest, w_rest, theirs))
     inward = {d: [(3 - d, 3), (4 + d, 4)] for d in (1, 2, 3)}
     held = [lax.ppermute(rest, "tensor", inward[d]) for d in (1, 2, 3)]
     wide = [lax.ppermute(w_rest, "tensor", inward[d]) for d in (1, 2, 3)]
 
     a, b = hop(a, b, 3)
     x = jnp.where(low, b, a)
+    x, *held = lax.optimization_barrier((x, *held))
     rows = put(rows, x, jnp.where(low, me + 4, me - 4))
-
-    held = after(x, *held)
+    pair = jnp.where(zh == 0, jnp.stack([mine, theirs]), jnp.stack([theirs, mine]))
     near = jnp.concatenate((rest,) + tuple(held))
     far = lax.ppermute(near, "tensor", [(3, 4), (4, 3)])
 
@@ -109,12 +105,14 @@
         pairs = [(j, j + 1) for j in range(s, 7)] + [(j + 1, j) for j in range(7 - s)]
         return lax.ppermute(x, "tensor", pairs)
 
+    synced = lax.all_to_all(jnp.broadcast_to(pair[None], (32, 2, 16, 512)), PLANE, 0, 0, tiled=True)
+
     x = hop_out(x, 4)
     rows = put(rows, x, jnp.where(low, me + 5, me - 5))
     x = hop_out(x, 5)
     rows = put(rows, x, jnp.where(low, me + 6, me - 6))
 
-    far, synced, *wide = after(x, far, synced, *wide)
+    rows, far, synced, *wide = lax.optimization_barrier((rows, far, synced, *wide))
     synced = synced.transpose(1, 0, 2, 3).reshape(1024, 512)
     wide = jnp.concatenate([w_rest] + wide, axis=1)
     near, far = dot(near, wide), dot(far, wide)

time: 199 us -> 205 us (1.030)
  starting transfers between devices: 93.7 us -> 109 us
  waiting for transfers between devices: 54.6 us -> 50.8 us
  matrix products: 22.8 us -> 20.7 us
  local copies, waits for them, and re-layouts: 18 us -> 15.9 us
    ppermute x3, starting transfers between devices: 7.21 us -> 27.6 us  [body(): wide = [lax.ppermute(w_rest, 'tensor', inward[d]) for d in (1, 2, 3)]]
    ppermute x3, waiting for transfers between devices: 41.7 us -> 29.6 us  [hop_out(): return lax.ppermute(x, 'tensor', pairs)]
    ppermute x4, waiting for transfers between devices: 9.09 us -> 17.4 us  [hop(): b = lax.ppermute(b, 'tensor', [(j + 1, j) for j in range(7 - s)])]
    ppermute x3, starting transfers between devices: 20.2 us -> 16.4 us  [body(): held = [lax.ppermute(rest, 'tensor', inward[d]) for d in (1, 2, 3)]]
    dot_general x13, matrix products: 22.8 us -> 20.7 us  [dot(): return jnp.dot(a, b, preferred_element_type=jnp.float32)]
    unnamed x33, local copies, waits for them, and re-layouts: 9.46 us -> 7.34 us
  transfers between devices with their start and end apart: 25 -> 25, of which waited for: 7 -> 8; matrix products, arithmetic and copies ran while one was open for 19% -> 15% of each run, Pallas kernels for 0% -> 0%
where the time goes in v3:
time: 205 us; the launch traced here: 203 us
  starting transfers between devices  109 us (53%)
  waiting for transfers between devices  50.8 us (25%)
  matrix products  20.7 us (10%)
  local copies, waits for them, and re-layouts  15.9 us (8%)
  other arithmetic  5.49 us (3%)
    ppermute x3, waiting for transfers between devices, hop_out(): return lax.ppermute(x, 'tensor', pairs)  29.6 us
    ppermute x3, starting transfers between devices, body(): wide = [lax.ppermute(w_rest, 'tensor', inward[d]) for d in (1, 2, 3)]  27.6 us
    dot_general x13, matrix products, dot(): return jnp.dot(a, b, preferred_element_type=jnp.float32)  20.7 us
    ppermute x4, waiting for transfers between devices, hop(): b = lax.ppermute(b, 'tensor', [(j + 1, j) for j in range(7 - s)])  17.4 us
    ppermute x3, starting transfers between devices, body(): held = [lax.ppermute(rest, 'tensor', inward[d]) for d in (1, 2, 3)]  16.4 us
    ppermute x1, starting transfers between devices, body(): theirs = lax.ppermute(mine, 'zh', [(0, 1), (1, 0)])  15.2 us
    ppermute x1, starting transfers between devices, body(): came = lax.ppermute(other, 'zh', [(0, 1), (1, 0)])  15 us
    all_to_all x1, starting transfers between devices, body(): pieces = lax.all_to_all(params, PLANE, 0, 0, tiled=True)  7.56 us
  transfers between devices with their start and end apart: 25, of which 8 were waited for; matrix products, arithmetic and copies ran while one was open for 15% of the time, Pallas kernels for 0%

profile of v3, /device:TPU:6, one launch (start us, length us, event | category | flops | bytes accessed | tf_op | source)
XLA Modules:
  0.0 203.5 jit_solution(3304174003972434172)
XLA Ops:
  1.4 1.5 fusion
  2.9 1.6 fusion.2
  4.5 0.9 slice.57
  5.5 4.7 %collective-permute-start = (bf16[64,6144]{1,0:T(8,128)(2,1)}, bf16[64,6144]{1,0:T(8,128)(2,1)}, u32[]{:S(2)}, u32[]{:S(2)}) collective-permute-start(bf16[64,6144]{1,0:T(8,128)(2,1)} %slice.57), channel_id=1, source_target_pairs={{0,1},{1,2},{2,3},{3,4},{4,5},{5,6},{6,7},{8,9},{9,10},{10,11},{11... | collective-permute-start | bytes 2359304 | tf_op jit(solution)/shard_map/ppermute | solution.py:66
  10.2 1.3 collective-permute-start.1
  11.5 1.0 copy.30
  12.5 7.6 %all-to-all-start = ((bf16[32,2,16,512]{3,2,1,0:T(8,128)(2,1)}), bf16[32,2,16,512]{3,2,1,0:T(8,128)(2,1)S(1)}, u32[]{:S(2)}, u32[]{:S(2)}) async-start(bf16[32,2,16,512]{3,2,1,0:T(8,128)(2,1)} %copy.30), calls=%async_computation | async-start | bytes 2097152 | tf_op jit(solution)/shard_map/all_to_all | solution.py:51
  20.3 1.9 fusion.28
  22.2 0.9 slice_bitcast_fusion
  23.1 3.3 %collective-permute-done = bf16[64,6144]{1,0:T(8,128)(2,1)} collective-permute-done((bf16[64,6144]{1,0:T(8,128)(2,1)}, bf16[64,6144]{1,0:T(8,128)(2,1)}, u32[]{:S(2)}, u32[]{:S(2)}) %collective-permute-start) | collective-permute-done | bytes 786464 | tf_op jit(solution)/shard_map/ppermute | solution.py:66
  27.1 4.3 %collective-permute-done.1 = bf16[64,6144]{1,0:T(8,128)(2,1)} collective-permute-done((bf16[64,6144]{1,0:T(8,128)(2,1)}, bf16[64,6144]{1,0:T(8,128)(2,1)}, u32[]{:S(2)}, u32[]{:S(2)}) %collective-permute-start.1) | collective-permute-done | bytes 786464 | tf_op jit(solution)/shard_map/ppermute | solution.py:67
  31.4 1.3 collective-permute-start.3
  32.7 1.5 fusion.34
  34.9 15.0 %collective-permute-start.6 = (f32[16,512]{1,0:T(8,128)S(1)}, f32[16,512]{1,0:T(8,128)S(1)}, u32[]{:S(2)}, u32[]{:S(2)}) collective-permute-start(f32[16,512]{1,0:T(8,128)S(1)} %dynamic-slice_bitcast_fusion), channel_id=1, source_target_pairs={{0,256},{256,0},{1,257},{257,1},{2,258},{258,2},{3,259},{259,3},{4... | collective-permute-start | bytes 98312 | tf_op jit(solution)/shard_map/ppermute | solution.py:78
  49.9 2.1 %fusion.40 = f32[22,64,128]{2,1,0:T(8,128)S(1)} fusion(f32[22,64,128]{2,1,0:T(8,128)S(1)} %fusion.34, s32[]{:T(128)S(6)} %select_n.95, bf16[64,6144]{1,0:T(8,128)(2,1)} %collective-permute-done.1, bf16[1,8192,128]{2,1,0:T(8,128)(2,1)} %param.8), kind=kOutput, calls=%fused_computation.36 | convolution fusion | flops 100663296 | bytes 2392068 | tf_op jit(solution)/shard_map/dot_general | solution.py:32
  52.7 1.3 collective-permute-start.5
  54.6 15.2 %collective-permute-start.7 = (bf16[16,512]{1,0:T(8,128)(2,1)S(1)}, bf16[16,512]{1,0:T(8,128)(2,1)S(1)}, u32[]{:S(2)}, u32[]{:S(2)}) collective-permute-start(bf16[16,512]{1,0:T(8,128)(2,1)S(1)} %get-tuple-element.40), channel_id=1, source_target_pairs={{0,256},{256,0},{1,257},{257,1},{2,258},{258,2},{3,259},{259,3},{4... | collective-permute-start | bytes 49160 | tf_op jit(solution)/shard_map/ppermute | solution.py:86
  70.3 1.5 fusion.52
  71.8 12.6 %collective-permute-done.5 = bf16[64,6144]{1,0:T(8,128)(2,1)S(1)} collective-permute-done((bf16[64,6144]{1,0:T(8,128)(2,1)}, bf16[64,6144]{1,0:T(8,128)(2,1)S(1)}, u32[]{:S(2)}, u32[]{:S(2)}) %collective-permute-start.5) | collective-permute-done | bytes 786464 | tf_op jit(solution)/shard_map/ppermute | solution.py:67
  84.4 1.3 collective-permute-start.8
  88.6 15.0 %collective-permute-start.12 = (bf16[64,2048]{1,0:T(8,128)(2,1)S(1)}, bf16[64,2048]{1,0:T(8,128)(2,1)S(1)}, u32[]{:S(2)}, u32[]{:S(2)}) collective-permute-start(bf16[64,2048]{1,0:T(8,128)(2,1)S(1)} %slice.58), channel_id=1, source_target_pairs={{0,3},{7,4},{8,11},{15,12},{16,19},{23,20},{24,27},{31,28},{32,35}... | collective-permute-start | bytes 786440 | tf_op jit(solution)/shard_map/ppermute | solution.py:93
  104.9 1.5 collective-permute-start.16
  106.4 1.5 collective-permute-start.17
  108.0 24.7 %collective-permute-start.18 = (bf16[2048,128]{1,0:T(8,128)(2,1)}, bf16[2048,128]{1,0:T(8,128)(2,1)}, u32[]{:S(2)}, u32[]{:S(2)}) collective-permute-start(bf16[2048,128]{1,0:T(8,128)(2,1)} %slice_bitcast_fusion), channel_id=1, source_target_pairs={{0,3},{7,4},{8,11},{15,12},{16,19},{23,20},{24,27},{31,28},{32,35}... | collective-permute-start | bytes 1572872 | tf_op jit(solution)/shard_map/ppermute | solution.py:94
  133.4 1.3 collective-permute-start.13
  134.7 1.1 broadcast_in_dim.67
  135.8 7.4 %all-to-all-start.1 = ((bf16[32,2,16,512]{3,2,1,0:T(8,128)(2,1)}), bf16[32,2,16,512]{3,2,1,0:T(8,128)(2,1)S(1)}, u32[]{:S(2)}, u32[]{:S(2)}) async-start(bf16[32,2,16,512]{3,2,1,0:T(8,128)(2,1)} %broadcast_in_dim.67), calls=%async_computation.1 | async-start | bytes 2097152 | tf_op jit(solution)/shard_map/all_to_all | solution.py:108
  143.2 0.7 constant_dynamic-update-slice_fusion.2
  145.4 1.6 collective-permute-start.15
  147.0 2.9 %collective-permute-done.13 = bf16[64,6144]{1,0:T(8,128)(2,1)} collective-permute-done((bf16[64,6144]{1,0:T(8,128)(2,1)S(1)}, bf16[64,6144]{1,0:T(8,128)(2,1)}, u32[]{:S(2)}, u32[]{:S(2)}) %collective-permute-start.13) | collective-permute-done | bytes 786464 | tf_op jit(solution)/shard_map/ppermute | solution.py:106
  149.9 1.3 collective-permute-start.14
  151.2 1.1 constant_dynamic-update-slice_fusion.7
  152.4 2.2 %fusion.70 = f32[22,64,128]{2,1,0:T(8,128)} fusion(f32[22,64,128]{2,1,0:T(8,128)} %copy-done.1, s32[]{:T(128)S(6)} %select_n.105, bf16[64,6144]{1,0:T(8,128)(2,1)} %copy-done.3, bf16[1,8192,128]{2,1,0:T(8,128)(2,1)S(1)} %copy-done.8), kind=kOutput, calls=%fused_computation.46 | convolution fusion | flops 100663296 | bytes 2392068 | tf_op jit(solution)/shard_map/dot_general | solution.py:32
  154.5 2.1 %fusion.76 = f32[22,64,128]{2,1,0:T(8,128)} fusion(f32[22,64,128]{2,1,0:T(8,128)} %fusion.70, s32[]{:T(128)S(6)} %select_n.107, bf16[64,6144]{1,0:T(8,128)(2,1)} %collective-permute-done.13, bf16[1,8192,128]{2,1,0:T(8,128)(2,1)S(1)} %copy-done.8), kind=kOutput, calls=%fused_computation.48 | convolution fusion | flops 100663296 | bytes 2392068 | tf_op jit(solution)/shard_map/dot_general | solution.py:32
  156.7 13.1 %collective-permute-done.14 = bf16[64,6144]{1,0:T(8,128)(2,1)} collective-permute-done((bf16[64,6144]{1,0:T(8,128)(2,1)}, bf16[64,6144]{1,0:T(8,128)(2,1)}, u32[]{:S(2)}, u32[]{:S(2)}) %collective-permute-start.14) | collective-permute-done | bytes 786464 | tf_op jit(solution)/shard_map/ppermute | solution.py:106
  169.8 2.1 %fusion.82 = f32[22,64,128]{2,1,0:T(8,128)} fusion(f32[22,64,128]{2,1,0:T(8,128)} %fusion.76, s32[]{:T(128)S(6)} %select_n.109, bf16[64,6144]{1,0:T(8,128)(2,1)} %collective-permute-done.14, bf16[1,8192,128]{2,1,0:T(8,128)(2,1)S(1)} %copy-done.8), kind=kOutput, calls=%fused_computation.50 | convolution fusion | flops 100663296 | bytes 2392068 | tf_op jit(solution)/shard_map/dot_general | solution.py:32
  171.9 1.3 constant_dynamic-update-slice_fusion.6
  173.2 1.2 constant_dynamic-update-slice_fusion.5
  174.4 1.2 constant_dynamic-update-slice_fusion.4
  175.6 1.3 collective-permute-start.19
  176.9 1.0 fusion.123
  177.9 2.9 %broadcast_select_fusion.1 = (f32[256,512]{0,1:T(8,128)S(1)}, f32[256,512]{0,1:T(8,128)S(1)}) fusion(f32[256,512]{0,1:T(8,128)S(1)} %fusion.123, pred[]{:T(512)S(6)} %lt.52, bf16[256,2048]{1,0:T(8,128)(2,1)} %collective-permute-done.15, bf16[2048,512]{1,0:T(8,128)(2,1)} %copy-done), kind=kOutput, calls=%fused_computation.62 | convolution fusion | flops 537133056 | bytes 4718593 | tf_op jit(solution)/shard_map/dot_general | solution.py:32
  181.3 1.4 collective-permute-start.22
  184.1 1.1 copy.38
  185.1 13.6 %collective-permute-done.19 = bf16[64,6144]{1,0:T(8,128)(2,1)} collective-permute-done((bf16[64,6144]{1,0:T(8,128)(2,1)}, bf16[64,6144]{1,0:T(8,128)(2,1)}, u32[]{:S(2)}, u32[]{:S(2)}) %collective-permute-start.19) | collective-permute-done | bytes 786464 | tf_op jit(solution)/shard_map/ppermute | solution.py:106
  198.7 2.2 %fusion.88 = f32[22,64,128]{2,1,0:T(8,128)} fusion(f32[22,64,128]{2,1,0:T(8,128)} %fusion.82, s32[]{:T(128)S(6)} %select_n.113, bf16[64,6144]{1,0:T(8,128)(2,1)} %collective-permute-done.19, bf16[1,8192,128]{2,1,0:T(8,128)(2,1)S(1)} %copy-done.9), kind=kOutput, calls=%fused_computation.52 | convolution fusion | flops 100663296 | bytes 2392068 | tf_op jit(solution)/shard_map/dot_general | solution.py:32
  200.9 1.0 slice.59
  202.7 0.8 copy.39
  (78 shorter events, 13.2 us)
Async XLA Ops:
  2.9 8.6 %copy-start.2 = (bf16[1,1,1024,512]{3,2,1,0:T(8,128)(2,1)S(1)}, bf16[1,1,1024,512]{3,2,1,0:T(8,128)(2,1)}, u32[]{:S(2)}) copy-start(bf16[1,1,1024,512]{3,2,1,0:T(8,128)(2,1)} %param.9) | copy-start | bytes 3145732
  5.5 20.9 %collective-permute-start = (bf16[64,6144]{1,0:T(8,128)(2,1)}, bf16[64,6144]{1,0:T(8,128)(2,1)}, u32[]{:S(2)}, u32[]{:S(2)}) collective-permute-start(bf16[64,6144]{1,0:T(8,128)(2,1)} %slice.57), channel_id=1, source_target_pairs={{0,1},{1,2},{2,3},{3,4},{4,5},{5,6},{6,7},{8,9},{9,10},{10,11},{11... | collective-permute-start | bytes 2359304 | tf_op jit(solution)/shard_map/ppermute | solution.py:66
  10.2 21.2 %collective-permute-start.1 = (bf16[64,6144]{1,0:T(8,128)(2,1)}, bf16[64,6144]{1,0:T(8,128)(2,1)}, u32[]{:S(2)}, u32[]{:S(2)}) collective-permute-start(bf16[64,6144]{1,0:T(8,128)(2,1)} %slice.57), channel_id=1, source_target_pairs={{1,0},{2,1},{3,2},{4,3},{5,4},{6,5},{7,6},{9,8},{10,9},{11,10},{12... | collective-permute-start | bytes 2359304 | tf_op jit(solution)/shard_map/ppermute | solution.py:67
  12.5 22.2 %all-to-all-start = ((bf16[32,2,16,512]{3,2,1,0:T(8,128)(2,1)}), bf16[32,2,16,512]{3,2,1,0:T(8,128)(2,1)S(1)}, u32[]{:S(2)}, u32[]{:S(2)}) async-start(bf16[32,2,16,512]{3,2,1,0:T(8,128)(2,1)} %copy.30), calls=%async_computation | async-start | bytes 2097152 | tf_op jit(solution)/shard_map/all_to_all | solution.py:51
  20.2 2.1 %copy-start.6 = (bf16[1,8192,128]{2,1,0:T(8,128)(2,1)S(1)}, bf16[1,8192,128]{2,1,0:T(8,128)(2,1)}, u32[]{:S(2)}) copy-start(bf16[1,8192,128]{2,1,0:T(8,128)(2,1)} %param.8) | copy-start | bytes 6291460
  26.4 25.6 %collective-permute-start.2 = (bf16[64,6144]{1,0:T(8,128)(2,1)}, bf16[64,6144]{1,0:T(8,128)(2,1)S(1)}, u32[]{:S(2)}, u32[]{:S(2)}) collective-permute-start(bf16[64,6144]{1,0:T(8,128)(2,1)} %collective-permute-done), channel_id=1, source_target_pairs={{1,2},{2,3},{3,4},{4,5},{5,6},{6,7},{9,10},{10,11},{11,12},{12,13}... | collective-permute-start | bytes 2359304 | tf_op jit(solution)/shard_map/ppermute | solution.py:66
  31.4 21.3 %collective-permute-start.3 = (bf16[64,6144]{1,0:T(8,128)(2,1)}, bf16[64,6144]{1,0:T(8,128)(2,1)}, u32[]{:S(2)}, u32[]{:S(2)}) collective-permute-start(bf16[64,6144]{1,0:T(8,128)(2,1)} %collective-permute-done.1), channel_id=1, source_target_pairs={{1,0},{2,1},{3,2},{4,3},{5,4},{6,5},{9,8},{10,9},{11,10},{12,11},{... | collective-permute-start | bytes 2359304 | tf_op jit(solution)/shard_map/ppermute | solution.py:67
  34.2 19.8 %copy-start.11 = (f32[1,16,512]{2,1,0:T(8,128)S(1)}, f32[1,16,512]{2,1,0:T(8,128)}, u32[]{:S(2)}) copy-start(f32[1,16,512]{2,1,0:T(8,128)} %param.11) | copy-start | bytes 98308
  34.2 19.8 %copy-start.12 = (f32[1,16,512]{2,1,0:T(8,128)S(1)}, f32[1,16,512]{2,1,0:T(8,128)}, u32[]{:S(2)}) copy-start(f32[1,16,512]{2,1,0:T(8,128)} %param.10) | copy-start | bytes 98308
  34.7 35.1 %copy-start.7 = (bf16[1,8192,128]{2,1,0:T(8,128)(2,1)S(1)}, bf16[1,8192,128]{2,1,0:T(8,128)(2,1)}, u32[]{:S(2)}) copy-start(bf16[1,8192,128]{2,1,0:T(8,128)(2,1)} %param.8) | copy-start | bytes 6291460
  34.9 17.0 %collective-permute-start.6 = (f32[16,512]{1,0:T(8,128)S(1)}, f32[16,512]{1,0:T(8,128)S(1)}, u32[]{:S(2)}, u32[]{:S(2)}) collective-permute-start(f32[16,512]{1,0:T(8,128)S(1)} %dynamic-slice_bitcast_fusion), channel_id=1, source_target_pairs={{0,256},{256,0},{1,257},{257,1},{2,258},{258,2},{3,259},{259,3},{4... | collective-permute-start | bytes 98312 | tf_op jit(solution)/shard_map/ppermute | solution.py:78
  52.0 33.7 %collective-permute-start.4 = (bf16[64,6144]{1,0:T(8,128)(2,1)S(1)}, bf16[64,6144]{1,0:T(8,128)(2,1)S(1)}, u32[]{:S(2)}, u32[]{:S(2)}) collective-permute-start(bf16[64,6144]{1,0:T(8,128)(2,1)S(1)} %collective-permute-done.2), channel_id=1, source_target_pairs={{2,3},{3,4},{4,5},{5,6},{6,7},{10,11},{11,12},{12,13},{13,14},{14,... | collective-permute-start | bytes 2359304 | tf_op jit(solution)/shard_map/ppermute | solution.py:66
  52.7 31.7 %collective-permute-start.5 = (bf16[64,6144]{1,0:T(8,128)(2,1)}, bf16[64,6144]{1,0:T(8,128)(2,1)S(1)}, u32[]{:S(2)}, u32[]{:S(2)}) collective-permute-start(bf16[64,6144]{1,0:T(8,128)(2,1)} %collective-permute-done.3), channel_id=1, source_target_pairs={{1,0},{2,1},{3,2},{4,3},{5,4},{9,8},{10,9},{11,10},{12,11},{13,12}... | collective-permute-start | bytes 2359304 | tf_op jit(solution)/shard_map/ppermute | solution.py:67
  54.6 32.6 %collective-permute-start.7 = (bf16[16,512]{1,0:T(8,128)(2,1)S(1)}, bf16[16,512]{1,0:T(8,128)(2,1)S(1)}, u32[]{:S(2)}, u32[]{:S(2)}) collective-permute-start(bf16[16,512]{1,0:T(8,128)(2,1)S(1)} %get-tuple-element.40), channel_id=1, source_target_pairs={{0,256},{256,0},{1,257},{257,1},{2,258},{258,2},{3,259},{259,3},{4... | collective-permute-start | bytes 49160 | tf_op jit(solution)/shard_map/ppermute | solution.py:86
  84.4 20.6 %collective-permute-start.8 = (bf16[64,6144]{1,0:T(8,128)(2,1)S(1)}, bf16[64,6144]{1,0:T(8,128)(2,1)S(1)}, u32[]{:S(2)}, u32[]{:S(2)}) collective-permute-start(bf16[64,6144]{1,0:T(8,128)(2,1)S(1)} %collective-permute-done.5), channel_id=1, source_target_pairs={{1,0},{2,1},{3,2},{4,3},{9,8},{10,9},{11,10},{12,11},{17,16},{18,1... | collective-permute-start | bytes 2359304 | tf_op jit(solution)/shard_map/ppermute | solution.py:67
  85.7 20.7 %collective-permute-start.9 = (bf16[64,6144]{1,0:T(8,128)(2,1)S(1)}, bf16[64,6144]{1,0:T(8,128)(2,1)S(1)}, u32[]{:S(2)}, u32[]{:S(2)}) collective-permute-start(bf16[64,6144]{1,0:T(8,128)(2,1)S(1)} %collective-permute-done.4), channel_id=1, source_target_pairs={{3,4},{4,5},{5,6},{6,7},{11,12},{12,13},{13,14},{14,15},{19,20},{2... | collective-permute-start | bytes 2359304 | tf_op jit(solution)/shard_map/ppermute | solution.py:66
  87.2 62.7 %copy-start.1 = (f32[22,64,128]{2,1,0:T(8,128)}, f32[22,64,128]{2,1,0:T(8,128)S(1)}, u32[]{:S(2)}) copy-start(f32[22,64,128]{2,1,0:T(8,128)S(1)} %fusion.64) | copy-start | bytes 2162692
  87.2 20.7 %collective-permute-start.10 = (bf16[64,2048]{1,0:T(8,128)(2,1)S(1)}, bf16[64,2048]{1,0:T(8,128)(2,1)S(1)}, u32[]{:S(2)}, u32[]{:S(2)}) collective-permute-start(bf16[64,2048]{1,0:T(8,128)(2,1)S(1)} %slice.58), channel_id=1, source_target_pairs={{2,3},{5,4},{10,11},{13,12},{18,19},{21,20},{26,27},{29,28},{34,35... | collective-permute-start | bytes 786440 | tf_op jit(solution)/shard_map/ppermute | solution.py:93
  87.9 44.7 %collective-permute-start.11 = (bf16[64,2048]{1,0:T(8,128)(2,1)S(1)}, bf16[64,2048]{1,0:T(8,128)(2,1)S(1)}, u32[]{:S(2)}, u32[]{:S(2)}) collective-permute-start(bf16[64,2048]{1,0:T(8,128)(2,1)S(1)} %slice.58), channel_id=1, source_target_pairs={{1,3},{6,4},{9,11},{14,12},{17,19},{22,20},{25,27},{30,28},{33,35}... | collective-permute-start | bytes 786440 | tf_op jit(solution)/shard_map/ppermute | solution.py:93
  88.6 44.1 %collective-permute-start.12 = (bf16[64,2048]{1,0:T(8,128)(2,1)S(1)}, bf16[64,2048]{1,0:T(8,128)(2,1)S(1)}, u32[]{:S(2)}, u32[]{:S(2)}) collective-permute-start(bf16[64,2048]{1,0:T(8,128)(2,1)S(1)} %slice.58), channel_id=1, source_target_pairs={{0,3},{7,4},{8,11},{15,12},{16,19},{23,20},{24,27},{31,28},{32,35}... | collective-permute-start | bytes 786440 | tf_op jit(solution)/shard_map/ppermute | solution.py:93
  104.9 67.0 %collective-permute-start.16 = (bf16[2048,128]{1,0:T(8,128)(2,1)}, bf16[2048,128]{1,0:T(8,128)(2,1)}, u32[]{:S(2)}, u32[]{:S(2)}) collective-permute-start(bf16[2048,128]{1,0:T(8,128)(2,1)} %slice_bitcast_fusion), channel_id=1, source_target_pairs={{2,3},{5,4},{10,11},{13,12},{18,19},{21,20},{26,27},{29,28},{34,35... | collective-permute-start | bytes 1572872 | tf_op jit(solution)/shard_map/ppermute | solution.py:94
  106.4 65.5 %collective-permute-start.17 = (bf16[2048,128]{1,0:T(8,128)(2,1)}, bf16[2048,128]{1,0:T(8,128)(2,1)}, u32[]{:S(2)}, u32[]{:S(2)}) collective-permute-start(bf16[2048,128]{1,0:T(8,128)(2,1)} %slice_bitcast_fusion), channel_id=1, source_target_pairs={{1,3},{6,4},{9,11},{14,12},{17,19},{22,20},{25,27},{30,28},{33,35}... | collective-permute-start | bytes 1572872 | tf_op jit(solution)/shard_map/ppermute | solution.py:94
  108.0 36.7 %copy-start.3 = (bf16[64,6144]{1,0:T(8,128)(2,1)}, bf16[64,6144]{1,0:T(8,128)(2,1)S(1)}, u32[]{:S(2)}) copy-start(bf16[64,6144]{1,0:T(8,128)(2,1)S(1)} %broadcast_select_fusion) | copy-start | bytes 2359300
  108.0 63.9 %collective-permute-start.18 = (bf16[2048,128]{1,0:T(8,128)(2,1)}, bf16[2048,128]{1,0:T(8,128)(2,1)}, u32[]{:S(2)}, u32[]{:S(2)}) collective-permute-start(bf16[2048,128]{1,0:T(8,128)(2,1)} %slice_bitcast_fusion), channel_id=1, source_target_pairs={{0,3},{7,4},{8,11},{15,12},{16,19},{23,20},{24,27},{31,28},{32,35}... | collective-permute-start | bytes 1572872 | tf_op jit(solution)/shard_map/ppermute | solution.py:94
  132.7 0.7 copy-start.4
  133.4 16.5 %collective-permute-start.13 = (bf16[64,6144]{1,0:T(8,128)(2,1)S(1)}, bf16[64,6144]{1,0:T(8,128)(2,1)}, u32[]{:S(2)}, u32[]{:S(2)}) collective-permute-start(bf16[64,6144]{1,0:T(8,128)(2,1)S(1)} %broadcast_select_fusion), channel_id=1, source_target_pairs={{4,5},{5,6},{6,7},{1,0},{2,1},{3,2},{12,13},{13,14},{14,15},{9,8},... | collective-permute-start | bytes 2359304 | tf_op jit(solution)/shard_map/ppermute | solution.py:106
  134.7 10.0 %copy-start.5 = (bf16[64,2048]{1,0:T(8,128)(2,1)S(1)}, bf16[64,2048]{1,0:T(8,128)(2,1)}, u32[]{:S(2)}) copy-start(bf16[64,2048]{1,0:T(8,128)(2,1)} %copy-done.4) | copy-start | bytes 786436
  135.8 36.1 %all-to-all-start.1 = ((bf16[32,2,16,512]{3,2,1,0:T(8,128)(2,1)}), bf16[32,2,16,512]{3,2,1,0:T(8,128)(2,1)S(1)}, u32[]{:S(2)}, u32[]{:S(2)}) async-start(bf16[32,2,16,512]{3,2,1,0:T(8,128)(2,1)} %broadcast_in_dim.67), calls=%async_computation.1 | async-start | bytes 2097152 | tf_op jit(solution)/shard_map/all_to_all | solution.py:108
  143.2 9.1 %copy-start.8 = (bf16[1,8192,128]{2,1,0:T(8,128)(2,1)S(1)}, bf16[1,8192,128]{2,1,0:T(8,128)(2,1)}, u32[]{:S(2)}) copy-start(bf16[1,8192,128]{2,1,0:T(8,128)(2,1)} %param.8) | copy-start | bytes 6291460
  145.4 26.5 %collective-permute-start.15 = (bf16[256,2048]{1,0:T(8,128)(2,1)}, bf16[256,2048]{1,0:T(8,128)(2,1)}, u32[]{:S(2)}, u32[]{:S(2)}) collective-permute-start(bf16[256,2048]{1,0:T(8,128)(2,1)} %constant_dynamic-update-slice_fusion), channel_id=1, source_target_pairs={{3,4},{4,3},{11,12},{12,11},{19,20},{20,19},{27,28},{28,27},{35,36... | collective-permute-start | bytes 3145736 | tf_op jit(solution)/shard_map/ppermute | solution.py:102
  149.9 19.8 %collective-permute-start.14 = (bf16[64,6144]{1,0:T(8,128)(2,1)}, bf16[64,6144]{1,0:T(8,128)(2,1)}, u32[]{:S(2)}, u32[]{:S(2)}) collective-permute-start(bf16[64,6144]{1,0:T(8,128)(2,1)} %collective-permute-done.13), channel_id=1, source_target_pairs={{5,6},{6,7},{1,0},{2,1},{13,14},{14,15},{9,8},{10,9},{21,22},{22,2... | collective-permute-start | bytes 2359304 | tf_op jit(solution)/shard_map/ppermute | solution.py:106
  171.9 5.0 %copy-start.10 = (bf16[256,2048]{1,0:T(8,128)(2,1)S(1)}, bf16[256,2048]{1,0:T(8,128)(2,1)}, u32[]{:S(2)}) copy-start(bf16[256,2048]{1,0:T(8,128)(2,1)} %constant_dynamic-update-slice_fusion) | copy-start | bytes 3145732
  175.5 1.4 copy-start
  175.6 23.2 %collective-permute-start.19 = (bf16[64,6144]{1,0:T(8,128)(2,1)}, bf16[64,6144]{1,0:T(8,128)(2,1)}, u32[]{:S(2)}, u32[]{:S(2)}) collective-permute-start(bf16[64,6144]{1,0:T(8,128)(2,1)} %collective-permute-done.14), channel_id=1, source_target_pairs={{6,7},{1,0},{14,15},{9,8},{22,23},{17,16},{30,31},{25,24},{38,39},... | collective-permute-start | bytes 2359304 | tf_op jit(solution)/shard_map/ppermute | solution.py:106
  181.2 17.5 %copy-start.9 = (bf16[1,8192,128]{2,1,0:T(8,128)(2,1)S(1)}, bf16[1,8192,128]{2,1,0:T(8,128)(2,1)}, u32[]{:S(2)}) copy-start(bf16[1,8192,128]{2,1,0:T(8,128)(2,1)} %param.8) | copy-start | bytes 6291460
  181.3 20.7 %collective-permute-start.22 = (bf16[512,128]{0,1:T(8,128)(2,1)S(1)}, bf16[512,128]{0,1:T(8,128)(2,1)S(1)}, u32[]{:S(2)}, u32[]{:S(2)}) collective-permute-start(bf16[512,128]{0,1:T(8,128)(2,1)S(1)} %get-tuple-element.45), channel_id=1, source_target_pairs={{3,0},{4,7},{11,8},{12,15},{19,16},{20,23},{27,24},{28,31},{35,32}... | collective-permute-start | bytes 393224 | tf_op jit(solution)/shard_map/ppermute | solution.py:124
  182.7 19.3 %collective-permute-start.21 = (bf16[512,128]{0,1:T(8,128)(2,1)S(1)}, bf16[512,128]{0,1:T(8,128)(2,1)S(1)}, u32[]{:S(2)}, u32[]{:S(2)}) collective-permute-start(bf16[512,128]{0,1:T(8,128)(2,1)S(1)} %get-tuple-element.46), channel_id=1, source_target_pairs={{3,1},{4,6},{11,9},{12,14},{19,17},{20,22},{27,25},{28,30},{35,33}... | collective-permute-start | bytes 393224 | tf_op jit(solution)/shard_map/ppermute | solution.py:124
  183.4 18.6 %collective-permute-start.20 = (bf16[512,128]{0,1:T(8,128)(2,1)S(1)}, bf16[512,128]{0,1:T(8,128)(2,1)S(1)}, u32[]{:S(2)}, u32[]{:S(2)}) collective-permute-start(bf16[512,128]{0,1:T(8,128)(2,1)S(1)} %get-tuple-element.44), channel_id=1, source_target_pairs={{3,2},{4,5},{11,10},{12,13},{19,18},{20,21},{27,26},{28,29},{35,34... | collective-permute-start | bytes 393224 | tf_op jit(solution)/shard_map/ppermute | solution.py:124

commit v4 on v3

v4 whole, which is shorter than its diff:
```python
import math

import jax
import jax.numpy as jnp
from jax import lax
from jax.sharding import Mesh
from jax.sharding import PartitionSpec as P

HD = 128


EPSILON = 1e-05
ROPE_BASE = 500000.0
LR_OUTER = 0.7
MOMENTUM_OUTER = 0.9

PLANE = ("y", "x", "core")
REPLICA = ("zh",) + PLANE

K_LINE = 5632


def rotary_tables(rows):
    half = HD // 2
    index = jnp.arange(half).astype(jnp.float32)
    inverse = jnp.exp(-(2.0 * index / HD) * math.log(ROPE_BASE))
    angles = jnp.arange(rows).astype(jnp.float32)[:, None] * inverse[None, :]
    return jnp.cos(angles), jnp.sin(angles)


def dot(a, b):
    return jnp.dot(a, b, preferred_element_type=jnp.float32)


def nesterov(outer_rows, moment_rows, summed, replicas):
    delta = outer_rows - summed / replicas
    moment_next = MOMENTUM_OUTER * moment_rows + delta
    outer_next = outer_rows - LR_OUTER * (delta + MOMENTUM_OUTER * moment_next)
    return (outer_next, moment_next)


def body(tokens, norm_gain, key_weight, inner_params, outer_params, outer_momentum):
    me = lax.axis_index("tensor")
    zh = lax.axis_index("zh")
    low = me < 4
    block_f32 = tokens.astype(jnp.float32)
    scale = lax.rsqrt(jnp.mean(block_f32 * block_f32, axis=-1, keepdims=True) + EPSILON)
    normed = (block_f32 * scale * norm_gain.astype(jnp.float32)).astype(jnp.bfloat16)
    weight = key_weight[0]
    shard, rest = normed[:, :K_LINE], normed[:, K_LINE:]
    w_line, w_rest = weight[:K_LINE], weight[K_LINE:]

    line = lax.all_gather(shard, "tensor", axis=0, tiled=True)

    inward = {d: [(3 - d, 3), (4 + d, 4)] for d in (1, 2, 3)}
    held = [lax.ppermute(rest, "tensor", inward[d]) for d in (1, 2, 3)]
    wide = [lax.ppermute(w_rest, "tensor", inward[d]) for d in (1, 2, 3)]
    near = jnp.concatenate([rest] + held)
    far = lax.ppermute(near, "tensor", [(3, 4), (4, 3)])
    wide = jnp.concatenate([w_rest] + wide, axis=1)
    near, far = dot(near, wide), dot(far, wide)
    first = jnp.where(low, near, far).reshape(4, 64, 512)[::-1].reshape(256, 512)
    both = jnp.concatenate([first, jnp.where(low, far, near)])
    middle = jnp.where((me == 3) | (me == 4), both[:, :HD], 0.0)
    for d in (1, 2, 3):
        block = both[:, HD * d : HD * d + HD].astype(jnp.bfloat16)
        middle += lax.ppermute(block, "tensor", [(3, 3 - d), (4, 4 + d)]).astype(jnp.float32)

    params = inner_params[0, 0].reshape(2, 32, 16, 512).transpose(1, 0, 2, 3)
    pieces = lax.all_to_all(params, PLANE, 0, 0, tiled=True)
    partial = jnp.sum(pieces.astype(jnp.float32), axis=0)
    other = lax.dynamic_index_in_dim(partial, 1 - zh, 0, keepdims=False)
    own = lax.dynamic_index_in_dim(partial, zh, 0, keepdims=False)
    came = lax.ppermute(other, "zh", [(0, 1), (1, 0)])
    outer_next, moment_next = nesterov(outer_params[0], outer_momentum[0], own + came, 64)
    mine = outer_next.astype(jnp.bfloat16)
    theirs = lax.ppermute(mine, "zh", [(0, 1), (1, 0)])
    pair = jnp.where(zh == 0, jnp.stack([mine, theirs]), jnp.stack([theirs, mine]))
    synced = lax.all_to_all(jnp.broadcast_to(pair[None], (32, 2, 16, 512)), PLANE, 0, 0, tiled=True)
    synced = synced.transpose(1, 0, 2, 3).reshape(1024, 512)

    projected = dot(line, w_line) + middle
    cosine, sine = rotary_tables(512)
    first, second = projected[:, : HD // 2], projected[:, HD // 2 :]
    key_rows = jnp.concatenate(
        [first * cosine - second * sine, second * cosine + first * sine], axis=-1
    ).astype(jnp.bfloat16)
    return (key_rows, outer_next[None], moment_next[None], synced[None])


def solution(mesh):
    fine = Mesh(mesh.devices.reshape(2, 4, 4, 2, 8), REPLICA + ("tensor",))
    in_specs = (
        P(REPLICA + ("tensor",), None),
        P(),
        P(REPLICA, None, "tensor"),
        P(REPLICA, "tensor", None, None),
        P("tensor", REPLICA, None),
        P("tensor", REPLICA, None),
    )
    out_specs = (
        P(REPLICA, "tensor"),
        P("tensor", REPLICA, None),
        P("tensor", REPLICA, None),
        P("tensor", None, None),
    )
    return jax.shard_map(body, mesh=fine, in_specs=in_specs, out_specs=out_specs, check_vma=False)
```

time: 205 us -> 229 us (1.12)
  waiting for transfers between devices: 50.8 us -> 106 us
  starting transfers between devices: 109 us -> 82.4 us
  between operations: 1.27 us -> 14.4 us
  local copies, waits for them, and re-layouts: 15.9 us -> 6.54 us
  matrix products: 20.7 us -> 12 us
    ppermute x3, waiting for transfers between devices: 0.01 us -> 62.1 us  [body(): lax.ppermute(block, 'tensor', [(3, 3 - d), (4, 4 + d)]).astype(jnp.float32)]
    ppermute x11 -> x0, waiting for transfers between devices: 50.3 us -> none  [the longest x3 29.6 us: hop_out(): return lax.ppermute(x, 'tensor', pairs)]
    ppermute x1, waiting for transfers between devices: 0.01 us -> 27.2 us  [body(): came = lax.ppermute(other, 'zh', [(0, 1), (1, 0)])]
    ppermute x11 -> x0, starting transfers between devices: 15.8 us -> none  [the longest x4 6.83 us: hop(): a = lax.ppermute(a, 'tensor', [(j, j + 1) for j in range(s, 7)])]
    ppermute x1, starting transfers between devices: 15.2 us -> 1.91 us  [body(): theirs = lax.ppermute(mine, 'zh', [(0, 1), (1, 0)])]
    ppermute x1, waiting for transfers between devices: 0.01 us -> 8.99 us  [body(): theirs = lax.ppermute(mine, 'zh', [(0, 1), (1, 0)])]
    dot_general x13 -> x3, matrix products: 20.7 us -> 12 us  [dot(): return jnp.dot(a, b, preferred_element_type=jnp.float32)]
    all_to_all x1, waiting for transfers between devices: 0.01 us -> 8.2 us  [body(): lax.all_to_all(jnp.broadcast_to(pair[None], (32, 2, 16, 512)), PLANE, 0,...]
  transfers between devices with their start and end apart: 25 -> 15, of which waited for: 8 -> 4; matrix products, arithmetic and copies ran while one was open for 15% -> 6% of each run, Pallas kernels for 0% -> 0%
where the time goes in v4:
time: 229 us; the launch traced here: 228 us
  waiting for transfers between devices  106 us (46%)
  starting transfers between devices  82.4 us (36%)
  between operations  14.4 us (6%)
  matrix products  12 us (5%)
  other arithmetic  6.59 us (3%)
  local copies, waits for them, and re-layouts  6.54 us (3%)
    ppermute x3, waiting for transfers between devices, body(): lax.ppermute(block, 'tensor', [(3, 3 - d), (4, 4 + d)]).astype(jnp.float32)  62.1 us
    ppermute x3, starting transfers between devices, body(): wide = [lax.ppermute(w_rest, 'tensor', inward[d]) for d in (1, 2, 3)]  33 us
    ppermute x1, waiting for transfers between devices, body(): came = lax.ppermute(other, 'zh', [(0, 1), (1, 0)])  27.2 us
    ppermute x1, starting transfers between devices, body(): came = lax.ppermute(other, 'zh', [(0, 1), (1, 0)])  17.4 us
    dot_general x3, matrix products, dot(): return jnp.dot(a, b, preferred_element_type=jnp.float32)  12 us
    ppermute x3, starting transfers between devices, body(): held = [lax.ppermute(rest, 'tensor', inward[d]) for d in (1, 2, 3)]  9.88 us
    ppermute x1, waiting for transfers between devices, body(): theirs = lax.ppermute(mine, 'zh', [(0, 1), (1, 0)])  8.99 us
    all_to_all x1, starting transfers between devices, body(): lax.all_to_all(jnp.broadcast_to(pair[None], (32, 2, 16, 512)), PLANE, 0,...  8.27 us
  transfers between devices with their start and end apart: 15, of which 4 were waited for; matrix products, arithmetic and copies ran while one was open for 6% of the time, Pallas kernels for 0%

profile of v4, /device:TPU:6, one launch (start us, length us, event | category | flops | bytes accessed | tf_op | source)
XLA Modules:
  0.0 228.3 jit_solution(10674889902741891217)
XLA Ops:
  7.2 0.0 all-gather.2.cloned.1.call-start
  7.2 0.7 convert_element_type.55
  7.9 1.5 fusion
  9.5 0.0 copy-start
  9.5 1.6 fusion.2
  11.1 0.9 slice.51
  12.0 0.0 all-gather.2.cloned.1.call-update
  12.1 0.7 collective-permute-start
  12.8 0.7 collective-permute-start.1
  13.5 8.5 %collective-permute-start.2 = (bf16[64,2560]{1,0:T(8,128)(2,1)S(1)}, bf16[64,2560]{1,0:T(8,128)(2,1)}, u32[]{:S(2)}, u32[]{:S(2)}) collective-permute-start(bf16[64,2560]{1,0:T(8,128)(2,1)S(1)} %slice.52), channel_id=1, source_target_pairs={{0,3},{7,4},{8,11},{15,12},{16,19},{23,20},{24,27},{31,28},{32,35}... | collective-permute-start | bytes 983048 | tf_op jit(solution)/shard_map/ppermute | solution.py:56
  22.0 1.1 copy.35
  23.0 7.6 %all-to-all-start = ((bf16[32,2,16,512]{3,2,1,0:T(8,128)(2,1)}), bf16[32,2,16,512]{3,2,1,0:T(8,128)(2,1)S(1)}, u32[]{:S(2)}, u32[]{:S(2)}) async-start(bf16[32,2,16,512]{3,2,1,0:T(8,128)(2,1)} %copy.35), calls=%async_computation | async-start | bytes 2097152 | tf_op jit(solution)/shard_map/all_to_all | solution.py:70
  30.6 0.0 copy-start.3
  30.6 0.0 copy-start.4
  30.6 0.0 collective-permute-done
  30.7 0.0 collective-permute-done.1
  30.7 0.0 collective-permute-done.2
  30.7 1.3 pad_maximum_fusion.1
  32.0 1.8 collective-permute-start.6
  33.8 1.1 slice_bitcast_fusion
  34.9 1.5 collective-permute-start.3
  36.4 1.6 collective-permute-start.4
  38.0 29.9 %collective-permute-start.5 = (bf16[2560,128]{1,0:T(8,128)(2,1)S(1)}, bf16[2560,128]{1,0:T(8,128)(2,1)}, u32[]{:S(2)}, u32[]{:S(2)}) collective-permute-start(bf16[2560,128]{1,0:T(8,128)(2,1)S(1)} %slice_bitcast_fusion), channel_id=1, source_target_pairs={{0,3},{7,4},{8,11},{15,12},{16,19},{23,20},{24,27},{31,28},{32,35}... | collective-permute-start | bytes 1966088 | tf_op jit(solution)/shard_map/ppermute | solution.py:57
  67.9 0.2 convert_reduce_fusion
  68.0 17.4 %collective-permute-start.10 = (f32[16,512]{1,0:T(8,128)S(1)}, f32[16,512]{1,0:T(8,128)S(1)}, u32[]{:S(2)}, u32[]{:S(2)}) collective-permute-start(f32[16,512]{1,0:T(8,128)S(1)} %dynamic-slice_bitcast_fusion), channel_id=1, source_target_pairs={{0,256},{256,0},{1,257},{257,1},{2,258},{258,2},{3,259},{259,3},{4... | collective-permute-start | bytes 98312 | tf_op jit(solution)/shard_map/ppermute | solution.py:74
  85.4 27.2 %collective-permute-done.10 = f32[16,512]{1,0:T(8,128)S(1)} collective-permute-done((f32[16,512]{1,0:T(8,128)S(1)}, f32[16,512]{1,0:T(8,128)S(1)}, u32[]{:S(2)}, u32[]{:S(2)}) %collective-permute-start.10) | collective-permute-done | bytes 32800 | tf_op jit(solution)/shard_map/ppermute | solution.py:74
  112.6 0.6 fusion.28
  113.3 1.9 collective-permute-start.11
  115.2 0.0 collective-permute-done.3
  115.2 0.0 collective-permute-done.5
  115.2 3.7 %fusion.8 = f32[256,512]{0,1:T(8,128)} fusion(bf16[2560,128]{1,0:T(8,128)(2,1)} %collective-permute-done.5, bf16[2560,128]{1,0:T(8,128)(2,1)} %collective-permute-done.4, bf16[2560,128]{1,0:T(8,128)(2,1)} %collective-permute-done.3, bf16[2560,128]{1,0:T(8,128)(2,1)S(1)} %slice_bitcast_fusion, bf16[64,2560]{1,0:T(8,128)(2,1)} %collective-permute-done.2, ...), kind=kOutput, calls=%fused_computation.17 | convolution fusion | flops 686817280 | bytes 4456448 | tf_op jit(solution)/shard_map/dot_general | solution.py:32
  118.9 9.0 %collective-permute-done.11 = bf16[16,512]{1,0:T(8,128)(2,1)S(1)} collective-permute-done((bf16[16,512]{1,0:T(8,128)(2,1)S(1)}, bf16[16,512]{1,0:T(8,128)(2,1)S(1)}, u32[]{:S(2)}, u32[]{:S(2)}) %collective-permute-start.11) | collective-permute-done | bytes 16416 | tf_op jit(solution)/shard_map/ppermute | solution.py:77
  127.9 1.1 broadcast_in_dim.23
  129.0 8.3 %all-to-all-start.1 = ((bf16[32,2,16,512]{3,2,1,0:T(8,128)(2,1)}), bf16[32,2,16,512]{3,2,1,0:T(8,128)(2,1)S(1)}, u32[]{:S(2)}, u32[]{:S(2)}) async-start(bf16[32,2,16,512]{3,2,1,0:T(8,128)(2,1)} %broadcast_in_dim.23), calls=%async_computation.1 | async-start | bytes 2097152 | tf_op jit(solution)/shard_map/all_to_all | solution.py:79
  137.3 3.2 %broadcast_select_fusion = (f32[256,512]{0,1:T(8,128)S(1)}, f32[256,512]{0,1:T(8,128)S(1)}) fusion(f32[256,512]{0,1:T(8,128)} %fusion.8, pred[]{:T(512)S(6)} %lt.10, bf16[256,2560]{1,0:T(8,128)(2,1)} %collective-permute-done.6, bf16[2560,128]{1,0:T(8,128)(2,1)} %collective-permute-done.5, bf16[2560,128]{1,0:T(8,128)(2,1)} %collective-permute-done.4, ...), kind=kOutput, calls=%fused_computation.24 | convolution fusion | flops 681836544 | bytes 5505025 | tf_op jit(solution)/shard_map/dot_general | solution.py:32
  140.5 0.2 copy.31
  140.7 0.2 copy.34
  141.0 0.1 fusion.6
  141.0 0.7 collective-permute-start.7
  141.7 0.7 collective-permute-start.8
  142.4 1.3 collective-permute-start.9
  143.7 8.2 %all-to-all-done.1 = bf16[32,2,16,512]{3,2,1,0:T(8,128)(2,1)S(1)} async-done(((bf16[32,2,16,512]{3,2,1,0:T(8,128)(2,1)}), bf16[32,2,16,512]{3,2,1,0:T(8,128)(2,1)S(1)}, u32[]{:S(2)}, u32[]{:S(2)}) %all-to-all-start.1) | async-done | bytes 1048608 | tf_op jit(solution)/shard_map/all_to_all | solution.py:79
  151.9 1.1 copy.36
  153.0 0.0 collective-permute-done.8
  153.0 62.1 %collective-permute-done.9 = bf16[512,128]{0,1:T(8,128)(2,1)S(1)} collective-permute-done((bf16[512,128]{0,1:T(8,128)(2,1)S(1)}, bf16[512,128]{0,1:T(8,128)(2,1)S(1)}, u32[]{:S(2)}, u32[]{:S(2)}) %collective-permute-start.9) | collective-permute-done | bytes 131104 | tf_op jit(solution)/shard_map/ppermute | solution.py:67
  215.0 5.1 %fusion.14 = f32[512,128]{0,1:T(8,128)S(1)} fusion(f32[256,512]{0,1:T(8,128)S(1)} %copy.34, f32[256,512]{0,1:T(8,128)S(1)} %get-tuple-element.22, bf16[512,128]{0,1:T(8,128)(2,1)S(1)} %collective-permute-done.9, bf16[512,128]{0,1:T(8,128)(2,1)S(1)} %collective-permute-done.8, bf16[512,128]{0,1:T(8,128)(2,1)S(1)} %collective-permute-done.7, pred[]{:T(512)S(6)} %or.3, ...), kind=kOutput, calls=%fused_computation.23 | convolution fusion | flops 738787328 | bytes 8912897 | tf_op jit(solution)/shard_map/dot_general | solution.py:32
  220.1 0.6 fusion.20
  220.7 0.8 copy.37
  (21 shorter events, 0.2 us)
Async XLA Ops:
  7.2 207.9 %all-gather.2.cloned.1.call-start = ((), (), s32[]{:S(2)}) async-start(), calls=%async_computation.2 | async-start | bytes 6488064 | tf_op jit(solution)/shard_map/all_gather | solution.py:53
  9.5 12.5 %copy-start = (bf16[1,1,1024,512]{3,2,1,0:T(8,128)(2,1)S(1)}, bf16[1,1,1024,512]{3,2,1,0:T(8,128)(2,1)}, u32[]{:S(2)}) copy-start(bf16[1,1,1024,512]{3,2,1,0:T(8,128)(2,1)} %param.9) | copy-start | bytes 3145732
  12.1 18.6 %collective-permute-start = (bf16[64,2560]{1,0:T(8,128)(2,1)S(1)}, bf16[64,2560]{1,0:T(8,128)(2,1)S(1)}, u32[]{:S(2)}, u32[]{:S(2)}) collective-permute-start(bf16[64,2560]{1,0:T(8,128)(2,1)S(1)} %slice.52), channel_id=1, source_target_pairs={{2,3},{5,4},{10,11},{13,12},{18,19},{21,20},{26,27},{29,28},{34,35... | collective-permute-start | bytes 983048 | tf_op jit(solution)/shard_map/ppermute | solution.py:56
  12.8 17.9 %collective-permute-start.1 = (bf16[64,2560]{1,0:T(8,128)(2,1)S(1)}, bf16[64,2560]{1,0:T(8,128)(2,1)S(1)}, u32[]{:S(2)}, u32[]{:S(2)}) collective-permute-start(bf16[64,2560]{1,0:T(8,128)(2,1)S(1)} %slice.52), channel_id=1, source_target_pairs={{1,3},{6,4},{9,11},{14,12},{17,19},{22,20},{25,27},{30,28},{33,35}... | collective-permute-start | bytes 983048 | tf_op jit(solution)/shard_map/ppermute | solution.py:56
  13.5 17.2 %collective-permute-start.2 = (bf16[64,2560]{1,0:T(8,128)(2,1)S(1)}, bf16[64,2560]{1,0:T(8,128)(2,1)}, u32[]{:S(2)}, u32[]{:S(2)}) collective-permute-start(bf16[64,2560]{1,0:T(8,128)(2,1)S(1)} %slice.52), channel_id=1, source_target_pairs={{0,3},{7,4},{8,11},{15,12},{16,19},{23,20},{24,27},{31,28},{32,35}... | collective-permute-start | bytes 983048 | tf_op jit(solution)/shard_map/ppermute | solution.py:56
  23.0 44.8 %all-to-all-start = ((bf16[32,2,16,512]{3,2,1,0:T(8,128)(2,1)}), bf16[32,2,16,512]{3,2,1,0:T(8,128)(2,1)S(1)}, u32[]{:S(2)}, u32[]{:S(2)}) async-start(bf16[32,2,16,512]{3,2,1,0:T(8,128)(2,1)} %copy.35), calls=%async_computation | async-start | bytes 2097152 | tf_op jit(solution)/shard_map/all_to_all | solution.py:70
  30.6 82.0 %copy-start.3 = (f32[1,16,512]{2,1,0:T(8,128)S(1)}, f32[1,16,512]{2,1,0:T(8,128)}, u32[]{:S(2)}) copy-start(f32[1,16,512]{2,1,0:T(8,128)} %param.11) | copy-start | bytes 98308
  30.6 82.0 %copy-start.4 = (f32[1,16,512]{2,1,0:T(8,128)S(1)}, f32[1,16,512]{2,1,0:T(8,128)}, u32[]{:S(2)}) copy-start(f32[1,16,512]{2,1,0:T(8,128)} %param.10) | copy-start | bytes 98308
  30.7 1.3 copy-start.1
  30.7 1.3 copy-start.2
  32.0 105.3 %collective-permute-start.6 = (bf16[256,2560]{1,0:T(8,128)(2,1)S(1)}, bf16[256,2560]{1,0:T(8,128)(2,1)}, u32[]{:S(2)}, u32[]{:S(2)}) collective-permute-start(bf16[256,2560]{1,0:T(8,128)(2,1)S(1)} %pad_maximum_fusion.1), channel_id=1, source_target_pairs={{3,4},{4,3},{11,12},{12,11},{19,20},{20,19},{27,28},{28,27},{35,36... | collective-permute-start | bytes 3932168 | tf_op jit(solution)/shard_map/ppermute | solution.py:59
  34.9 80.3 %collective-permute-start.3 = (bf16[2560,128]{1,0:T(8,128)(2,1)S(1)}, bf16[2560,128]{1,0:T(8,128)(2,1)}, u32[]{:S(2)}, u32[]{:S(2)}) collective-permute-start(bf16[2560,128]{1,0:T(8,128)(2,1)S(1)} %slice_bitcast_fusion), channel_id=1, source_target_pairs={{2,3},{5,4},{10,11},{13,12},{18,19},{21,20},{26,27},{29,28},{34,35... | collective-permute-start | bytes 1966088 | tf_op jit(solution)/shard_map/ppermute | solution.py:57
  36.4 78.8 %collective-permute-start.4 = (bf16[2560,128]{1,0:T(8,128)(2,1)S(1)}, bf16[2560,128]{1,0:T(8,128)(2,1)}, u32[]{:S(2)}, u32[]{:S(2)}) collective-permute-start(bf16[2560,128]{1,0:T(8,128)(2,1)S(1)} %slice_bitcast_fusion), channel_id=1, source_target_pairs={{1,3},{6,4},{9,11},{14,12},{17,19},{22,20},{25,27},{30,28},{33,35}... | collective-permute-start | bytes 1966088 | tf_op jit(solution)/shard_map/ppermute | solution.py:57
  38.0 77.2 %collective-permute-start.5 = (bf16[2560,128]{1,0:T(8,128)(2,1)S(1)}, bf16[2560,128]{1,0:T(8,128)(2,1)}, u32[]{:S(2)}, u32[]{:S(2)}) collective-permute-start(bf16[2560,128]{1,0:T(8,128)(2,1)S(1)} %slice_bitcast_fusion), channel_id=1, source_target_pairs={{0,3},{7,4},{8,11},{15,12},{16,19},{23,20},{24,27},{31,28},{32,35}... | collective-permute-start | bytes 1966088 | tf_op jit(solution)/shard_map/ppermute | solution.py:57
  68.0 44.6 %collective-permute-start.10 = (f32[16,512]{1,0:T(8,128)S(1)}, f32[16,512]{1,0:T(8,128)S(1)}, u32[]{:S(2)}, u32[]{:S(2)}) collective-permute-start(f32[16,512]{1,0:T(8,128)S(1)} %dynamic-slice_bitcast_fusion), channel_id=1, source_target_pairs={{0,256},{256,0},{1,257},{257,1},{2,258},{258,2},{3,259},{259,3},{4... | collective-permute-start | bytes 98312 | tf_op jit(solution)/shard_map/ppermute | solution.py:74
  113.3 14.7 %collective-permute-start.11 = (bf16[16,512]{1,0:T(8,128)(2,1)S(1)}, bf16[16,512]{1,0:T(8,128)(2,1)S(1)}, u32[]{:S(2)}, u32[]{:S(2)}) collective-permute-start(bf16[16,512]{1,0:T(8,128)(2,1)S(1)} %get-tuple-element.20), channel_id=1, source_target_pairs={{0,256},{256,0},{1,257},{257,1},{2,258},{258,2},{3,259},{259,3},{4... | collective-permute-start | bytes 49160 | tf_op jit(solution)/shard_map/ppermute | solution.py:77
  129.0 22.9 %all-to-all-start.1 = ((bf16[32,2,16,512]{3,2,1,0:T(8,128)(2,1)}), bf16[32,2,16,512]{3,2,1,0:T(8,128)(2,1)S(1)}, u32[]{:S(2)}, u32[]{:S(2)}) async-start(bf16[32,2,16,512]{3,2,1,0:T(8,128)(2,1)} %broadcast_in_dim.23), calls=%async_computation.1 | async-start | bytes 2097152 | tf_op jit(solution)/shard_map/all_to_all | solution.py:79
  141.0 11.9 %collective-permute-start.7 = (bf16[512,128]{0,1:T(8,128)(2,1)S(1)}, bf16[512,128]{0,1:T(8,128)(2,1)S(1)}, u32[]{:S(2)}, u32[]{:S(2)}) collective-permute-start(bf16[512,128]{0,1:T(8,128)(2,1)S(1)} %get-tuple-element.24), channel_id=1, source_target_pairs={{3,2},{4,5},{11,10},{12,13},{19,18},{20,21},{27,26},{28,29},{35,34... | collective-permute-start | bytes 393224 | tf_op jit(solution)/shard_map/ppermute | solution.py:67
  141.7 11.3 %collective-permute-start.8 = (bf16[512,128]{0,1:T(8,128)(2,1)S(1)}, bf16[512,128]{0,1:T(8,128)(2,1)S(1)}, u32[]{:S(2)}, u32[]{:S(2)}) collective-permute-start(bf16[512,128]{0,1:T(8,128)(2,1)S(1)} %get-tuple-element.26), channel_id=1, source_target_pairs={{3,1},{4,6},{11,9},{12,14},{19,17},{20,22},{27,25},{28,30},{35,33}... | collective-permute-start | bytes 393224 | tf_op jit(solution)/shard_map/ppermute | solution.py:67
  142.4 72.6 %collective-permute-start.9 = (bf16[512,128]{0,1:T(8,128)(2,1)S(1)}, bf16[512,128]{0,1:T(8,128)(2,1)S(1)}, u32[]{:S(2)}, u32[]{:S(2)}) collective-permute-start(bf16[512,128]{0,1:T(8,128)(2,1)S(1)} %get-tuple-element.25), channel_id=1, source_target_pairs={{3,0},{4,7},{11,8},{12,15},{19,16},{20,23},{27,24},{28,31},{35,32}... | collective-permute-start | bytes 393224 | tf_op jit(solution)/shard_map/ppermute | solution.py:67
Sparse Core Ops, SparseCore 0:
  12.2 171.3 all-gather.1

commit v5 on v4

v5 whole, which is shorter than its diff:
```python
import math

import jax
import jax.numpy as jnp
from jax import lax
from jax.sharding import Mesh
from jax.sharding import PartitionSpec as P

HD = 128


EPSILON = 1e-05
ROPE_BASE = 500000.0
LR_OUTER = 0.7
MOMENTUM_OUTER = 0.9

PLANE = ("y", "x", "core")
REPLICA = ("zh",) + PLANE

K_LINE = 6144


def rotary_tables(rows):
    half = HD // 2
    index = jnp.arange(half).astype(jnp.float32)
    inverse = jnp.exp(-(2.0 * index / HD) * math.log(ROPE_BASE))
    angles = jnp.arange(rows).astype(jnp.float32)[:, None] * inverse[None, :]
    return jnp.cos(angles), jnp.sin(angles)


def dot(a, b):
    return jnp.dot(a, b, preferred_element_type=jnp.float32)


def nesterov(outer_rows, moment_rows, summed, replicas):
    delta = outer_rows - summed / replicas
    moment_next = MOMENTUM_OUTER * moment_rows + delta
    outer_next = outer_rows - LR_OUTER * (delta + MOMENTUM_OUTER * moment_next)
    return (outer_next, moment_next)


hold = lax.optimization_barrier


def body(tokens, norm_gain, key_weight, inner_params, outer_params, outer_momentum):
    me = lax.axis_index("tensor")
    zh = lax.axis_index("zh")
    low = me < 4

    params = inner_params[0, 0].reshape(2, 32, 16, 512).transpose(1, 0, 2, 3)
    pieces = lax.all_to_all(params, PLANE, 0, 0, tiled=True)
    state = jnp.concatenate([outer_params, outer_momentum])
    state_other = lax.ppermute(state, "zh", [(0, 1), (1, 0)])

    block_f32 = tokens.astype(jnp.float32)
    scale = lax.rsqrt(jnp.mean(block_f32 * block_f32, axis=-1, keepdims=True) + EPSILON)
    normed = (block_f32 * scale * norm_gain.astype(jnp.float32)).astype(jnp.bfloat16)
    weight = key_weight[0]
    shard, rest = normed[:, :K_LINE], normed[:, K_LINE:]
    w_line, w_rest = weight[:K_LINE], weight[K_LINE:]

    rows = jnp.zeros((22, 64, HD), jnp.float32)

    def put(rows, block, at):
        return lax.dynamic_update_slice(rows, dot(block, w_line)[None], (7 + at, 0, 0))

    def hop(a, b, s):
        a = lax.ppermute(a, "tensor", [(j, j + 1) for j in range(s, 7)])
        b = lax.ppermute(b, "tensor", [(j + 1, j) for j in range(7 - s)])
        return a, b

    def hop_out(x, s):
        pairs = [(j, j + 1) for j in range(s, 7)] + [(j + 1, j) for j in range(7 - s)]
        return lax.ppermute(x, "tensor", pairs)

    def inward(x, d):
        return lax.ppermute(x, "tensor", [(3 - d, 4 - d), (4 + d, 3 + d)])

    a, b = hop(shard, shard, 0)
    rows = put(rows, shard, me)

    rows0 = put(put(rows, a, me - 1), b, me + 1)
    a, b = hop(a, b, 1)
    rows, pieces, state_other, rest, w_rest = hold((rows0, pieces, state_other, rest, w_rest))
    partial = jnp.sum(pieces.astype(jnp.float32), axis=0)
    came = lax.ppermute(partial, "zh", [(0, 1), (1, 0)])
    t3, w3 = inward(rest, 3), inward(w_rest, 3)

    rows1 = put(put(rows, a, me - 2), b, me + 2)
    a, b = hop(a, b, 2)
    rows, came, t3, w3 = hold((rows1, came, t3, w3))
    t2 = inward(jnp.concatenate([t3, rest]), 2)
    summed = partial + came
    ours = jnp.where(zh == 0, jnp.stack([state, state_other]), jnp.stack([state_other, state]))
    outer_pair, moment_pair = nesterov(ours[:, 0], ours[:, 1], summed, 64)
    outer_next = lax.dynamic_index_in_dim(outer_pair, zh, 0)
    moment_next = lax.dynamic_index_in_dim(moment_pair, zh, 0)
    pair = outer_pair.astype(jnp.bfloat16)

    rows2 = put(put(rows, a, me - 3), b, me + 3)
    a, b = hop(a, b, 3)
    rows, t2, w3 = hold((rows2, t2, w3))
    t1 = inward(jnp.concatenate([t2, rest]), 1)
    w3 = inward(w3, 2)

    x = jnp.where(low, b, a)
    rows3 = put(rows, x, jnp.where(low, me + 4, me - 4))
    x = hop_out(x, 4)
    rows, t1, w3, w2 = hold((rows3, t1, w3, w_rest))
    near = jnp.concatenate([t1, rest])
    far = lax.ppermute(near, "tensor", [(3, 4), (4, 3)])
    w13 = inward(jnp.concatenate([w_rest, w3]), 1)
    w2 = inward(w2, 2)

    rows4 = put(rows, x, jnp.where(low, me + 5, me - 5))
    x = hop_out(x, 5)
    rows, w2, pair = hold((rows4, w2, pair))
    w2 = inward(w2, 1)
    synced = lax.all_to_all(jnp.broadcast_to(pair[None], (32, 2, 16, 512)), PLANE, 0, 0, tiled=True)

    rows5 = put(rows, x, jnp.where(low, me + 6, me - 6))
    x = hop_out(x, 6)
    rows, far, w13, w2 = hold((rows5, far, w13, w2))
    size = w_rest.shape[0]
    wide = jnp.concatenate([w_rest, w13[:size], w2, w13[size:]], axis=1)
    near, far = dot(near, wide), dot(far, wide)
    last = jnp.where(low, far, near).reshape(4, 64, 512)[::-1].reshape(256, 512)
    both = jnp.concatenate([jnp.where(low, near, far), last])
    middle = jnp.where((me == 3) | (me == 4), both[:, :HD], 0.0)
    for d in (1, 2, 3):
        block = both[:, HD * d : HD * d + HD].astype(jnp.bfloat16)
        middle += lax.ppermute(block, "tensor", [(3, 3 - d), (4, 4 + d)]).astype(jnp.float32)

    rows = put(rows, x, jnp.where(low, me + 7, me - 7))
    synced = synced.transpose(1, 0, 2, 3).reshape(1024, 512)
    projected = rows[7:15].reshape(512, HD) + middle
    cosine, sine = rotary_tables(512)
    first, second = projected[:, : HD // 2], projected[:, HD // 2 :]
    key_rows = jnp.concatenate(
        [first * cosine - second * sine, second * cosine + first * sine], axis=-1
    ).astype(jnp.bfloat16)
    return (key_rows, outer_next, moment_next, synced[None])


def solution(mesh):
    fine = Mesh(mesh.devices.reshape(2, 4, 4, 2, 8), REPLICA + ("tensor",))
    in_specs = (
        P(REPLICA + ("tensor",), None),
        P(),
        P(REPLICA, None, "tensor"),
        P(REPLICA, "tensor", None, None),
        P("tensor", REPLICA, None),
        P("tensor", REPLICA, None),
    )
    out_specs = (
        P(REPLICA, "tensor"),
        P("tensor", REPLICA, None),
        P("tensor", REPLICA, None),
        P("tensor", None, None),
    )
    return jax.shard_map(body, mesh=fine, in_specs=in_specs, out_specs=out_specs, check_vma=False)
```

time: 229 us -> 177 us (0.77)
  waiting for transfers between devices: 106 us -> 73.5 us
  starting transfers between devices: 82.4 us -> 64.2 us
  between operations: 14.4 us -> 1.32 us
  matrix products: 12 us -> 19.5 us
  local copies, waits for them, and re-layouts: 6.54 us -> 10.2 us
    ppermute x3, waiting for transfers between devices: 62.1 us -> 0.01 us  [body(): lax.ppermute(block, 'tensor', [(3, 3 - d), (4, 4 + d)]).astype(jnp.float32)]
    ppermute x8 -> x21, waiting for transfers between devices: 36.2 us -> 68.7 us  [the longest x3 32.5 us: hop_out(): return lax.ppermute(x, 'tensor', pairs)]
    ppermute x8 -> x21, starting transfers between devices: 62.1 us -> 46.5 us  [the longest x1 14.8 us: body(): state_other = lax.ppermute(state, 'zh', [(0, 1), (1, 0)])]
    all_to_all x1, waiting for transfers between devices: 8.2 us -> 0.01 us  [body(): lax.all_to_all(jnp.broadcast_to(pair[None], (32, 2, 16, 512)), PLANE, 0,...]
    dot_general x3 -> x13, matrix products: 12 us -> 19.5 us  [dot(): return jnp.dot(a, b, preferred_element_type=jnp.float32)]
    all_to_all x1, waiting for transfers between devices: 0.01 us -> 4.85 us  [body(): pieces = lax.all_to_all(params, PLANE, 0, 0, tiled=True)]
    all_to_all x1, starting transfers between devices: 8.27 us -> 5.89 us  [body(): lax.all_to_all(jnp.broadcast_to(pair[None], (32, 2, 16, 512)), PLANE, 0,...]
  transfers between devices with their start and end apart: 15 -> 27, of which waited for: 4 -> 9; matrix products, arithmetic and copies ran while one was open for 6% -> 17% of each run, Pallas kernels for 0% -> 0%
where the time goes in v5:
time: 177 us; the launch traced here: 175 us
  waiting for transfers between devices  73.5 us (42%)
  starting transfers between devices  64.2 us (36%)
  matrix products  19.5 us (11%)
  local copies, waits for them, and re-layouts  10.2 us (6%)
  other arithmetic  6.03 us (3%)
    ppermute x3, waiting for transfers between devices, hop_out(): return lax.ppermute(x, 'tensor', pairs)  32.5 us
    ppermute x4, waiting for transfers between devices, hop(): b = lax.ppermute(b, 'tensor', [(j + 1, j) for j in range(7 - s)])  23.9 us
    dot_general x13, matrix products, dot(): return jnp.dot(a, b, preferred_element_type=jnp.float32)  19.5 us
    ppermute x1, starting transfers between devices, body(): state_other = lax.ppermute(state, 'zh', [(0, 1), (1, 0)])  14.8 us
    ppermute x8, starting transfers between devices, inward(): return lax.ppermute(x, 'tensor', [(3 - d, 4 - d), (4 + d, 3 + d)])  11.9 us
    ppermute x1, waiting for transfers between devices, body(): came = lax.ppermute(partial, 'zh', [(0, 1), (1, 0)])  10.5 us
    ppermute x4, starting transfers between devices, hop(): a = lax.ppermute(a, 'tensor', [(j, j + 1) for j in range(s, 7)])  7.69 us
    all_to_all x1, starting transfers between devices, body(): pieces = lax.all_to_all(params, PLANE, 0, 0, tiled=True)  7.56 us
  transfers between devices with their start and end apart: 27, of which 9 were waited for; matrix products, arithmetic and copies ran while one was open for 17% of the time, Pallas kernels for 0%

profile of v5, /device:TPU:6, one launch (start us, length us, event | category | flops | bytes accessed | tf_op | source)
XLA Modules:
  0.0 174.8 jit_solution(6227210767210418357)
XLA Ops:
  1.4 1.5 fusion
  2.9 1.6 fusion.2
  4.6 0.9 slice.71
  5.5 4.7 %collective-permute-start = (bf16[64,6144]{1,0:T(8,128)(2,1)}, bf16[64,6144]{1,0:T(8,128)(2,1)}, u32[]{:S(2)}, u32[]{:S(2)}) collective-permute-start(bf16[64,6144]{1,0:T(8,128)(2,1)} %slice.71), channel_id=1, source_target_pairs={{0,1},{1,2},{2,3},{3,4},{4,5},{5,6},{6,7},{8,9},{9,10},{10,11},{11... | collective-permute-start | bytes 2359304 | tf_op jit(solution)/shard_map/ppermute | solution.py:68
  10.2 1.3 collective-permute-start.1
  11.5 14.8 %collective-permute-start.2 = (f32[2,16,512]{2,1,0:T(8,128)S(1)}, f32[2,16,512]{2,1,0:T(8,128)S(1)}, u32[]{:S(2)}, u32[]{:S(2)}) collective-permute-start(f32[2,16,512]{2,1,0:T(8,128)S(1)} %constant_dynamic-update-slice_fusion), channel_id=1, source_target_pairs={{0,256},{256,0},{1,257},{257,1},{2,258},{258,2},{3,259},{259,3},{4... | collective-permute-start | bytes 196616 | tf_op jit(solution)/shard_map/ppermute | solution.py:53
  26.4 1.0 copy.30
  27.4 7.6 %all-to-all-start = ((bf16[32,2,16,512]{3,2,1,0:T(8,128)(2,1)}), bf16[32,2,16,512]{3,2,1,0:T(8,128)(2,1)S(1)}, u32[]{:S(2)}, u32[]{:S(2)}) async-start(bf16[32,2,16,512]{3,2,1,0:T(8,128)(2,1)} %copy.30), calls=%async_computation | async-start | bytes 2097152 | tf_op jit(solution)/shard_map/all_to_all | solution.py:51
  35.1 1.9 %fusion.28 = f32[22,64,128]{2,1,0:T(8,128)S(1)} fusion(f32[22,64,128]{2,1,0:T(8,128)S(1)} %broadcast_in_dim.50, s32[]{:T(128)S(6)} %select_n.87, bf16[64,8192]{1,0:T(8,128)(2,1)S(1)} %fusion.2, bf16[1,8192,128]{2,1,0:T(8,128)(2,1)} %param.8), kind=kOutput, calls=%fused_computation.33 | convolution fusion | flops 100663296 | bytes 2392068 | tf_op jit(solution)/shard_map/dot_general | solution.py:32
  37.2 1.6 collective-permute-start.3
  38.7 1.3 collective-permute-start.4
  40.0 1.5 fusion.34
  41.6 1.5 fusion.40
  43.1 1.7 collective-permute-done.2
  44.8 4.9 %all-to-all-done = bf16[32,2,16,512]{3,2,1,0:T(8,128)(2,1)S(1)} async-done(((bf16[32,2,16,512]{3,2,1,0:T(8,128)(2,1)}), bf16[32,2,16,512]{3,2,1,0:T(8,128)(2,1)S(1)}, u32[]{:S(2)}, u32[]{:S(2)}) %all-to-all-start) | async-done | bytes 1048608 | tf_op jit(solution)/shard_map/all_to_all | solution.py:51
  49.6 4.7 %collective-permute-start.7 = (bf16[2048,128]{1,0:T(8,128)(2,1)S(1)}, bf16[2048,128]{1,0:T(8,128)(2,1)S(1)}, u32[]{:S(2)}, u32[]{:S(2)}) collective-permute-start(bf16[2048,128]{1,0:T(8,128)(2,1)S(1)} %slice_bitcast_fusion), channel_id=1, source_target_pairs={{0,1},{7,6},{8,9},{15,14},{16,17},{23,22},{24,25},{31,30},{32,33},... | collective-permute-start | bytes 1572872 | tf_op jit(solution)/shard_map/ppermute | solution.py:77
  54.3 1.3 collective-permute-start.6
  55.8 3.1 %collective-permute-start.5 = (f32[2,16,512]{2,1,0:T(8,128)S(1)}, f32[2,16,512]{2,1,0:T(8,128)S(1)}, u32[]{:S(2)}, u32[]{:S(2)}) collective-permute-start(f32[2,16,512]{2,1,0:T(8,128)S(1)} %convert_reduce_fusion), channel_id=1, source_target_pairs={{0,256},{256,0},{1,257},{257,1},{2,258},{258,2},{3,259},{259,3},{4... | collective-permute-start | bytes 196616 | tf_op jit(solution)/shard_map/ppermute | solution.py:86
  59.7 3.8 %collective-permute-done.4 = bf16[64,6144]{1,0:T(8,128)(2,1)} collective-permute-done((bf16[64,6144]{1,0:T(8,128)(2,1)}, bf16[64,6144]{1,0:T(8,128)(2,1)}, u32[]{:S(2)}, u32[]{:S(2)}) %collective-permute-start.4) | collective-permute-done | bytes 786464 | tf_op jit(solution)/shard_map/ppermute | solution.py:69
  63.5 1.3 collective-permute-start.9
  64.7 2.1 %fusion.46 = f32[22,64,128]{2,1,0:T(8,128)S(1)} fusion(f32[22,64,128]{2,1,0:T(8,128)S(1)} %fusion.40, s32[]{:T(128)S(6)} %select_n.90, bf16[64,6144]{1,0:T(8,128)(2,1)} %collective-permute-done.3, bf16[1,8192,128]{2,1,0:T(8,128)(2,1)} %param.8), kind=kOutput, calls=%fused_computation.39 | convolution fusion | flops 100663296 | bytes 2392068 | tf_op jit(solution)/shard_map/dot_general | solution.py:32
  66.8 1.6 fusion.52
  68.4 10.5 %collective-permute-done.5 = f32[2,16,512]{2,1,0:T(8,128)S(1)} collective-permute-done((f32[2,16,512]{2,1,0:T(8,128)S(1)}, f32[2,16,512]{2,1,0:T(8,128)S(1)}, u32[]{:S(2)}, u32[]{:S(2)}) %collective-permute-start.5) | collective-permute-done | bytes 65568 | tf_op jit(solution)/shard_map/ppermute | solution.py:86
  79.7 5.2 %collective-permute-done.9 = bf16[64,6144]{1,0:T(8,128)(2,1)S(1)} collective-permute-done((bf16[64,6144]{1,0:T(8,128)(2,1)}, bf16[64,6144]{1,0:T(8,128)(2,1)S(1)}, u32[]{:S(2)}, u32[]{:S(2)}) %collective-permute-start.9) | collective-permute-done | bytes 786464 | tf_op jit(solution)/shard_map/ppermute | solution.py:69
  84.9 1.3 collective-permute-start.11
  89.2 14.9 %collective-permute-done.11 = bf16[64,6144]{1,0:T(8,128)(2,1)S(1)} collective-permute-done((bf16[64,6144]{1,0:T(8,128)(2,1)S(1)}, bf16[64,6144]{1,0:T(8,128)(2,1)S(1)}, u32[]{:S(2)}, u32[]{:S(2)}) %collective-permute-start.11) | collective-permute-done | bytes 786464 | tf_op jit(solution)/shard_map/ppermute | solution.py:69
  104.3 1.3 collective-permute-start.15
  106.0 1.0 pad_maximum_fusion.2
  107.1 1.6 collective-permute-start.19
  108.7 1.5 collective-permute-start.16
  110.2 1.0 constant_dynamic-update-slice_fusion.3
  111.8 1.6 collective-permute-start.18
  113.5 14.0 %collective-permute-done.15 = bf16[64,6144]{1,0:T(8,128)(2,1)} collective-permute-done((bf16[64,6144]{1,0:T(8,128)(2,1)S(1)}, bf16[64,6144]{1,0:T(8,128)(2,1)}, u32[]{:S(2)}, u32[]{:S(2)}) %collective-permute-start.15) | collective-permute-done | bytes 786464 | tf_op jit(solution)/shard_map/ppermute | solution.py:74
  127.5 1.3 collective-permute-start.17
  128.8 1.6 fusion.76
  131.8 1.1 broadcast_in_dim.63
  132.9 5.9 %all-to-all-start.1 = ((bf16[32,2,16,512]{3,2,1,0:T(8,128)(2,1)}), bf16[32,2,16,512]{3,2,1,0:T(8,128)(2,1)S(1)}, u32[]{:S(2)}, u32[]{:S(2)}) async-start(bf16[32,2,16,512]{3,2,1,0:T(8,128)(2,1)} %broadcast_in_dim.63), calls=%async_computation.1 | async-start | bytes 2097152 | tf_op jit(solution)/shard_map/all_to_all | solution.py:119
  138.8 8.1 %collective-permute-done.17 = bf16[64,6144]{1,0:T(8,128)(2,1)} collective-permute-done((bf16[64,6144]{1,0:T(8,128)(2,1)}, bf16[64,6144]{1,0:T(8,128)(2,1)}, u32[]{:S(2)}, u32[]{:S(2)}) %collective-permute-start.17) | collective-permute-done | bytes 786464 | tf_op jit(solution)/shard_map/ppermute | solution.py:74
  146.8 2.1 %fusion.82 = f32[22,64,128]{2,1,0:T(8,128)S(1)} fusion(f32[22,64,128]{2,1,0:T(8,128)S(1)} %fusion.76, s32[]{:T(128)S(6)} %select_n.103, bf16[64,6144]{1,0:T(8,128)(2,1)} %collective-permute-done.17, bf16[1,8192,128]{2,1,0:T(8,128)(2,1)} %param.8), kind=kOutput, calls=%fused_computation.51 | convolution fusion | flops 100663296 | bytes 2392068 | tf_op jit(solution)/shard_map/dot_general | solution.py:32
  148.9 1.5 fusion.125
  150.4 1.3 collective-permute-start.21
  151.7 2.2 %fusion.93 = f32[256,512]{0,1:T(8,128)S(1)} fusion(bf16[256,2048]{1,0:T(8,128)(2,1)} %constant_dynamic-update-slice_fusion.2, bf16[2048,128]{1,0:T(8,128)(2,1)S(1)} %get-tuple-element.63, bf16[2048,128]{1,0:T(8,128)(2,1)S(1)} %collective-permute-done.20, bf16[2048,128]{1,0:T(8,128)(2,1)S(1)} %get-tuple-element.62, bf16[2048,128]{1,0:T(8,128)(2,1)S(1)} %slice_bitcast_fusion), kind=kOutput, calls=%fused_computation.61 | convolution fusion | flops 545259520 | bytes 3670016 | tf_op jit(solution)/shard_map/dot_general | solution.py:32
  153.9 2.3 %broadcast_select_fusion.1 = (f32[256,512]{0,1:T(8,128)S(1)}, f32[256,512]{0,1:T(8,128)S(1)}) fusion(f32[256,512]{0,1:T(8,128)S(1)} %fusion.93, pred[]{:T(512)S(6)} %lt.48, bf16[256,2048]{1,0:T(8,128)(2,1)} %collective-permute-done.18, bf16[2048,128]{1,0:T(8,128)(2,1)S(1)} %get-tuple-element.63, bf16[2048,128]{1,0:T(8,128)(2,1)} %copy-done.6, ...), kind=kOutput, calls=%fused_computation.68 | convolution fusion | flops 545521664 | bytes 4718593 | tf_op jit(solution)/shard_map/dot_general | solution.py:32
  158.8 1.3 collective-permute-start.24
  160.1 1.1 copy.38
  161.2 10.4 %collective-permute-done.21 = bf16[64,6144]{1,0:T(8,128)(2,1)} collective-permute-done((bf16[64,6144]{1,0:T(8,128)(2,1)}, bf16[64,6144]{1,0:T(8,128)(2,1)}, u32[]{:S(2)}, u32[]{:S(2)}) %collective-permute-start.21) | collective-permute-done | bytes 786464 | tf_op jit(solution)/shard_map/ppermute | solution.py:74
  171.6 1.5 fusion.88
  174.0 0.8 copy.39
  (70 shorter events, 11.5 us)
Async XLA Ops:
  2.9 8.6 %copy-start.4 = (f32[1,16,512]{2,1,0:T(8,128)S(1)}, f32[1,16,512]{2,1,0:T(8,128)}, u32[]{:S(2)}) copy-start(f32[1,16,512]{2,1,0:T(8,128)} %param.10) | copy-start | bytes 98308
  2.9 8.6 %copy-start.5 = (f32[1,16,512]{2,1,0:T(8,128)S(1)}, f32[1,16,512]{2,1,0:T(8,128)}, u32[]{:S(2)}) copy-start(f32[1,16,512]{2,1,0:T(8,128)} %param.11) | copy-start | bytes 98308
  2.9 23.5 %copy-start = (bf16[1,1,1024,512]{3,2,1,0:T(8,128)(2,1)S(1)}, bf16[1,1,1024,512]{3,2,1,0:T(8,128)(2,1)}, u32[]{:S(2)}) copy-start(bf16[1,1,1024,512]{3,2,1,0:T(8,128)(2,1)} %param.9) | copy-start | bytes 3145732
  5.5 31.7 %collective-permute-start = (bf16[64,6144]{1,0:T(8,128)(2,1)}, bf16[64,6144]{1,0:T(8,128)(2,1)}, u32[]{:S(2)}, u32[]{:S(2)}) collective-permute-start(bf16[64,6144]{1,0:T(8,128)(2,1)} %slice.71), channel_id=1, source_target_pairs={{0,1},{1,2},{2,3},{3,4},{4,5},{5,6},{6,7},{8,9},{9,10},{10,11},{11... | collective-permute-start | bytes 2359304 | tf_op jit(solution)/shard_map/ppermute | solution.py:68
  10.2 28.5 %collective-permute-start.1 = (bf16[64,6144]{1,0:T(8,128)(2,1)}, bf16[64,6144]{1,0:T(8,128)(2,1)}, u32[]{:S(2)}, u32[]{:S(2)}) collective-permute-start(bf16[64,6144]{1,0:T(8,128)(2,1)} %slice.71), channel_id=1, source_target_pairs={{1,0},{2,1},{3,2},{4,3},{5,4},{6,5},{7,6},{9,8},{10,9},{11,10},{12... | collective-permute-start | bytes 2359304 | tf_op jit(solution)/shard_map/ppermute | solution.py:69
  11.5 33.2 %collective-permute-start.2 = (f32[2,16,512]{2,1,0:T(8,128)S(1)}, f32[2,16,512]{2,1,0:T(8,128)S(1)}, u32[]{:S(2)}, u32[]{:S(2)}) collective-permute-start(f32[2,16,512]{2,1,0:T(8,128)S(1)} %constant_dynamic-update-slice_fusion), channel_id=1, source_target_pairs={{0,256},{256,0},{1,257},{257,1},{2,258},{258,2},{3,259},{259,3},{4... | collective-permute-start | bytes 196616 | tf_op jit(solution)/shard_map/ppermute | solution.py:53
  27.4 22.2 %all-to-all-start = ((bf16[32,2,16,512]{3,2,1,0:T(8,128)(2,1)}), bf16[32,2,16,512]{3,2,1,0:T(8,128)(2,1)S(1)}, u32[]{:S(2)}, u32[]{:S(2)}) async-start(bf16[32,2,16,512]{3,2,1,0:T(8,128)(2,1)} %copy.30), calls=%async_computation | async-start | bytes 2097152 | tf_op jit(solution)/shard_map/all_to_all | solution.py:51
  35.0 2.1 %copy-start.1 = (bf16[1,8192,128]{2,1,0:T(8,128)(2,1)S(1)}, bf16[1,8192,128]{2,1,0:T(8,128)(2,1)}, u32[]{:S(2)}) copy-start(bf16[1,8192,128]{2,1,0:T(8,128)(2,1)} %param.8) | copy-start | bytes 6291460
  37.2 21.8 %collective-permute-start.3 = (bf16[64,6144]{1,0:T(8,128)(2,1)}, bf16[64,6144]{1,0:T(8,128)(2,1)}, u32[]{:S(2)}, u32[]{:S(2)}) collective-permute-start(bf16[64,6144]{1,0:T(8,128)(2,1)} %collective-permute-done), channel_id=1, source_target_pairs={{1,2},{2,3},{3,4},{4,5},{5,6},{6,7},{9,10},{10,11},{11,12},{12,13}... | collective-permute-start | bytes 2359304 | tf_op jit(solution)/shard_map/ppermute | solution.py:68
  38.7 24.7 %collective-permute-start.4 = (bf16[64,6144]{1,0:T(8,128)(2,1)}, bf16[64,6144]{1,0:T(8,128)(2,1)}, u32[]{:S(2)}, u32[]{:S(2)}) collective-permute-start(bf16[64,6144]{1,0:T(8,128)(2,1)} %collective-permute-done.1), channel_id=1, source_target_pairs={{1,0},{2,1},{3,2},{4,3},{5,4},{6,5},{9,8},{10,9},{11,10},{12,11},{... | collective-permute-start | bytes 2359304 | tf_op jit(solution)/shard_map/ppermute | solution.py:69
  49.6 17.2 %copy-start.2 = (bf16[1,8192,128]{2,1,0:T(8,128)(2,1)S(1)}, bf16[1,8192,128]{2,1,0:T(8,128)(2,1)}, u32[]{:S(2)}) copy-start(bf16[1,8192,128]{2,1,0:T(8,128)(2,1)} %param.8) | copy-start | bytes 6291460
  49.6 29.3 %collective-permute-start.7 = (bf16[2048,128]{1,0:T(8,128)(2,1)S(1)}, bf16[2048,128]{1,0:T(8,128)(2,1)S(1)}, u32[]{:S(2)}, u32[]{:S(2)}) collective-permute-start(bf16[2048,128]{1,0:T(8,128)(2,1)S(1)} %slice_bitcast_fusion), channel_id=1, source_target_pairs={{0,1},{7,6},{8,9},{15,14},{16,17},{23,22},{24,25},{31,30},{32,33},... | collective-permute-start | bytes 1572872 | tf_op jit(solution)/shard_map/ppermute | solution.py:77
  54.3 24.6 %collective-permute-start.6 = (bf16[64,2048]{1,0:T(8,128)(2,1)S(1)}, bf16[64,2048]{1,0:T(8,128)(2,1)S(1)}, u32[]{:S(2)}, u32[]{:S(2)}) collective-permute-start(bf16[64,2048]{1,0:T(8,128)(2,1)S(1)} %slice.72), channel_id=1, source_target_pairs={{0,1},{7,6},{8,9},{15,14},{16,17},{23,22},{24,25},{31,30},{32,33},... | collective-permute-start | bytes 786440 | tf_op jit(solution)/shard_map/ppermute | solution.py:77
  55.8 23.1 %collective-permute-start.5 = (f32[2,16,512]{2,1,0:T(8,128)S(1)}, f32[2,16,512]{2,1,0:T(8,128)S(1)}, u32[]{:S(2)}, u32[]{:S(2)}) collective-permute-start(f32[2,16,512]{2,1,0:T(8,128)S(1)} %convert_reduce_fusion), channel_id=1, source_target_pairs={{0,256},{256,0},{1,257},{257,1},{2,258},{258,2},{3,259},{259,3},{4... | collective-permute-start | bytes 196616 | tf_op jit(solution)/shard_map/ppermute | solution.py:86
  59.0 27.2 %collective-permute-start.8 = (bf16[64,6144]{1,0:T(8,128)(2,1)}, bf16[64,6144]{1,0:T(8,128)(2,1)S(1)}, u32[]{:S(2)}, u32[]{:S(2)}) collective-permute-start(bf16[64,6144]{1,0:T(8,128)(2,1)} %collective-permute-done.3), channel_id=1, source_target_pairs={{2,3},{3,4},{4,5},{5,6},{6,7},{10,11},{11,12},{12,13},{13,14},{14,... | collective-permute-start | bytes 2359304 | tf_op jit(solution)/shard_map/ppermute | solution.py:68
  63.5 21.4 %collective-permute-start.9 = (bf16[64,6144]{1,0:T(8,128)(2,1)}, bf16[64,6144]{1,0:T(8,128)(2,1)S(1)}, u32[]{:S(2)}, u32[]{:S(2)}) collective-permute-start(bf16[64,6144]{1,0:T(8,128)(2,1)} %collective-permute-done.4), channel_id=1, source_target_pairs={{1,0},{2,1},{3,2},{4,3},{5,4},{9,8},{10,9},{11,10},{12,11},{13,12}... | collective-permute-start | bytes 2359304 | tf_op jit(solution)/shard_map/ppermute | solution.py:69
  79.0 8.8 %collective-permute-start.10 = (bf16[128,2048]{1,0:T(8,128)(2,1)S(1)}, bf16[128,2048]{1,0:T(8,128)(2,1)S(1)}, u32[]{:S(2)}, u32[]{:S(2)}) collective-permute-start(bf16[128,2048]{1,0:T(8,128)(2,1)S(1)} %pad_maximum_fusion.4), channel_id=1, source_target_pairs={{1,2},{6,5},{9,10},{14,13},{17,18},{22,21},{25,26},{30,29},{33,34}... | collective-permute-start | bytes 1572872 | tf_op jit(solution)/shard_map/ppermute | solution.py:77
  84.9 19.3 %collective-permute-start.11 = (bf16[64,6144]{1,0:T(8,128)(2,1)S(1)}, bf16[64,6144]{1,0:T(8,128)(2,1)S(1)}, u32[]{:S(2)}, u32[]{:S(2)}) collective-permute-start(bf16[64,6144]{1,0:T(8,128)(2,1)S(1)} %collective-permute-done.9), channel_id=1, source_target_pairs={{1,0},{2,1},{3,2},{4,3},{9,8},{10,9},{11,10},{12,11},{17,16},{18,1... | collective-permute-start | bytes 2359304 | tf_op jit(solution)/shard_map/ppermute | solution.py:69
  86.2 18.0 %collective-permute-start.12 = (bf16[64,6144]{1,0:T(8,128)(2,1)S(1)}, bf16[64,6144]{1,0:T(8,128)(2,1)S(1)}, u32[]{:S(2)}, u32[]{:S(2)}) collective-permute-start(bf16[64,6144]{1,0:T(8,128)(2,1)S(1)} %collective-permute-done.8), channel_id=1, source_target_pairs={{3,4},{4,5},{5,6},{6,7},{11,12},{12,13},{13,14},{14,15},{19,20},{2... | collective-permute-start | bytes 2359304 | tf_op jit(solution)/shard_map/ppermute | solution.py:68
  87.8 18.2 %collective-permute-start.13 = (bf16[192,2048]{1,0:T(8,128)(2,1)S(1)}, bf16[192,2048]{1,0:T(8,128)(2,1)S(1)}, u32[]{:S(2)}, u32[]{:S(2)}) collective-permute-start(bf16[192,2048]{1,0:T(8,128)(2,1)S(1)} %pad_maximum_fusion.3), channel_id=1, source_target_pairs={{2,3},{5,4},{10,11},{13,12},{18,19},{21,20},{26,27},{29,28},{34,35... | collective-permute-start | bytes 2359304 | tf_op jit(solution)/shard_map/ppermute | solution.py:77
  88.5 17.5 %collective-permute-start.14 = (bf16[2048,128]{1,0:T(8,128)(2,1)S(1)}, bf16[2048,128]{1,0:T(8,128)(2,1)S(1)}, u32[]{:S(2)}, u32[]{:S(2)}) collective-permute-start(bf16[2048,128]{1,0:T(8,128)(2,1)S(1)} %collective-permute-done.7), channel_id=1, source_target_pairs={{1,2},{6,5},{9,10},{14,13},{17,18},{22,21},{25,26},{30,29},{33,34}... | collective-permute-start | bytes 1572872 | tf_op jit(solution)/shard_map/ppermute | solution.py:77
  104.3 23.2 %collective-permute-start.15 = (bf16[64,6144]{1,0:T(8,128)(2,1)S(1)}, bf16[64,6144]{1,0:T(8,128)(2,1)}, u32[]{:S(2)}, u32[]{:S(2)}) collective-permute-start(bf16[64,6144]{1,0:T(8,128)(2,1)S(1)} %broadcast_select_fusion), channel_id=1, source_target_pairs={{4,5},{5,6},{6,7},{1,0},{2,1},{3,2},{12,13},{13,14},{14,15},{9,8},... | collective-permute-start | bytes 2359304 | tf_op jit(solution)/shard_map/ppermute | solution.py:74
  107.1 41.8 %collective-permute-start.19 = (bf16[4096,128]{1,0:T(8,128)(2,1)}, bf16[4096,128]{1,0:T(8,128)(2,1)}, u32[]{:S(2)}, u32[]{:S(2)}) collective-permute-start(bf16[4096,128]{1,0:T(8,128)(2,1)} %pad_maximum_fusion.2), channel_id=1, source_target_pairs={{2,3},{5,4},{10,11},{13,12},{18,19},{21,20},{26,27},{29,28},{34,35... | collective-permute-start | bytes 3145736 | tf_op jit(solution)/shard_map/ppermute | solution.py:77
  108.7 21.7 %collective-permute-start.16 = (bf16[2048,128]{1,0:T(8,128)(2,1)S(1)}, bf16[2048,128]{1,0:T(8,128)(2,1)}, u32[]{:S(2)}, u32[]{:S(2)}) collective-permute-start(bf16[2048,128]{1,0:T(8,128)(2,1)S(1)} %slice_bitcast_fusion), channel_id=1, source_target_pairs={{1,2},{6,5},{9,10},{14,13},{17,18},{22,21},{25,26},{30,29},{33,34}... | collective-permute-start | bytes 1572872 | tf_op jit(solution)/shard_map/ppermute | solution.py:77
  111.8 37.1 %collective-permute-start.18 = (bf16[256,2048]{1,0:T(8,128)(2,1)}, bf16[256,2048]{1,0:T(8,128)(2,1)}, u32[]{:S(2)}, u32[]{:S(2)}) collective-permute-start(bf16[256,2048]{1,0:T(8,128)(2,1)} %constant_dynamic-update-slice_fusion.2), channel_id=1, source_target_pairs={{3,4},{4,3},{11,12},{12,11},{19,20},{20,19},{27,28},{28,27},{35,36... | collective-permute-start | bytes 3145736 | tf_op jit(solution)/shard_map/ppermute | solution.py:111
  127.5 19.3 %collective-permute-start.17 = (bf16[64,6144]{1,0:T(8,128)(2,1)}, bf16[64,6144]{1,0:T(8,128)(2,1)}, u32[]{:S(2)}, u32[]{:S(2)}) collective-permute-start(bf16[64,6144]{1,0:T(8,128)(2,1)} %collective-permute-done.15), channel_id=1, source_target_pairs={{5,6},{6,7},{1,0},{2,1},{13,14},{14,15},{9,8},{10,9},{21,22},{22,2... | collective-permute-start | bytes 2359304 | tf_op jit(solution)/shard_map/ppermute | solution.py:74
  130.4 18.5 %collective-permute-start.20 = (bf16[2048,128]{1,0:T(8,128)(2,1)}, bf16[2048,128]{1,0:T(8,128)(2,1)S(1)}, u32[]{:S(2)}, u32[]{:S(2)}) collective-permute-start(bf16[2048,128]{1,0:T(8,128)(2,1)} %collective-permute-done.16), channel_id=1, source_target_pairs={{2,3},{5,4},{10,11},{13,12},{18,19},{21,20},{26,27},{29,28},{34,35... | collective-permute-start | bytes 1572872 | tf_op jit(solution)/shard_map/ppermute | solution.py:77
  132.9 27.2 %all-to-all-start.1 = ((bf16[32,2,16,512]{3,2,1,0:T(8,128)(2,1)}), bf16[32,2,16,512]{3,2,1,0:T(8,128)(2,1)S(1)}, u32[]{:S(2)}, u32[]{:S(2)}) async-start(bf16[32,2,16,512]{3,2,1,0:T(8,128)(2,1)} %broadcast_in_dim.63), calls=%async_computation.1 | async-start | bytes 2097152 | tf_op jit(solution)/shard_map/all_to_all | solution.py:119
  148.9 2.8 %copy-start.6 = (bf16[2048,128]{1,0:T(8,128)(2,1)}, bf16[2048,128]{1,0:T(8,128)(2,1)S(1)}, u32[]{:S(2)}) copy-start(bf16[2048,128]{1,0:T(8,128)(2,1)S(1)} %collective-permute-done.20) | copy-start | bytes 1572868
  150.4 21.2 %collective-permute-start.21 = (bf16[64,6144]{1,0:T(8,128)(2,1)}, bf16[64,6144]{1,0:T(8,128)(2,1)}, u32[]{:S(2)}, u32[]{:S(2)}) collective-permute-start(bf16[64,6144]{1,0:T(8,128)(2,1)} %collective-permute-done.17), channel_id=1, source_target_pairs={{6,7},{1,0},{14,15},{9,8},{22,23},{17,16},{30,31},{25,24},{38,39},... | collective-permute-start | bytes 2359304 | tf_op jit(solution)/shard_map/ppermute | solution.py:74
  157.5 15.9 %collective-permute-start.22 = (bf16[512,128]{0,1:T(8,128)(2,1)}, bf16[512,128]{0,1:T(8,128)(2,1)S(1)}, u32[]{:S(2)}, u32[]{:S(2)}) collective-permute-start(bf16[512,128]{0,1:T(8,128)(2,1)} %get-tuple-element.64), channel_id=1, source_target_pairs={{3,2},{4,5},{11,10},{12,13},{19,18},{20,21},{27,26},{28,29},{35,34... | collective-permute-start | bytes 393224 | tf_op jit(solution)/shard_map/ppermute | solution.py:132
  158.1 15.2 %collective-permute-start.23 = (bf16[512,128]{0,1:T(8,128)(2,1)}, bf16[512,128]{0,1:T(8,128)(2,1)S(1)}, u32[]{:S(2)}, u32[]{:S(2)}) collective-permute-start(bf16[512,128]{0,1:T(8,128)(2,1)} %get-tuple-element.66), channel_id=1, source_target_pairs={{3,1},{4,6},{11,9},{12,14},{19,17},{20,22},{27,25},{28,30},{35,33}... | collective-permute-start | bytes 393224 | tf_op jit(solution)/shard_map/ppermute | solution.py:132
  158.8 14.5 %collective-permute-start.24 = (bf16[512,128]{0,1:T(8,128)(2,1)}, bf16[512,128]{0,1:T(8,128)(2,1)S(1)}, u32[]{:S(2)}, u32[]{:S(2)}) collective-permute-start(bf16[512,128]{0,1:T(8,128)(2,1)} %get-tuple-element.65), channel_id=1, source_target_pairs={{3,0},{4,7},{11,8},{12,15},{19,16},{20,23},{27,24},{28,31},{35,32}... | collective-permute-start | bytes 393224 | tf_op jit(solution)/shard_map/ppermute | solution.py:132
  160.1 11.5 %copy-start.3 = (bf16[1,8192,128]{2,1,0:T(8,128)(2,1)S(1)}, bf16[1,8192,128]{2,1,0:T(8,128)(2,1)}, u32[]{:S(2)}) copy-start(bf16[1,8192,128]{2,1,0:T(8,128)(2,1)} %param.8) | copy-start | bytes 6291460

commit v6 on v5

v6 whole, which is shorter than its diff:
```python
import math

import jax
import jax.numpy as jnp
from jax import lax
from jax.experimental import pallas as pl
from jax.experimental.pallas import tpu as pltpu
from jax.sharding import Mesh
from jax.sharding import PartitionSpec as P

HD = 128


EPSILON = 1e-05
ROPE_BASE = 500000.0
LR_OUTER = 0.7
MOMENTUM_OUTER = 0.9

PLANE = ("y", "x", "core")
REPLICA = ("zh",) + PLANE

K_LINE = 5888


def rotary_tables(rows):
    half = HD // 2
    index = jnp.arange(half).astype(jnp.float32)
    inverse = jnp.exp(-(2.0 * index / HD) * math.log(ROPE_BASE))
    angles = jnp.arange(rows).astype(jnp.float32)[:, None] * inverse[None, :]
    return jnp.cos(angles), jnp.sin(angles)


def dot(a, b):
    return jnp.dot(a, b, preferred_element_type=jnp.float32)


def nesterov(outer_rows, moment_rows, summed, replicas):
    delta = outer_rows - summed / replicas
    moment_next = MOMENTUM_OUTER * moment_rows + delta
    outer_next = outer_rows - LR_OUTER * (delta + MOMENTUM_OUTER * moment_next)
    return (outer_next, moment_next)


hold = lax.optimization_barrier


def middle_kernel(low, near, far, w0, w13, w2, *outs):
    is_low = low[0] == 1
    size = w0.shape[0]
    w1, w3 = w13.at[:size], w13.at[size:]
    for pair, out in (((w0, w1), outs[:2]), ((w2, w3), outs[2:])):
        w = jnp.concatenate([pair[0][...], pair[1][...]], axis=1)
        p, q = dot(near[...], w), dot(far[...], w)
        first, last = jnp.where(is_low, p, q), jnp.where(is_low, q, p)
        for i, ref in enumerate(out):
            cols = slice(HD * i, HD * i + HD)
            ref[:256] = first[:, cols].astype(ref.dtype)
            for k in range(4):
                ref[256 + 64 * k : 320 + 64 * k] = last[192 - 64 * k : 256 - 64 * k, cols].astype(ref.dtype)


def middle_products(low, near, far, *weights):
    types = (jnp.float32, jnp.bfloat16, jnp.bfloat16, jnp.bfloat16)
    return pl.pallas_call(
        middle_kernel,
        out_shape=[jax.ShapeDtypeStruct((512, HD), t) for t in types],
        in_specs=[pl.BlockSpec(memory_space=pltpu.SMEM)] + [pl.BlockSpec(memory_space=pltpu.VMEM)] * 5,
        out_specs=[pl.BlockSpec(memory_space=pltpu.VMEM)] * 4,
        cost_estimate=pl.CostEstimate(flops=0, bytes_accessed=0, transcendentals=0),
        compiler_params=pltpu.CompilerParams(vmem_limit_bytes=24 << 20),
    )(low.astype(jnp.int32).reshape(1), near, far, *weights)


def body(tokens, norm_gain, key_weight, inner_params, outer_params, outer_momentum):
    me = lax.axis_index("tensor")
    zh = lax.axis_index("zh")
    low = me < 4

    params = inner_params[0, 0].reshape(2, 32, 16, 512).transpose(1, 0, 2, 3)
    pieces = lax.all_to_all(params, PLANE, 0, 0, tiled=True)

    gain = norm_gain.astype(jnp.float32)
    block_f32 = tokens.astype(jnp.float32)
    scale = lax.rsqrt(jnp.mean(block_f32 * block_f32, axis=-1, keepdims=True) + EPSILON)

    def normed(block, gain):
        return (block.astype(jnp.float32) * scale * gain).astype(jnp.bfloat16)

    weight = key_weight[0]
    w_line, w_rest = weight[:K_LINE], weight[K_LINE:]
    shard = normed(tokens[:, :K_LINE], gain[:K_LINE])

    rows = jnp.zeros((22, 64, HD), jnp.float32)

    def put(rows, block, at):
        return lax.dynamic_update_slice(rows, dot(block, w_line)[None], (7 + at, 0, 0))

    def hop(a, b, s):
        a = lax.ppermute(a, "tensor", [(j, j + 1) for j in range(s, 7)])
        b = lax.ppermute(b, "tensor", [(j + 1, j) for j in range(7 - s)])
        return a, b

    def hop_out(x, s):
        pairs = [(j, j + 1) for j in range(s, 7)] + [(j + 1, j) for j in range(7 - s)]
        return lax.ppermute(x, "tensor", pairs)

    def inward(x, d):
        return lax.ppermute(x, "tensor", [(3 - d, 4 - d), (4 + d, 3 + d)])

    a, b = hop(shard, shard, 0)
    rows = put(rows, shard, me)
    rows, rest_in = hold((rows, tokens[:, K_LINE:]))
    rest = normed(rest_in, gain[K_LINE:])

    rows0 = put(put(rows, a, me - 1), b, me + 1)
    a, b = hop(a, b, 1)
    rows, pieces, rest, w_rest = hold((rows0, pieces, rest, w_rest))
    t3, w3 = inward(rest, 3), inward(w_rest, 3)
    partial = jnp.sum(pieces.astype(jnp.float32), axis=0)
    other = lax.dynamic_index_in_dim(partial, 1 - zh, 0, keepdims=False)
    own = lax.dynamic_index_in_dim(partial, zh, 0, keepdims=False)
    came = lax.ppermute(other, "zh", [(0, 1), (1, 0)])

    rows1 = put(put(rows, a, me - 2), b, me + 2)
    a, b = hop(a, b, 2)
    rows, came, t3, w3 = hold((rows1, came, t3, w3))
    t2 = inward(jnp.concatenate([t3, rest]), 2)
    outer_next, moment_next = nesterov(outer_params[0], outer_momentum[0], own + came, 64)
    mine = outer_next.astype(jnp.bfloat16)
    theirs = lax.ppermute(mine, "zh", [(0, 1), (1, 0)])

    rows2 = put(put(rows, a, me - 3), b, me + 3)
    a, b = hop(a, b, 3)
    rows, t2, w3, theirs = hold((rows2, t2, w3, theirs))
    t1 = inward(jnp.concatenate([t2, rest]), 1)
    w3 = inward(w3, 2)
    pair = jnp.where(zh == 0, jnp.stack([mine, theirs]), jnp.stack([theirs, mine]))

    x = jnp.where(low, b, a)
    rows3 = put(rows, x, jnp.where(low, me + 4, me - 4))
    x = hop_out(x, 4)
    rows, t1, w3, w1, w2, pair = hold((rows3, t1, w3, w_rest, w_rest, pair))
    near = jnp.concatenate([t1, rest])
    far = lax.ppermute(near, "tensor", [(3, 4), (4, 3)])
    w13 = inward(jnp.concatenate([w1, w3]), 1)
    w2 = inward(w2, 2)

    rows4 = put(rows, x, jnp.where(low, me + 5, me - 5))
    x = hop_out(x, 5)
    rows, w2, w13, far = hold((rows4, w2, w13, far))
    w2 = inward(w2, 1)
    synced = lax.all_to_all(jnp.broadcast_to(pair[None], (32, 2, 16, 512)), PLANE, 0, 0, tiled=True)

    y = hop_out(x, 6)
    rows, w2, synced = hold((rows, w2, synced))
    rows5 = put(rows, x, jnp.where(low, me + 6, me - 6))
    rows, w2 = hold((rows5, w2))
    blocks = middle_products(low, near, far, w_rest, w13, w2)
    middle = jnp.where((me == 3) | (me == 4), blocks[0], 0.0)
    for d in (3, 2, 1):
        back = lax.ppermute(blocks[d], "tensor", [(3, 3 - d), (4, 4 + d)])
        middle += back.astype(jnp.float32)

    rows = put(rows, y, jnp.where(low, me + 7, me - 7))
    synced = synced.transpose(1, 0, 2, 3).reshape(1024, 512)
    projected = rows[7:15].reshape(512, HD) + middle
    cosine, sine = rotary_tables(512)
    first, second = projected[:, : HD // 2], projected[:, HD // 2 :]
    key_rows = jnp.concatenate(
        [first * cosine - second * sine, second * cosine + first * sine], axis=-1
    ).astype(jnp.bfloat16)
    return (key_rows, outer_next[None], moment_next[None], synced[None])


def solution(mesh):
    fine = Mesh(mesh.devices.reshape(2, 4, 4, 2, 8), REPLICA + ("tensor",))
    in_specs = (
        P(REPLICA + ("tensor",), None),
        P(),
        P(REPLICA, None, "tensor"),
        P(REPLICA, "tensor", None, None),
        P("tensor", REPLICA, None),
        P("tensor", REPLICA, None),
    )
    out_specs = (
        P(REPLICA, "tensor"),
        P("tensor", REPLICA, None),
        P("tensor", REPLICA, None),
        P("tensor", None, None),
    )
    return jax.shard_map(body, mesh=fine, in_specs=in_specs, out_specs=out_specs, check_vma=False)
```

time: 177 us -> 169 us (0.955)
  the two profiles are of different devices: /device:TPU:6 before, /device:TPU:64 now
where the time goes in v6:
time: 169 us; the launch traced here: 167 us
  starting transfers between devices  95.1 us (56%)
  waiting for transfers between devices  29.9 us (18%)
  matrix products  22.3 us (13%)
  local copies, waits for them, and re-layouts  9.16 us (5%)
  other arithmetic  7.11 us (4%)
  Pallas kernels  2.65 us (2%)
    ppermute x8, starting transfers between devices, inward(): return lax.ppermute(x, 'tensor', [(3 - d, 4 - d), (4 + d, 3 + d)])  22.9 us
    dot_general x11, matrix products, dot(): return jnp.dot(a, b, preferred_element_type=jnp.float32)  22.3 us
    ppermute x1, starting transfers between devices, body(): came = lax.ppermute(other, 'zh', [(0, 1), (1, 0)])  13.8 us
    ppermute x4, starting transfers between devices, hop(): b = lax.ppermute(b, 'tensor', [(j + 1, j) for j in range(7 - s)])  11.6 us
    ppermute x4, starting transfers between devices, hop(): a = lax.ppermute(a, 'tensor', [(j, j + 1) for j in range(s, 7)])  11.3 us
    ppermute x3, starting transfers between devices, hop_out(): return lax.ppermute(x, 'tensor', pairs)  11.2 us
    ppermute x8, waiting for transfers between devices, inward(): return lax.ppermute(x, 'tensor', [(3 - d, 4 - d), (4 + d, 3 + d)])  10.8 us
    ppermute x4, waiting for transfers between devices, hop(): b = lax.ppermute(b, 'tensor', [(j + 1, j) for j in range(7 - s)])  9.1 us
  transfers between devices with their start and end apart: 27, of which 12 were waited for; matrix products, arithmetic and copies ran while one was open for 19% of the time, Pallas kernels for 2%

profile of v6, /device:TPU:64, one launch (start us, length us, event | category | flops | bytes accessed | tf_op | source)
XLA Modules:
  0.0 167.3 jit_solution(3472172383547897912)
XLA Ops:
  0.7 1.7 %multiply_reduce_fusion = f32[64]{0:T(128)S(1)} fusion(bf16[64,8192]{1,0:T(8,128)(2,1)} %param.6), kind=kLoop, calls=%fused_computation.1 | loop fusion | flops 1572800 | bytes 1048832 | tf_op jit(solution)/shard_map/reduce_sum | solution.py:84
  3.1 1.1 multiply_convert_fusion
  4.2 3.8 %collective-permute-start = (bf16[64,5888]{1,0:T(8,128)(2,1)}, bf16[64,5888]{1,0:T(8,128)(2,1)}, u32[]{:S(2)}, u32[]{:S(2)}) collective-permute-start(bf16[64,5888]{1,0:T(8,128)(2,1)} %multiply_convert_fusion), channel_id=1, source_target_pairs={{0,1},{1,2},{2,3},{3,4},{4,5},{5,6},{6,7},{8,9},{9,10},{10,11},{11... | collective-permute-start | bytes 2261000 | tf_op jit(solution)/shard_map/ppermute | solution.py:99
  8.0 2.0 %collective-permute-start.1 = (bf16[64,5888]{1,0:T(8,128)(2,1)}, bf16[64,5888]{1,0:T(8,128)(2,1)}, u32[]{:S(2)}, u32[]{:S(2)}) collective-permute-start(bf16[64,5888]{1,0:T(8,128)(2,1)} %multiply_convert_fusion), channel_id=1, source_target_pairs={{1,0},{2,1},{3,2},{4,3},{5,4},{6,5},{7,6},{9,8},{10,9},{11,10},{12... | collective-permute-start | bytes 2261000 | tf_op jit(solution)/shard_map/ppermute | solution.py:100
  10.1 1.1 copy.12
  11.1 7.3 %all-to-all-start = ((bf16[32,2,16,512]{3,2,1,0:T(8,128)(2,1)}), bf16[32,2,16,512]{3,2,1,0:T(8,128)(2,1)S(1)}, u32[]{:S(2)}, u32[]{:S(2)}) async-start(bf16[32,2,16,512]{3,2,1,0:T(8,128)(2,1)} %copy.12), calls=%async_computation | async-start | bytes 2097152 | tf_op jit(solution)/shard_map/all_to_all | solution.py:80
  18.5 1.1 slice_bitcast_fusion.w0
  19.7 2.1 %fusion.25 = f32[22,64,128]{2,1,0:T(8,128)S(1)} fusion(f32[22,64,128]{2,1,0:T(8,128)S(1)} %broadcast_in_dim.57, s32[]{:T(128)S(6)} %select_n.77, bf16[64,5888]{1,0:T(8,128)(2,1)} %multiply_convert_fusion, bf16[1,8192,128]{2,1,0:T(8,128)(2,1)} %param.8), kind=kOutput, calls=%fused_computation.27 | convolution fusion | flops 96468992 | bytes 2293764 | tf_op jit(solution)/shard_map/dot_general | solution.py:34
  22.8 2.2 %collective-permute-done = bf16[64,5888]{1,0:T(8,128)(2,1)} collective-permute-done((bf16[64,5888]{1,0:T(8,128)(2,1)}, bf16[64,5888]{1,0:T(8,128)(2,1)}, u32[]{:S(2)}, u32[]{:S(2)}) %collective-permute-start) | collective-permute-done | bytes 753696 | tf_op jit(solution)/shard_map/ppermute | solution.py:99
  25.0 4.5 %collective-permute-start.2 = (bf16[64,5888]{1,0:T(8,128)(2,1)}, bf16[64,5888]{1,0:T(8,128)(2,1)}, u32[]{:S(2)}, u32[]{:S(2)}) collective-permute-start(bf16[64,5888]{1,0:T(8,128)(2,1)} %collective-permute-done), channel_id=1, source_target_pairs={{1,2},{2,3},{3,4},{4,5},{5,6},{6,7},{9,10},{10,11},{11,12},{12,13}... | collective-permute-start | bytes 2261000 | tf_op jit(solution)/shard_map/ppermute | solution.py:99
  29.9 1.9 %collective-permute-start.3 = (bf16[64,5888]{1,0:T(8,128)(2,1)}, bf16[64,5888]{1,0:T(8,128)(2,1)}, u32[]{:S(2)}, u32[]{:S(2)}) collective-permute-start(bf16[64,5888]{1,0:T(8,128)(2,1)} %collective-permute-done.1), channel_id=1, source_target_pairs={{1,0},{2,1},{3,2},{4,3},{5,4},{6,5},{9,8},{10,9},{11,10},{12,11},{... | collective-permute-start | bytes 2261000 | tf_op jit(solution)/shard_map/ppermute | solution.py:100
  31.8 2.7 %fusion.31 = f32[22,64,128]{2,1,0:T(8,128)} fusion(f32[22,64,128]{2,1,0:T(8,128)} %copy-done.1, s32[]{:T(128)S(6)} %select_n.78, bf16[64,5888]{1,0:T(8,128)(2,1)} %collective-permute-done, bf16[1,8192,128]{2,1,0:T(8,128)(2,1)} %param.8), kind=kOutput, calls=%fused_computation.29 | convolution fusion | flops 96468992 | bytes 2293764 | tf_op jit(solution)/shard_map/dot_general | solution.py:34
  34.5 2.2 %fusion.37 = f32[22,64,128]{2,1,0:T(8,128)} fusion(f32[22,64,128]{2,1,0:T(8,128)} %fusion.31, s32[]{:T(128)S(6)} %select_n.79, bf16[64,5888]{1,0:T(8,128)(2,1)} %collective-permute-done.1, bf16[1,8192,128]{2,1,0:T(8,128)(2,1)S(1)} %copy-done.3), kind=kOutput, calls=%fused_computation.31 | convolution fusion | flops 96468992 | bytes 2293764 | tf_op jit(solution)/shard_map/dot_general | solution.py:34
  38.4 13.8 %collective-permute-start.4 = (f32[16,512]{1,0:T(8,128)S(1)}, f32[16,512]{1,0:T(8,128)S(1)}, u32[]{:S(2)}, u32[]{:S(2)}) collective-permute-start(f32[16,512]{1,0:T(8,128)S(1)} %dynamic-slice_bitcast_fusion), channel_id=1, source_target_pairs={{0,256},{256,0},{1,257},{257,1},{2,258},{258,2},{3,259},{259,3},{4... | collective-permute-start | bytes 98312 | tf_op jit(solution)/shard_map/ppermute | solution.py:122
  52.1 2.3 %collective-permute-start.7 = (bf16[64,5888]{1,0:T(8,128)(2,1)}, bf16[64,5888]{1,0:T(8,128)(2,1)S(1)}, u32[]{:S(2)}, u32[]{:S(2)}) collective-permute-start(bf16[64,5888]{1,0:T(8,128)(2,1)} %collective-permute-done.2), channel_id=1, source_target_pairs={{2,3},{3,4},{4,5},{5,6},{6,7},{10,11},{11,12},{12,13},{13,14},{14,... | collective-permute-start | bytes 2261000 | tf_op jit(solution)/shard_map/ppermute | solution.py:99
  54.5 2.7 %collective-permute-start.8 = (bf16[64,5888]{1,0:T(8,128)(2,1)}, bf16[64,5888]{1,0:T(8,128)(2,1)S(1)}, u32[]{:S(2)}, u32[]{:S(2)}) collective-permute-start(bf16[64,5888]{1,0:T(8,128)(2,1)} %collective-permute-done.3), channel_id=1, source_target_pairs={{1,0},{2,1},{3,2},{4,3},{5,4},{9,8},{10,9},{11,10},{12,11},{13,12}... | collective-permute-start | bytes 2261000 | tf_op jit(solution)/shard_map/ppermute | solution.py:100
  57.2 2.7 %fusion.43 = f32[22,64,128]{2,1,0:T(8,128)} fusion(f32[22,64,128]{2,1,0:T(8,128)} %fusion.37, s32[]{:T(128)S(6)} %select_n.80, bf16[64,5888]{1,0:T(8,128)(2,1)} %collective-permute-done.2, bf16[1,8192,128]{2,1,0:T(8,128)(2,1)} %param.8), kind=kOutput, calls=%fused_computation.33 | convolution fusion | flops 96468992 | bytes 2293764 | tf_op jit(solution)/shard_map/dot_general | solution.py:34
  59.8 2.2 %fusion.49 = f32[22,64,128]{2,1,0:T(8,128)} fusion(f32[22,64,128]{2,1,0:T(8,128)} %fusion.43, s32[]{:T(128)S(6)} %select_n.81, bf16[64,5888]{1,0:T(8,128)(2,1)} %collective-permute-done.3, bf16[1,8192,128]{2,1,0:T(8,128)(2,1)S(1)} %copy-done.4), kind=kOutput, calls=%fused_computation.35 | convolution fusion | flops 96468992 | bytes 2293764 | tf_op jit(solution)/shard_map/dot_general | solution.py:34
  62.1 1.3 collective-permute-start.9
  64.0 8.8 %collective-permute-start.10 = (bf16[16,512]{1,0:T(8,128)(2,1)S(1)}, bf16[16,512]{1,0:T(8,128)(2,1)S(1)}, u32[]{:S(2)}, u32[]{:S(2)}) collective-permute-start(bf16[16,512]{1,0:T(8,128)(2,1)S(1)} %get-tuple-element.70), channel_id=1, source_target_pairs={{0,256},{256,0},{1,257},{257,1},{2,258},{258,2},{3,259},{259,3},{4... | collective-permute-start | bytes 49160 | tf_op jit(solution)/shard_map/ppermute | solution.py:130
  72.8 3.9 %collective-permute-done.8 = bf16[64,5888]{1,0:T(8,128)(2,1)S(1)} collective-permute-done((bf16[64,5888]{1,0:T(8,128)(2,1)}, bf16[64,5888]{1,0:T(8,128)(2,1)S(1)}, u32[]{:S(2)}, u32[]{:S(2)}) %collective-permute-start.8) | collective-permute-done | bytes 753696 | tf_op jit(solution)/shard_map/ppermute | solution.py:100
  76.7 5.0 %collective-permute-start.11 = (bf16[64,5888]{1,0:T(8,128)(2,1)S(1)}, bf16[64,5888]{1,0:T(8,128)(2,1)S(1)}, u32[]{:S(2)}, u32[]{:S(2)}) collective-permute-start(bf16[64,5888]{1,0:T(8,128)(2,1)S(1)} %collective-permute-done.8), channel_id=1, source_target_pairs={{1,0},{2,1},{3,2},{4,3},{9,8},{10,9},{11,10},{12,11},{17,16},{18,1... | collective-permute-start | bytes 2261000 | tf_op jit(solution)/shard_map/ppermute | solution.py:100
  84.6 6.3 %collective-permute-start.13 = (bf16[192,2304]{1,0:T(8,128)(2,1)S(1)}, bf16[192,2304]{1,0:T(8,128)(2,1)S(1)}, u32[]{:S(2)}, u32[]{:S(2)}) collective-permute-start(bf16[192,2304]{1,0:T(8,128)(2,1)S(1)} %pad_maximum_fusion.1), channel_id=1, source_target_pairs={{2,3},{5,4},{10,11},{13,12},{18,19},{21,20},{26,27},{29,28},{34,35... | collective-permute-start | bytes 2654216 | tf_op jit(solution)/shard_map/ppermute | solution.py:108
  90.9 1.3 collective-permute-start.14
  92.2 4.8 %collective-permute-done.11 = bf16[64,5888]{1,0:T(8,128)(2,1)S(1)} collective-permute-done((bf16[64,5888]{1,0:T(8,128)(2,1)S(1)}, bf16[64,5888]{1,0:T(8,128)(2,1)S(1)}, u32[]{:S(2)}, u32[]{:S(2)}) %collective-permute-start.11) | collective-permute-done | bytes 753696 | tf_op jit(solution)/shard_map/ppermute | solution.py:100
  97.0 4.4 %collective-permute-start.15 = (bf16[64,5888]{1,0:T(8,128)(2,1)S(1)}, bf16[64,5888]{1,0:T(8,128)(2,1)}, u32[]{:S(2)}, u32[]{:S(2)}) collective-permute-start(bf16[64,5888]{1,0:T(8,128)(2,1)S(1)} %broadcast_select_fusion), channel_id=1, source_target_pairs={{4,5},{5,6},{6,7},{1,0},{2,1},{3,2},{12,13},{13,14},{14,15},{9,8},... | collective-permute-start | bytes 2261000 | tf_op jit(solution)/shard_map/ppermute | solution.py:105
  101.4 1.0 fusion.67
  102.5 1.7 %collective-permute-done.14 = bf16[2304,128]{1,0:T(8,128)(2,1)S(1)} collective-permute-done((bf16[2304,128]{1,0:T(8,128)(2,1)S(1)}, bf16[2304,128]{1,0:T(8,128)(2,1)S(1)}, u32[]{:S(2)}, u32[]{:S(2)}) %collective-permute-start.14) | collective-permute-done | bytes 589856 | tf_op jit(solution)/shard_map/ppermute | solution.py:108
  104.2 2.2 %collective-permute-done.13 = bf16[192,2304]{1,0:T(8,128)(2,1)S(1)} collective-permute-done((bf16[192,2304]{1,0:T(8,128)(2,1)S(1)}, bf16[192,2304]{1,0:T(8,128)(2,1)S(1)}, u32[]{:S(2)}, u32[]{:S(2)}) %collective-permute-start.13) | collective-permute-done | bytes 884768 | tf_op jit(solution)/shard_map/ppermute | solution.py:108
  107.2 1.1 pad_maximum_fusion
  108.3 6.8 %collective-permute-start.17 = (bf16[4608,128]{1,0:T(8,128)(2,1)}, bf16[4608,128]{1,0:T(8,128)(2,1)}, u32[]{:S(2)}, u32[]{:S(2)}) collective-permute-start(bf16[4608,128]{1,0:T(8,128)(2,1)} %pad_maximum_fusion), channel_id=1, source_target_pairs={{2,3},{5,4},{10,11},{13,12},{18,19},{21,20},{26,27},{29,28},{34,35... | collective-permute-start | bytes 3538952 | tf_op jit(solution)/shard_map/ppermute | solution.py:108
  115.7 5.3 %collective-permute-start.20 = (bf16[64,5888]{1,0:T(8,128)(2,1)}, bf16[64,5888]{1,0:T(8,128)(2,1)}, u32[]{:S(2)}, u32[]{:S(2)}) collective-permute-start(bf16[64,5888]{1,0:T(8,128)(2,1)} %collective-permute-done.15), channel_id=1, source_target_pairs={{5,6},{6,7},{1,0},{2,1},{13,14},{14,15},{9,8},{10,9},{21,22},{22,2... | collective-permute-start | bytes 2261000 | tf_op jit(solution)/shard_map/ppermute | solution.py:105
  121.0 1.3 collective-permute-start.16
  122.3 1.1 broadcast_in_dim.67
  123.4 4.7 %all-to-all-start.1 = ((bf16[32,2,16,512]{3,2,1,0:T(8,128)(2,1)}), bf16[32,2,16,512]{3,2,1,0:T(8,128)(2,1)}, u32[]{:S(2)}, u32[]{:S(2)}) async-start(bf16[32,2,16,512]{3,2,1,0:T(8,128)(2,1)} %broadcast_in_dim.67), calls=%async_computation.1 | async-start | bytes 2097152 | tf_op jit(solution)/shard_map/all_to_all | solution.py:152
  128.0 2.6 %fusion.73 = f32[22,64,128]{2,1,0:T(8,128)} fusion(f32[22,64,128]{2,1,0:T(8,128)} %fusion.67, s32[]{:T(128)S(6)} %select_n.93, bf16[64,5888]{1,0:T(8,128)(2,1)} %collective-permute-done.15, bf16[1,8192,128]{2,1,0:T(8,128)(2,1)} %param.8), kind=kOutput, calls=%fused_computation.43 | convolution fusion | flops 96468992 | bytes 2293764 | tf_op jit(solution)/shard_map/dot_general | solution.py:34
  130.7 4.1 %collective-permute-done.16 = bf16[2304,128]{1,0:T(8,128)(2,1)S(1)} collective-permute-done((bf16[2304,128]{1,0:T(8,128)(2,1)S(1)}, bf16[2304,128]{1,0:T(8,128)(2,1)S(1)}, u32[]{:S(2)}, u32[]{:S(2)}) %collective-permute-start.16) | collective-permute-done | bytes 589856 | tf_op jit(solution)/shard_map/ppermute | solution.py:108
  135.8 4.4 %collective-permute-start.19 = (bf16[2304,128]{1,0:T(8,128)(2,1)}, bf16[2304,128]{1,0:T(8,128)(2,1)S(1)}, u32[]{:S(2)}, u32[]{:S(2)}) collective-permute-start(bf16[2304,128]{1,0:T(8,128)(2,1)} %copy-done.9), channel_id=1, source_target_pairs={{2,3},{5,4},{10,11},{13,12},{18,19},{21,20},{26,27},{29,28},{34,35... | collective-permute-start | bytes 1769480 | tf_op jit(solution)/shard_map/ppermute | solution.py:108
  140.3 1.5 collective-permute-start.21
  141.8 3.5 %all-to-all-done.1 = bf16[32,2,16,512]{3,2,1,0:T(8,128)(2,1)} async-done(((bf16[32,2,16,512]{3,2,1,0:T(8,128)(2,1)}), bf16[32,2,16,512]{3,2,1,0:T(8,128)(2,1)}, u32[]{:S(2)}, u32[]{:S(2)}) %all-to-all-start.1) | async-done | bytes 1048608 | tf_op jit(solution)/shard_map/all_to_all | solution.py:152
  145.3 2.6 %collective-permute-done.19.w2 = bf16[2304,128]{1,0:T(8,128)(2,1)S(1)} collective-permute-done((bf16[2304,128]{1,0:T(8,128)(2,1)}, bf16[2304,128]{1,0:T(8,128)(2,1)S(1)}, u32[]{:S(2)}, u32[]{:S(2)}) %collective-permute-start.19) | collective-permute-done | bytes 589856 | tf_op jit(solution)/shard_map/ppermute | solution.py:108
  148.0 2.6 %fusion.79 = f32[22,64,128]{2,1,0:T(8,128)} fusion(f32[22,64,128]{2,1,0:T(8,128)} %fusion.73, s32[]{:T(128)S(6)} %select_n.95, bf16[64,5888]{1,0:T(8,128)(2,1)} %collective-permute-done.20, bf16[1,8192,128]{2,1,0:T(8,128)(2,1)} %param.8), kind=kOutput, calls=%fused_computation.45 | convolution fusion | flops 96468992 | bytes 2293764 | tf_op jit(solution)/shard_map/dot_general | solution.py:34
  150.6 2.6 %shard_map.93 = (f32[512,128]{1,0:T(8,128)S(1)}, bf16[512,128]{1,0:T(8,128)(2,1)S(1)}, bf16[512,128]{1,0:T(8,128)(2,1)S(1)}, bf16[512,128]{1,0:T(8,128)(2,1)S(1)}) custom-call(s32[1]{0:T(128)} %bitcast.22.low, bf16[256,2304]{1,0:T(8,128)(2,1)S(1)} %constant_dynamic-update-slice_fusion.near, bf16[256,2304]{1,0:T(8,128)(2,1)S(1)} %collective-permute-done.18.far, ...), custom_call_target="tpu_custom_call" | custom-call | tf_op jit(solution)/shard_map/pallas_call | solution.py:64
  154.8 1.3 collective-permute-start.24
  156.1 2.3 %copy.14 = bf16[32,2,16,512]{3,2,0,1:T(8,128)(2,1)} copy(bf16[32,2,16,512]{3,2,1,0:T(8,128)(2,1)} %all-to-all-done.1) | data formatting | bytes 2097152 | tf_op jit(solution)/shard_map/optimization_barrier | solution.py:155
  158.3 2.2 %fusion.85 = f32[22,64,128]{2,1,0:T(8,128)} fusion(f32[22,64,128]{2,1,0:T(8,128)} %fusion.79, s32[]{:T(128)S(6)} %select_n.97, bf16[64,5888]{1,0:T(8,128)(2,1)} %collective-permute-done.21, bf16[1,8192,128]{2,1,0:T(8,128)(2,1)S(1)} %copy-done.5), kind=kOutput, calls=%fused_computation.47 | convolution fusion | flops 96468992 | bytes 2293764 | tf_op jit(solution)/shard_map/dot_general | solution.py:34
  161.5 3.7 %collective-permute-done.24 = bf16[512,128]{1,0:T(8,128)(2,1)S(1)} collective-permute-done((bf16[512,128]{1,0:T(8,128)(2,1)S(1)}, bf16[512,128]{1,0:T(8,128)(2,1)S(1)}, u32[]{:S(2)}, u32[]{:S(2)}) %collective-permute-start.24) | collective-permute-done | bytes 131104 | tf_op jit(solution)/shard_map/ppermute | solution.py:161
  165.3 1.2 fusion.93
  (67 shorter events, 13.4 us)
Async XLA Ops:
  0.6 2.4 %copy-start = (bf16[64,8192]{1,0:T(8,128)(2,1)S(1)}, bf16[64,8192]{1,0:T(8,128)(2,1)}, u32[]{:S(2)}) copy-start(bf16[64,8192]{1,0:T(8,128)(2,1)} %param.6) | copy-start | bytes 3145732
  0.6 9.4 %copy-start.2 = (bf16[1,1,1024,512]{3,2,1,0:T(8,128)(2,1)S(1)}, bf16[1,1,1024,512]{3,2,1,0:T(8,128)(2,1)}, u32[]{:S(2)}) copy-start(bf16[1,1,1024,512]{3,2,1,0:T(8,128)(2,1)} %param.9) | copy-start | bytes 3145732
  4.2 20.8 %collective-permute-start = (bf16[64,5888]{1,0:T(8,128)(2,1)}, bf16[64,5888]{1,0:T(8,128)(2,1)}, u32[]{:S(2)}, u32[]{:S(2)}) collective-permute-start(bf16[64,5888]{1,0:T(8,128)(2,1)} %multiply_convert_fusion), channel_id=1, source_target_pairs={{0,1},{1,2},{2,3},{3,4},{4,5},{5,6},{6,7},{8,9},{9,10},{10,11},{11... | collective-permute-start | bytes 2261000 | tf_op jit(solution)/shard_map/ppermute | solution.py:99
  8.0 21.9 %collective-permute-start.1 = (bf16[64,5888]{1,0:T(8,128)(2,1)}, bf16[64,5888]{1,0:T(8,128)(2,1)}, u32[]{:S(2)}, u32[]{:S(2)}) collective-permute-start(bf16[64,5888]{1,0:T(8,128)(2,1)} %multiply_convert_fusion), channel_id=1, source_target_pairs={{1,0},{2,1},{3,2},{4,3},{5,4},{6,5},{7,6},{9,8},{10,9},{11,10},{12... | collective-permute-start | bytes 2261000 | tf_op jit(solution)/shard_map/ppermute | solution.py:100
  11.1 25.5 %all-to-all-start = ((bf16[32,2,16,512]{3,2,1,0:T(8,128)(2,1)}), bf16[32,2,16,512]{3,2,1,0:T(8,128)(2,1)S(1)}, u32[]{:S(2)}, u32[]{:S(2)}) async-start(bf16[32,2,16,512]{3,2,1,0:T(8,128)(2,1)} %copy.12), calls=%async_computation | async-start | bytes 2097152 | tf_op jit(solution)/shard_map/all_to_all | solution.py:80
  19.6 3.0 %copy-start.6 = (bf16[8192]{0:T(1024)(128)(2,1)S(1)}, bf16[8192]{0:T(1024)(128)(2,1)}, u32[]{:S(2)}) copy-start(bf16[8192]{0:T(1024)(128)(2,1)} %param.7) | copy-start | bytes 49156
  19.6 3.0 %slice-start = ((bf16[64,8192]{1,0:T(8,128)(2,1)}), bf16[64,2304]{1,0:T(8,128)(2,1)S(1)}, s32[]{:S(2)}) async-start(bf16[64,8192]{1,0:T(8,128)(2,1)} %param.6), calls=%async_computation.2 | async-start | bytes 589824 | tf_op jit(solution)/shard_map/slice | solution.py:112
  21.7 0.9 copy-start.1
  22.7 11.8 %copy-start.3 = (bf16[1,8192,128]{2,1,0:T(8,128)(2,1)S(1)}, bf16[1,8192,128]{2,1,0:T(8,128)(2,1)}, u32[]{:S(2)}) copy-start(bf16[1,8192,128]{2,1,0:T(8,128)(2,1)} %param.8) | copy-start | bytes 6291460
  25.0 27.2 %collective-permute-start.2 = (bf16[64,5888]{1,0:T(8,128)(2,1)}, bf16[64,5888]{1,0:T(8,128)(2,1)}, u32[]{:S(2)}, u32[]{:S(2)}) collective-permute-start(bf16[64,5888]{1,0:T(8,128)(2,1)} %collective-permute-done), channel_id=1, source_target_pairs={{1,2},{2,3},{3,4},{4,5},{5,6},{6,7},{9,10},{10,11},{11,12},{12,13}... | collective-permute-start | bytes 2261000 | tf_op jit(solution)/shard_map/ppermute | solution.py:99
  29.9 24.6 %collective-permute-start.3 = (bf16[64,5888]{1,0:T(8,128)(2,1)}, bf16[64,5888]{1,0:T(8,128)(2,1)}, u32[]{:S(2)}, u32[]{:S(2)}) collective-permute-start(bf16[64,5888]{1,0:T(8,128)(2,1)} %collective-permute-done.1), channel_id=1, source_target_pairs={{1,0},{2,1},{3,2},{4,3},{5,4},{6,5},{9,8},{10,9},{11,10},{12,11},{... | collective-permute-start | bytes 2261000 | tf_op jit(solution)/shard_map/ppermute | solution.py:100
  36.7 23.2 %copy-start.4 = (bf16[1,8192,128]{2,1,0:T(8,128)(2,1)S(1)}, bf16[1,8192,128]{2,1,0:T(8,128)(2,1)}, u32[]{:S(2)}) copy-start(bf16[1,8192,128]{2,1,0:T(8,128)(2,1)} %param.8) | copy-start | bytes 6291460
  36.7 25.4 %collective-permute-start.6 = (bf16[2304,128]{1,0:T(8,128)(2,1)S(1)}, bf16[2304,128]{1,0:T(8,128)(2,1)S(1)}, u32[]{:S(2)}, u32[]{:S(2)}) collective-permute-start(bf16[2304,128]{1,0:T(8,128)(2,1)S(1)} %slice_bitcast_fusion.w0), channel_id=1, source_target_pairs={{0,1},{7,6},{8,9},{15,14},{16,17},{23,22},{24,25},{31,30},{32,33},... | collective-permute-start | bytes 1769480 | tf_op jit(solution)/shard_map/ppermute | solution.py:108
  37.5 24.5 %collective-permute-start.5 = (bf16[64,2304]{1,0:T(8,128)(2,1)S(1)}, bf16[64,2304]{1,0:T(8,128)(2,1)S(1)}, u32[]{:S(2)}, u32[]{:S(2)}) collective-permute-start(bf16[64,2304]{1,0:T(8,128)(2,1)S(1)} %multiply_convert_fusion.1), channel_id=1, source_target_pairs={{0,1},{7,6},{8,9},{15,14},{16,17},{23,22},{24,25},{31,30},{32,33},... | collective-permute-start | bytes 884744 | tf_op jit(solution)/shard_map/ppermute | solution.py:108
  38.4 23.7 %collective-permute-start.4 = (f32[16,512]{1,0:T(8,128)S(1)}, f32[16,512]{1,0:T(8,128)S(1)}, u32[]{:S(2)}, u32[]{:S(2)}) collective-permute-start(f32[16,512]{1,0:T(8,128)S(1)} %dynamic-slice_bitcast_fusion), channel_id=1, source_target_pairs={{0,256},{256,0},{1,257},{257,1},{2,258},{258,2},{3,259},{259,3},{4... | collective-permute-start | bytes 98312 | tf_op jit(solution)/shard_map/ppermute | solution.py:122
  52.1 29.6 %collective-permute-start.7 = (bf16[64,5888]{1,0:T(8,128)(2,1)}, bf16[64,5888]{1,0:T(8,128)(2,1)S(1)}, u32[]{:S(2)}, u32[]{:S(2)}) collective-permute-start(bf16[64,5888]{1,0:T(8,128)(2,1)} %collective-permute-done.2), channel_id=1, source_target_pairs={{2,3},{3,4},{4,5},{5,6},{6,7},{10,11},{11,12},{12,13},{13,14},{14,... | collective-permute-start | bytes 2261000 | tf_op jit(solution)/shard_map/ppermute | solution.py:99
  54.5 22.2 %collective-permute-start.8 = (bf16[64,5888]{1,0:T(8,128)(2,1)}, bf16[64,5888]{1,0:T(8,128)(2,1)S(1)}, u32[]{:S(2)}, u32[]{:S(2)}) collective-permute-start(bf16[64,5888]{1,0:T(8,128)(2,1)} %collective-permute-done.3), channel_id=1, source_target_pairs={{1,0},{2,1},{3,2},{4,3},{5,4},{9,8},{10,9},{11,10},{12,11},{13,12}... | collective-permute-start | bytes 2261000 | tf_op jit(solution)/shard_map/ppermute | solution.py:100
  59.8 3.5 %copy-start.7 = (f32[1,16,512]{2,1,0:T(8,128)S(1)}, f32[1,16,512]{2,1,0:T(8,128)}, u32[]{:S(2)}) copy-start(f32[1,16,512]{2,1,0:T(8,128)} %param.11) | copy-start | bytes 98308
  59.8 3.5 %copy-start.8 = (f32[1,16,512]{2,1,0:T(8,128)S(1)}, f32[1,16,512]{2,1,0:T(8,128)}, u32[]{:S(2)}) copy-start(f32[1,16,512]{2,1,0:T(8,128)} %param.10) | copy-start | bytes 98308
  62.1 22.5 %collective-permute-start.9 = (bf16[128,2304]{1,0:T(8,128)(2,1)S(1)}, bf16[128,2304]{1,0:T(8,128)(2,1)S(1)}, u32[]{:S(2)}, u32[]{:S(2)}) collective-permute-start(bf16[128,2304]{1,0:T(8,128)(2,1)S(1)} %pad_maximum_fusion.2), channel_id=1, source_target_pairs={{1,2},{6,5},{9,10},{14,13},{17,18},{22,21},{25,26},{30,29},{33,34}... | collective-permute-start | bytes 1769480 | tf_op jit(solution)/shard_map/ppermute | solution.py:108
  64.0 20.5 %collective-permute-start.10 = (bf16[16,512]{1,0:T(8,128)(2,1)S(1)}, bf16[16,512]{1,0:T(8,128)(2,1)S(1)}, u32[]{:S(2)}, u32[]{:S(2)}) collective-permute-start(bf16[16,512]{1,0:T(8,128)(2,1)S(1)} %get-tuple-element.70), channel_id=1, source_target_pairs={{0,256},{256,0},{1,257},{257,1},{2,258},{258,2},{3,259},{259,3},{4... | collective-permute-start | bytes 49160 | tf_op jit(solution)/shard_map/ppermute | solution.py:130
  76.7 20.3 %collective-permute-start.11 = (bf16[64,5888]{1,0:T(8,128)(2,1)S(1)}, bf16[64,5888]{1,0:T(8,128)(2,1)S(1)}, u32[]{:S(2)}, u32[]{:S(2)}) collective-permute-start(bf16[64,5888]{1,0:T(8,128)(2,1)S(1)} %collective-permute-done.8), channel_id=1, source_target_pairs={{1,0},{2,1},{3,2},{4,3},{9,8},{10,9},{11,10},{12,11},{17,16},{18,1... | collective-permute-start | bytes 2261000 | tf_op jit(solution)/shard_map/ppermute | solution.py:100
  81.7 15.2 %collective-permute-start.12 = (bf16[64,5888]{1,0:T(8,128)(2,1)S(1)}, bf16[64,5888]{1,0:T(8,128)(2,1)S(1)}, u32[]{:S(2)}, u32[]{:S(2)}) collective-permute-start(bf16[64,5888]{1,0:T(8,128)(2,1)S(1)} %collective-permute-done.7), channel_id=1, source_target_pairs={{3,4},{4,5},{5,6},{6,7},{11,12},{12,13},{13,14},{14,15},{19,20},{2... | collective-permute-start | bytes 2261000 | tf_op jit(solution)/shard_map/ppermute | solution.py:99
  84.6 21.8 %collective-permute-start.13 = (bf16[192,2304]{1,0:T(8,128)(2,1)S(1)}, bf16[192,2304]{1,0:T(8,128)(2,1)S(1)}, u32[]{:S(2)}, u32[]{:S(2)}) collective-permute-start(bf16[192,2304]{1,0:T(8,128)(2,1)S(1)} %pad_maximum_fusion.1), channel_id=1, source_target_pairs={{2,3},{5,4},{10,11},{13,12},{18,19},{21,20},{26,27},{29,28},{34,35... | collective-permute-start | bytes 2654216 | tf_op jit(solution)/shard_map/ppermute | solution.py:108
  90.9 13.3 %collective-permute-start.14 = (bf16[2304,128]{1,0:T(8,128)(2,1)S(1)}, bf16[2304,128]{1,0:T(8,128)(2,1)S(1)}, u32[]{:S(2)}, u32[]{:S(2)}) collective-permute-start(bf16[2304,128]{1,0:T(8,128)(2,1)S(1)} %collective-permute-done.6), channel_id=1, source_target_pairs={{1,2},{6,5},{9,10},{14,13},{17,18},{22,21},{25,26},{30,29},{33,34}... | collective-permute-start | bytes 1769480 | tf_op jit(solution)/shard_map/ppermute | solution.py:108
  97.0 18.6 %collective-permute-start.15 = (bf16[64,5888]{1,0:T(8,128)(2,1)S(1)}, bf16[64,5888]{1,0:T(8,128)(2,1)}, u32[]{:S(2)}, u32[]{:S(2)}) collective-permute-start(bf16[64,5888]{1,0:T(8,128)(2,1)S(1)} %broadcast_select_fusion), channel_id=1, source_target_pairs={{4,5},{5,6},{6,7},{1,0},{2,1},{3,2},{12,13},{13,14},{14,15},{9,8},... | collective-permute-start | bytes 2261000 | tf_op jit(solution)/shard_map/ppermute | solution.py:105
  106.4 28.3 %collective-permute-start.18 = (bf16[256,2304]{1,0:T(8,128)(2,1)S(1)}, bf16[256,2304]{1,0:T(8,128)(2,1)S(1)}, u32[]{:S(2)}, u32[]{:S(2)}) collective-permute-start(bf16[256,2304]{1,0:T(8,128)(2,1)S(1)} %constant_dynamic-update-slice_fusion.near), channel_id=1, source_target_pairs={{3,4},{4,3},{11,12},{12,11},{19,20},{20,19},{27,28},{28,27},{35,36... | collective-permute-start | bytes 3538952 | tf_op jit(solution)/shard_map/ppermute | solution.py:144
  108.3 27.5 %collective-permute-start.17 = (bf16[4608,128]{1,0:T(8,128)(2,1)}, bf16[4608,128]{1,0:T(8,128)(2,1)}, u32[]{:S(2)}, u32[]{:S(2)}) collective-permute-start(bf16[4608,128]{1,0:T(8,128)(2,1)} %pad_maximum_fusion), channel_id=1, source_target_pairs={{2,3},{5,4},{10,11},{13,12},{18,19},{21,20},{26,27},{29,28},{34,35... | collective-permute-start | bytes 3538952 | tf_op jit(solution)/shard_map/ppermute | solution.py:108
  115.7 24.6 %collective-permute-start.20 = (bf16[64,5888]{1,0:T(8,128)(2,1)}, bf16[64,5888]{1,0:T(8,128)(2,1)}, u32[]{:S(2)}, u32[]{:S(2)}) collective-permute-start(bf16[64,5888]{1,0:T(8,128)(2,1)} %collective-permute-done.15), channel_id=1, source_target_pairs={{5,6},{6,7},{1,0},{2,1},{13,14},{14,15},{9,8},{10,9},{21,22},{22,2... | collective-permute-start | bytes 2261000 | tf_op jit(solution)/shard_map/ppermute | solution.py:105
  121.0 13.8 %collective-permute-start.16 = (bf16[2304,128]{1,0:T(8,128)(2,1)S(1)}, bf16[2304,128]{1,0:T(8,128)(2,1)S(1)}, u32[]{:S(2)}, u32[]{:S(2)}) collective-permute-start(bf16[2304,128]{1,0:T(8,128)(2,1)S(1)} %slice_bitcast_fusion.w0), channel_id=1, source_target_pairs={{1,2},{6,5},{9,10},{14,13},{17,18},{22,21},{25,26},{30,29},{33,34}... | collective-permute-start | bytes 1769480 | tf_op jit(solution)/shard_map/ppermute | solution.py:108
  123.4 22.0 %all-to-all-start.1 = ((bf16[32,2,16,512]{3,2,1,0:T(8,128)(2,1)}), bf16[32,2,16,512]{3,2,1,0:T(8,128)(2,1)}, u32[]{:S(2)}, u32[]{:S(2)}) async-start(bf16[32,2,16,512]{3,2,1,0:T(8,128)(2,1)} %broadcast_in_dim.67), calls=%async_computation.1 | async-start | bytes 2097152 | tf_op jit(solution)/shard_map/all_to_all | solution.py:152
  134.8 0.8 copy-start.9
  135.8 12.1 %collective-permute-start.19 = (bf16[2304,128]{1,0:T(8,128)(2,1)}, bf16[2304,128]{1,0:T(8,128)(2,1)S(1)}, u32[]{:S(2)}, u32[]{:S(2)}) collective-permute-start(bf16[2304,128]{1,0:T(8,128)(2,1)} %copy-done.9), channel_id=1, source_target_pairs={{2,3},{5,4},{10,11},{13,12},{18,19},{21,20},{26,27},{29,28},{34,35... | collective-permute-start | bytes 1769480 | tf_op jit(solution)/shard_map/ppermute | solution.py:108
  140.3 18.1 %collective-permute-start.21 = (bf16[64,5888]{1,0:T(8,128)(2,1)}, bf16[64,5888]{1,0:T(8,128)(2,1)}, u32[]{:S(2)}, u32[]{:S(2)}) collective-permute-start(bf16[64,5888]{1,0:T(8,128)(2,1)} %collective-permute-done.20), channel_id=1, source_target_pairs={{6,7},{1,0},{14,15},{9,8},{22,23},{17,16},{30,31},{25,24},{38,39},... | collective-permute-start | bytes 2261000 | tf_op jit(solution)/shard_map/ppermute | solution.py:105
  153.3 5.1 %copy-start.5 = (bf16[1,8192,128]{2,1,0:T(8,128)(2,1)S(1)}, bf16[1,8192,128]{2,1,0:T(8,128)(2,1)}, u32[]{:S(2)}) copy-start(bf16[1,8192,128]{2,1,0:T(8,128)(2,1)} %param.8) | copy-start | bytes 6291460
  153.3 8.2 %collective-permute-start.22 = (bf16[512,128]{1,0:T(8,128)(2,1)S(1)}, bf16[512,128]{1,0:T(8,128)(2,1)S(1)}, u32[]{:S(2)}, u32[]{:S(2)}) collective-permute-start(bf16[512,128]{1,0:T(8,128)(2,1)S(1)} %get-tuple-element.66), channel_id=1, source_target_pairs={{3,0},{4,7},{11,8},{12,15},{19,16},{20,23},{27,24},{28,31},{35,32}... | collective-permute-start | bytes 393224 | tf_op jit(solution)/shard_map/ppermute | solution.py:161
  154.1 7.4 %collective-permute-start.23 = (bf16[512,128]{1,0:T(8,128)(2,1)S(1)}, bf16[512,128]{1,0:T(8,128)(2,1)S(1)}, u32[]{:S(2)}, u32[]{:S(2)}) collective-permute-start(bf16[512,128]{1,0:T(8,128)(2,1)S(1)} %get-tuple-element.67), channel_id=1, source_target_pairs={{3,1},{4,6},{11,9},{12,14},{19,17},{20,22},{27,25},{28,30},{35,33}... | collective-permute-start | bytes 393224 | tf_op jit(solution)/shard_map/ppermute | solution.py:161
  154.8 10.4 %collective-permute-start.24 = (bf16[512,128]{1,0:T(8,128)(2,1)S(1)}, bf16[512,128]{1,0:T(8,128)(2,1)S(1)}, u32[]{:S(2)}, u32[]{:S(2)}) collective-permute-start(bf16[512,128]{1,0:T(8,128)(2,1)S(1)} %get-tuple-element.68), channel_id=1, source_target_pairs={{3,2},{4,5},{11,10},{12,13},{19,18},{20,21},{27,26},{28,29},{35,34... | collective-permute-start | bytes 393224 | tf_op jit(solution)/shard_map/ppermute | solution.py:161

commit v7 on v6

--- a/solution.py
+++ b/solution.py
@@ -27,7 +27,8 @@
     index = jnp.arange(half).astype(jnp.float32)
     inverse = jnp.exp(-(2.0 * index / HD) * math.log(ROPE_BASE))
     angles = jnp.arange(rows).astype(jnp.float32)[:, None] * inverse[None, :]
-    return jnp.cos(angles), jnp.sin(angles)
+    cosine, sine = jnp.cos(angles), jnp.sin(angles)
+    return jnp.concatenate([cosine, cosine], axis=1), jnp.concatenate([-sine, sine], axis=1)
 
 
 def dot(a, b):
@@ -42,6 +43,59 @@
 
 
 hold = lax.optimization_barrier
+
+
+VMEM = pl.BlockSpec(memory_space=pltpu.VMEM)
+SMEM = pl.BlockSpec(memory_space=pltpu.SMEM)
+LINE = pl.BlockSpec((K_LINE, HD), lambda i: (0, 0))
+FREE = dict(
+    grid=(1,),
+    cost_estimate=pl.CostEstimate(flops=0, bytes_accessed=0, transcendentals=0),
+    compiler_params=pltpu.CompilerParams(vmem_limit_bytes=24 << 20),
+)
+
+
+def products_kernel(weight, *refs):
+    n = len(refs) // 2
+    both = dot(jnp.concatenate([block[...] for block in refs[:n]]), weight[...])
+    for i, out in enumerate(refs[n:]):
+        out[...] = both[64 * i : 64 * i + 64]
+
+
+def products_cost(n):
+    return pl.CostEstimate(flops=n * 2_000_000_000, bytes_accessed=0, transcendentals=0)
+
+
+def products(weight, *blocks):
+    return pl.pallas_call(
+        products_kernel,
+        out_shape=[jax.ShapeDtypeStruct((64, HD), jnp.float32)] * len(blocks),
+        in_specs=[LINE] + [VMEM] * len(blocks),
+        out_specs=[VMEM] * len(blocks),
+        **dict(FREE, cost_estimate=products_cost(len(blocks))),
+    )(weight, *blocks)
+
+
+def last_kernel(at, weight, block, blocks, middle, back1, back2, back3, keep, turn, out, rows):
+    for i in range(blocks.shape[0]):
+        rows[pl.ds(pl.multiple_of(at[i] * 64, 64), 64)] = blocks[i]
+    last = pl.multiple_of(at[blocks.shape[0]] * 64, 64)
+    rows[pl.ds(last, 64)] = dot(block[...], weight[...])
+    keys = rows[7 * 64 : 15 * 64] + jnp.where(at[blocks.shape[0] + 1] == 1, middle[...], 0.0)
+    for back in (back1, back2, back3):
+        keys += back[...].astype(jnp.float32)
+    out[...] = (keys * keep[...] + pltpu.roll(keys, HD // 2, 1) * turn[...]).astype(out.dtype)
+
+
+def last_step(at, weight, block, blocks, *rest):
+    return pl.pallas_call(
+        last_kernel,
+        out_shape=jax.ShapeDtypeStruct((512, HD), jnp.bfloat16),
+        in_specs=[SMEM, LINE] + [VMEM] * (2 + len(rest)),
+        out_specs=VMEM,
+        scratch_shapes=[pltpu.VMEM((22 * 64, HD), jnp.float32)],
+        **FREE,
+    )(at, weight, block, blocks, *rest)
 
 
 def middle_kernel(low, near, far, w0, w13, w2, *outs):
@@ -64,10 +118,9 @@
     return pl.pallas_call(
         middle_kernel,
         out_shape=[jax.ShapeDtypeStruct((512, HD), t) for t in types],
-        in_specs=[pl.BlockSpec(memory_space=pltpu.SMEM)] + [pl.BlockSpec(memory_space=pltpu.VMEM)] * 5,
-        out_specs=[pl.BlockSpec(memory_space=pltpu.VMEM)] * 4,
-        cost_estimate=pl.CostEstimate(flops=0, bytes_accessed=0, transcendentals=0),
-        compiler_params=pltpu.CompilerParams(vmem_limit_bytes=24 << 20),
+        in_specs=[SMEM] + [VMEM] * 5,
+        out_specs=[VMEM] * 4,
+        **FREE,
     )(low.astype(jnp.int32).reshape(1), near, far, *weights)
 
 
@@ -87,13 +140,8 @@
         return (block.astype(jnp.float32) * scale * gain).astype(jnp.bfloat16)
 
     weight = key_weight[0]
-    w_line, w_rest = weight[:K_LINE], weight[K_LINE:]
+    w_rest = weight[K_LINE:]
     shard = normed(tokens[:, :K_LINE], gain[:K_LINE])
-
-    rows = jnp.zeros((22, 64, HD), jnp.float32)
-
-    def put(rows, block, at):
-        return lax.dynamic_update_slice(rows, dot(block, w_line)[None], (7 + at, 0, 0))
 
     def hop(a, b, s):
         a = lax.ppermute(a, "tensor", [(j, j + 1) for j in range(s, 7)])
@@ -108,67 +156,61 @@
         return lax.ppermute(x, "tensor", [(3 - d, 4 - d), (4 + d, 3 + d)])
 
     a, b = hop(shard, shard, 0)
-    rows = put(rows, shard, me)
-    rows, rest_in = hold((rows, tokens[:, K_LINE:]))
+    (y,) = products(weight, shard)
+    y, rest_in = hold((y, tokens[:, K_LINE:]))
     rest = normed(rest_in, gain[K_LINE:])
 
-    rows0 = put(put(rows, a, me - 1), b, me + 1)
+    y0 = products(weight, a, b)
     a, b = hop(a, b, 1)
-    rows, pieces, rest, w_rest = hold((rows0, pieces, rest, w_rest))
+    y0, pieces, rest, w_rest = hold((y0, pieces, rest, w_rest))
     t3, w3 = inward(rest, 3), inward(w_rest, 3)
     partial = jnp.sum(pieces.astype(jnp.float32), axis=0)
     other = lax.dynamic_index_in_dim(partial, 1 - zh, 0, keepdims=False)
     own = lax.dynamic_index_in_dim(partial, zh, 0, keepdims=False)
     came = lax.ppermute(other, "zh", [(0, 1), (1, 0)])
 
-    rows1 = put(put(rows, a, me - 2), b, me + 2)
+    y1 = products(weight, a, b)
     a, b = hop(a, b, 2)
-    rows, came, t3, w3 = hold((rows1, came, t3, w3))
+    y1, came, t3, w3 = hold((y1, came, t3, w3))
     t2 = inward(jnp.concatenate([t3, rest]), 2)
     outer_next, moment_next = nesterov(outer_params[0], outer_momentum[0], own + came, 64)
     mine = outer_next.astype(jnp.bfloat16)
     theirs = lax.ppermute(mine, "zh", [(0, 1), (1, 0)])
 
-    rows2 = put(put(rows, a, me - 3), b, me + 3)
+    y2 = products(weight, a, b)
     a, b = hop(a, b, 3)
-    rows, t2, w3, theirs = hold((rows2, t2, w3, theirs))
+    y2, t2, w3, theirs = hold((y2, t2, w3, theirs))
     t1 = inward(jnp.concatenate([t2, rest]), 1)
     w3 = inward(w3, 2)
     pair = jnp.where(zh == 0, jnp.stack([mine, theirs]), jnp.stack([theirs, mine]))
 
     x = jnp.where(low, b, a)
-    rows3 = put(rows, x, jnp.where(low, me + 4, me - 4))
+    (y3,) = products(weight, x)
     x = hop_out(x, 4)
-    rows, t1, w3, w1, w2, pair = hold((rows3, t1, w3, w_rest, w_rest, pair))
+    y3, t1, w3, w1, w2, pair = hold((y3, t1, w3, w_rest, w_rest, pair))
     near = jnp.concatenate([t1, rest])
     far = lax.ppermute(near, "tensor", [(3, 4), (4, 3)])
     w13 = inward(jnp.concatenate([w1, w3]), 1)
     w2 = inward(w2, 2)
 
-    rows4 = put(rows, x, jnp.where(low, me + 5, me - 5))
+    (y4,) = products(weight, x)
     x = hop_out(x, 5)
-    rows, w2, w13, far = hold((rows4, w2, w13, far))
+    y4, w2, w13, far = hold((y4, w2, w13, far))
     w2 = inward(w2, 1)
     synced = lax.all_to_all(jnp.broadcast_to(pair[None], (32, 2, 16, 512)), PLANE, 0, 0, tiled=True)
 
-    y = hop_out(x, 6)
-    rows, w2, synced = hold((rows, w2, synced))
-    rows5 = put(rows, x, jnp.where(low, me + 6, me - 6))
-    rows, w2 = hold((rows5, w2))
+    x5, synced = hold((x, synced))
+    (y5,) = products(weight, x5)
+    x = hop_out(x, 6)
     blocks = middle_products(low, near, far, w_rest, w13, w2)
-    middle = jnp.where((me == 3) | (me == 4), blocks[0], 0.0)
-    for d in (3, 2, 1):
-        back = lax.ppermute(blocks[d], "tensor", [(3, 3 - d), (4, 4 + d)])
-        middle += back.astype(jnp.float32)
-
-    rows = put(rows, y, jnp.where(low, me + 7, me - 7))
+    backs = [lax.ppermute(blocks[d], "tensor", [(3, 3 - d), (4, 4 + d)]) for d in (1, 2, 3)]
+
+    at = [me] + [me + d for d in (-1, 1, -2, 2, -3, 3)]
+    at += [jnp.where(low, me + d, me - d) for d in (4, 5, 6, 7)]
+    at = jnp.stack([7 + i for i in at] + [((me == 3) | (me == 4)).astype(jnp.int32)])
+    done = jnp.stack([y, *y0, *y1, *y2, y3, y4, y5])
     synced = synced.transpose(1, 0, 2, 3).reshape(1024, 512)
-    projected = rows[7:15].reshape(512, HD) + middle
-    cosine, sine = rotary_tables(512)
-    first, second = projected[:, : HD // 2], projected[:, HD // 2 :]
-    key_rows = jnp.concatenate(
-        [first * cosine - second * sine, second * cosine + first * sine], axis=-1
-    ).astype(jnp.bfloat16)
+    key_rows = last_step(at, weight, x, done, blocks[0], *backs, *rotary_tables(512))
     return (key_rows, outer_next[None], moment_next[None], synced[None])
 
 

time: 169 us -> 171 us (1.012)
  the two profiles are of different devices: /device:TPU:64 before, /device:TPU:6 now
where the time goes in v7:
time: 171 us; the launch traced here: 170 us
  waiting for transfers between devices  66.6 us (39%)
  starting transfers between devices  65.6 us (38%)
  local copies, waits for them, and re-layouts  14.3 us (8%)
  Pallas kernels  12.2 us (7%)
  other arithmetic  10.4 us (6%)
    ppermute x3, waiting for transfers between devices, hop_out(): return lax.ppermute(x, 'tensor', pairs)  18.1 us
    ppermute x4, waiting for transfers between devices, hop(): b = lax.ppermute(b, 'tensor', [(j + 1, j) for j in range(7 - s)])  16.2 us
    ppermute x3, waiting for transfers between devices, body(): lax.ppermute(blocks[d], 'tensor', [(3, 3 - d), (4, 4 + d)])  15.5 us
    ppermute x1, starting transfers between devices, body(): came = lax.ppermute(other, 'zh', [(0, 1), (1, 0)])  14 us
    all_to_all x1, starting transfers between devices, body(): pieces = lax.all_to_all(params, PLANE, 0, 0, tiled=True)  10.3 us
    ppermute x8, starting transfers between devices, inward(): return lax.ppermute(x, 'tensor', [(3 - d, 4 - d), (4 + d, 3 + d)])  8.63 us
    unnamed x50, local copies, waits for them, and re-layouts  8.46 us
    ppermute x1, waiting for transfers between devices, body(): came = lax.ppermute(other, 'zh', [(0, 1), (1, 0)])  8.19 us
  transfers between devices with their start and end apart: 27, of which 8 were waited for; matrix products, arithmetic and copies ran while one was open for 11% of the time, Pallas kernels for 6%

profile of v7, /device:TPU:6, one launch (start us, length us, event | category | flops | bytes accessed | tf_op | source)
XLA Modules:
  0.0 170.3 jit_solution(11589426308780355218)
XLA Ops:
  0.7 1.7 multiply_reduce_fusion
  2.3 0.7 slice.24
  3.3 1.3 collective-permute-start
  4.6 5.4 %collective-permute-start.4 = (bf16[64,5888]{1,0:T(8,128)(2,1)S(1)}, bf16[64,5888]{1,0:T(8,128)(2,1)}, u32[]{:S(2)}, u32[]{:S(2)}) collective-permute-start(bf16[64,5888]{1,0:T(8,128)(2,1)S(1)} %multiply_convert_fusion.refs_0_), channel_id=1, source_target_pairs={{0,1},{1,2},{2,3},{3,4},{4,5},{5,6},{6,7},{8,9},{9,10},{10,11},{11... | collective-permute-start | bytes 2261000 | tf_op jit(solution)/shard_map/ppermute | solution.py:147
  10.0 1.1 copy.10
  11.1 10.3 %all-to-all-start = ((bf16[32,2,16,512]{3,2,1,0:T(8,128)(2,1)}), bf16[32,2,16,512]{3,2,1,0:T(8,128)(2,1)}, u32[]{:S(2)}, u32[]{:S(2)}) async-start(bf16[32,2,16,512]{3,2,1,0:T(8,128)(2,1)} %copy.10), calls=%async_computation | async-start | bytes 2097152 | tf_op jit(solution)/shard_map/all_to_all | solution.py:133
  22.4 0.8 multiply_convert_fusion.1
  23.3 1.9 %fusion = (f32[512,64]{1,0:T(8,128)}, f32[512,64]{1,0:T(8,128)}, f32[512,64]{1,0:T(8,128)}) fusion(f32[64]{0:T(128)S(1)} %multiply_exponential_fusion, f32[512]{0:T(512)S(1)} %iota_convert_fusion), kind=kLoop, calls=%fused_computation.13 | loop fusion | flops 65536 | bytes 395520 | tf_op jit(solution)/shard_map/neg | solution.py:31
  25.2 1.3 collective-permute-start.1
  26.5 0.7 collective-permute-start.5
  27.9 1.9 %shard_map.94 = (f32[64,128]{1,0:T(8,128)S(1)}, f32[64,128]{1,0:T(8,128)S(1)}) custom-call(bf16[8192,128]{1,0:T(8,128)(2,1)S(1)} %bitcast.76, bf16[64,5888]{1,0:T(8,128)(2,1)} %collective-permute-done.4.refs_0_, bf16[64,5888]{1,0:T(8,128)(2,1)} %collective-permute-done.refs_1_), custom_call_target="tpu_custom_call" | custom-call | flops 4000000000 | tf_op jit(solution)/shard_map/pallas_call | solution.py:70
  29.8 6.3 %all-to-all-done = bf16[32,2,16,512]{3,2,1,0:T(8,128)(2,1)} async-done(((bf16[32,2,16,512]{3,2,1,0:T(8,128)(2,1)}), bf16[32,2,16,512]{3,2,1,0:T(8,128)(2,1)}, u32[]{:S(2)}, u32[]{:S(2)}) %all-to-all-start) | async-done | bytes 1048608 | tf_op jit(solution)/shard_map/all_to_all | solution.py:133
  36.2 1.3 collective-permute-start.13
  37.5 1.4 convert_reduce_fusion
  38.9 14.0 %collective-permute-start.11 = (f32[16,512]{1,0:T(8,128)S(1)}, f32[16,512]{1,0:T(8,128)S(1)}, u32[]{:S(2)}, u32[]{:S(2)}) collective-permute-start(f32[16,512]{1,0:T(8,128)S(1)} %dynamic-slice_bitcast_fusion), channel_id=1, source_target_pairs={{0,256},{256,0},{1,257},{257,1},{2,258},{258,2},{3,259},{259,3},{4... | collective-permute-start | bytes 98312 | tf_op jit(solution)/shard_map/ppermute | solution.py:170
  52.9 1.3 collective-permute-start.12
  54.3 1.3 collective-permute-start.2
  55.6 0.7 collective-permute-start.6
  56.3 1.7 shard_map.95
  58.0 8.2 %collective-permute-done.11 = f32[16,512]{1,0:T(8,128)S(1)} collective-permute-done((f32[16,512]{1,0:T(8,128)S(1)}, f32[16,512]{1,0:T(8,128)S(1)}, u32[]{:S(2)}, u32[]{:S(2)}) %collective-permute-start.11) | collective-permute-done | bytes 32800 | tf_op jit(solution)/shard_map/ppermute | solution.py:170
  66.2 0.7 collective-permute-start.14
  67.6 7.7 %collective-permute-start.15 = (bf16[16,512]{1,0:T(8,128)(2,1)S(1)}, bf16[16,512]{1,0:T(8,128)(2,1)S(1)}, u32[]{:S(2)}, u32[]{:S(2)}) collective-permute-start(bf16[16,512]{1,0:T(8,128)(2,1)S(1)} %get-tuple-element.82), channel_id=1, source_target_pairs={{0,256},{256,0},{1,257},{257,1},{2,258},{258,2},{3,259},{259,3},{4... | collective-permute-start | bytes 49160 | tf_op jit(solution)/shard_map/ppermute | solution.py:178
  75.3 1.8 %collective-permute-done.2.refs_1_ = bf16[64,5888]{1,0:T(8,128)(2,1)S(1)} collective-permute-done((bf16[64,5888]{1,0:T(8,128)(2,1)}, bf16[64,5888]{1,0:T(8,128)(2,1)S(1)}, u32[]{:S(2)}, u32[]{:S(2)}) %collective-permute-start.2) | collective-permute-done | bytes 753696 | tf_op jit(solution)/shard_map/ppermute | solution.py:148
  77.2 1.3 collective-permute-start.3
  78.5 0.7 collective-permute-start.7
  79.8 2.3 %collective-permute-done.15 = bf16[16,512]{1,0:T(8,128)(2,1)S(1)} collective-permute-done((bf16[16,512]{1,0:T(8,128)(2,1)S(1)}, bf16[16,512]{1,0:T(8,128)(2,1)S(1)}, u32[]{:S(2)}, u32[]{:S(2)}) %collective-permute-start.15) | collective-permute-done | bytes 16416 | tf_op jit(solution)/shard_map/ppermute | solution.py:178
  82.1 0.7 collective-permute-start.16
  83.6 14.4 %collective-permute-done.3 = bf16[64,5888]{1,0:T(8,128)(2,1)S(1)} collective-permute-done((bf16[64,5888]{1,0:T(8,128)(2,1)S(1)}, bf16[64,5888]{1,0:T(8,128)(2,1)S(1)}, u32[]{:S(2)}, u32[]{:S(2)}) %collective-permute-start.3) | collective-permute-done | bytes 753696 | tf_op jit(solution)/shard_map/ppermute | solution.py:148
  98.0 1.3 collective-permute-start.8
  100.4 0.9 collective-permute-start.20
  101.3 1.1 pad_maximum_fusion
  102.4 1.7 %collective-permute-start.19 = (bf16[4608,128]{1,0:T(8,128)(2,1)}, bf16[4608,128]{1,0:T(8,128)(2,1)}, u32[]{:S(2)}, u32[]{:S(2)}) collective-permute-start(bf16[4608,128]{1,0:T(8,128)(2,1)} %pad_maximum_fusion), channel_id=1, source_target_pairs={{2,3},{5,4},{10,11},{13,12},{18,19},{21,20},{26,27},{29,28},{34,35... | collective-permute-start | bytes 3538952 | tf_op jit(solution)/shard_map/ppermute | solution.py:156
  104.9 13.1 %collective-permute-done.8.refs_0_ = bf16[64,5888]{1,0:T(8,128)(2,1)} collective-permute-done((bf16[64,5888]{1,0:T(8,128)(2,1)S(1)}, bf16[64,5888]{1,0:T(8,128)(2,1)}, u32[]{:S(2)}, u32[]{:S(2)}) %collective-permute-start.8) | collective-permute-done | bytes 753696 | tf_op jit(solution)/shard_map/ppermute | solution.py:153
  118.1 1.3 collective-permute-start.9
  120.0 1.5 collective-permute-start.18
  122.7 1.1 broadcast_in_dim.6
  123.8 4.7 %all-to-all-start.1 = ((bf16[32,2,16,512]{3,2,1,0:T(8,128)(2,1)}), bf16[32,2,16,512]{3,2,1,0:T(8,128)(2,1)}, u32[]{:S(2)}, u32[]{:S(2)}) async-start(bf16[32,2,16,512]{3,2,1,0:T(8,128)(2,1)} %broadcast_in_dim.6), calls=%async_computation.1 | async-start | bytes 2097152 | tf_op jit(solution)/shard_map/all_to_all | solution.py:200
  128.5 1.6 copy-done.1
  130.1 1.5 shard_map.98
  132.4 5.0 %collective-permute-done.9 = bf16[64,5888]{1,0:T(8,128)(2,1)} collective-permute-done((bf16[64,5888]{1,0:T(8,128)(2,1)}, bf16[64,5888]{1,0:T(8,128)(2,1)}, u32[]{:S(2)}, u32[]{:S(2)}) %collective-permute-start.9) | collective-permute-done | bytes 753696 | tf_op jit(solution)/shard_map/ppermute | solution.py:153
  137.4 1.3 collective-permute-start.10
  140.5 3.4 %shard_map.99 = (f32[512,128]{1,0:T(8,128)S(1)}, bf16[512,128]{1,0:T(8,128)(2,1)}, bf16[512,128]{1,0:T(8,128)(2,1)}, bf16[512,128]{1,0:T(8,128)(2,1)}) custom-call(s32[1]{0:T(128)} %bitcast.32.low, bf16[256,2304]{1,0:T(8,128)(2,1)S(1)} %constant_dynamic-update-slice_fusion.near, bf16[256,2304]{1,0:T(8,128)(2,1)S(1)} %collective-permute-done.20.far, ...), custom_call_target="tpu_custom_call" | custom-call | tf_op jit(solution)/shard_map/pallas_call | solution.py:118
  144.6 0.8 collective-permute-start.22
  146.0 1.3 collective-permute-start.24
  148.0 2.3 %copy.11 = bf16[32,2,16,512]{3,2,0,1:T(8,128)(2,1)} copy(bf16[32,2,16,512]{3,2,1,0:T(8,128)(2,1)} %all-to-all-done.1) | data formatting | bytes 2097152 | tf_op jit(solution)/shard_map/optimization_barrier | solution.py:202
  150.2 2.2 %shard_map.101.blocks = f32[10,64,128]{2,1,0:T(8,128)} fusion(f32[10,64,128]{2,1,0:T(8,128)} %bitcast_dynamic-update-slice_fusion.1, bf16[8192,128]{1,0:T(8,128)(2,1)S(1)} %bitcast.81, bf16[64,5888]{1,0:T(8,128)(2,1)} %collective-permute-done.9), kind=kCustom, calls=%fused_computation.15 | custom fusion | flops 2000000000 | bytes 2883584 | tf_op jit(solution)/shard_map/pallas_call | solution.py:70
  152.4 15.5 %collective-permute-done.24.back3 = bf16[512,128]{1,0:T(8,128)(2,1)S(1)} collective-permute-done((bf16[512,128]{1,0:T(8,128)(2,1)}, bf16[512,128]{1,0:T(8,128)(2,1)S(1)}, u32[]{:S(2)}, u32[]{:S(2)}) %collective-permute-start.24) | collective-permute-done | bytes 131104 | tf_op jit(solution)/shard_map/ppermute | solution.py:206
  167.9 2.4 %shard_map.100 = bf16[512,128]{1,0:T(8,128)(2,1)} custom-call(s32[12]{0:T(128)S(1)} %stack.102.at, bf16[8192,128]{1,0:T(8,128)(2,1)S(1)} %bitcast.82, bf16[64,5888]{1,0:T(8,128)(2,1)} %collective-permute-done.10.block, f32[10,64,128]{2,1,0:T(8,128)} %shard_map.101.blocks, f32[512,128]{1,0:T(8,128)S(1)} %copy-done.4, ...), custom_call_target="tpu_custom_call" | custom-call | tf_op jit(solution)/shard_map/pallas_call | solution.py:91
  (91 shorter events, 12.3 us)
Async XLA Ops:
  0.6 2.4 %copy-start.12 = (bf16[64,8192]{1,0:T(8,128)(2,1)S(1)}, bf16[64,8192]{1,0:T(8,128)(2,1)}, u32[]{:S(2)}) copy-start(bf16[64,8192]{1,0:T(8,128)(2,1)} %param.6) | copy-start | bytes 3145732
  0.6 9.4 %copy-start.13 = (bf16[1,1,1024,512]{3,2,1,0:T(8,128)(2,1)S(1)}, bf16[1,1,1024,512]{3,2,1,0:T(8,128)(2,1)}, u32[]{:S(2)}) copy-start(bf16[1,1,1024,512]{3,2,1,0:T(8,128)(2,1)} %param.9) | copy-start | bytes 3145732
  3.3 21.9 %collective-permute-start = (bf16[64,5888]{1,0:T(8,128)(2,1)S(1)}, bf16[64,5888]{1,0:T(8,128)(2,1)}, u32[]{:S(2)}, u32[]{:S(2)}) collective-permute-start(bf16[64,5888]{1,0:T(8,128)(2,1)S(1)} %multiply_convert_fusion.refs_0_), channel_id=1, source_target_pairs={{1,0},{2,1},{3,2},{4,3},{5,4},{6,5},{7,6},{9,8},{10,9},{11,10},{12... | collective-permute-start | bytes 2261000 | tf_op jit(solution)/shard_map/ppermute | solution.py:148
  4.6 21.9 %collective-permute-start.4 = (bf16[64,5888]{1,0:T(8,128)(2,1)S(1)}, bf16[64,5888]{1,0:T(8,128)(2,1)}, u32[]{:S(2)}, u32[]{:S(2)}) collective-permute-start(bf16[64,5888]{1,0:T(8,128)(2,1)S(1)} %multiply_convert_fusion.refs_0_), channel_id=1, source_target_pairs={{0,1},{1,2},{2,3},{3,4},{4,5},{5,6},{6,7},{8,9},{9,10},{10,11},{11... | collective-permute-start | bytes 2261000 | tf_op jit(solution)/shard_map/ppermute | solution.py:147
  11.1 10.3 %copy-start.17 = (bf16[8192]{0:T(1024)(128)(2,1)S(1)}, bf16[8192]{0:T(1024)(128)(2,1)}, u32[]{:S(2)}) copy-start(bf16[8192]{0:T(1024)(128)(2,1)} %param.7) | copy-start | bytes 49156
  11.1 10.3 %copy-start = (bf16[1,8192,128]{2,1,0:T(8,128)(2,1)S(1)}, bf16[1,8192,128]{2,1,0:T(8,128)(2,1)}, u32[]{:S(2)}) copy-start(bf16[1,8192,128]{2,1,0:T(8,128)(2,1)} %param.8) | copy-start | bytes 6291460
  11.1 25.0 %all-to-all-start = ((bf16[32,2,16,512]{3,2,1,0:T(8,128)(2,1)}), bf16[32,2,16,512]{3,2,1,0:T(8,128)(2,1)}, u32[]{:S(2)}, u32[]{:S(2)}) async-start(bf16[32,2,16,512]{3,2,1,0:T(8,128)(2,1)} %copy.10), calls=%async_computation | async-start | bytes 2097152 | tf_op jit(solution)/shard_map/all_to_all | solution.py:133
  21.5 1.0 slice-start
  25.2 29.0 %collective-permute-start.1 = (bf16[64,5888]{1,0:T(8,128)(2,1)}, bf16[64,5888]{1,0:T(8,128)(2,1)}, u32[]{:S(2)}, u32[]{:S(2)}) collective-permute-start(bf16[64,5888]{1,0:T(8,128)(2,1)} %collective-permute-done.refs_1_), channel_id=1, source_target_pairs={{1,0},{2,1},{3,2},{4,3},{5,4},{6,5},{9,8},{10,9},{11,10},{12,11},{... | collective-permute-start | bytes 2261000 | tf_op jit(solution)/shard_map/ppermute | solution.py:148
  26.5 29.1 %collective-permute-start.5 = (bf16[64,5888]{1,0:T(8,128)(2,1)}, bf16[64,5888]{1,0:T(8,128)(2,1)S(1)}, u32[]{:S(2)}, u32[]{:S(2)}) collective-permute-start(bf16[64,5888]{1,0:T(8,128)(2,1)} %collective-permute-done.4.refs_0_), channel_id=1, source_target_pairs={{1,2},{2,3},{3,4},{4,5},{5,6},{6,7},{9,10},{10,11},{11,12},{12,13}... | collective-permute-start | bytes 2261000 | tf_op jit(solution)/shard_map/ppermute | solution.py:147
  36.2 30.0 %collective-permute-start.13 = (bf16[2304,128]{1,0:T(8,128)(2,1)S(1)}, bf16[2304,128]{1,0:T(8,128)(2,1)S(1)}, u32[]{:S(2)}, u32[]{:S(2)}) collective-permute-start(bf16[2304,128]{1,0:T(8,128)(2,1)S(1)} %slice_bitcast_fusion.w0), channel_id=1, source_target_pairs={{0,1},{7,6},{8,9},{15,14},{16,17},{23,22},{24,25},{31,30},{32,33},... | collective-permute-start | bytes 1769480 | tf_op jit(solution)/shard_map/ppermute | solution.py:156
  38.9 27.3 %copy-start.11 = (bf16[64,2304]{1,0:T(8,128)(2,1)S(1)}, bf16[64,2304]{1,0:T(8,128)(2,1)}, u32[]{:S(2)}) copy-start(bf16[64,2304]{1,0:T(8,128)(2,1)} %multiply_convert_fusion.1) | copy-start | bytes 884740
  38.9 28.0 %copy-start.18 = (f32[1,16,512]{2,1,0:T(8,128)S(1)}, f32[1,16,512]{2,1,0:T(8,128)}, u32[]{:S(2)}) copy-start(f32[1,16,512]{2,1,0:T(8,128)} %param.11) | copy-start | bytes 98308
  38.9 28.0 %copy-start.19 = (f32[1,16,512]{2,1,0:T(8,128)S(1)}, f32[1,16,512]{2,1,0:T(8,128)}, u32[]{:S(2)}) copy-start(f32[1,16,512]{2,1,0:T(8,128)} %param.10) | copy-start | bytes 98308
  38.9 27.2 %collective-permute-start.11 = (f32[16,512]{1,0:T(8,128)S(1)}, f32[16,512]{1,0:T(8,128)S(1)}, u32[]{:S(2)}, u32[]{:S(2)}) collective-permute-start(f32[16,512]{1,0:T(8,128)S(1)} %dynamic-slice_bitcast_fusion), channel_id=1, source_target_pairs={{0,256},{256,0},{1,257},{257,1},{2,258},{258,2},{3,259},{259,3},{4... | collective-permute-start | bytes 98312 | tf_op jit(solution)/shard_map/ppermute | solution.py:170
  52.9 13.2 %collective-permute-start.12 = (bf16[64,2304]{1,0:T(8,128)(2,1)}, bf16[64,2304]{1,0:T(8,128)(2,1)S(1)}, u32[]{:S(2)}, u32[]{:S(2)}) collective-permute-start(bf16[64,2304]{1,0:T(8,128)(2,1)} %multiply_convert_fusion.1), channel_id=1, source_target_pairs={{0,1},{7,6},{8,9},{15,14},{16,17},{23,22},{24,25},{31,30},{32,33},... | collective-permute-start | bytes 884744 | tf_op jit(solution)/shard_map/ppermute | solution.py:156
  54.3 22.9 %collective-permute-start.2 = (bf16[64,5888]{1,0:T(8,128)(2,1)}, bf16[64,5888]{1,0:T(8,128)(2,1)S(1)}, u32[]{:S(2)}, u32[]{:S(2)}) collective-permute-start(bf16[64,5888]{1,0:T(8,128)(2,1)} %collective-permute-done.1.refs_1_), channel_id=1, source_target_pairs={{1,0},{2,1},{3,2},{4,3},{5,4},{9,8},{10,9},{11,10},{12,11},{13,12}... | collective-permute-start | bytes 2261000 | tf_op jit(solution)/shard_map/ppermute | solution.py:148
  55.6 22.9 %collective-permute-start.6 = (bf16[64,5888]{1,0:T(8,128)(2,1)S(1)}, bf16[64,5888]{1,0:T(8,128)(2,1)S(1)}, u32[]{:S(2)}, u32[]{:S(2)}) collective-permute-start(bf16[64,5888]{1,0:T(8,128)(2,1)S(1)} %collective-permute-done.5.refs_0_), channel_id=1, source_target_pairs={{2,3},{3,4},{4,5},{5,6},{6,7},{10,11},{11,12},{12,13},{13,14},{14,... | collective-permute-start | bytes 2261000 | tf_op jit(solution)/shard_map/ppermute | solution.py:147
  66.2 15.8 %collective-permute-start.14 = (bf16[128,2304]{1,0:T(8,128)(2,1)S(1)}, bf16[128,2304]{1,0:T(8,128)(2,1)S(1)}, u32[]{:S(2)}, u32[]{:S(2)}) collective-permute-start(bf16[128,2304]{1,0:T(8,128)(2,1)S(1)} %pad_maximum_fusion.2), channel_id=1, source_target_pairs={{1,2},{6,5},{9,10},{14,13},{17,18},{22,21},{25,26},{30,29},{33,34}... | collective-permute-start | bytes 1769480 | tf_op jit(solution)/shard_map/ppermute | solution.py:156
  67.6 14.4 %collective-permute-start.15 = (bf16[16,512]{1,0:T(8,128)(2,1)S(1)}, bf16[16,512]{1,0:T(8,128)(2,1)S(1)}, u32[]{:S(2)}, u32[]{:S(2)}) collective-permute-start(bf16[16,512]{1,0:T(8,128)(2,1)S(1)} %get-tuple-element.82), channel_id=1, source_target_pairs={{0,256},{256,0},{1,257},{257,1},{2,258},{258,2},{3,259},{259,3},{4... | collective-permute-start | bytes 49160 | tf_op jit(solution)/shard_map/ppermute | solution.py:178
  77.2 20.8 %collective-permute-start.3 = (bf16[64,5888]{1,0:T(8,128)(2,1)S(1)}, bf16[64,5888]{1,0:T(8,128)(2,1)S(1)}, u32[]{:S(2)}, u32[]{:S(2)}) collective-permute-start(bf16[64,5888]{1,0:T(8,128)(2,1)S(1)} %collective-permute-done.2.refs_1_), channel_id=1, source_target_pairs={{1,0},{2,1},{3,2},{4,3},{9,8},{10,9},{11,10},{12,11},{17,16},{18,1... | collective-permute-start | bytes 2261000 | tf_op jit(solution)/shard_map/ppermute | solution.py:148
  78.5 19.5 %collective-permute-start.7 = (bf16[64,5888]{1,0:T(8,128)(2,1)S(1)}, bf16[64,5888]{1,0:T(8,128)(2,1)S(1)}, u32[]{:S(2)}, u32[]{:S(2)}) collective-permute-start(bf16[64,5888]{1,0:T(8,128)(2,1)S(1)} %collective-permute-done.6.refs_0_), channel_id=1, source_target_pairs={{3,4},{4,5},{5,6},{6,7},{11,12},{12,13},{13,14},{14,15},{19,20},{2... | collective-permute-start | bytes 2261000 | tf_op jit(solution)/shard_map/ppermute | solution.py:147
  79.7 18.2 %copy-start.5 = (f32[64,128]{1,0:T(8,128)}, f32[64,128]{1,0:T(8,128)S(1)}, u32[]{:S(2)}) copy-start(f32[64,128]{1,0:T(8,128)S(1)} %get-tuple-element.62) | copy-start | bytes 98308
  79.8 18.2 %copy-start.7 = (f32[64,128]{1,0:T(8,128)}, f32[64,128]{1,0:T(8,128)S(1)}, u32[]{:S(2)}) copy-start(f32[64,128]{1,0:T(8,128)S(1)} %get-tuple-element.61) | copy-start | bytes 98308
  82.1 17.7 %collective-permute-start.16 = (bf16[192,2304]{1,0:T(8,128)(2,1)S(1)}, bf16[192,2304]{1,0:T(8,128)(2,1)S(1)}, u32[]{:S(2)}, u32[]{:S(2)}) collective-permute-start(bf16[192,2304]{1,0:T(8,128)(2,1)S(1)} %pad_maximum_fusion.1), channel_id=1, source_target_pairs={{2,3},{5,4},{10,11},{13,12},{18,19},{21,20},{26,27},{29,28},{34,35... | collective-permute-start | bytes 2654216 | tf_op jit(solution)/shard_map/ppermute | solution.py:156
  82.8 16.9 %collective-permute-start.17 = (bf16[2304,128]{1,0:T(8,128)(2,1)S(1)}, bf16[2304,128]{1,0:T(8,128)(2,1)S(1)}, u32[]{:S(2)}, u32[]{:S(2)}) collective-permute-start(bf16[2304,128]{1,0:T(8,128)(2,1)S(1)} %collective-permute-done.13), channel_id=1, source_target_pairs={{1,2},{6,5},{9,10},{14,13},{17,18},{22,21},{25,26},{30,29},{33,34}... | collective-permute-start | bytes 1769480 | tf_op jit(solution)/shard_map/ppermute | solution.py:156
  98.0 20.0 %collective-permute-start.8 = (bf16[64,5888]{1,0:T(8,128)(2,1)S(1)}, bf16[64,5888]{1,0:T(8,128)(2,1)}, u32[]{:S(2)}, u32[]{:S(2)}) collective-permute-start(bf16[64,5888]{1,0:T(8,128)(2,1)S(1)} %broadcast_select_fusion.refs_0_), channel_id=1, source_target_pairs={{4,5},{5,6},{6,7},{1,0},{2,1},{3,2},{12,13},{13,14},{14,15},{9,8},... | collective-permute-start | bytes 2261000 | tf_op jit(solution)/shard_map/ppermute | solution.py:153
  99.7 0.6 copy-start.9
  100.4 3.7 %copy-start.14 = (f32[512,64]{1,0:T(8,128)S(1)}, f32[512,64]{1,0:T(8,128)}, u32[]{:S(2)}) copy-start(f32[512,64]{1,0:T(8,128)} %get-tuple-element.85) | copy-start | bytes 393220
  100.4 3.7 %copy-start.15 = (f32[512,64]{1,0:T(8,128)S(1)}, f32[512,64]{1,0:T(8,128)}, u32[]{:S(2)}) copy-start(f32[512,64]{1,0:T(8,128)} %get-tuple-element.86) | copy-start | bytes 393220
  100.4 3.7 %copy-start.16 = (f32[512,64]{1,0:T(8,128)S(1)}, f32[512,64]{1,0:T(8,128)}, u32[]{:S(2)}) copy-start(f32[512,64]{1,0:T(8,128)} %get-tuple-element.87) | copy-start | bytes 393220
  100.4 31.3 %collective-permute-start.20 = (bf16[256,2304]{1,0:T(8,128)(2,1)S(1)}, bf16[256,2304]{1,0:T(8,128)(2,1)S(1)}, u32[]{:S(2)}, u32[]{:S(2)}) collective-permute-start(bf16[256,2304]{1,0:T(8,128)(2,1)S(1)} %constant_dynamic-update-slice_fusion.near), channel_id=1, source_target_pairs={{3,4},{4,3},{11,12},{12,11},{19,20},{20,19},{27,28},{28,27},{35,36... | collective-permute-start | bytes 3538952 | tf_op jit(solution)/shard_map/ppermute | solution.py:192
  102.4 29.3 %collective-permute-start.19 = (bf16[4608,128]{1,0:T(8,128)(2,1)}, bf16[4608,128]{1,0:T(8,128)(2,1)}, u32[]{:S(2)}, u32[]{:S(2)}) collective-permute-start(bf16[4608,128]{1,0:T(8,128)(2,1)} %pad_maximum_fusion), channel_id=1, source_target_pairs={{2,3},{5,4},{10,11},{13,12},{18,19},{21,20},{26,27},{29,28},{34,35... | collective-permute-start | bytes 3538952 | tf_op jit(solution)/shard_map/ppermute | solution.py:156
  118.1 19.3 %collective-permute-start.9 = (bf16[64,5888]{1,0:T(8,128)(2,1)}, bf16[64,5888]{1,0:T(8,128)(2,1)}, u32[]{:S(2)}, u32[]{:S(2)}) collective-permute-start(bf16[64,5888]{1,0:T(8,128)(2,1)} %collective-permute-done.8.refs_0_), channel_id=1, source_target_pairs={{5,6},{6,7},{1,0},{2,1},{13,14},{14,15},{9,8},{10,9},{21,22},{22,2... | collective-permute-start | bytes 2261000 | tf_op jit(solution)/shard_map/ppermute | solution.py:153
  120.0 11.7 %collective-permute-start.18 = (bf16[2304,128]{1,0:T(8,128)(2,1)S(1)}, bf16[2304,128]{1,0:T(8,128)(2,1)}, u32[]{:S(2)}, u32[]{:S(2)}) collective-permute-start(bf16[2304,128]{1,0:T(8,128)(2,1)S(1)} %slice_bitcast_fusion.w0), channel_id=1, source_target_pairs={{1,2},{6,5},{9,10},{14,13},{17,18},{22,21},{25,26},{30,29},{33,34}... | collective-permute-start | bytes 1769480 | tf_op jit(solution)/shard_map/ppermute | solution.py:156
  123.8 24.2 %all-to-all-start.1 = ((bf16[32,2,16,512]{3,2,1,0:T(8,128)(2,1)}), bf16[32,2,16,512]{3,2,1,0:T(8,128)(2,1)}, u32[]{:S(2)}, u32[]{:S(2)}) async-start(bf16[32,2,16,512]{3,2,1,0:T(8,128)(2,1)} %broadcast_in_dim.6), calls=%async_computation.1 | async-start | bytes 2097152 | tf_op jit(solution)/shard_map/all_to_all | solution.py:200
  128.5 1.6 copy-start.1
  130.1 8.6 %copy-start.8 = (f32[64,128]{1,0:T(8,128)S(1)}, f32[64,128]{1,0:T(8,128)}, u32[]{:S(2)}) copy-start(f32[64,128]{1,0:T(8,128)} %copy-done.7) | copy-start | bytes 98308
  130.1 9.2 %copy-start.6 = (f32[64,128]{1,0:T(8,128)S(1)}, f32[64,128]{1,0:T(8,128)}, u32[]{:S(2)}) copy-start(f32[64,128]{1,0:T(8,128)} %copy-done.5) | copy-start | bytes 98308
  130.1 9.8 %copy-start.10 = (f32[64,128]{1,0:T(8,128)S(1)}, f32[64,128]{1,0:T(8,128)}, u32[]{:S(2)}) copy-start(f32[64,128]{1,0:T(8,128)} %copy-done.9) | copy-start | bytes 98308
  131.7 8.8 %collective-permute-start.21 = (bf16[2304,128]{1,0:T(8,128)(2,1)}, bf16[2304,128]{1,0:T(8,128)(2,1)S(1)}, u32[]{:S(2)}, u32[]{:S(2)}) collective-permute-start(bf16[2304,128]{1,0:T(8,128)(2,1)} %collective-permute-done.18), channel_id=1, source_target_pairs={{2,3},{5,4},{10,11},{13,12},{18,19},{21,20},{26,27},{29,28},{34,35... | collective-permute-start | bytes 1769480 | tf_op jit(solution)/shard_map/ppermute | solution.py:156
  137.4 30.5 %collective-permute-start.10 = (bf16[64,5888]{1,0:T(8,128)(2,1)}, bf16[64,5888]{1,0:T(8,128)(2,1)}, u32[]{:S(2)}, u32[]{:S(2)}) collective-permute-start(bf16[64,5888]{1,0:T(8,128)(2,1)} %collective-permute-done.9), channel_id=1, source_target_pairs={{6,7},{1,0},{14,15},{9,8},{22,23},{17,16},{30,31},{25,24},{38,39},... | collective-permute-start | bytes 2261000 | tf_op jit(solution)/shard_map/ppermute | solution.py:153
  143.9 0.7 copy-start.3
  144.6 5.7 %copy-start.2 = (bf16[1,8192,128]{2,1,0:T(8,128)(2,1)S(1)}, bf16[1,8192,128]{2,1,0:T(8,128)(2,1)}, u32[]{:S(2)}) copy-start(bf16[1,8192,128]{2,1,0:T(8,128)(2,1)} %param.8) | copy-start | bytes 6291460
  144.6 7.8 %collective-permute-start.22 = (bf16[512,128]{1,0:T(8,128)(2,1)}, bf16[512,128]{1,0:T(8,128)(2,1)S(1)}, u32[]{:S(2)}, u32[]{:S(2)}) collective-permute-start(bf16[512,128]{1,0:T(8,128)(2,1)} %get-tuple-element.78), channel_id=1, source_target_pairs={{3,2},{4,5},{11,10},{12,13},{19,18},{20,21},{27,26},{28,29},{35,34... | collective-permute-start | bytes 393224 | tf_op jit(solution)/shard_map/ppermute | solution.py:206
  145.4 7.0 %collective-permute-start.23 = (bf16[512,128]{1,0:T(8,128)(2,1)}, bf16[512,128]{1,0:T(8,128)(2,1)S(1)}, u32[]{:S(2)}, u32[]{:S(2)}) collective-permute-start(bf16[512,128]{1,0:T(8,128)(2,1)} %get-tuple-element.79), channel_id=1, source_target_pairs={{3,1},{4,6},{11,9},{12,14},{19,17},{20,22},{27,25},{28,30},{35,33}... | collective-permute-start | bytes 393224 | tf_op jit(solution)/shard_map/ppermute | solution.py:206
  146.0 21.8 %collective-permute-start.24 = (bf16[512,128]{1,0:T(8,128)(2,1)}, bf16[512,128]{1,0:T(8,128)(2,1)S(1)}, u32[]{:S(2)}, u32[]{:S(2)}) collective-permute-start(bf16[512,128]{1,0:T(8,128)(2,1)} %get-tuple-element.80), channel_id=1, source_target_pairs={{3,0},{4,7},{11,8},{12,15},{19,16},{20,23},{27,24},{28,31},{35,32}... | collective-permute-start | bytes 393224 | tf_op jit(solution)/shard_map/ppermute | solution.py:206
  150.2 17.6 %copy-start.4 = (f32[512,128]{1,0:T(8,128)S(1)}, f32[512,128]{1,0:T(8,128)}, u32[]{:S(2)}) copy-start(f32[512,128]{1,0:T(8,128)} %copy-done.3) | copy-start | bytes 786436

commit v8 on v7

--- a/solution.py
+++ b/solution.py
@@ -76,26 +76,64 @@
     )(weight, *blocks)
 
 
-def last_kernel(at, weight, block, blocks, middle, back1, back2, back3, keep, turn, out, rows):
-    for i in range(blocks.shape[0]):
-        rows[pl.ds(pl.multiple_of(at[i] * 64, 64), 64)] = blocks[i]
-    last = pl.multiple_of(at[blocks.shape[0]] * 64, 64)
-    rows[pl.ds(last, 64)] = dot(block[...], weight[...])
-    keys = rows[7 * 64 : 15 * 64] + jnp.where(at[blocks.shape[0] + 1] == 1, middle[...], 0.0)
+def last_kernel(at, weight, block, *refs):
+    n = len(refs) - 8
+    blocks, (middle, back1, back2, back3, keep, turn, out, rows) = refs[:n], refs[n:]
+    for i, ref in enumerate(blocks):
+        rows[pl.ds(pl.multiple_of(at[i] * 64, 64), 64)] = ref[...]
+    rows[pl.ds(pl.multiple_of(at[n] * 64, 64), 64)] = dot(block[...], weight[...])
+    keys = rows[7 * 64 : 15 * 64] + jnp.where(at[n + 1] == 1, middle[...], 0.0)
     for back in (back1, back2, back3):
         keys += back[...].astype(jnp.float32)
     out[...] = (keys * keep[...] + pltpu.roll(keys, HD // 2, 1) * turn[...]).astype(out.dtype)
 
 
-def last_step(at, weight, block, blocks, *rest):
+def last_step(at, weight, block, *rest):
     return pl.pallas_call(
         last_kernel,
         out_shape=jax.ShapeDtypeStruct((512, HD), jnp.bfloat16),
-        in_specs=[SMEM, LINE] + [VMEM] * (2 + len(rest)),
+        in_specs=[SMEM, LINE] + [VMEM] * (1 + len(rest)),
         out_specs=VMEM,
         scratch_shapes=[pltpu.VMEM((22 * 64, HD), jnp.float32)],
         **FREE,
-    )(at, weight, block, blocks, *rest)
+    )(at, weight, block, *rest)
+
+
+def sum_kernel(zh, pieces, other, own):
+    for out, half in ((other, 1 - zh[0]), (own, zh[0])):
+        total = pieces[0, half].astype(jnp.float32)
+        for i in range(1, pieces.shape[0]):
+            total += pieces[i, half].astype(jnp.float32)
+        out[...] = total
+
+
+def sum_pieces(zh, pieces):
+    return pl.pallas_call(
+        sum_kernel,
+        out_shape=[jax.ShapeDtypeStruct((16, 512), jnp.float32)] * 2,
+        in_specs=[SMEM, VMEM],
+        out_specs=[VMEM] * 2,
+        **dict(FREE, cost_estimate=products_cost(2)),
+    )(zh.reshape(1), pieces)
+
+
+def update_kernel(outer, moment, own, came, outer_next, moment_next, rounded):
+    summed = own[...] + came[...]
+    new_outer, new_moment = nesterov(outer[0], moment[0], summed, 64)
+    outer_next[0] = new_outer
+    moment_next[0] = new_moment
+    rounded[...] = new_outer.astype(rounded.dtype)
+
+
+def update(outer, moment, own, came):
+    shape = jax.ShapeDtypeStruct((1, 16, 512), jnp.float32)
+    return pl.pallas_call(
+        update_kernel,
+        out_shape=[shape, shape, jax.ShapeDtypeStruct((16, 512), jnp.bfloat16)],
+        in_specs=[VMEM] * 4,
+        out_specs=[VMEM] * 3,
+        **dict(FREE, cost_estimate=products_cost(2)),
+    )(outer, moment, own, came)
 
 
 def middle_kernel(low, near, far, w0, w13, w2, *outs):
@@ -162,39 +200,38 @@
 
     y0 = products(weight, a, b)
     a, b = hop(a, b, 1)
-    y0, pieces, rest, w_rest = hold((y0, pieces, rest, w_rest))
+    y0, rest, w_rest = hold((y0, rest, w_rest))
     t3, w3 = inward(rest, 3), inward(w_rest, 3)
-    partial = jnp.sum(pieces.astype(jnp.float32), axis=0)
-    other = lax.dynamic_index_in_dim(partial, 1 - zh, 0, keepdims=False)
-    own = lax.dynamic_index_in_dim(partial, zh, 0, keepdims=False)
-    came = lax.ppermute(other, "zh", [(0, 1), (1, 0)])
 
     y1 = products(weight, a, b)
     a, b = hop(a, b, 2)
-    y1, came, t3, w3 = hold((y1, came, t3, w3))
+    y1, t3, w3 = hold((y1, t3, w3))
     t2 = inward(jnp.concatenate([t3, rest]), 2)
-    outer_next, moment_next = nesterov(outer_params[0], outer_momentum[0], own + came, 64)
-    mine = outer_next.astype(jnp.bfloat16)
-    theirs = lax.ppermute(mine, "zh", [(0, 1), (1, 0)])
 
     y2 = products(weight, a, b)
     a, b = hop(a, b, 3)
-    y2, t2, w3, theirs = hold((y2, t2, w3, theirs))
+    y2, t2, w3, pieces = hold((y2, t2, w3, pieces))
     t1 = inward(jnp.concatenate([t2, rest]), 1)
     w3 = inward(w3, 2)
-    pair = jnp.where(zh == 0, jnp.stack([mine, theirs]), jnp.stack([theirs, mine]))
+    other, own = sum_pieces(zh, pieces)
+    came = lax.ppermute(other, "zh", [(0, 1), (1, 0)])
 
     x = jnp.where(low, b, a)
     (y3,) = products(weight, x)
     x = hop_out(x, 4)
-    y3, t1, w3, w1, w2, pair = hold((y3, t1, w3, w_rest, w_rest, pair))
+    y3, t1, w3, w1, w2, came = hold((y3, t1, w3, w_rest, w_rest, came))
+    w13, t1 = hold((jnp.concatenate([w1, w3]), t1))
+    w13 = inward(w13, 1)
     near = jnp.concatenate([t1, rest])
     far = lax.ppermute(near, "tensor", [(3, 4), (4, 3)])
-    w13 = inward(jnp.concatenate([w1, w3]), 1)
     w2 = inward(w2, 2)
-
-    (y4,) = products(weight, x)
+    outer_next, moment_next, mine = update(outer_params, outer_momentum, own, came)
+    theirs = lax.ppermute(mine, "zh", [(0, 1), (1, 0)])
+
+    x4, theirs = hold((x, theirs))
+    (y4,) = products(weight, x4)
     x = hop_out(x, 5)
+    pair = jnp.where(zh == 0, jnp.stack([mine, theirs]), jnp.stack([theirs, mine]))
     y4, w2, w13, far = hold((y4, w2, w13, far))
     w2 = inward(w2, 1)
     synced = lax.all_to_all(jnp.broadcast_to(pair[None], (32, 2, 16, 512)), PLANE, 0, 0, tiled=True)
@@ -208,10 +245,11 @@
     at = [me] + [me + d for d in (-1, 1, -2, 2, -3, 3)]
     at += [jnp.where(low, me + d, me - d) for d in (4, 5, 6, 7)]
     at = jnp.stack([7 + i for i in at] + [((me == 3) | (me == 4)).astype(jnp.int32)])
-    done = jnp.stack([y, *y0, *y1, *y2, y3, y4, y5])
     synced = synced.transpose(1, 0, 2, 3).reshape(1024, 512)
-    key_rows = last_step(at, weight, x, done, blocks[0], *backs, *rotary_tables(512))
-    return (key_rows, outer_next[None], moment_next[None], synced[None])
+    key_rows = last_step(
+        at, weight, x, y, *y0, *y1, *y2, y3, y4, y5, blocks[0], *backs, *rotary_tables(512)
+    )
+    return (key_rows, outer_next, moment_next, synced[None])
 
 
 def solution(mesh):

time: 171 us -> 199 us (1.16); the launches traced: 170 us -> 196 us
  waiting for transfers between devices: 66.6 us -> 87.9 us
  starting transfers between devices: 65.6 us -> 72.3 us
  local copies, waits for them, and re-layouts: 14.3 us -> 8.56 us
  Pallas kernels: 12.2 us -> 16.6 us
    ppermute x1, waiting for transfers between devices: 2.28 us -> 11.9 us  [body(): theirs = lax.ppermute(mine, 'zh', [(0, 1), (1, 0)])]
    ppermute x8, starting transfers between devices: 8.63 us -> 17.5 us  [inward(): return lax.ppermute(x, 'tensor', [(3 - d, 4 - d), (4 + d, 3 + d)])]
    ppermute x4, waiting for transfers between devices: 16.2 us -> 24.7 us  [hop(): b = lax.ppermute(b, 'tensor', [(j + 1, j) for j in range(7 - s)])]
    ppermute x1, waiting for transfers between devices: 8.19 us -> 0.01 us  [body(): came = lax.ppermute(other, 'zh', [(0, 1), (1, 0)])]
    all_to_all x1, waiting for transfers between devices: 0.01 us -> 7.4 us  [body(): lax.all_to_all(jnp.broadcast_to(pair[None], (32, 2, 16, 512)), PLANE, 0,...]
    all_to_all x1, waiting for transfers between devices: 6.31 us -> 0.01 us  [body(): pieces = lax.all_to_all(params, PLANE, 0, 0, tiled=True)]
    unnamed x50 -> x47, local copies, waits for them, and re-layouts: 8.46 us -> 3.24 us
    ppermute x1, starting transfers between devices: 7.74 us -> 2.54 us  [body(): theirs = lax.ppermute(mine, 'zh', [(0, 1), (1, 0)])]
  transfers between devices with their start and end apart: 27 -> 27, of which waited for: 8 -> 7; matrix products, arithmetic and copies ran while one was open for 11% -> 6% of each run, Pallas kernels for 6% -> 7%
where the time goes in v8:
time: 199 us; the launch traced here: 196 us
  waiting for transfers between devices  87.9 us (44%)
  starting transfers between devices  72.3 us (36%)
  Pallas kernels  16.6 us (8%)
  other arithmetic  9.44 us (5%)
  local copies, waits for them, and re-layouts  8.56 us (4%)
    ppermute x4, waiting for transfers between devices, hop(): b = lax.ppermute(b, 'tensor', [(j + 1, j) for j in range(7 - s)])  24.7 us
    ppermute x3, waiting for transfers between devices, hop_out(): return lax.ppermute(x, 'tensor', pairs)  22.2 us
    ppermute x3, waiting for transfers between devices, body(): lax.ppermute(blocks[d], 'tensor', [(3, 3 - d), (4, 4 + d)])  19.8 us
    ppermute x8, starting transfers between devices, inward(): return lax.ppermute(x, 'tensor', [(3 - d, 4 - d), (4 + d, 3 + d)])  17.5 us
    ppermute x1, starting transfers between devices, body(): came = lax.ppermute(other, 'zh', [(0, 1), (1, 0)])  14.6 us
    ppermute x1, waiting for transfers between devices, body(): theirs = lax.ppermute(mine, 'zh', [(0, 1), (1, 0)])  11.9 us
    ppermute x4, starting transfers between devices, hop(): a = lax.ppermute(a, 'tensor', [(j, j + 1) for j in range(s, 7)])  10.1 us
    pallas_call x7, Pallas kernels, products(): pl.pallas_call(products_kernel, out_shape=[jax.ShapeDtypeStruct((64, HD),...  9.32 us
  transfers between devices with their start and end apart: 27, of which 7 were waited for; matrix products, arithmetic and copies ran while one was open for 6% of the time, Pallas kernels for 7%

profile of v8, /device:TPU:6, one launch (start us, length us, event | category | flops | bytes accessed | tf_op | source)
XLA Modules:
  0.0 196.2 jit_solution(4927141884948096472)
XLA Ops:
  0.6 1.7 multiply_reduce_fusion
  3.1 1.4 multiply_convert_fusion.refs_0_
  4.4 1.3 collective-permute-start
  5.7 5.4 %collective-permute-start.4 = (bf16[64,5888]{1,0:T(8,128)(2,1)S(1)}, bf16[64,5888]{1,0:T(8,128)(2,1)}, u32[]{:S(2)}, u32[]{:S(2)}) collective-permute-start(bf16[64,5888]{1,0:T(8,128)(2,1)S(1)} %multiply_convert_fusion.refs_0_), channel_id=1, source_target_pairs={{0,1},{1,2},{2,3},{3,4},{4,5},{5,6},{6,7},{8,9},{9,10},{10,11},{11... | collective-permute-start | bytes 2261000 | tf_op jit(solution)/shard_map/ppermute | solution.py:185
  11.9 13.3 %collective-permute-done.refs_1_ = bf16[64,5888]{1,0:T(8,128)(2,1)} collective-permute-done((bf16[64,5888]{1,0:T(8,128)(2,1)S(1)}, bf16[64,5888]{1,0:T(8,128)(2,1)}, u32[]{:S(2)}, u32[]{:S(2)}) %collective-permute-start) | collective-permute-done | bytes 753696 | tf_op jit(solution)/shard_map/ppermute | solution.py:186
  25.2 1.3 collective-permute-start.1
  26.5 1.6 collective-permute-start.5
  28.9 2.0 %shard_map.94 = (f32[64,128]{1,0:T(8,128)S(1)}, f32[64,128]{1,0:T(8,128)S(1)}) custom-call(bf16[8192,128]{1,0:T(8,128)(2,1)S(1)} %bitcast.27, bf16[64,5888]{1,0:T(8,128)(2,1)} %collective-permute-done.4.refs_0_, bf16[64,5888]{1,0:T(8,128)(2,1)} %collective-permute-done.refs_1_), custom_call_target="tpu_custom_call" | custom-call | flops 4000000000 | tf_op jit(solution)/shard_map/pallas_call | solution.py:70
  30.9 8.6 %collective-permute-start.12 = (bf16[2304,128]{1,0:T(8,128)(2,1)S(1)}, bf16[2304,128]{1,0:T(8,128)(2,1)}, u32[]{:S(2)}, u32[]{:S(2)}) collective-permute-start(bf16[2304,128]{1,0:T(8,128)(2,1)S(1)} %slice_bitcast_fusion.w0), channel_id=1, source_target_pairs={{0,1},{7,6},{8,9},{15,14},{16,17},{23,22},{24,25},{31,30},{32,33},... | collective-permute-start | bytes 1769480 | tf_op jit(solution)/shard_map/ppermute | solution.py:194
  39.5 1.1 copy.15
  40.5 7.6 %all-to-all-start = ((bf16[32,2,16,512]{3,2,1,0:T(8,128)(2,1)}), bf16[32,2,16,512]{3,2,1,0:T(8,128)(2,1)}, u32[]{:S(2)}, u32[]{:S(2)}) async-start(bf16[32,2,16,512]{3,2,1,0:T(8,128)(2,1)} %bitcast.35), calls=%async_computation | async-start | bytes 2097152 | tf_op jit(solution)/shard_map/all_to_all | solution.py:171
  48.2 1.4 collective-permute-start.11
  49.6 1.3 collective-permute-start.2
  51.0 1.6 collective-permute-start.6
  52.5 1.7 shard_map.95
  54.8 2.0 %collective-permute-done.11 = bf16[64,2304]{1,0:T(8,128)(2,1)S(1)} collective-permute-done((bf16[64,2304]{1,0:T(8,128)(2,1)}, bf16[64,2304]{1,0:T(8,128)(2,1)S(1)}, u32[]{:S(2)}, u32[]{:S(2)}) %collective-permute-start.11) | collective-permute-done | bytes 294944 | tf_op jit(solution)/shard_map/ppermute | solution.py:194
  56.8 0.9 pad_maximum_fusion.2
  57.7 1.5 collective-permute-start.13
  59.1 11.4 %collective-permute-done.2.refs_1_ = bf16[64,5888]{1,0:T(8,128)(2,1)} collective-permute-done((bf16[64,5888]{1,0:T(8,128)(2,1)S(1)}, bf16[64,5888]{1,0:T(8,128)(2,1)}, u32[]{:S(2)}, u32[]{:S(2)}) %collective-permute-start.2) | collective-permute-done | bytes 753696 | tf_op jit(solution)/shard_map/ppermute | solution.py:186
  70.5 1.4 collective-permute-start.3
  72.0 1.6 collective-permute-start.7
  73.5 1.9 shard_map.96
  76.1 1.1 pad_maximum_fusion.1
  78.6 1.4 shard_map.98
  80.0 14.6 %collective-permute-start.16 = (f32[16,512]{1,0:T(8,128)S(1)}, f32[16,512]{1,0:T(8,128)S(1)}, u32[]{:S(2)}, u32[]{:S(2)}) collective-permute-start(f32[16,512]{1,0:T(8,128)S(1)} %get-tuple-element.71), channel_id=1, source_target_pairs={{0,256},{256,0},{1,257},{257,1},{2,258},{258,2},{3,259},{259,3},{4... | collective-permute-start | bytes 98312 | tf_op jit(solution)/shard_map/ppermute | solution.py:217
  94.7 1.2 broadcast_select_fusion.refs_0_
  96.3 1.3 collective-permute-start.8
  97.6 1.1 pad_maximum_fusion
  99.6 1.7 collective-permute-start.19
  101.3 1.5 collective-permute-start.18
  102.8 22.2 %collective-permute-done.8.refs_0_ = bf16[64,5888]{1,0:T(8,128)(2,1)} collective-permute-done((bf16[64,5888]{1,0:T(8,128)(2,1)S(1)}, bf16[64,5888]{1,0:T(8,128)(2,1)}, u32[]{:S(2)}, u32[]{:S(2)}) %collective-permute-start.8) | collective-permute-done | bytes 753696 | tf_op jit(solution)/shard_map/ppermute | solution.py:191
  124.9 1.3 collective-permute-start.9
  126.9 2.5 %collective-permute-start.17 = (bf16[16,512]{1,0:T(8,128)(2,1)S(1)}, bf16[16,512]{1,0:T(8,128)(2,1)S(1)}, u32[]{:S(2)}, u32[]{:S(2)}) collective-permute-start(bf16[16,512]{1,0:T(8,128)(2,1)S(1)} %get-tuple-element.75), channel_id=1, source_target_pairs={{0,256},{256,0},{1,257},{257,1},{2,258},{258,2},{3,259},{259,3},{4... | collective-permute-start | bytes 49160 | tf_op jit(solution)/shard_map/ppermute | solution.py:229
  129.4 11.9 %collective-permute-done.17 = bf16[16,512]{1,0:T(8,128)(2,1)S(1)} collective-permute-done((bf16[16,512]{1,0:T(8,128)(2,1)S(1)}, bf16[16,512]{1,0:T(8,128)(2,1)S(1)}, u32[]{:S(2)}, u32[]{:S(2)}) %collective-permute-start.17) | collective-permute-done | bytes 16416 | tf_op jit(solution)/shard_map/ppermute | solution.py:229
  141.3 1.1 broadcast_in_dim.2
  142.4 7.2 %all-to-all-start.1 = ((bf16[32,2,16,512]{3,2,1,0:T(8,128)(2,1)}), bf16[32,2,16,512]{3,2,1,0:T(8,128)(2,1)}, u32[]{:S(2)}, u32[]{:S(2)}) async-start(bf16[32,2,16,512]{3,2,1,0:T(8,128)(2,1)} %broadcast_in_dim.2), calls=%async_computation.1 | async-start | bytes 2097152 | tf_op jit(solution)/shard_map/all_to_all | solution.py:237
  149.8 1.6 copy-done.1
  151.4 1.5 shard_map.100.refs_8_
  152.9 1.5 collective-permute-start.21
  154.4 1.3 collective-permute-start.10
  155.8 1.0 fusion
  157.0 7.4 %all-to-all-done.1 = bf16[32,2,16,512]{3,2,1,0:T(8,128)(2,1)} async-done(((bf16[32,2,16,512]{3,2,1,0:T(8,128)(2,1)}), bf16[32,2,16,512]{3,2,1,0:T(8,128)(2,1)}, u32[]{:S(2)}, u32[]{:S(2)}) %all-to-all-start.1) | async-done | bytes 1048608 | tf_op jit(solution)/shard_map/all_to_all | solution.py:237
  164.4 2.3 %copy.13 = bf16[32,2,16,512]{3,2,0,1:T(8,128)(2,1)} copy(bf16[32,2,16,512]{3,2,1,0:T(8,128)(2,1)} %all-to-all-done.1) | data formatting | bytes 2097152 | tf_op jit(solution)/shard_map/optimization_barrier | solution.py:239
  166.7 2.9 %shard_map.102 = (f32[512,128]{1,0:T(8,128)S(1)}, bf16[512,128]{1,0:T(8,128)(2,1)S(1)}, bf16[512,128]{1,0:T(8,128)(2,1)S(1)}, bf16[512,128]{1,0:T(8,128)(2,1)S(1)}) custom-call(s32[1]{0:T(128)} %bitcast.19.low, bf16[256,2304]{1,0:T(8,128)(2,1)S(1)} %constant_dynamic-update-slice_fusion.near, bf16[256,2304]{1,0:T(8,128)(2,1)S(1)} %collective-permute-done.20.far, ...), custom_call_target="tpu_custom_call" | custom-call | tf_op jit(solution)/shard_map/pallas_call | solution.py:156
  171.0 1.4 collective-permute-start.24
  172.5 1.5 shard_map.101.refs_9_
  174.0 19.8 %collective-permute-done.24.refs_13_ = bf16[512,128]{1,0:T(8,128)(2,1)S(1)} collective-permute-done((bf16[512,128]{1,0:T(8,128)(2,1)S(1)}, bf16[512,128]{1,0:T(8,128)(2,1)S(1)}, u32[]{:S(2)}, u32[]{:S(2)}) %collective-permute-start.24) | collective-permute-done | bytes 131104 | tf_op jit(solution)/shard_map/ppermute | solution.py:243
  193.8 2.3 %shard_map.103 = bf16[512,128]{1,0:T(8,128)(2,1)} custom-call(s32[12]{0:T(128)S(1)} %stack.69.at, bf16[8192,128]{1,0:T(8,128)(2,1)S(1)} %bitcast.33, bf16[64,5888]{1,0:T(8,128)(2,1)} %collective-permute-done.10.block, f32[64,128]{1,0:T(8,128)S(1)} %shard_map.93.refs_0_, f32[64,128]{1,0:T(8,128)S(1)} %get-tuple-element.54.refs_1_, f32[64,128]{1,0:T(8,128)S(1)} %copy-done.4, ...), custom_call_target="tpu_custom_call" | custom-call | tf_op jit(solution)/shard_map/pallas_call | solution.py:92
  (87 shorter events, 8.6 us)
Async XLA Ops:
  0.6 10.5 %copy-start = (bf16[1,8192,128]{2,1,0:T(8,128)(2,1)S(1)}, bf16[1,8192,128]{2,1,0:T(8,128)(2,1)}, u32[]{:S(2)}) copy-start(bf16[1,8192,128]{2,1,0:T(8,128)(2,1)} %param.8) | copy-start | bytes 6291460
  4.4 20.8 %collective-permute-start = (bf16[64,5888]{1,0:T(8,128)(2,1)S(1)}, bf16[64,5888]{1,0:T(8,128)(2,1)}, u32[]{:S(2)}, u32[]{:S(2)}) collective-permute-start(bf16[64,5888]{1,0:T(8,128)(2,1)S(1)} %multiply_convert_fusion.refs_0_), channel_id=1, source_target_pairs={{1,0},{2,1},{3,2},{4,3},{5,4},{6,5},{7,6},{9,8},{10,9},{11,10},{12... | collective-permute-start | bytes 2261000 | tf_op jit(solution)/shard_map/ppermute | solution.py:186
  5.7 20.8 %collective-permute-start.4 = (bf16[64,5888]{1,0:T(8,128)(2,1)S(1)}, bf16[64,5888]{1,0:T(8,128)(2,1)}, u32[]{:S(2)}, u32[]{:S(2)}) collective-permute-start(bf16[64,5888]{1,0:T(8,128)(2,1)S(1)} %multiply_convert_fusion.refs_0_), channel_id=1, source_target_pairs={{0,1},{1,2},{2,3},{3,4},{4,5},{5,6},{6,7},{8,9},{9,10},{10,11},{11... | collective-permute-start | bytes 2261000 | tf_op jit(solution)/shard_map/ppermute | solution.py:185
  11.5 16.5 %slice-start = ((bf16[64,8192]{1,0:T(8,128)(2,1)}), bf16[64,2304]{1,0:T(8,128)(2,1)S(1)}, s32[]{:S(2)}) async-start(bf16[64,8192]{1,0:T(8,128)(2,1)} %param.6), calls=%async_computation.2 | async-start | bytes 589824 | tf_op jit(solution)/shard_map/slice | solution.py:198
  25.2 24.5 %collective-permute-start.1 = (bf16[64,5888]{1,0:T(8,128)(2,1)}, bf16[64,5888]{1,0:T(8,128)(2,1)S(1)}, u32[]{:S(2)}, u32[]{:S(2)}) collective-permute-start(bf16[64,5888]{1,0:T(8,128)(2,1)} %collective-permute-done.refs_1_), channel_id=1, source_target_pairs={{1,0},{2,1},{3,2},{4,3},{5,4},{6,5},{9,8},{10,9},{11,10},{12,11},{... | collective-permute-start | bytes 2261000 | tf_op jit(solution)/shard_map/ppermute | solution.py:186
  26.5 24.5 %collective-permute-start.5 = (bf16[64,5888]{1,0:T(8,128)(2,1)}, bf16[64,5888]{1,0:T(8,128)(2,1)}, u32[]{:S(2)}, u32[]{:S(2)}) collective-permute-start(bf16[64,5888]{1,0:T(8,128)(2,1)} %collective-permute-done.4.refs_0_), channel_id=1, source_target_pairs={{1,2},{2,3},{3,4},{4,5},{5,6},{6,7},{9,10},{10,11},{11,12},{12,13}... | collective-permute-start | bytes 2261000 | tf_op jit(solution)/shard_map/ppermute | solution.py:185
  28.9 10.6 %copy-start.21 = (bf16[1,1,1024,512]{3,2,1,0:T(8,128)(2,1)S(1)}, bf16[1,1,1024,512]{3,2,1,0:T(8,128)(2,1)}, u32[]{:S(2)}) copy-start(bf16[1,1,1024,512]{3,2,1,0:T(8,128)(2,1)} %param.9) | copy-start | bytes 3145732
  30.9 9.6 %copy-start.3 = (f32[64,128]{1,0:T(8,128)}, f32[64,128]{1,0:T(8,128)S(1)}, u32[]{:S(2)}) copy-start(f32[64,128]{1,0:T(8,128)S(1)} %get-tuple-element.55.refs_2_) | copy-start | bytes 98308
  30.9 25.9 %collective-permute-start.12 = (bf16[2304,128]{1,0:T(8,128)(2,1)S(1)}, bf16[2304,128]{1,0:T(8,128)(2,1)}, u32[]{:S(2)}, u32[]{:S(2)}) collective-permute-start(bf16[2304,128]{1,0:T(8,128)(2,1)S(1)} %slice_bitcast_fusion.w0), channel_id=1, source_target_pairs={{0,1},{7,6},{8,9},{15,14},{16,17},{23,22},{24,25},{31,30},{32,33},... | collective-permute-start | bytes 1769480 | tf_op jit(solution)/shard_map/ppermute | solution.py:194
  40.5 35.5 %all-to-all-start = ((bf16[32,2,16,512]{3,2,1,0:T(8,128)(2,1)}), bf16[32,2,16,512]{3,2,1,0:T(8,128)(2,1)}, u32[]{:S(2)}, u32[]{:S(2)}) async-start(bf16[32,2,16,512]{3,2,1,0:T(8,128)(2,1)} %bitcast.35), calls=%async_computation | async-start | bytes 2097152 | tf_op jit(solution)/shard_map/all_to_all | solution.py:171
  48.2 8.6 %copy-start.19 = (bf16[64,2304]{1,0:T(8,128)(2,1)S(1)}, bf16[64,2304]{1,0:T(8,128)(2,1)}, u32[]{:S(2)}) copy-start(bf16[64,2304]{1,0:T(8,128)(2,1)} %multiply_convert_fusion.1) | copy-start | bytes 884740
  48.2 8.6 %collective-permute-start.11 = (bf16[64,2304]{1,0:T(8,128)(2,1)}, bf16[64,2304]{1,0:T(8,128)(2,1)S(1)}, u32[]{:S(2)}, u32[]{:S(2)}) collective-permute-start(bf16[64,2304]{1,0:T(8,128)(2,1)} %multiply_convert_fusion.1), channel_id=1, source_target_pairs={{0,1},{7,6},{8,9},{15,14},{16,17},{23,22},{24,25},{31,30},{32,33},... | collective-permute-start | bytes 884744 | tf_op jit(solution)/shard_map/ppermute | solution.py:194
  49.6 20.9 %collective-permute-start.2 = (bf16[64,5888]{1,0:T(8,128)(2,1)S(1)}, bf16[64,5888]{1,0:T(8,128)(2,1)}, u32[]{:S(2)}, u32[]{:S(2)}) collective-permute-start(bf16[64,5888]{1,0:T(8,128)(2,1)S(1)} %collective-permute-done.1.refs_1_), channel_id=1, source_target_pairs={{1,0},{2,1},{3,2},{4,3},{5,4},{9,8},{10,9},{11,10},{12,11},{13,12}... | collective-permute-start | bytes 2261000 | tf_op jit(solution)/shard_map/ppermute | solution.py:186
  51.0 21.0 %collective-permute-start.6 = (bf16[64,5888]{1,0:T(8,128)(2,1)}, bf16[64,5888]{1,0:T(8,128)(2,1)}, u32[]{:S(2)}, u32[]{:S(2)}) collective-permute-start(bf16[64,5888]{1,0:T(8,128)(2,1)} %collective-permute-done.5.refs_0_), channel_id=1, source_target_pairs={{2,3},{3,4},{4,5},{5,6},{6,7},{10,11},{11,12},{12,13},{13,14},{14,... | collective-permute-start | bytes 2261000 | tf_op jit(solution)/shard_map/ppermute | solution.py:185
  54.8 20.7 %copy-start.7 = (f32[64,128]{1,0:T(8,128)}, f32[64,128]{1,0:T(8,128)S(1)}, u32[]{:S(2)}) copy-start(f32[64,128]{1,0:T(8,128)S(1)} %get-tuple-element.61.refs_4_) | copy-start | bytes 98308
  57.7 18.4 %collective-permute-start.13 = (bf16[128,2304]{1,0:T(8,128)(2,1)}, bf16[128,2304]{1,0:T(8,128)(2,1)}, u32[]{:S(2)}, u32[]{:S(2)}) collective-permute-start(bf16[128,2304]{1,0:T(8,128)(2,1)} %pad_maximum_fusion.2), channel_id=1, source_target_pairs={{1,2},{6,5},{9,10},{14,13},{17,18},{22,21},{25,26},{30,29},{33,34}... | collective-permute-start | bytes 1769480 | tf_op jit(solution)/shard_map/ppermute | solution.py:194
  70.5 5.5 %copy-start.20 = (bf16[64,2304]{1,0:T(8,128)(2,1)S(1)}, bf16[64,2304]{1,0:T(8,128)(2,1)}, u32[]{:S(2)}) copy-start(bf16[64,2304]{1,0:T(8,128)(2,1)} %multiply_convert_fusion.1) | copy-start | bytes 884740
  70.5 24.1 %collective-permute-start.3 = (bf16[64,5888]{1,0:T(8,128)(2,1)}, bf16[64,5888]{1,0:T(8,128)(2,1)}, u32[]{:S(2)}, u32[]{:S(2)}) collective-permute-start(bf16[64,5888]{1,0:T(8,128)(2,1)} %collective-permute-done.2.refs_1_), channel_id=1, source_target_pairs={{1,0},{2,1},{3,2},{4,3},{9,8},{10,9},{11,10},{12,11},{17,16},{18,1... | collective-permute-start | bytes 2261000 | tf_op jit(solution)/shard_map/ppermute | solution.py:186
  72.0 22.7 %collective-permute-start.7 = (bf16[64,5888]{1,0:T(8,128)(2,1)}, bf16[64,5888]{1,0:T(8,128)(2,1)}, u32[]{:S(2)}, u32[]{:S(2)}) collective-permute-start(bf16[64,5888]{1,0:T(8,128)(2,1)} %collective-permute-done.6.refs_0_), channel_id=1, source_target_pairs={{3,4},{4,5},{5,6},{6,7},{11,12},{12,13},{13,14},{14,15},{19,20},{2... | collective-permute-start | bytes 2261000 | tf_op jit(solution)/shard_map/ppermute | solution.py:185
  76.1 4.0 %copy-start.11 = (f32[64,128]{1,0:T(8,128)}, f32[64,128]{1,0:T(8,128)S(1)}, u32[]{:S(2)}) copy-start(f32[64,128]{1,0:T(8,128)S(1)} %get-tuple-element.67.refs_6_) | copy-start | bytes 98308
  77.2 20.4 %collective-permute-start.14 = (bf16[192,2304]{1,0:T(8,128)(2,1)S(1)}, bf16[192,2304]{1,0:T(8,128)(2,1)S(1)}, u32[]{:S(2)}, u32[]{:S(2)}) collective-permute-start(bf16[192,2304]{1,0:T(8,128)(2,1)S(1)} %pad_maximum_fusion.1), channel_id=1, source_target_pairs={{2,3},{5,4},{10,11},{13,12},{18,19},{21,20},{26,27},{29,28},{34,35... | collective-permute-start | bytes 2654216 | tf_op jit(solution)/shard_map/ppermute | solution.py:194
  77.9 19.7 %collective-permute-start.15 = (bf16[2304,128]{1,0:T(8,128)(2,1)}, bf16[2304,128]{1,0:T(8,128)(2,1)S(1)}, u32[]{:S(2)}, u32[]{:S(2)}) collective-permute-start(bf16[2304,128]{1,0:T(8,128)(2,1)} %collective-permute-done.12), channel_id=1, source_target_pairs={{1,2},{6,5},{9,10},{14,13},{17,18},{22,21},{25,26},{30,29},{33,34}... | collective-permute-start | bytes 1769480 | tf_op jit(solution)/shard_map/ppermute | solution.py:194
  80.0 17.6 %collective-permute-start.16 = (f32[16,512]{1,0:T(8,128)S(1)}, f32[16,512]{1,0:T(8,128)S(1)}, u32[]{:S(2)}, u32[]{:S(2)}) collective-permute-start(f32[16,512]{1,0:T(8,128)S(1)} %get-tuple-element.71), channel_id=1, source_target_pairs={{0,256},{256,0},{1,257},{257,1},{2,258},{258,2},{3,259},{259,3},{4... | collective-permute-start | bytes 98312 | tf_op jit(solution)/shard_map/ppermute | solution.py:217
  96.3 2.5 %copy-start.13 = (f32[64,128]{1,0:T(8,128)}, f32[64,128]{1,0:T(8,128)S(1)}, u32[]{:S(2)}) copy-start(f32[64,128]{1,0:T(8,128)S(1)} %shard_map.97.refs_7_) | copy-start | bytes 98308
  96.3 28.6 %collective-permute-start.8 = (bf16[64,5888]{1,0:T(8,128)(2,1)S(1)}, bf16[64,5888]{1,0:T(8,128)(2,1)}, u32[]{:S(2)}, u32[]{:S(2)}) collective-permute-start(bf16[64,5888]{1,0:T(8,128)(2,1)S(1)} %broadcast_select_fusion.refs_0_), channel_id=1, source_target_pairs={{4,5},{5,6},{6,7},{1,0},{2,1},{3,2},{12,13},{13,14},{14,15},{9,8},... | collective-permute-start | bytes 2261000 | tf_op jit(solution)/shard_map/ppermute | solution.py:191
  98.8 27.5 %copy-start.17 = (f32[1,16,512]{2,1,0:T(8,128)S(1)}, f32[1,16,512]{2,1,0:T(8,128)}, u32[]{:S(2)}) copy-start(f32[1,16,512]{2,1,0:T(8,128)} %outer.1) | copy-start | bytes 98308
  98.8 27.5 %copy-start.18 = (f32[1,16,512]{2,1,0:T(8,128)S(1)}, f32[1,16,512]{2,1,0:T(8,128)}, u32[]{:S(2)}) copy-start(f32[1,16,512]{2,1,0:T(8,128)} %moment.1) | copy-start | bytes 98308
  98.9 54.1 %collective-permute-start.20 = (bf16[256,2304]{1,0:T(8,128)(2,1)S(1)}, bf16[256,2304]{1,0:T(8,128)(2,1)S(1)}, u32[]{:S(2)}, u32[]{:S(2)}) collective-permute-start(bf16[256,2304]{1,0:T(8,128)(2,1)S(1)} %constant_dynamic-update-slice_fusion.near), channel_id=1, source_target_pairs={{3,4},{4,3},{11,12},{12,11},{19,20},{20,19},{27,28},{28,27},{35,36... | collective-permute-start | bytes 3538952 | tf_op jit(solution)/shard_map/ppermute | solution.py:226
  99.6 53.3 %collective-permute-start.19 = (bf16[4608,128]{1,0:T(8,128)(2,1)}, bf16[4608,128]{1,0:T(8,128)(2,1)}, u32[]{:S(2)}, u32[]{:S(2)}) collective-permute-start(bf16[4608,128]{1,0:T(8,128)(2,1)} %pad_maximum_fusion), channel_id=1, source_target_pairs={{2,3},{5,4},{10,11},{13,12},{18,19},{21,20},{26,27},{29,28},{34,35... | collective-permute-start | bytes 3538952 | tf_op jit(solution)/shard_map/ppermute | solution.py:194
  101.3 51.6 %collective-permute-start.18 = (bf16[2304,128]{1,0:T(8,128)(2,1)S(1)}, bf16[2304,128]{1,0:T(8,128)(2,1)}, u32[]{:S(2)}, u32[]{:S(2)}) collective-permute-start(bf16[2304,128]{1,0:T(8,128)(2,1)S(1)} %slice_bitcast_fusion.w0), channel_id=1, source_target_pairs={{1,2},{6,5},{9,10},{14,13},{17,18},{22,21},{25,26},{30,29},{33,34}... | collective-permute-start | bytes 1769480 | tf_op jit(solution)/shard_map/ppermute | solution.py:194
  124.9 29.5 %collective-permute-start.9 = (bf16[64,5888]{1,0:T(8,128)(2,1)}, bf16[64,5888]{1,0:T(8,128)(2,1)}, u32[]{:S(2)}, u32[]{:S(2)}) collective-permute-start(bf16[64,5888]{1,0:T(8,128)(2,1)} %collective-permute-done.8.refs_0_), channel_id=1, source_target_pairs={{5,6},{6,7},{1,0},{2,1},{13,14},{14,15},{9,8},{10,9},{21,22},{22,2... | collective-permute-start | bytes 2261000 | tf_op jit(solution)/shard_map/ppermute | solution.py:191
  126.9 14.5 %collective-permute-start.17 = (bf16[16,512]{1,0:T(8,128)(2,1)S(1)}, bf16[16,512]{1,0:T(8,128)(2,1)S(1)}, u32[]{:S(2)}, u32[]{:S(2)}) collective-permute-start(bf16[16,512]{1,0:T(8,128)(2,1)S(1)} %get-tuple-element.75), channel_id=1, source_target_pairs={{0,256},{256,0},{1,257},{257,1},{2,258},{258,2},{3,259},{259,3},{4... | collective-permute-start | bytes 49160 | tf_op jit(solution)/shard_map/ppermute | solution.py:229
  142.4 21.9 %all-to-all-start.1 = ((bf16[32,2,16,512]{3,2,1,0:T(8,128)(2,1)}), bf16[32,2,16,512]{3,2,1,0:T(8,128)(2,1)}, u32[]{:S(2)}, u32[]{:S(2)}) async-start(bf16[32,2,16,512]{3,2,1,0:T(8,128)(2,1)} %broadcast_in_dim.2), calls=%async_computation.1 | async-start | bytes 2097152 | tf_op jit(solution)/shard_map/all_to_all | solution.py:237
  149.8 1.6 copy-start.1
  152.9 3.8 %copy-start.15 = (f32[64,128]{1,0:T(8,128)}, f32[64,128]{1,0:T(8,128)S(1)}, u32[]{:S(2)}) copy-start(f32[64,128]{1,0:T(8,128)S(1)} %shard_map.100.refs_8_) | copy-start | bytes 98308
  152.9 13.7 %collective-permute-start.21 = (bf16[2304,128]{1,0:T(8,128)(2,1)}, bf16[2304,128]{1,0:T(8,128)(2,1)}, u32[]{:S(2)}, u32[]{:S(2)}) collective-permute-start(bf16[2304,128]{1,0:T(8,128)(2,1)} %collective-permute-done.18), channel_id=1, source_target_pairs={{2,3},{5,4},{10,11},{13,12},{18,19},{21,20},{26,27},{29,28},{34,35... | collective-permute-start | bytes 1769480 | tf_op jit(solution)/shard_map/ppermute | solution.py:194
  154.4 39.3 %collective-permute-start.10 = (bf16[64,5888]{1,0:T(8,128)(2,1)}, bf16[64,5888]{1,0:T(8,128)(2,1)}, u32[]{:S(2)}, u32[]{:S(2)}) collective-permute-start(bf16[64,5888]{1,0:T(8,128)(2,1)} %collective-permute-done.9.refs_0_), channel_id=1, source_target_pairs={{6,7},{1,0},{14,15},{9,8},{22,23},{17,16},{30,31},{25,24},{38,39},... | collective-permute-start | bytes 2261000 | tf_op jit(solution)/shard_map/ppermute | solution.py:191
  166.6 5.8 %copy-start.2 = (bf16[1,8192,128]{2,1,0:T(8,128)(2,1)S(1)}, bf16[1,8192,128]{2,1,0:T(8,128)(2,1)}, u32[]{:S(2)}) copy-start(bf16[1,8192,128]{2,1,0:T(8,128)(2,1)} %param.8) | copy-start | bytes 6291460
  169.6 4.4 %collective-permute-start.22 = (bf16[512,128]{1,0:T(8,128)(2,1)S(1)}, bf16[512,128]{1,0:T(8,128)(2,1)S(1)}, u32[]{:S(2)}, u32[]{:S(2)}) collective-permute-start(bf16[512,128]{1,0:T(8,128)(2,1)S(1)} %get-tuple-element.90), channel_id=1, source_target_pairs={{3,2},{4,5},{11,10},{12,13},{19,18},{20,21},{27,26},{28,29},{35,34... | collective-permute-start | bytes 393224 | tf_op jit(solution)/shard_map/ppermute | solution.py:243
  170.3 3.7 %collective-permute-start.23 = (bf16[512,128]{1,0:T(8,128)(2,1)S(1)}, bf16[512,128]{1,0:T(8,128)(2,1)S(1)}, u32[]{:S(2)}, u32[]{:S(2)}) collective-permute-start(bf16[512,128]{1,0:T(8,128)(2,1)S(1)} %get-tuple-element.91), channel_id=1, source_target_pairs={{3,1},{4,6},{11,9},{12,14},{19,17},{20,22},{27,25},{28,30},{35,33}... | collective-permute-start | bytes 393224 | tf_op jit(solution)/shard_map/ppermute | solution.py:243
  171.0 22.8 %copy-start.4 = (f32[64,128]{1,0:T(8,128)S(1)}, f32[64,128]{1,0:T(8,128)}, u32[]{:S(2)}) copy-start(f32[64,128]{1,0:T(8,128)} %copy-done.3) | copy-start | bytes 98308
  171.0 22.8 %copy-start.6 = (f32[64,128]{1,0:T(8,128)S(1)}, f32[64,128]{1,0:T(8,128)}, u32[]{:S(2)}) copy-start(f32[64,128]{1,0:T(8,128)} %copy-done.5) | copy-start | bytes 98308
  171.0 22.8 %copy-start.8 = (f32[64,128]{1,0:T(8,128)S(1)}, f32[64,128]{1,0:T(8,128)}, u32[]{:S(2)}) copy-start(f32[64,128]{1,0:T(8,128)} %copy-done.7) | copy-start | bytes 98308
  171.0 22.8 %copy-start.10 = (f32[64,128]{1,0:T(8,128)S(1)}, f32[64,128]{1,0:T(8,128)}, u32[]{:S(2)}) copy-start(f32[64,128]{1,0:T(8,128)} %copy-done.9) | copy-start | bytes 98308
  171.0 22.8 %copy-start.12 = (f32[64,128]{1,0:T(8,128)S(1)}, f32[64,128]{1,0:T(8,128)}, u32[]{:S(2)}) copy-start(f32[64,128]{1,0:T(8,128)} %copy-done.11) | copy-start | bytes 98308
  171.0 22.8 %copy-start.14 = (f32[64,128]{1,0:T(8,128)S(1)}, f32[64,128]{1,0:T(8,128)}, u32[]{:S(2)}) copy-start(f32[64,128]{1,0:T(8,128)} %copy-done.13) | copy-start | bytes 98308
  171.0 22.8 %copy-start.16 = (f32[64,128]{1,0:T(8,128)S(1)}, f32[64,128]{1,0:T(8,128)}, u32[]{:S(2)}) copy-start(f32[64,128]{1,0:T(8,128)} %copy-done.15) | copy-start | bytes 98308
  171.0 22.7 %collective-permute-start.24 = (bf16[512,128]{1,0:T(8,128)(2,1)S(1)}, bf16[512,128]{1,0:T(8,128)(2,1)S(1)}, u32[]{:S(2)}, u32[]{:S(2)}) collective-permute-start(bf16[512,128]{1,0:T(8,128)(2,1)S(1)} %get-tuple-element.92), channel_id=1, source_target_pairs={{3,0},{4,7},{11,8},{12,15},{19,16},{20,23},{27,24},{28,31},{35,32}... | collective-permute-start | bytes 393224 | tf_op jit(solution)/shard_map/ppermute | solution.py:243
  (3 other events, 1.9 us)

commit v9 on v6

--- a/solution.py
+++ b/solution.py
@@ -19,7 +19,7 @@
 PLANE = ("y", "x", "core")
 REPLICA = ("zh",) + PLANE
 
-K_LINE = 5888
+K_LINE = 6144
 
 
 def rotary_tables(rows):
@@ -152,9 +152,8 @@
     synced = lax.all_to_all(jnp.broadcast_to(pair[None], (32, 2, 16, 512)), PLANE, 0, 0, tiled=True)
 
     y = hop_out(x, 6)
-    rows, w2, synced = hold((rows, w2, synced))
-    rows5 = put(rows, x, jnp.where(low, me + 6, me - 6))
-    rows, w2 = hold((rows5, w2))
+    rows, synced = hold((rows, synced))
+    rows = put(rows, x, jnp.where(low, me + 6, me - 6))
     blocks = middle_products(low, near, far, w_rest, w13, w2)
     middle = jnp.where((me == 3) | (me == 4), blocks[0], 0.0)
     for d in (3, 2, 1):

time: 169 us -> 170 us (level)
  the two profiles are of different devices: /device:TPU:64 before, /device:TPU:6 now
where the time goes in v9:
time: 170 us; the launch traced here: 167 us
  waiting for transfers between devices  66.8 us (39%)
  starting transfers between devices  63 us (37%)
  matrix products  16.9 us (10%)
  local copies, waits for them, and re-layouts  8.43 us (5%)
  other arithmetic  8.14 us (5%)
  Pallas kernels  2.62 us (2%)
    ppermute x3, waiting for transfers between devices, hop_out(): return lax.ppermute(x, 'tensor', pairs)  26.5 us
    dot_general x11, matrix products, dot(): return jnp.dot(a, b, preferred_element_type=jnp.float32)  16.9 us
    ppermute x4, waiting for transfers between devices, hop(): b = lax.ppermute(b, 'tensor', [(j + 1, j) for j in range(7 - s)])  15.1 us
    ppermute x1, starting transfers between devices, body(): came = lax.ppermute(other, 'zh', [(0, 1), (1, 0)])  14.6 us
    ppermute x8, starting transfers between devices, inward(): return lax.ppermute(x, 'tensor', [(3 - d, 4 - d), (4 + d, 3 + d)])  12.1 us
    ppermute x1, waiting for transfers between devices, body(): came = lax.ppermute(other, 'zh', [(0, 1), (1, 0)])  11 us
    ppermute x4, starting transfers between devices, hop(): a = lax.ppermute(a, 'tensor', [(j, j + 1) for j in range(s, 7)])  7.68 us
    all_to_all x1, starting transfers between devices, body(): pieces = lax.all_to_all(params, PLANE, 0, 0, tiled=True)  7.56 us
  transfers between devices with their start and end apart: 27, of which 10 were waited for; matrix products, arithmetic and copies ran while one was open for 15% of the time, Pallas kernels for 2%

profile of v9, /device:TPU:6, one launch (start us, length us, event | category | flops | bytes accessed | tf_op | source)
XLA Modules:
  0.0 167.1 jit_solution(2450440222777091084)
XLA Ops:
  0.6 1.6 multiply_reduce_fusion
  3.0 2.3 %multiply_convert_fusion = bf16[64,6144]{1,0:T(8,128)(2,1)} fusion(f32[6144]{0:T(1024)S(1)} %slice.44, f32[64]{0:T(128)S(1)} %add_rsqrt_fusion, bf16[64,8192]{1,0:T(8,128)(2,1)} %param.6), kind=kLoop, calls=%fused_computation.24 | loop fusion | flops 1572864 | bytes 1597696 | tf_op jit(solution)/shard_map/convert_element_type | solution.py:87
  5.3 4.7 %collective-permute-start = (bf16[64,6144]{1,0:T(8,128)(2,1)}, bf16[64,6144]{1,0:T(8,128)(2,1)}, u32[]{:S(2)}, u32[]{:S(2)}) collective-permute-start(bf16[64,6144]{1,0:T(8,128)(2,1)} %multiply_convert_fusion), channel_id=1, source_target_pairs={{0,1},{1,2},{2,3},{3,4},{4,5},{5,6},{6,7},{8,9},{9,10},{10,11},{11... | collective-permute-start | bytes 2359304 | tf_op jit(solution)/shard_map/ppermute | solution.py:99
  10.0 1.3 collective-permute-start.1
  11.3 1.1 copy.12
  12.3 7.6 %all-to-all-start = ((bf16[32,2,16,512]{3,2,1,0:T(8,128)(2,1)}), bf16[32,2,16,512]{3,2,1,0:T(8,128)(2,1)S(1)}, u32[]{:S(2)}, u32[]{:S(2)}) async-start(bf16[32,2,16,512]{3,2,1,0:T(8,128)(2,1)} %copy.12), calls=%async_computation | async-start | bytes 2097152 | tf_op jit(solution)/shard_map/all_to_all | solution.py:80
  20.0 2.1 %fusion.25 = f32[22,64,128]{2,1,0:T(8,128)S(1)} fusion(f32[22,64,128]{2,1,0:T(8,128)S(1)} %broadcast_in_dim.57, s32[]{:T(128)S(6)} %select_n.77, bf16[64,6144]{1,0:T(8,128)(2,1)} %multiply_convert_fusion, bf16[1,8192,128]{2,1,0:T(8,128)(2,1)} %param.8), kind=kOutput, calls=%fused_computation.26 | convolution fusion | flops 100663296 | bytes 2392068 | tf_op jit(solution)/shard_map/dot_general | solution.py:34
  22.1 1.2 slice_bitcast_fusion.w0
  23.5 2.7 %collective-permute-done = bf16[64,6144]{1,0:T(8,128)(2,1)} collective-permute-done((bf16[64,6144]{1,0:T(8,128)(2,1)}, bf16[64,6144]{1,0:T(8,128)(2,1)}, u32[]{:S(2)}, u32[]{:S(2)}) %collective-permute-start) | collective-permute-done | bytes 786464 | tf_op jit(solution)/shard_map/ppermute | solution.py:99
  26.2 1.5 collective-permute-start.2
  27.7 3.4 %collective-permute-done.1 = bf16[64,6144]{1,0:T(8,128)(2,1)} collective-permute-done((bf16[64,6144]{1,0:T(8,128)(2,1)}, bf16[64,6144]{1,0:T(8,128)(2,1)}, u32[]{:S(2)}, u32[]{:S(2)}) %collective-permute-start.1) | collective-permute-done | bytes 786464 | tf_op jit(solution)/shard_map/ppermute | solution.py:100
  31.2 1.3 collective-permute-start.3
  32.5 2.1 %fusion.31 = f32[22,64,128]{2,1,0:T(8,128)S(1)} fusion(f32[22,64,128]{2,1,0:T(8,128)S(1)} %fusion.25, s32[]{:T(128)S(6)} %select_n.78, bf16[64,6144]{1,0:T(8,128)(2,1)} %collective-permute-done, bf16[1,8192,128]{2,1,0:T(8,128)(2,1)} %param.8), kind=kOutput, calls=%fused_computation.28 | convolution fusion | flops 100663296 | bytes 2392068 | tf_op jit(solution)/shard_map/dot_general | solution.py:34
  34.5 1.5 fusion.37
  36.1 4.9 %collective-permute-start.6 = (bf16[2048,128]{1,0:T(8,128)(2,1)S(1)}, bf16[2048,128]{1,0:T(8,128)(2,1)S(1)}, u32[]{:S(2)}, u32[]{:S(2)}) collective-permute-start(bf16[2048,128]{1,0:T(8,128)(2,1)S(1)} %slice_bitcast_fusion.w0), channel_id=1, source_target_pairs={{0,1},{7,6},{8,9},{15,14},{16,17},{23,22},{24,25},{31,30},{32,33},... | collective-permute-start | bytes 1572872 | tf_op jit(solution)/shard_map/ppermute | solution.py:108
  41.0 1.3 collective-permute-start.5
  42.5 14.6 %collective-permute-start.4 = (f32[16,512]{1,0:T(8,128)S(1)}, f32[16,512]{1,0:T(8,128)S(1)}, u32[]{:S(2)}, u32[]{:S(2)}) collective-permute-start(f32[16,512]{1,0:T(8,128)S(1)} %dynamic-slice_bitcast_fusion), channel_id=1, source_target_pairs={{0,256},{256,0},{1,257},{257,1},{2,258},{258,2},{3,259},{259,3},{4... | collective-permute-start | bytes 98312 | tf_op jit(solution)/shard_map/ppermute | solution.py:122
  57.9 1.3 collective-permute-start.8
  59.2 2.1 %fusion.43 = f32[22,64,128]{2,1,0:T(8,128)S(1)} fusion(f32[22,64,128]{2,1,0:T(8,128)S(1)} %fusion.37, s32[]{:T(128)S(6)} %select_n.80, bf16[64,6144]{1,0:T(8,128)(2,1)} %collective-permute-done.2, bf16[1,8192,128]{2,1,0:T(8,128)(2,1)} %param.8), kind=kOutput, calls=%fused_computation.32 | convolution fusion | flops 100663296 | bytes 2392068 | tf_op jit(solution)/shard_map/dot_general | solution.py:34
  61.3 1.6 fusion.49
  62.9 11.0 %collective-permute-done.4 = f32[16,512]{1,0:T(8,128)S(1)} collective-permute-done((f32[16,512]{1,0:T(8,128)S(1)}, f32[16,512]{1,0:T(8,128)S(1)}, u32[]{:S(2)}, u32[]{:S(2)}) %collective-permute-start.4) | collective-permute-done | bytes 32800 | tf_op jit(solution)/shard_map/ppermute | solution.py:122
  74.6 1.9 %collective-permute-start.10 = (bf16[16,512]{1,0:T(8,128)(2,1)S(1)}, bf16[16,512]{1,0:T(8,128)(2,1)S(1)}, u32[]{:S(2)}, u32[]{:S(2)}) collective-permute-start(bf16[16,512]{1,0:T(8,128)(2,1)S(1)} %get-tuple-element.64), channel_id=1, source_target_pairs={{0,256},{256,0},{1,257},{257,1},{2,258},{258,2},{3,259},{259,3},{4... | collective-permute-start | bytes 49160 | tf_op jit(solution)/shard_map/ppermute | solution.py:130
  77.2 2.7 %collective-permute-done.8 = bf16[64,6144]{1,0:T(8,128)(2,1)S(1)} collective-permute-done((bf16[64,6144]{1,0:T(8,128)(2,1)}, bf16[64,6144]{1,0:T(8,128)(2,1)S(1)}, u32[]{:S(2)}, u32[]{:S(2)}) %collective-permute-start.8) | collective-permute-done | bytes 786464 | tf_op jit(solution)/shard_map/ppermute | solution.py:100
  80.0 1.3 collective-permute-start.11
  82.8 6.2 %collective-permute-done.10 = bf16[16,512]{1,0:T(8,128)(2,1)S(1)} collective-permute-done((bf16[16,512]{1,0:T(8,128)(2,1)S(1)}, bf16[16,512]{1,0:T(8,128)(2,1)S(1)}, u32[]{:S(2)}, u32[]{:S(2)}) %collective-permute-start.10) | collective-permute-done | bytes 16416 | tf_op jit(solution)/shard_map/ppermute | solution.py:130
  90.5 8.9 %collective-permute-done.11 = bf16[64,6144]{1,0:T(8,128)(2,1)S(1)} collective-permute-done((bf16[64,6144]{1,0:T(8,128)(2,1)S(1)}, bf16[64,6144]{1,0:T(8,128)(2,1)S(1)}, u32[]{:S(2)}, u32[]{:S(2)}) %collective-permute-start.11) | collective-permute-done | bytes 786464 | tf_op jit(solution)/shard_map/ppermute | solution.py:100
  99.5 1.3 collective-permute-start.15
  102.1 1.0 pad_maximum_fusion
  103.1 1.6 collective-permute-start.17
  104.8 13.7 %collective-permute-done.15 = bf16[64,6144]{1,0:T(8,128)(2,1)} collective-permute-done((bf16[64,6144]{1,0:T(8,128)(2,1)S(1)}, bf16[64,6144]{1,0:T(8,128)(2,1)}, u32[]{:S(2)}, u32[]{:S(2)}) %collective-permute-start.15) | collective-permute-done | bytes 786464 | tf_op jit(solution)/shard_map/ppermute | solution.py:105
  118.5 1.3 collective-permute-start.19
  119.8 1.5 collective-permute-start.16
  121.3 1.1 broadcast_in_dim.67
  122.4 6.7 %all-to-all-start.1 = ((bf16[32,2,16,512]{3,2,1,0:T(8,128)(2,1)}), bf16[32,2,16,512]{3,2,1,0:T(8,128)(2,1)}, u32[]{:S(2)}, u32[]{:S(2)}) async-start(bf16[32,2,16,512]{3,2,1,0:T(8,128)(2,1)} %broadcast_in_dim.67), calls=%async_computation.1 | async-start | bytes 2097152 | tf_op jit(solution)/shard_map/all_to_all | solution.py:152
  129.1 2.1 %fusion.73 = f32[22,64,128]{2,1,0:T(8,128)S(1)} fusion(f32[22,64,128]{2,1,0:T(8,128)S(1)} %fusion.67, s32[]{:T(128)S(6)} %select_n.93, bf16[64,6144]{1,0:T(8,128)(2,1)} %collective-permute-done.15, bf16[1,8192,128]{2,1,0:T(8,128)(2,1)} %param.8), kind=kOutput, calls=%fused_computation.42 | convolution fusion | flops 100663296 | bytes 2392068 | tf_op jit(solution)/shard_map/dot_general | solution.py:34
  131.2 0.9 copy-done
  132.8 4.5 %collective-permute-done.19 = bf16[64,6144]{1,0:T(8,128)(2,1)} collective-permute-done((bf16[64,6144]{1,0:T(8,128)(2,1)}, bf16[64,6144]{1,0:T(8,128)(2,1)}, u32[]{:S(2)}, u32[]{:S(2)}) %collective-permute-start.19) | collective-permute-done | bytes 786464 | tf_op jit(solution)/shard_map/ppermute | solution.py:105
  137.3 1.3 collective-permute-start.20
  138.6 5.2 %all-to-all-done.1 = bf16[32,2,16,512]{3,2,1,0:T(8,128)(2,1)} async-done(((bf16[32,2,16,512]{3,2,1,0:T(8,128)(2,1)}), bf16[32,2,16,512]{3,2,1,0:T(8,128)(2,1)}, u32[]{:S(2)}, u32[]{:S(2)}) %all-to-all-start.1) | async-done | bytes 1048608 | tf_op jit(solution)/shard_map/all_to_all | solution.py:152
  143.9 2.3 %copy.14 = bf16[32,2,16,512]{3,2,0,1:T(8,128)(2,1)} copy(bf16[32,2,16,512]{3,2,1,0:T(8,128)(2,1)} %all-to-all-done.1) | data formatting | bytes 2097152 | tf_op jit(solution)/shard_map/optimization_barrier | solution.py:155
  146.1 2.6 %shard_map.93 = (f32[512,128]{1,0:T(8,128)S(1)}, bf16[512,128]{1,0:T(8,128)(2,1)S(1)}, bf16[512,128]{1,0:T(8,128)(2,1)S(1)}, bf16[512,128]{1,0:T(8,128)(2,1)S(1)}) custom-call(s32[1]{0:T(128)} %bitcast.22.low, bf16[256,2048]{1,0:T(8,128)(2,1)S(1)} %constant_dynamic-update-slice_fusion.near, bf16[256,2048]{1,0:T(8,128)(2,1)S(1)} %collective-permute-done.18.far, ...), custom_call_target="tpu_custom_call" | custom-call | tf_op jit(solution)/shard_map/pallas_call | solution.py:64
  148.8 1.3 collective-permute-start.22
  151.4 2.2 %fusion.79 = f32[22,64,128]{2,1,0:T(8,128)} fusion(f32[22,64,128]{2,1,0:T(8,128)} %copy-done, s32[]{:T(128)S(6)} %select_n.95, bf16[64,6144]{1,0:T(8,128)(2,1)} %collective-permute-done.19, bf16[1,8192,128]{2,1,0:T(8,128)(2,1)S(1)} %copy-done.4), kind=kOutput, calls=%fused_computation.44 | convolution fusion | flops 100663296 | bytes 2392068 | tf_op jit(solution)/shard_map/dot_general | solution.py:34
  153.6 8.3 %collective-permute-done.20 = bf16[64,6144]{1,0:T(8,128)(2,1)} collective-permute-done((bf16[64,6144]{1,0:T(8,128)(2,1)}, bf16[64,6144]{1,0:T(8,128)(2,1)}, u32[]{:S(2)}, u32[]{:S(2)}) %collective-permute-start.20) | collective-permute-done | bytes 786464 | tf_op jit(solution)/shard_map/ppermute | solution.py:105
  161.9 2.2 %fusion.85 = f32[22,64,128]{2,1,0:T(8,128)} fusion(f32[22,64,128]{2,1,0:T(8,128)} %fusion.79, s32[]{:T(128)S(6)} %select_n.97, bf16[64,6144]{1,0:T(8,128)(2,1)} %collective-permute-done.20, bf16[1,8192,128]{2,1,0:T(8,128)(2,1)S(1)} %copy-done.4), kind=kOutput, calls=%fused_computation.46 | convolution fusion | flops 100663296 | bytes 2392068 | tf_op jit(solution)/shard_map/dot_general | solution.py:34
  164.1 1.0 slice.46
  165.1 1.2 fusion.93
  166.4 0.8 pad_maximum_fusion.3
  (63 shorter events, 9.7 us)
Async XLA Ops:
  0.6 10.6 %copy-start.1 = (bf16[1,1,1024,512]{3,2,1,0:T(8,128)(2,1)S(1)}, bf16[1,1,1024,512]{3,2,1,0:T(8,128)(2,1)}, u32[]{:S(2)}) copy-start(bf16[1,1,1024,512]{3,2,1,0:T(8,128)(2,1)} %param.9) | copy-start | bytes 3145732
  5.3 20.9 %collective-permute-start = (bf16[64,6144]{1,0:T(8,128)(2,1)}, bf16[64,6144]{1,0:T(8,128)(2,1)}, u32[]{:S(2)}, u32[]{:S(2)}) collective-permute-start(bf16[64,6144]{1,0:T(8,128)(2,1)} %multiply_convert_fusion), channel_id=1, source_target_pairs={{0,1},{1,2},{2,3},{3,4},{4,5},{5,6},{6,7},{8,9},{9,10},{10,11},{11... | collective-permute-start | bytes 2359304 | tf_op jit(solution)/shard_map/ppermute | solution.py:99
  10.0 21.2 %collective-permute-start.1 = (bf16[64,6144]{1,0:T(8,128)(2,1)}, bf16[64,6144]{1,0:T(8,128)(2,1)}, u32[]{:S(2)}, u32[]{:S(2)}) collective-permute-start(bf16[64,6144]{1,0:T(8,128)(2,1)} %multiply_convert_fusion), channel_id=1, source_target_pairs={{1,0},{2,1},{3,2},{4,3},{5,4},{6,5},{7,6},{9,8},{10,9},{11,10},{12... | collective-permute-start | bytes 2359304 | tf_op jit(solution)/shard_map/ppermute | solution.py:100
  11.3 8.7 %copy-start.5 = (bf16[8192]{0:T(1024)(128)(2,1)S(1)}, bf16[8192]{0:T(1024)(128)(2,1)}, u32[]{:S(2)}) copy-start(bf16[8192]{0:T(1024)(128)(2,1)} %param.7) | copy-start | bytes 49156
  12.3 23.7 %all-to-all-start = ((bf16[32,2,16,512]{3,2,1,0:T(8,128)(2,1)}), bf16[32,2,16,512]{3,2,1,0:T(8,128)(2,1)S(1)}, u32[]{:S(2)}, u32[]{:S(2)}) async-start(bf16[32,2,16,512]{3,2,1,0:T(8,128)(2,1)} %copy.12), calls=%async_computation | async-start | bytes 2097152 | tf_op jit(solution)/shard_map/all_to_all | solution.py:80
  20.0 3.4 %slice-start = ((bf16[64,8192]{1,0:T(8,128)(2,1)}), bf16[64,2048]{1,0:T(8,128)(2,1)S(1)}, s32[]{:S(2)}) async-start(bf16[64,8192]{1,0:T(8,128)(2,1)} %param.6), calls=%async_computation.2 | async-start | bytes 524288 | tf_op jit(solution)/shard_map/slice | solution.py:112
  22.1 12.4 %copy-start.2 = (bf16[1,8192,128]{2,1,0:T(8,128)(2,1)S(1)}, bf16[1,8192,128]{2,1,0:T(8,128)(2,1)}, u32[]{:S(2)}) copy-start(bf16[1,8192,128]{2,1,0:T(8,128)(2,1)} %param.8) | copy-start | bytes 6291460
  26.2 31.0 %collective-permute-start.2 = (bf16[64,6144]{1,0:T(8,128)(2,1)}, bf16[64,6144]{1,0:T(8,128)(2,1)}, u32[]{:S(2)}, u32[]{:S(2)}) collective-permute-start(bf16[64,6144]{1,0:T(8,128)(2,1)} %collective-permute-done), channel_id=1, source_target_pairs={{1,2},{2,3},{3,4},{4,5},{5,6},{6,7},{9,10},{10,11},{11,12},{12,13}... | collective-permute-start | bytes 2359304 | tf_op jit(solution)/shard_map/ppermute | solution.py:99
  31.2 26.7 %collective-permute-start.3 = (bf16[64,6144]{1,0:T(8,128)(2,1)}, bf16[64,6144]{1,0:T(8,128)(2,1)}, u32[]{:S(2)}, u32[]{:S(2)}) collective-permute-start(bf16[64,6144]{1,0:T(8,128)(2,1)} %collective-permute-done.1), channel_id=1, source_target_pairs={{1,0},{2,1},{3,2},{4,3},{5,4},{6,5},{9,8},{10,9},{11,10},{12,11},{... | collective-permute-start | bytes 2359304 | tf_op jit(solution)/shard_map/ppermute | solution.py:100
  36.1 25.2 %copy-start.3 = (bf16[1,8192,128]{2,1,0:T(8,128)(2,1)S(1)}, bf16[1,8192,128]{2,1,0:T(8,128)(2,1)}, u32[]{:S(2)}) copy-start(bf16[1,8192,128]{2,1,0:T(8,128)(2,1)} %param.8) | copy-start | bytes 6291460
  36.1 37.8 %collective-permute-start.6 = (bf16[2048,128]{1,0:T(8,128)(2,1)S(1)}, bf16[2048,128]{1,0:T(8,128)(2,1)S(1)}, u32[]{:S(2)}, u32[]{:S(2)}) collective-permute-start(bf16[2048,128]{1,0:T(8,128)(2,1)S(1)} %slice_bitcast_fusion.w0), channel_id=1, source_target_pairs={{0,1},{7,6},{8,9},{15,14},{16,17},{23,22},{24,25},{31,30},{32,33},... | collective-permute-start | bytes 1572872 | tf_op jit(solution)/shard_map/ppermute | solution.py:108
  41.0 32.9 %collective-permute-start.5 = (bf16[64,2048]{1,0:T(8,128)(2,1)S(1)}, bf16[64,2048]{1,0:T(8,128)(2,1)S(1)}, u32[]{:S(2)}, u32[]{:S(2)}) collective-permute-start(bf16[64,2048]{1,0:T(8,128)(2,1)S(1)} %multiply_convert_fusion.1), channel_id=1, source_target_pairs={{0,1},{7,6},{8,9},{15,14},{16,17},{23,22},{24,25},{31,30},{32,33},... | collective-permute-start | bytes 786440 | tf_op jit(solution)/shard_map/ppermute | solution.py:108
  42.5 31.4 %copy-start.6 = (f32[1,16,512]{2,1,0:T(8,128)S(1)}, f32[1,16,512]{2,1,0:T(8,128)}, u32[]{:S(2)}) copy-start(f32[1,16,512]{2,1,0:T(8,128)} %param.11) | copy-start | bytes 98308
  42.5 31.4 %copy-start.7 = (f32[1,16,512]{2,1,0:T(8,128)S(1)}, f32[1,16,512]{2,1,0:T(8,128)}, u32[]{:S(2)}) copy-start(f32[1,16,512]{2,1,0:T(8,128)} %param.10) | copy-start | bytes 98308
  42.5 31.4 %collective-permute-start.4 = (f32[16,512]{1,0:T(8,128)S(1)}, f32[16,512]{1,0:T(8,128)S(1)}, u32[]{:S(2)}, u32[]{:S(2)}) collective-permute-start(f32[16,512]{1,0:T(8,128)S(1)} %dynamic-slice_bitcast_fusion), channel_id=1, source_target_pairs={{0,256},{256,0},{1,257},{257,1},{2,258},{258,2},{3,259},{259,3},{4... | collective-permute-start | bytes 98312 | tf_op jit(solution)/shard_map/ppermute | solution.py:122
  57.2 24.1 %collective-permute-start.7 = (bf16[64,6144]{1,0:T(8,128)(2,1)}, bf16[64,6144]{1,0:T(8,128)(2,1)S(1)}, u32[]{:S(2)}, u32[]{:S(2)}) collective-permute-start(bf16[64,6144]{1,0:T(8,128)(2,1)} %collective-permute-done.2), channel_id=1, source_target_pairs={{2,3},{3,4},{4,5},{5,6},{6,7},{10,11},{11,12},{12,13},{13,14},{14,... | collective-permute-start | bytes 2359304 | tf_op jit(solution)/shard_map/ppermute | solution.py:99
  57.9 22.0 %collective-permute-start.8 = (bf16[64,6144]{1,0:T(8,128)(2,1)}, bf16[64,6144]{1,0:T(8,128)(2,1)S(1)}, u32[]{:S(2)}, u32[]{:S(2)}) collective-permute-start(bf16[64,6144]{1,0:T(8,128)(2,1)} %collective-permute-done.3), channel_id=1, source_target_pairs={{1,0},{2,1},{3,2},{4,3},{5,4},{9,8},{10,9},{11,10},{12,11},{13,12}... | collective-permute-start | bytes 2359304 | tf_op jit(solution)/shard_map/ppermute | solution.py:100
  74.6 14.5 %collective-permute-start.10 = (bf16[16,512]{1,0:T(8,128)(2,1)S(1)}, bf16[16,512]{1,0:T(8,128)(2,1)S(1)}, u32[]{:S(2)}, u32[]{:S(2)}) collective-permute-start(bf16[16,512]{1,0:T(8,128)(2,1)S(1)} %get-tuple-element.64), channel_id=1, source_target_pairs={{0,256},{256,0},{1,257},{257,1},{2,258},{258,2},{3,259},{259,3},{4... | collective-permute-start | bytes 49160 | tf_op jit(solution)/shard_map/ppermute | solution.py:130
  76.5 12.5 %collective-permute-start.9 = (bf16[128,2048]{1,0:T(8,128)(2,1)S(1)}, bf16[128,2048]{1,0:T(8,128)(2,1)S(1)}, u32[]{:S(2)}, u32[]{:S(2)}) collective-permute-start(bf16[128,2048]{1,0:T(8,128)(2,1)S(1)} %pad_maximum_fusion.2), channel_id=1, source_target_pairs={{1,2},{6,5},{9,10},{14,13},{17,18},{22,21},{25,26},{30,29},{33,34}... | collective-permute-start | bytes 1572872 | tf_op jit(solution)/shard_map/ppermute | solution.py:108
  80.0 19.5 %collective-permute-start.11 = (bf16[64,6144]{1,0:T(8,128)(2,1)S(1)}, bf16[64,6144]{1,0:T(8,128)(2,1)S(1)}, u32[]{:S(2)}, u32[]{:S(2)}) collective-permute-start(bf16[64,6144]{1,0:T(8,128)(2,1)S(1)} %collective-permute-done.8), channel_id=1, source_target_pairs={{1,0},{2,1},{3,2},{4,3},{9,8},{10,9},{11,10},{12,11},{17,16},{18,1... | collective-permute-start | bytes 2359304 | tf_op jit(solution)/shard_map/ppermute | solution.py:100
  81.3 18.2 %collective-permute-start.12 = (bf16[64,6144]{1,0:T(8,128)(2,1)S(1)}, bf16[64,6144]{1,0:T(8,128)(2,1)S(1)}, u32[]{:S(2)}, u32[]{:S(2)}) collective-permute-start(bf16[64,6144]{1,0:T(8,128)(2,1)S(1)} %collective-permute-done.7), channel_id=1, source_target_pairs={{3,4},{4,5},{5,6},{6,7},{11,12},{12,13},{13,14},{14,15},{19,20},{2... | collective-permute-start | bytes 2359304 | tf_op jit(solution)/shard_map/ppermute | solution.py:99
  89.1 12.2 %collective-permute-start.13 = (bf16[192,2048]{1,0:T(8,128)(2,1)S(1)}, bf16[192,2048]{1,0:T(8,128)(2,1)S(1)}, u32[]{:S(2)}, u32[]{:S(2)}) collective-permute-start(bf16[192,2048]{1,0:T(8,128)(2,1)S(1)} %pad_maximum_fusion.1), channel_id=1, source_target_pairs={{2,3},{5,4},{10,11},{13,12},{18,19},{21,20},{26,27},{29,28},{34,35... | collective-permute-start | bytes 2359304 | tf_op jit(solution)/shard_map/ppermute | solution.py:108
  89.8 11.4 %collective-permute-start.14 = (bf16[2048,128]{1,0:T(8,128)(2,1)S(1)}, bf16[2048,128]{1,0:T(8,128)(2,1)S(1)}, u32[]{:S(2)}, u32[]{:S(2)}) collective-permute-start(bf16[2048,128]{1,0:T(8,128)(2,1)S(1)} %collective-permute-done.6), channel_id=1, source_target_pairs={{1,2},{6,5},{9,10},{14,13},{17,18},{22,21},{25,26},{30,29},{33,34}... | collective-permute-start | bytes 1572872 | tf_op jit(solution)/shard_map/ppermute | solution.py:108
  99.5 18.9 %collective-permute-start.15 = (bf16[64,6144]{1,0:T(8,128)(2,1)S(1)}, bf16[64,6144]{1,0:T(8,128)(2,1)}, u32[]{:S(2)}, u32[]{:S(2)}) collective-permute-start(bf16[64,6144]{1,0:T(8,128)(2,1)S(1)} %broadcast_select_fusion), channel_id=1, source_target_pairs={{4,5},{5,6},{6,7},{1,0},{2,1},{3,2},{12,13},{13,14},{14,15},{9,8},... | collective-permute-start | bytes 2359304 | tf_op jit(solution)/shard_map/ppermute | solution.py:105
  101.4 29.8 %collective-permute-start.18 = (bf16[256,2048]{1,0:T(8,128)(2,1)S(1)}, bf16[256,2048]{1,0:T(8,128)(2,1)S(1)}, u32[]{:S(2)}, u32[]{:S(2)}) collective-permute-start(bf16[256,2048]{1,0:T(8,128)(2,1)S(1)} %constant_dynamic-update-slice_fusion.near), channel_id=1, source_target_pairs={{3,4},{4,3},{11,12},{12,11},{19,20},{20,19},{27,28},{28,27},{35,36... | collective-permute-start | bytes 3145736 | tf_op jit(solution)/shard_map/ppermute | solution.py:144
  103.1 28.9 %collective-permute-start.17 = (bf16[4096,128]{1,0:T(8,128)(2,1)}, bf16[4096,128]{1,0:T(8,128)(2,1)}, u32[]{:S(2)}, u32[]{:S(2)}) collective-permute-start(bf16[4096,128]{1,0:T(8,128)(2,1)} %pad_maximum_fusion), channel_id=1, source_target_pairs={{2,3},{5,4},{10,11},{13,12},{18,19},{21,20},{26,27},{29,28},{34,35... | collective-permute-start | bytes 3145736 | tf_op jit(solution)/shard_map/ppermute | solution.py:108
  118.5 18.8 %collective-permute-start.19 = (bf16[64,6144]{1,0:T(8,128)(2,1)}, bf16[64,6144]{1,0:T(8,128)(2,1)}, u32[]{:S(2)}, u32[]{:S(2)}) collective-permute-start(bf16[64,6144]{1,0:T(8,128)(2,1)} %collective-permute-done.15), channel_id=1, source_target_pairs={{5,6},{6,7},{1,0},{2,1},{13,14},{14,15},{9,8},{10,9},{21,22},{22,2... | collective-permute-start | bytes 2359304 | tf_op jit(solution)/shard_map/ppermute | solution.py:105
  119.8 11.4 %collective-permute-start.16 = (bf16[2048,128]{1,0:T(8,128)(2,1)S(1)}, bf16[2048,128]{1,0:T(8,128)(2,1)}, u32[]{:S(2)}, u32[]{:S(2)}) collective-permute-start(bf16[2048,128]{1,0:T(8,128)(2,1)S(1)} %slice_bitcast_fusion.w0), channel_id=1, source_target_pairs={{1,2},{6,5},{9,10},{14,13},{17,18},{22,21},{25,26},{30,29},{33,34}... | collective-permute-start | bytes 1572872 | tf_op jit(solution)/shard_map/ppermute | solution.py:108
  122.4 21.5 %all-to-all-start.1 = ((bf16[32,2,16,512]{3,2,1,0:T(8,128)(2,1)}), bf16[32,2,16,512]{3,2,1,0:T(8,128)(2,1)}, u32[]{:S(2)}, u32[]{:S(2)}) async-start(bf16[32,2,16,512]{3,2,1,0:T(8,128)(2,1)} %broadcast_in_dim.67), calls=%async_computation.1 | async-start | bytes 2097152 | tf_op jit(solution)/shard_map/all_to_all | solution.py:152
  131.2 0.9 copy-start
  132.1 14.1 %collective-permute-start.21 = (bf16[2048,128]{1,0:T(8,128)(2,1)}, bf16[2048,128]{1,0:T(8,128)(2,1)S(1)}, u32[]{:S(2)}, u32[]{:S(2)}) collective-permute-start(bf16[2048,128]{1,0:T(8,128)(2,1)} %collective-permute-done.16), channel_id=1, source_target_pairs={{2,3},{5,4},{10,11},{13,12},{18,19},{21,20},{26,27},{29,28},{34,35... | collective-permute-start | bytes 1572872 | tf_op jit(solution)/shard_map/ppermute | solution.py:108
  137.3 24.6 %collective-permute-start.20 = (bf16[64,6144]{1,0:T(8,128)(2,1)}, bf16[64,6144]{1,0:T(8,128)(2,1)}, u32[]{:S(2)}, u32[]{:S(2)}) collective-permute-start(bf16[64,6144]{1,0:T(8,128)(2,1)} %collective-permute-done.19), channel_id=1, source_target_pairs={{6,7},{1,0},{14,15},{9,8},{22,23},{17,16},{30,31},{25,24},{38,39},... | collective-permute-start | bytes 2359304 | tf_op jit(solution)/shard_map/ppermute | solution.py:105
  146.1 5.3 %copy-start.4 = (bf16[1,8192,128]{2,1,0:T(8,128)(2,1)S(1)}, bf16[1,8192,128]{2,1,0:T(8,128)(2,1)}, u32[]{:S(2)}) copy-start(bf16[1,8192,128]{2,1,0:T(8,128)(2,1)} %param.8) | copy-start | bytes 6291460
  148.8 16.3 %collective-permute-start.22 = (bf16[512,128]{1,0:T(8,128)(2,1)S(1)}, bf16[512,128]{1,0:T(8,128)(2,1)S(1)}, u32[]{:S(2)}, u32[]{:S(2)}) collective-permute-start(bf16[512,128]{1,0:T(8,128)(2,1)S(1)} %get-tuple-element.60), channel_id=1, source_target_pairs={{3,0},{4,7},{11,8},{12,15},{19,16},{20,23},{27,24},{28,31},{35,32}... | collective-permute-start | bytes 393224 | tf_op jit(solution)/shard_map/ppermute | solution.py:160
  150.1 15.0 %collective-permute-start.23 = (bf16[512,128]{1,0:T(8,128)(2,1)S(1)}, bf16[512,128]{1,0:T(8,128)(2,1)S(1)}, u32[]{:S(2)}, u32[]{:S(2)}) collective-permute-start(bf16[512,128]{1,0:T(8,128)(2,1)S(1)} %get-tuple-element.61), channel_id=1, source_target_pairs={{3,1},{4,6},{11,9},{12,14},{19,17},{20,22},{27,25},{28,30},{35,33}... | collective-permute-start | bytes 393224 | tf_op jit(solution)/shard_map/ppermute | solution.py:160
  150.7 14.3 %collective-permute-start.24 = (bf16[512,128]{1,0:T(8,128)(2,1)S(1)}, bf16[512,128]{1,0:T(8,128)(2,1)S(1)}, u32[]{:S(2)}, u32[]{:S(2)}) collective-permute-start(bf16[512,128]{1,0:T(8,128)(2,1)S(1)} %get-tuple-element.62), channel_id=1, source_target_pairs={{3,2},{4,5},{11,10},{12,13},{19,18},{20,21},{27,26},{28,29},{35,34... | collective-permute-start | bytes 393224 | tf_op jit(solution)/shard_map/ppermute | solution.py:160

commit v10 on v6

--- a/solution.py
+++ b/solution.py
@@ -44,28 +44,29 @@
 hold = lax.optimization_barrier
 
 
-def middle_kernel(low, near, far, w0, w13, w2, *outs):
+def middle_kernel(low, near, far, *refs):
     is_low = low[0] == 1
-    size = w0.shape[0]
-    w1, w3 = w13.at[:size], w13.at[size:]
-    for pair, out in (((w0, w1), outs[:2]), ((w2, w3), outs[2:])):
-        w = jnp.concatenate([pair[0][...], pair[1][...]], axis=1)
-        p, q = dot(near[...], w), dot(far[...], w)
-        first, last = jnp.where(is_low, p, q), jnp.where(is_low, q, p)
-        for i, ref in enumerate(out):
-            cols = slice(HD * i, HD * i + HD)
-            ref[:256] = first[:, cols].astype(ref.dtype)
-            for k in range(4):
-                ref[256 + 64 * k : 320 + 64 * k] = last[192 - 64 * k : 256 - 64 * k, cols].astype(ref.dtype)
+    n = len(refs) // 2
+    size = near.shape[1]
+    columns = [ref[i : i + size] for ref in refs[:n] for i in range(0, ref.shape[0], size)]
+    outs = refs[n:] if n == 1 else refs[2:]
+    w = jnp.concatenate(columns, axis=1)
+    p, q = dot(near[...], w), dot(far[...], w)
+    first, last = jnp.where(is_low, p, q), jnp.where(is_low, q, p)
+    for i, ref in enumerate(outs):
+        cols = slice(HD * i, HD * i + HD)
+        ref[:256] = first[:, cols].astype(ref.dtype)
+        for k in range(4):
+            ref[256 + 64 * k : 320 + 64 * k] = last[192 - 64 * k : 256 - 64 * k, cols].astype(ref.dtype)
 
 
 def middle_products(low, near, far, *weights):
-    types = (jnp.float32, jnp.bfloat16, jnp.bfloat16, jnp.bfloat16)
+    types = (jnp.bfloat16,) if len(weights) == 1 else (jnp.float32, jnp.bfloat16, jnp.bfloat16)
     return pl.pallas_call(
         middle_kernel,
         out_shape=[jax.ShapeDtypeStruct((512, HD), t) for t in types],
-        in_specs=[pl.BlockSpec(memory_space=pltpu.SMEM)] + [pl.BlockSpec(memory_space=pltpu.VMEM)] * 5,
-        out_specs=[pl.BlockSpec(memory_space=pltpu.VMEM)] * 4,
+        in_specs=[pl.BlockSpec(memory_space=pltpu.SMEM)] + [pl.BlockSpec(memory_space=pltpu.VMEM)] * (2 + len(weights)),
+        out_specs=[pl.BlockSpec(memory_space=pltpu.VMEM)] * len(types),
         cost_estimate=pl.CostEstimate(flops=0, bytes_accessed=0, transcendentals=0),
         compiler_params=pltpu.CompilerParams(vmem_limit_bytes=24 << 20),
     )(low.astype(jnp.int32).reshape(1), near, far, *weights)
@@ -153,12 +154,12 @@
 
     y = hop_out(x, 6)
     rows, w2, synced = hold((rows, w2, synced))
-    rows5 = put(rows, x, jnp.where(low, me + 6, me - 6))
-    rows, w2 = hold((rows5, w2))
-    blocks = middle_products(low, near, far, w_rest, w13, w2)
-    middle = jnp.where((me == 3) | (me == 4), blocks[0], 0.0)
-    for d in (3, 2, 1):
-        back = lax.ppermute(blocks[d], "tensor", [(3, 3 - d), (4, 4 + d)])
+    rows = put(rows, x, jnp.where(low, me + 6, me - 6))
+    mine3, back1, back3 = middle_products(low, near, far, w_rest, w13)
+    (back2,) = middle_products(low, near, far, w2)
+    middle = jnp.where((me == 3) | (me == 4), mine3, 0.0)
+    for d, block in ((3, back3), (1, back1), (2, back2)):
+        back = lax.ppermute(block, "tensor", [(3, 3 - d), (4, 4 + d)])
         middle += back.astype(jnp.float32)
 
     rows = put(rows, y, jnp.where(low, me + 7, me - 7))

time: 169 us -> 165 us (0.976)
  the two profiles are of different devices: /device:TPU:64 before, /device:TPU:6 now
where the time goes in v10:
time: 165 us; the launch traced here: 164 us
  starting transfers between devices  62.3 us (38%)
  waiting for transfers between devices  57.6 us (35%)
  matrix products  21.5 us (13%)
  local copies, waits for them, and re-layouts  9.86 us (6%)
  other arithmetic  7.12 us (4%)
  Pallas kernels  4.11 us (2%)
    ppermute x3, waiting for transfers between devices, hop_out(): return lax.ppermute(x, 'tensor', pairs)  26.1 us
    dot_general x11, matrix products, dot(): return jnp.dot(a, b, preferred_element_type=jnp.float32)  21.5 us
    ppermute x1, starting transfers between devices, body(): came = lax.ppermute(other, 'zh', [(0, 1), (1, 0)])  14.8 us
    ppermute x1, waiting for transfers between devices, body(): came = lax.ppermute(other, 'zh', [(0, 1), (1, 0)])  11.7 us
    ppermute x8, starting transfers between devices, inward(): return lax.ppermute(x, 'tensor', [(3 - d, 4 - d), (4 + d, 3 + d)])  11.2 us
    ppermute x4, waiting for transfers between devices, hop(): b = lax.ppermute(b, 'tensor', [(j + 1, j) for j in range(7 - s)])  9.61 us
    ppermute x1, waiting for transfers between devices, body(): theirs = lax.ppermute(mine, 'zh', [(0, 1), (1, 0)])  8.42 us
    all_to_all x1, starting transfers between devices, body(): pieces = lax.all_to_all(params, PLANE, 0, 0, tiled=True)  7.57 us
  transfers between devices with their start and end apart: 27, of which 9 were waited for; matrix products, arithmetic and copies ran while one was open for 19% of the time, Pallas kernels for 3%

profile of v10, /device:TPU:6, one launch (start us, length us, event | category | flops | bytes accessed | tf_op | source)
XLA Modules:
  0.0 163.6 jit_solution(17985497164834211924)
XLA Ops:
  0.7 1.7 %multiply_reduce_fusion = f32[64]{0:T(128)S(1)} fusion(bf16[64,8192]{1,0:T(8,128)(2,1)} %param.6), kind=kLoop, calls=%fused_computation.1 | loop fusion | flops 1572800 | bytes 1048832 | tf_op jit(solution)/shard_map/reduce_sum | solution.py:85
  3.1 1.1 multiply_convert_fusion
  4.2 4.7 %collective-permute-start = (bf16[64,5888]{1,0:T(8,128)(2,1)}, bf16[64,5888]{1,0:T(8,128)(2,1)}, u32[]{:S(2)}, u32[]{:S(2)}) collective-permute-start(bf16[64,5888]{1,0:T(8,128)(2,1)} %multiply_convert_fusion), channel_id=1, source_target_pairs={{0,1},{1,2},{2,3},{3,4},{4,5},{5,6},{6,7},{8,9},{9,10},{10,11},{11... | collective-permute-start | bytes 2261000 | tf_op jit(solution)/shard_map/ppermute | solution.py:100
  8.9 1.3 collective-permute-start.1
  10.2 1.1 copy.12
  11.2 7.6 %all-to-all-start = ((bf16[32,2,16,512]{3,2,1,0:T(8,128)(2,1)}), bf16[32,2,16,512]{3,2,1,0:T(8,128)(2,1)S(1)}, u32[]{:S(2)}, u32[]{:S(2)}) async-start(bf16[32,2,16,512]{3,2,1,0:T(8,128)(2,1)} %copy.12), calls=%async_computation | async-start | bytes 2097152 | tf_op jit(solution)/shard_map/all_to_all | solution.py:81
  18.8 1.1 slice_bitcast_fusion.refs_0_
  20.0 2.1 %fusion.25 = f32[22,64,128]{2,1,0:T(8,128)S(1)} fusion(f32[22,64,128]{2,1,0:T(8,128)S(1)} %broadcast_in_dim.57, s32[]{:T(128)S(6)} %select_n.77, bf16[64,5888]{1,0:T(8,128)(2,1)} %multiply_convert_fusion, bf16[1,8192,128]{2,1,0:T(8,128)(2,1)} %param.8), kind=kOutput, calls=%fused_computation.27 | convolution fusion | flops 96468992 | bytes 2293764 | tf_op jit(solution)/shard_map/dot_general | solution.py:34
  22.1 0.9 copy-done.3
  23.2 1.2 collective-permute-done
  25.1 4.3 %collective-permute-done.1 = bf16[64,5888]{1,0:T(8,128)(2,1)} collective-permute-done((bf16[64,5888]{1,0:T(8,128)(2,1)}, bf16[64,5888]{1,0:T(8,128)(2,1)}, u32[]{:S(2)}, u32[]{:S(2)}) %collective-permute-start.1) | collective-permute-done | bytes 753696 | tf_op jit(solution)/shard_map/ppermute | solution.py:101
  29.4 1.3 collective-permute-start.3
  30.7 2.6 %fusion.31 = f32[22,64,128]{2,1,0:T(8,128)} fusion(f32[22,64,128]{2,1,0:T(8,128)} %copy-done.3, s32[]{:T(128)S(6)} %select_n.78, bf16[64,5888]{1,0:T(8,128)(2,1)} %collective-permute-done, bf16[1,8192,128]{2,1,0:T(8,128)(2,1)} %param.8), kind=kOutput, calls=%fused_computation.29 | convolution fusion | flops 96468992 | bytes 2293764 | tf_op jit(solution)/shard_map/dot_general | solution.py:34
  33.3 2.1 %fusion.37 = f32[22,64,128]{2,1,0:T(8,128)} fusion(f32[22,64,128]{2,1,0:T(8,128)} %fusion.31, s32[]{:T(128)S(6)} %select_n.79, bf16[64,5888]{1,0:T(8,128)(2,1)} %collective-permute-done.1, bf16[1,8192,128]{2,1,0:T(8,128)(2,1)S(1)} %copy-done.5), kind=kOutput, calls=%fused_computation.31 | convolution fusion | flops 96468992 | bytes 2293764 | tf_op jit(solution)/shard_map/dot_general | solution.py:34
  35.5 4.7 %collective-permute-start.6 = (bf16[2304,128]{1,0:T(8,128)(2,1)S(1)}, bf16[2304,128]{1,0:T(8,128)(2,1)S(1)}, u32[]{:S(2)}, u32[]{:S(2)}) collective-permute-start(bf16[2304,128]{1,0:T(8,128)(2,1)S(1)} %slice_bitcast_fusion.refs_0_), channel_id=1, source_target_pairs={{0,1},{7,6},{8,9},{15,14},{16,17},{23,22},{24,25},{31,30},{32,33},... | collective-permute-start | bytes 1769480 | tf_op jit(solution)/shard_map/ppermute | solution.py:109
  40.2 1.3 collective-permute-start.5
  41.7 14.8 %collective-permute-start.4 = (f32[16,512]{1,0:T(8,128)S(1)}, f32[16,512]{1,0:T(8,128)S(1)}, u32[]{:S(2)}, u32[]{:S(2)}) collective-permute-start(f32[16,512]{1,0:T(8,128)S(1)} %dynamic-slice_bitcast_fusion), channel_id=1, source_target_pairs={{0,256},{256,0},{1,257},{257,1},{2,258},{258,2},{3,259},{259,3},{4... | collective-permute-start | bytes 98312 | tf_op jit(solution)/shard_map/ppermute | solution.py:123
  57.3 1.3 collective-permute-start.8
  58.6 2.4 %fusion.43 = f32[22,64,128]{2,1,0:T(8,128)} fusion(f32[22,64,128]{2,1,0:T(8,128)} %fusion.37, s32[]{:T(128)S(6)} %select_n.80, bf16[64,5888]{1,0:T(8,128)(2,1)S(1)} %collective-permute-done.2, bf16[1,8192,128]{2,1,0:T(8,128)(2,1)} %param.8), kind=kOutput, calls=%fused_computation.33 | convolution fusion | flops 96468992 | bytes 2293764 | tf_op jit(solution)/shard_map/dot_general | solution.py:34
  61.0 2.2 %fusion.49 = f32[22,64,128]{2,1,0:T(8,128)} fusion(f32[22,64,128]{2,1,0:T(8,128)} %fusion.43, s32[]{:T(128)S(6)} %select_n.81, bf16[64,5888]{1,0:T(8,128)(2,1)} %collective-permute-done.3, bf16[1,8192,128]{2,1,0:T(8,128)(2,1)S(1)} %copy-done.6), kind=kOutput, calls=%fused_computation.35 | convolution fusion | flops 96468992 | bytes 2293764 | tf_op jit(solution)/shard_map/dot_general | solution.py:34
  63.1 11.7 %collective-permute-done.4 = f32[16,512]{1,0:T(8,128)S(1)} collective-permute-done((f32[16,512]{1,0:T(8,128)S(1)}, f32[16,512]{1,0:T(8,128)S(1)}, u32[]{:S(2)}, u32[]{:S(2)}) %collective-permute-start.4) | collective-permute-done | bytes 32800 | tf_op jit(solution)/shard_map/ppermute | solution.py:123
  76.3 1.9 %collective-permute-start.10 = (bf16[16,512]{1,0:T(8,128)(2,1)S(1)}, bf16[16,512]{1,0:T(8,128)(2,1)S(1)}, u32[]{:S(2)}, u32[]{:S(2)}) collective-permute-start(bf16[16,512]{1,0:T(8,128)(2,1)S(1)} %get-tuple-element.64), channel_id=1, source_target_pairs={{0,256},{256,0},{1,257},{257,1},{2,258},{258,2},{3,259},{259,3},{4... | collective-permute-start | bytes 49160 | tf_op jit(solution)/shard_map/ppermute | solution.py:131
  78.2 1.3 collective-permute-start.11
  80.3 1.0 fusion.55
  81.3 1.0 fusion.61
  82.4 8.4 %collective-permute-done.10 = bf16[16,512]{1,0:T(8,128)(2,1)S(1)} collective-permute-done((bf16[16,512]{1,0:T(8,128)(2,1)S(1)}, bf16[16,512]{1,0:T(8,128)(2,1)S(1)}, u32[]{:S(2)}, u32[]{:S(2)}) %collective-permute-start.10) | collective-permute-done | bytes 16416 | tf_op jit(solution)/shard_map/ppermute | solution.py:131
  92.3 5.3 %collective-permute-done.11 = bf16[64,5888]{1,0:T(8,128)(2,1)S(1)} collective-permute-done((bf16[64,5888]{1,0:T(8,128)(2,1)S(1)}, bf16[64,5888]{1,0:T(8,128)(2,1)S(1)}, u32[]{:S(2)}, u32[]{:S(2)}) %collective-permute-start.11) | collective-permute-done | bytes 753696 | tf_op jit(solution)/shard_map/ppermute | solution.py:101
  97.7 1.3 collective-permute-start.15
  99.0 1.0 fusion.67
  100.9 1.1 pad_maximum_fusion
  102.0 1.7 %collective-permute-start.17 = (bf16[4608,128]{1,0:T(8,128)(2,1)}, bf16[4608,128]{1,0:T(8,128)(2,1)}, u32[]{:S(2)}, u32[]{:S(2)}) collective-permute-start(bf16[4608,128]{1,0:T(8,128)(2,1)} %pad_maximum_fusion), channel_id=1, source_target_pairs={{2,3},{5,4},{10,11},{13,12},{18,19},{21,20},{26,27},{29,28},{34,35... | collective-permute-start | bytes 3538952 | tf_op jit(solution)/shard_map/ppermute | solution.py:109
  103.7 12.3 %collective-permute-done.15 = bf16[64,5888]{1,0:T(8,128)(2,1)} collective-permute-done((bf16[64,5888]{1,0:T(8,128)(2,1)S(1)}, bf16[64,5888]{1,0:T(8,128)(2,1)}, u32[]{:S(2)}, u32[]{:S(2)}) %collective-permute-start.15) | collective-permute-done | bytes 753696 | tf_op jit(solution)/shard_map/ppermute | solution.py:106
  116.0 1.3 collective-permute-start.20
  118.0 1.1 broadcast_in_dim.67
  119.1 7.5 %all-to-all-start.1 = ((bf16[32,2,16,512]{3,2,1,0:T(8,128)(2,1)}), bf16[32,2,16,512]{3,2,1,0:T(8,128)(2,1)}, u32[]{:S(2)}, u32[]{:S(2)}) async-start(bf16[32,2,16,512]{3,2,1,0:T(8,128)(2,1)} %broadcast_in_dim.67), calls=%async_computation.1 | async-start | bytes 2097152 | tf_op jit(solution)/shard_map/all_to_all | solution.py:153
  126.5 2.6 %fusion.73 = f32[22,64,128]{2,1,0:T(8,128)} fusion(f32[22,64,128]{2,1,0:T(8,128)} %fusion.67, s32[]{:T(128)S(6)} %select_n.93, bf16[64,5888]{1,0:T(8,128)(2,1)} %collective-permute-done.15, bf16[1,8192,128]{2,1,0:T(8,128)(2,1)} %param.8), kind=kOutput, calls=%fused_computation.43 | convolution fusion | flops 96468992 | bytes 2293764 | tf_op jit(solution)/shard_map/dot_general | solution.py:34
  129.2 0.8 copy-done.11
  130.7 2.8 %collective-permute-done.20 = bf16[64,5888]{1,0:T(8,128)(2,1)} collective-permute-done((bf16[64,5888]{1,0:T(8,128)(2,1)}, bf16[64,5888]{1,0:T(8,128)(2,1)}, u32[]{:S(2)}, u32[]{:S(2)}) %collective-permute-start.20) | collective-permute-done | bytes 753696 | tf_op jit(solution)/shard_map/ppermute | solution.py:106
  133.5 1.3 collective-permute-start.21
  134.8 3.3 %shard_map.93 = (f32[512,128]{1,0:T(8,128)S(1)}, bf16[512,128]{1,0:T(8,128)(2,1)}, bf16[512,128]{1,0:T(8,128)(2,1)}) custom-call(s32[1]{0:T(128)} %bitcast.22.low, bf16[256,2304]{1,0:T(8,128)(2,1)S(1)} %constant_dynamic-update-slice_fusion.near, bf16[256,2304]{1,0:T(8,128)(2,1)S(1)} %collective-permute-done.18.far, ...), custom_call_target="tpu_custom_call" | custom-call | tf_op jit(solution)/shard_map/pallas_call | solution.py:65
  138.9 1.3 collective-permute-start.22
  142.1 0.8 collective-permute-start.24
  142.9 2.3 %copy.14 = bf16[32,2,16,512]{3,2,0,1:T(8,128)(2,1)} copy(bf16[32,2,16,512]{3,2,1,0:T(8,128)(2,1)} %all-to-all-done.1) | data formatting | bytes 2097152 | tf_op jit(solution)/shard_map/optimization_barrier | solution.py:156
  145.2 2.1 %fusion.79 = f32[22,64,128]{2,1,0:T(8,128)} fusion(f32[22,64,128]{2,1,0:T(8,128)} %fusion.73, s32[]{:T(128)S(6)} %select_n.95, bf16[64,5888]{1,0:T(8,128)(2,1)} %collective-permute-done.20, bf16[1,8192,128]{2,1,0:T(8,128)(2,1)S(1)} %copy-done.7), kind=kOutput, calls=%fused_computation.45 | convolution fusion | flops 96468992 | bytes 2293764 | tf_op jit(solution)/shard_map/dot_general | solution.py:34
  147.3 11.0 %collective-permute-done.21 = bf16[64,5888]{1,0:T(8,128)(2,1)} collective-permute-done((bf16[64,5888]{1,0:T(8,128)(2,1)}, bf16[64,5888]{1,0:T(8,128)(2,1)}, u32[]{:S(2)}, u32[]{:S(2)}) %collective-permute-start.21) | collective-permute-done | bytes 753696 | tf_op jit(solution)/shard_map/ppermute | solution.py:106
  158.3 2.1 %fusion.85 = f32[22,64,128]{2,1,0:T(8,128)} fusion(f32[22,64,128]{2,1,0:T(8,128)} %fusion.79, s32[]{:T(128)S(6)} %select_n.97, bf16[64,5888]{1,0:T(8,128)(2,1)} %collective-permute-done.21, bf16[1,8192,128]{2,1,0:T(8,128)(2,1)S(1)} %copy-done.7), kind=kOutput, calls=%fused_computation.47 | convolution fusion | flops 96468992 | bytes 2293764 | tf_op jit(solution)/shard_map/dot_general | solution.py:34
  160.5 1.0 slice.46
  161.6 1.2 fusion.93
  (72 shorter events, 11.9 us)
Async XLA Ops:
  0.6 2.4 %copy-start.2 = (bf16[64,8192]{1,0:T(8,128)(2,1)S(1)}, bf16[64,8192]{1,0:T(8,128)(2,1)}, u32[]{:S(2)}) copy-start(bf16[64,8192]{1,0:T(8,128)(2,1)} %param.6) | copy-start | bytes 3145732
  0.6 9.5 %copy-start.4 = (bf16[1,1,1024,512]{3,2,1,0:T(8,128)(2,1)S(1)}, bf16[1,1,1024,512]{3,2,1,0:T(8,128)(2,1)}, u32[]{:S(2)}) copy-start(bf16[1,1,1024,512]{3,2,1,0:T(8,128)(2,1)} %param.9) | copy-start | bytes 3145732
  4.2 20.2 %collective-permute-start = (bf16[64,5888]{1,0:T(8,128)(2,1)}, bf16[64,5888]{1,0:T(8,128)(2,1)}, u32[]{:S(2)}, u32[]{:S(2)}) collective-permute-start(bf16[64,5888]{1,0:T(8,128)(2,1)} %multiply_convert_fusion), channel_id=1, source_target_pairs={{0,1},{1,2},{2,3},{3,4},{4,5},{5,6},{6,7},{8,9},{9,10},{10,11},{11... | collective-permute-start | bytes 2261000 | tf_op jit(solution)/shard_map/ppermute | solution.py:100
  8.9 20.5 %collective-permute-start.1 = (bf16[64,5888]{1,0:T(8,128)(2,1)}, bf16[64,5888]{1,0:T(8,128)(2,1)}, u32[]{:S(2)}, u32[]{:S(2)}) collective-permute-start(bf16[64,5888]{1,0:T(8,128)(2,1)} %multiply_convert_fusion), channel_id=1, source_target_pairs={{1,0},{2,1},{3,2},{4,3},{5,4},{6,5},{7,6},{9,8},{10,9},{11,10},{12... | collective-permute-start | bytes 2261000 | tf_op jit(solution)/shard_map/ppermute | solution.py:101
  11.2 24.2 %all-to-all-start = ((bf16[32,2,16,512]{3,2,1,0:T(8,128)(2,1)}), bf16[32,2,16,512]{3,2,1,0:T(8,128)(2,1)S(1)}, u32[]{:S(2)}, u32[]{:S(2)}) async-start(bf16[32,2,16,512]{3,2,1,0:T(8,128)(2,1)} %copy.12), calls=%async_computation | async-start | bytes 2097152 | tf_op jit(solution)/shard_map/all_to_all | solution.py:81
  20.0 3.0 %copy-start.8 = (bf16[8192]{0:T(1024)(128)(2,1)S(1)}, bf16[8192]{0:T(1024)(128)(2,1)}, u32[]{:S(2)}) copy-start(bf16[8192]{0:T(1024)(128)(2,1)} %param.7) | copy-start | bytes 49156
  20.0 3.0 %slice-start = ((bf16[64,8192]{1,0:T(8,128)(2,1)}), bf16[64,2304]{1,0:T(8,128)(2,1)S(1)}, s32[]{:S(2)}) async-start(bf16[64,8192]{1,0:T(8,128)(2,1)} %param.6), calls=%async_computation.2 | async-start | bytes 589824 | tf_op jit(solution)/shard_map/slice | solution.py:113
  22.1 0.9 copy-start.3
  23.0 10.3 %copy-start.5 = (bf16[1,8192,128]{2,1,0:T(8,128)(2,1)S(1)}, bf16[1,8192,128]{2,1,0:T(8,128)(2,1)}, u32[]{:S(2)}) copy-start(bf16[1,8192,128]{2,1,0:T(8,128)(2,1)} %param.8) | copy-start | bytes 6291460
  24.4 32.1 %collective-permute-start.2 = (bf16[64,5888]{1,0:T(8,128)(2,1)}, bf16[64,5888]{1,0:T(8,128)(2,1)S(1)}, u32[]{:S(2)}, u32[]{:S(2)}) collective-permute-start(bf16[64,5888]{1,0:T(8,128)(2,1)} %collective-permute-done), channel_id=1, source_target_pairs={{1,2},{2,3},{3,4},{4,5},{5,6},{6,7},{9,10},{10,11},{11,12},{12,13}... | collective-permute-start | bytes 2261000 | tf_op jit(solution)/shard_map/ppermute | solution.py:100
  29.4 27.9 %collective-permute-start.3 = (bf16[64,5888]{1,0:T(8,128)(2,1)}, bf16[64,5888]{1,0:T(8,128)(2,1)}, u32[]{:S(2)}, u32[]{:S(2)}) collective-permute-start(bf16[64,5888]{1,0:T(8,128)(2,1)} %collective-permute-done.1), channel_id=1, source_target_pairs={{1,0},{2,1},{3,2},{4,3},{5,4},{6,5},{9,8},{10,9},{11,10},{12,11},{... | collective-permute-start | bytes 2261000 | tf_op jit(solution)/shard_map/ppermute | solution.py:101
  35.5 25.5 %copy-start.6 = (bf16[1,8192,128]{2,1,0:T(8,128)(2,1)S(1)}, bf16[1,8192,128]{2,1,0:T(8,128)(2,1)}, u32[]{:S(2)}) copy-start(bf16[1,8192,128]{2,1,0:T(8,128)(2,1)} %param.8) | copy-start | bytes 6291460
  35.5 39.4 %collective-permute-start.6 = (bf16[2304,128]{1,0:T(8,128)(2,1)S(1)}, bf16[2304,128]{1,0:T(8,128)(2,1)S(1)}, u32[]{:S(2)}, u32[]{:S(2)}) collective-permute-start(bf16[2304,128]{1,0:T(8,128)(2,1)S(1)} %slice_bitcast_fusion.refs_0_), channel_id=1, source_target_pairs={{0,1},{7,6},{8,9},{15,14},{16,17},{23,22},{24,25},{31,30},{32,33},... | collective-permute-start | bytes 1769480 | tf_op jit(solution)/shard_map/ppermute | solution.py:109
  40.2 34.7 %collective-permute-start.5 = (bf16[64,2304]{1,0:T(8,128)(2,1)S(1)}, bf16[64,2304]{1,0:T(8,128)(2,1)S(1)}, u32[]{:S(2)}, u32[]{:S(2)}) collective-permute-start(bf16[64,2304]{1,0:T(8,128)(2,1)S(1)} %multiply_convert_fusion.1), channel_id=1, source_target_pairs={{0,1},{7,6},{8,9},{15,14},{16,17},{23,22},{24,25},{31,30},{32,33},... | collective-permute-start | bytes 884744 | tf_op jit(solution)/shard_map/ppermute | solution.py:109
  41.7 33.2 %collective-permute-start.4 = (f32[16,512]{1,0:T(8,128)S(1)}, f32[16,512]{1,0:T(8,128)S(1)}, u32[]{:S(2)}, u32[]{:S(2)}) collective-permute-start(f32[16,512]{1,0:T(8,128)S(1)} %dynamic-slice_bitcast_fusion), channel_id=1, source_target_pairs={{0,256},{256,0},{1,257},{257,1},{2,258},{258,2},{3,259},{259,3},{4... | collective-permute-start | bytes 98312 | tf_op jit(solution)/shard_map/ppermute | solution.py:123
  56.5 23.0 %collective-permute-start.7 = (bf16[64,5888]{1,0:T(8,128)(2,1)S(1)}, bf16[64,5888]{1,0:T(8,128)(2,1)S(1)}, u32[]{:S(2)}, u32[]{:S(2)}) collective-permute-start(bf16[64,5888]{1,0:T(8,128)(2,1)S(1)} %collective-permute-done.2), channel_id=1, source_target_pairs={{2,3},{3,4},{4,5},{5,6},{6,7},{10,11},{11,12},{12,13},{13,14},{14,... | collective-permute-start | bytes 2261000 | tf_op jit(solution)/shard_map/ppermute | solution.py:100
  57.3 21.0 %collective-permute-start.8 = (bf16[64,5888]{1,0:T(8,128)(2,1)}, bf16[64,5888]{1,0:T(8,128)(2,1)S(1)}, u32[]{:S(2)}, u32[]{:S(2)}) collective-permute-start(bf16[64,5888]{1,0:T(8,128)(2,1)} %collective-permute-done.3), channel_id=1, source_target_pairs={{1,0},{2,1},{3,2},{4,3},{5,4},{9,8},{10,9},{11,10},{12,11},{13,12}... | collective-permute-start | bytes 2261000 | tf_op jit(solution)/shard_map/ppermute | solution.py:101
  61.0 14.7 %copy-start.9 = (f32[1,16,512]{2,1,0:T(8,128)S(1)}, f32[1,16,512]{2,1,0:T(8,128)}, u32[]{:S(2)}) copy-start(f32[1,16,512]{2,1,0:T(8,128)} %param.11) | copy-start | bytes 98308
  61.0 14.7 %copy-start.10 = (f32[1,16,512]{2,1,0:T(8,128)S(1)}, f32[1,16,512]{2,1,0:T(8,128)}, u32[]{:S(2)}) copy-start(f32[1,16,512]{2,1,0:T(8,128)} %param.10) | copy-start | bytes 98308
  74.9 15.8 %collective-permute-start.9 = (bf16[128,2304]{1,0:T(8,128)(2,1)S(1)}, bf16[128,2304]{1,0:T(8,128)(2,1)S(1)}, u32[]{:S(2)}, u32[]{:S(2)}) collective-permute-start(bf16[128,2304]{1,0:T(8,128)(2,1)S(1)} %pad_maximum_fusion.2), channel_id=1, source_target_pairs={{1,2},{6,5},{9,10},{14,13},{17,18},{22,21},{25,26},{30,29},{33,34}... | collective-permute-start | bytes 1769480 | tf_op jit(solution)/shard_map/ppermute | solution.py:109
  76.3 14.5 %collective-permute-start.10 = (bf16[16,512]{1,0:T(8,128)(2,1)S(1)}, bf16[16,512]{1,0:T(8,128)(2,1)S(1)}, u32[]{:S(2)}, u32[]{:S(2)}) collective-permute-start(bf16[16,512]{1,0:T(8,128)(2,1)S(1)} %get-tuple-element.64), channel_id=1, source_target_pairs={{0,256},{256,0},{1,257},{257,1},{2,258},{258,2},{3,259},{259,3},{4... | collective-permute-start | bytes 49160 | tf_op jit(solution)/shard_map/ppermute | solution.py:131
  78.2 19.4 %collective-permute-start.11 = (bf16[64,5888]{1,0:T(8,128)(2,1)S(1)}, bf16[64,5888]{1,0:T(8,128)(2,1)S(1)}, u32[]{:S(2)}, u32[]{:S(2)}) collective-permute-start(bf16[64,5888]{1,0:T(8,128)(2,1)S(1)} %collective-permute-done.8), channel_id=1, source_target_pairs={{1,0},{2,1},{3,2},{4,3},{9,8},{10,9},{11,10},{12,11},{17,16},{18,1... | collective-permute-start | bytes 2261000 | tf_op jit(solution)/shard_map/ppermute | solution.py:101
  79.6 18.1 %collective-permute-start.12 = (bf16[64,5888]{1,0:T(8,128)(2,1)S(1)}, bf16[64,5888]{1,0:T(8,128)(2,1)S(1)}, u32[]{:S(2)}, u32[]{:S(2)}) collective-permute-start(bf16[64,5888]{1,0:T(8,128)(2,1)S(1)} %collective-permute-done.7), channel_id=1, source_target_pairs={{3,4},{4,5},{5,6},{6,7},{11,12},{12,13},{13,14},{14,15},{19,20},{2... | collective-permute-start | bytes 2261000 | tf_op jit(solution)/shard_map/ppermute | solution.py:100
  90.8 9.2 %collective-permute-start.13 = (bf16[192,2304]{1,0:T(8,128)(2,1)S(1)}, bf16[192,2304]{1,0:T(8,128)(2,1)S(1)}, u32[]{:S(2)}, u32[]{:S(2)}) collective-permute-start(bf16[192,2304]{1,0:T(8,128)(2,1)S(1)} %pad_maximum_fusion.1), channel_id=1, source_target_pairs={{2,3},{5,4},{10,11},{13,12},{18,19},{21,20},{26,27},{29,28},{34,35... | collective-permute-start | bytes 2654216 | tf_op jit(solution)/shard_map/ppermute | solution.py:109
  91.6 8.5 %collective-permute-start.14 = (bf16[2304,128]{1,0:T(8,128)(2,1)S(1)}, bf16[2304,128]{1,0:T(8,128)(2,1)S(1)}, u32[]{:S(2)}, u32[]{:S(2)}) collective-permute-start(bf16[2304,128]{1,0:T(8,128)(2,1)S(1)} %collective-permute-done.6), channel_id=1, source_target_pairs={{1,2},{6,5},{9,10},{14,13},{17,18},{22,21},{25,26},{30,29},{33,34}... | collective-permute-start | bytes 1769480 | tf_op jit(solution)/shard_map/ppermute | solution.py:109
  97.7 18.3 %collective-permute-start.15 = (bf16[64,5888]{1,0:T(8,128)(2,1)S(1)}, bf16[64,5888]{1,0:T(8,128)(2,1)}, u32[]{:S(2)}, u32[]{:S(2)}) collective-permute-start(bf16[64,5888]{1,0:T(8,128)(2,1)S(1)} %broadcast_select_fusion), channel_id=1, source_target_pairs={{4,5},{5,6},{6,7},{1,0},{2,1},{3,2},{12,13},{13,14},{14,15},{9,8},... | collective-permute-start | bytes 2261000 | tf_op jit(solution)/shard_map/ppermute | solution.py:106
  100.1 29.1 %collective-permute-start.18 = (bf16[256,2304]{1,0:T(8,128)(2,1)S(1)}, bf16[256,2304]{1,0:T(8,128)(2,1)S(1)}, u32[]{:S(2)}, u32[]{:S(2)}) collective-permute-start(bf16[256,2304]{1,0:T(8,128)(2,1)S(1)} %constant_dynamic-update-slice_fusion.near), channel_id=1, source_target_pairs={{3,4},{4,3},{11,12},{12,11},{19,20},{20,19},{27,28},{28,27},{35,36... | collective-permute-start | bytes 3538952 | tf_op jit(solution)/shard_map/ppermute | solution.py:145
  102.0 28.0 %collective-permute-start.17 = (bf16[4608,128]{1,0:T(8,128)(2,1)}, bf16[4608,128]{1,0:T(8,128)(2,1)}, u32[]{:S(2)}, u32[]{:S(2)}) collective-permute-start(bf16[4608,128]{1,0:T(8,128)(2,1)} %pad_maximum_fusion), channel_id=1, source_target_pairs={{2,3},{5,4},{10,11},{13,12},{18,19},{21,20},{26,27},{29,28},{34,35... | collective-permute-start | bytes 3538952 | tf_op jit(solution)/shard_map/ppermute | solution.py:109
  116.0 17.5 %collective-permute-start.20 = (bf16[64,5888]{1,0:T(8,128)(2,1)}, bf16[64,5888]{1,0:T(8,128)(2,1)}, u32[]{:S(2)}, u32[]{:S(2)}) collective-permute-start(bf16[64,5888]{1,0:T(8,128)(2,1)} %collective-permute-done.15), channel_id=1, source_target_pairs={{5,6},{6,7},{1,0},{2,1},{13,14},{14,15},{9,8},{10,9},{21,22},{22,2... | collective-permute-start | bytes 2261000 | tf_op jit(solution)/shard_map/ppermute | solution.py:106
  117.3 11.9 %collective-permute-start.16 = (bf16[2304,128]{1,0:T(8,128)(2,1)S(1)}, bf16[2304,128]{1,0:T(8,128)(2,1)S(1)}, u32[]{:S(2)}, u32[]{:S(2)}) collective-permute-start(bf16[2304,128]{1,0:T(8,128)(2,1)S(1)} %slice_bitcast_fusion.refs_0_), channel_id=1, source_target_pairs={{1,2},{6,5},{9,10},{14,13},{17,18},{22,21},{25,26},{30,29},{33,34}... | collective-permute-start | bytes 1769480 | tf_op jit(solution)/shard_map/ppermute | solution.py:109
  119.1 22.2 %all-to-all-start.1 = ((bf16[32,2,16,512]{3,2,1,0:T(8,128)(2,1)}), bf16[32,2,16,512]{3,2,1,0:T(8,128)(2,1)}, u32[]{:S(2)}, u32[]{:S(2)}) async-start(bf16[32,2,16,512]{3,2,1,0:T(8,128)(2,1)} %broadcast_in_dim.67), calls=%async_computation.1 | async-start | bytes 2097152 | tf_op jit(solution)/shard_map/all_to_all | solution.py:153
  129.2 0.8 copy-start.11
  130.0 11.3 %collective-permute-start.19 = (bf16[2304,128]{1,0:T(8,128)(2,1)}, bf16[2304,128]{1,0:T(8,128)(2,1)S(1)}, u32[]{:S(2)}, u32[]{:S(2)}) collective-permute-start(bf16[2304,128]{1,0:T(8,128)(2,1)} %copy-done.11), channel_id=1, source_target_pairs={{2,3},{5,4},{10,11},{13,12},{18,19},{21,20},{26,27},{29,28},{34,35... | collective-permute-start | bytes 1769480 | tf_op jit(solution)/shard_map/ppermute | solution.py:109
  133.5 24.8 %collective-permute-start.21 = (bf16[64,5888]{1,0:T(8,128)(2,1)}, bf16[64,5888]{1,0:T(8,128)(2,1)}, u32[]{:S(2)}, u32[]{:S(2)}) collective-permute-start(bf16[64,5888]{1,0:T(8,128)(2,1)} %collective-permute-done.20), channel_id=1, source_target_pairs={{6,7},{1,0},{14,15},{9,8},{22,23},{17,16},{30,31},{25,24},{38,39},... | collective-permute-start | bytes 2261000 | tf_op jit(solution)/shard_map/ppermute | solution.py:106
  138.2 0.7 copy-start
  138.9 22.6 %collective-permute-start.22 = (bf16[512,128]{1,0:T(8,128)(2,1)}, bf16[512,128]{1,0:T(8,128)(2,1)S(1)}, u32[]{:S(2)}, u32[]{:S(2)}) collective-permute-start(bf16[512,128]{1,0:T(8,128)(2,1)} %get-tuple-element.60), channel_id=1, source_target_pairs={{3,0},{4,7},{11,8},{12,15},{19,16},{20,23},{27,24},{28,31},{35,32}... | collective-permute-start | bytes 393224 | tf_op jit(solution)/shard_map/ppermute | solution.py:162
  140.2 21.3 %collective-permute-start.23 = (bf16[512,128]{1,0:T(8,128)(2,1)}, bf16[512,128]{1,0:T(8,128)(2,1)S(1)}, u32[]{:S(2)}, u32[]{:S(2)}) collective-permute-start(bf16[512,128]{1,0:T(8,128)(2,1)} %get-tuple-element.61), channel_id=1, source_target_pairs={{3,2},{4,5},{11,10},{12,13},{19,18},{20,21},{27,26},{28,29},{35,34... | collective-permute-start | bytes 393224 | tf_op jit(solution)/shard_map/ppermute | solution.py:162
  142.1 3.1 %copy-start.7 = (bf16[1,8192,128]{2,1,0:T(8,128)(2,1)S(1)}, bf16[1,8192,128]{2,1,0:T(8,128)(2,1)}, u32[]{:S(2)}) copy-start(bf16[1,8192,128]{2,1,0:T(8,128)(2,1)} %param.8) | copy-start | bytes 6291460
  142.1 19.4 %collective-permute-start.24 = (bf16[512,128]{1,0:T(8,128)(2,1)S(1)}, bf16[512,128]{1,0:T(8,128)(2,1)S(1)}, u32[]{:S(2)}, u32[]{:S(2)}) collective-permute-start(bf16[512,128]{1,0:T(8,128)(2,1)S(1)} %shard_map.94), channel_id=1, source_target_pairs={{3,1},{4,6},{11,9},{12,14},{19,17},{20,22},{27,25},{28,30},{35,33}... | collective-permute-start | bytes 393224 | tf_op jit(solution)/shard_map/ppermute | solution.py:162
  147.3 14.2 %copy-start.1 = (f32[512,128]{1,0:T(8,128)S(1)}, f32[512,128]{1,0:T(8,128)}, u32[]{:S(2)}) copy-start(f32[512,128]{1,0:T(8,128)} %copy-done) | copy-start | bytes 786436

commit v11 on v10

--- a/solution.py
+++ b/solution.py
@@ -27,7 +27,8 @@
     index = jnp.arange(half).astype(jnp.float32)
     inverse = jnp.exp(-(2.0 * index / HD) * math.log(ROPE_BASE))
     angles = jnp.arange(rows).astype(jnp.float32)[:, None] * inverse[None, :]
-    return jnp.cos(angles), jnp.sin(angles)
+    cosine, sine = jnp.cos(angles), jnp.sin(angles)
+    return jnp.concatenate([cosine, cosine], axis=1), jnp.concatenate([-sine, sine], axis=1)
 
 
 def dot(a, b):
@@ -72,6 +73,32 @@
     )(low.astype(jnp.int32).reshape(1), near, far, *weights)
 
 
+def last_kernel(me, weight, block, rows, mine, back1, back2, back3, keep, turn, out):
+    at = me[0]
+    last = dot(block[...], weight[...])
+    keys = rows[7:15].reshape(512, HD) + jnp.where((at == 3) | (at == 4), mine[...], 0.0)
+    for back in (back1, back2, back3):
+        keys += back[...].astype(jnp.float32)
+    head = keys[:64] + jnp.where(at == 7, last, 0.0)
+    tail = keys[448:] + jnp.where(at == 0, last, 0.0)
+    keys = jnp.concatenate([head, keys[64:448], tail])
+    out[...] = (keys * keep[...] + pltpu.roll(keys, HD // 2, 1) * turn[...]).astype(out.dtype)
+
+
+def last_step(me, weight, *rest):
+    vmem = pl.BlockSpec(memory_space=pltpu.VMEM)
+    return pl.pallas_call(
+        last_kernel,
+        grid=(1,),
+        out_shape=jax.ShapeDtypeStruct((512, HD), jnp.bfloat16),
+        in_specs=[pl.BlockSpec(memory_space=pltpu.SMEM), pl.BlockSpec((K_LINE, HD), lambda i: (0, 0))]
+        + [vmem] * len(rest),
+        out_specs=vmem,
+        cost_estimate=pl.CostEstimate(flops=2 * 64 * K_LINE * HD, bytes_accessed=0, transcendentals=0),
+        compiler_params=pltpu.CompilerParams(vmem_limit_bytes=24 << 20),
+    )(me.reshape(1), weight, *rest)
+
+
 def body(tokens, norm_gain, key_weight, inner_params, outer_params, outer_momentum):
     me = lax.axis_index("tensor")
     zh = lax.axis_index("zh")
@@ -157,19 +184,12 @@
     rows = put(rows, x, jnp.where(low, me + 6, me - 6))
     mine3, back1, back3 = middle_products(low, near, far, w_rest, w13)
     (back2,) = middle_products(low, near, far, w2)
-    middle = jnp.where((me == 3) | (me == 4), mine3, 0.0)
-    for d, block in ((3, back3), (1, back1), (2, back2)):
-        back = lax.ppermute(block, "tensor", [(3, 3 - d), (4, 4 + d)])
-        middle += back.astype(jnp.float32)
-
-    rows = put(rows, y, jnp.where(low, me + 7, me - 7))
+    back1, back2, back3 = [
+        lax.ppermute(block, "tensor", [(3, 3 - d), (4, 4 + d)])
+        for d, block in ((1, back1), (2, back2), (3, back3))
+    ]
     synced = synced.transpose(1, 0, 2, 3).reshape(1024, 512)
-    projected = rows[7:15].reshape(512, HD) + middle
-    cosine, sine = rotary_tables(512)
-    first, second = projected[:, : HD // 2], projected[:, HD // 2 :]
-    key_rows = jnp.concatenate(
-        [first * cosine - second * sine, second * cosine + first * sine], axis=-1
-    ).astype(jnp.bfloat16)
+    key_rows = last_step(me, weight, y, rows, mine3, back1, back2, back3, *rotary_tables(512))
     return (key_rows, outer_next[None], moment_next[None], synced[None])
 
 

time: 165 us -> 168 us (1.018)
  the two profiles are of different devices: /device:TPU:6 before, /device:TPU:32 now
where the time goes in v11:
time: 168 us; the launch traced here: 166 us
  starting transfers between devices  98.7 us (59%)
  waiting for transfers between devices  27.9 us (17%)
  matrix products  13.8 us (8%)
  other arithmetic  9.21 us (5%)
  local copies, waits for them, and re-layouts  7.93 us (5%)
  Pallas kernels  7.66 us (5%)
    ppermute x8, starting transfers between devices, inward(): return lax.ppermute(x, 'tensor', [(3 - d, 4 - d), (4 + d, 3 + d)])  23.1 us
    ppermute x4, starting transfers between devices, hop(): b = lax.ppermute(b, 'tensor', [(j + 1, j) for j in range(7 - s)])  15.1 us
    ppermute x1, starting transfers between devices, body(): came = lax.ppermute(other, 'zh', [(0, 1), (1, 0)])  14.8 us
    dot_general x10, matrix products, dot(): return jnp.dot(a, b, preferred_element_type=jnp.float32)  13.8 us
    ppermute x1, starting transfers between devices, body(): theirs = lax.ppermute(mine, 'zh', [(0, 1), (1, 0)])  13.5 us
    ppermute x4, starting transfers between devices, hop(): a = lax.ppermute(a, 'tensor', [(j, j + 1) for j in range(s, 7)])  9.93 us
    ppermute x3, waiting for transfers between devices, hop_out(): return lax.ppermute(x, 'tensor', pairs)  9.43 us
    ppermute x3, starting transfers between devices, hop_out(): return lax.ppermute(x, 'tensor', pairs)  6.82 us
  transfers between devices with their start and end apart: 27, of which 7 were waited for; matrix products, arithmetic and copies ran while one was open for 16% of the time, Pallas kernels for 3%

profile of v11, /device:TPU:32, one launch (start us, length us, event | category | flops | bytes accessed | tf_op | source)
XLA Modules:
  0.0 166.3 jit_solution(11501838621523307199)
XLA Ops:
  0.7 1.7 %multiply_reduce_fusion = f32[64]{0:T(128)S(1)} fusion(bf16[64,8192]{1,0:T(8,128)(2,1)} %param.6), kind=kLoop, calls=%fused_computation.1 | loop fusion | flops 1572800 | bytes 1048832 | tf_op jit(solution)/shard_map/reduce_sum | solution.py:112
  3.1 1.1 multiply_convert_fusion
  4.2 3.8 %collective-permute-start.4 = (bf16[64,5888]{1,0:T(8,128)(2,1)}, bf16[64,5888]{1,0:T(8,128)(2,1)}, u32[]{:S(2)}, u32[]{:S(2)}) collective-permute-start(bf16[64,5888]{1,0:T(8,128)(2,1)} %multiply_convert_fusion), channel_id=1, source_target_pairs={{0,1},{1,2},{2,3},{3,4},{4,5},{5,6},{6,7},{8,9},{9,10},{10,11},{11... | collective-permute-start | bytes 2261000 | tf_op jit(solution)/shard_map/ppermute | solution.py:127
  8.0 5.7 %collective-permute-start = (bf16[64,5888]{1,0:T(8,128)(2,1)}, bf16[64,5888]{1,0:T(8,128)(2,1)}, u32[]{:S(2)}, u32[]{:S(2)}) collective-permute-start(bf16[64,5888]{1,0:T(8,128)(2,1)} %multiply_convert_fusion), channel_id=1, source_target_pairs={{1,0},{2,1},{3,2},{4,3},{5,4},{6,5},{7,6},{9,8},{10,9},{11,10},{12... | collective-permute-start | bytes 2261000 | tf_op jit(solution)/shard_map/ppermute | solution.py:128
  13.8 1.1 copy.10
  14.8 4.8 %all-to-all-start = ((bf16[32,2,16,512]{3,2,1,0:T(8,128)(2,1)}), bf16[32,2,16,512]{3,2,1,0:T(8,128)(2,1)}, u32[]{:S(2)}, u32[]{:S(2)}) async-start(bf16[32,2,16,512]{3,2,1,0:T(8,128)(2,1)} %copy.10), calls=%async_computation | async-start | bytes 2097152 | tf_op jit(solution)/shard_map/all_to_all | solution.py:108
  19.8 1.5 fusion.23
  21.3 1.7 %slice.28 = bf16[64,2304]{1,0:T(8,128)(2,1)} slice(bf16[64,8192]{1,0:T(8,128)(2,1)} %param.6), slice={[0:64], [5888:8192]} | slice | bytes 589824 | tf_op jit(solution)/shard_map/slice | solution.py:140
  23.1 1.8 %multiply_convert_fusion.1 = bf16[64,2304]{1,0:T(8,128)(2,1)} fusion(bf16[64,2304]{1,0:T(8,128)(2,1)} %slice.28, f32[2304]{0:T(1024)S(1)} %slice.33, f32[64]{0:T(128)S(1)} %add_rsqrt_fusion), kind=kLoop, calls=%fused_computation.48 | loop fusion | flops 589824 | bytes 599296 | tf_op jit(solution)/shard_map/convert_element_type | solution.py:115
  25.0 4.7 %collective-permute-start.5 = (bf16[64,5888]{1,0:T(8,128)(2,1)}, bf16[64,5888]{1,0:T(8,128)(2,1)}, u32[]{:S(2)}, u32[]{:S(2)}) collective-permute-start(bf16[64,5888]{1,0:T(8,128)(2,1)} %collective-permute-done.4), channel_id=1, source_target_pairs={{1,2},{2,3},{3,4},{4,5},{5,6},{6,7},{9,10},{10,11},{11,12},{12,13}... | collective-permute-start | bytes 2261000 | tf_op jit(solution)/shard_map/ppermute | solution.py:127
  29.7 1.9 %collective-permute-start.1 = (bf16[64,5888]{1,0:T(8,128)(2,1)}, bf16[64,5888]{1,0:T(8,128)(2,1)}, u32[]{:S(2)}, u32[]{:S(2)}) collective-permute-start(bf16[64,5888]{1,0:T(8,128)(2,1)} %collective-permute-done), channel_id=1, source_target_pairs={{1,0},{2,1},{3,2},{4,3},{5,4},{6,5},{9,8},{10,9},{11,10},{12,11},{... | collective-permute-start | bytes 2261000 | tf_op jit(solution)/shard_map/ppermute | solution.py:128
  31.6 1.5 fusion.29
  33.1 1.5 fusion.35
  34.7 2.3 %all-to-all-done = bf16[32,2,16,512]{3,2,1,0:T(8,128)(2,1)} async-done(((bf16[32,2,16,512]{3,2,1,0:T(8,128)(2,1)}), bf16[32,2,16,512]{3,2,1,0:T(8,128)(2,1)}, u32[]{:S(2)}, u32[]{:S(2)}) %all-to-all-start) | async-done | bytes 1048608 | tf_op jit(solution)/shard_map/all_to_all | solution.py:108
  36.9 1.3 collective-permute-start.13
  38.2 1.3 collective-permute-start.12
  39.5 1.4 convert_reduce_fusion
  40.9 14.8 %collective-permute-start.11 = (f32[16,512]{1,0:T(8,128)S(1)}, f32[16,512]{1,0:T(8,128)S(1)}, u32[]{:S(2)}, u32[]{:S(2)}) collective-permute-start(f32[16,512]{1,0:T(8,128)S(1)} %dynamic-slice_bitcast_fusion), channel_id=1, source_target_pairs={{0,256},{256,0},{1,257},{257,1},{2,258},{258,2},{3,259},{259,3},{4... | collective-permute-start | bytes 98312 | tf_op jit(solution)/shard_map/ppermute | solution.py:150
  56.4 4.6 %collective-permute-start.2 = (bf16[64,5888]{1,0:T(8,128)(2,1)}, bf16[64,5888]{1,0:T(8,128)(2,1)S(1)}, u32[]{:S(2)}, u32[]{:S(2)}) collective-permute-start(bf16[64,5888]{1,0:T(8,128)(2,1)} %collective-permute-done.1), channel_id=1, source_target_pairs={{1,0},{2,1},{3,2},{4,3},{5,4},{9,8},{10,9},{11,10},{12,11},{13,12}... | collective-permute-start | bytes 2261000 | tf_op jit(solution)/shard_map/ppermute | solution.py:128
  61.1 1.5 fusion.41
  62.6 1.6 fusion.47
  64.3 1.3 collective-permute-start.14
  66.3 13.5 %collective-permute-start.15 = (bf16[16,512]{1,0:T(8,128)(2,1)S(1)}, bf16[16,512]{1,0:T(8,128)(2,1)S(1)}, u32[]{:S(2)}, u32[]{:S(2)}) collective-permute-start(bf16[16,512]{1,0:T(8,128)(2,1)S(1)} %get-tuple-element.64), channel_id=1, source_target_pairs={{0,256},{256,0},{1,257},{257,1},{2,258},{258,2},{3,259},{259,3},{4... | collective-permute-start | bytes 49160 | tf_op jit(solution)/shard_map/ppermute | solution.py:158
  79.8 2.9 %collective-permute-start.3 = (bf16[64,5888]{1,0:T(8,128)(2,1)S(1)}, bf16[64,5888]{1,0:T(8,128)(2,1)S(1)}, u32[]{:S(2)}, u32[]{:S(2)}) collective-permute-start(bf16[64,5888]{1,0:T(8,128)(2,1)S(1)} %collective-permute-done.2), channel_id=1, source_target_pairs={{1,0},{2,1},{3,2},{4,3},{9,8},{10,9},{11,10},{12,11},{17,16},{18,1... | collective-permute-start | bytes 2261000 | tf_op jit(solution)/shard_map/ppermute | solution.py:128
  85.0 10.0 %collective-permute-start.17 = (bf16[2304,128]{1,0:T(8,128)(2,1)S(1)}, bf16[2304,128]{1,0:T(8,128)(2,1)S(1)}, u32[]{:S(2)}, u32[]{:S(2)}) collective-permute-start(bf16[2304,128]{1,0:T(8,128)(2,1)S(1)} %collective-permute-done.13), channel_id=1, source_target_pairs={{1,2},{6,5},{9,10},{14,13},{17,18},{22,21},{25,26},{30,29},{33,34}... | collective-permute-start | bytes 1769480 | tf_op jit(solution)/shard_map/ppermute | solution.py:136
  95.0 4.4 %collective-permute-done.3 = bf16[64,5888]{1,0:T(8,128)(2,1)S(1)} collective-permute-done((bf16[64,5888]{1,0:T(8,128)(2,1)S(1)}, bf16[64,5888]{1,0:T(8,128)(2,1)S(1)}, u32[]{:S(2)}, u32[]{:S(2)}) %collective-permute-start.3) | collective-permute-done | bytes 753696 | tf_op jit(solution)/shard_map/ppermute | solution.py:128
  99.5 2.5 %collective-permute-start.8 = (bf16[64,5888]{1,0:T(8,128)(2,1)S(1)}, bf16[64,5888]{1,0:T(8,128)(2,1)}, u32[]{:S(2)}, u32[]{:S(2)}) collective-permute-start(bf16[64,5888]{1,0:T(8,128)(2,1)S(1)} %broadcast_select_fusion), channel_id=1, source_target_pairs={{4,5},{5,6},{6,7},{1,0},{2,1},{3,2},{12,13},{13,14},{14,15},{9,8},... | collective-permute-start | bytes 2261000 | tf_op jit(solution)/shard_map/ppermute | solution.py:133
  102.4 2.6 %collective-permute-done.17 = bf16[2304,128]{1,0:T(8,128)(2,1)S(1)} collective-permute-done((bf16[2304,128]{1,0:T(8,128)(2,1)S(1)}, bf16[2304,128]{1,0:T(8,128)(2,1)S(1)}, u32[]{:S(2)}, u32[]{:S(2)}) %collective-permute-start.17) | collective-permute-done | bytes 589856 | tf_op jit(solution)/shard_map/ppermute | solution.py:136
  105.9 1.1 pad_maximum_fusion
  107.0 1.7 %collective-permute-start.19 = (bf16[4608,128]{1,0:T(8,128)(2,1)}, bf16[4608,128]{1,0:T(8,128)(2,1)}, u32[]{:S(2)}, u32[]{:S(2)}) collective-permute-start(bf16[4608,128]{1,0:T(8,128)(2,1)} %pad_maximum_fusion), channel_id=1, source_target_pairs={{2,3},{5,4},{10,11},{13,12},{18,19},{21,20},{26,27},{29,28},{34,35... | collective-permute-start | bytes 3538952 | tf_op jit(solution)/shard_map/ppermute | solution.py:136
  108.7 9.4 %collective-permute-done.8 = bf16[64,5888]{1,0:T(8,128)(2,1)} collective-permute-done((bf16[64,5888]{1,0:T(8,128)(2,1)S(1)}, bf16[64,5888]{1,0:T(8,128)(2,1)}, u32[]{:S(2)}, u32[]{:S(2)}) %collective-permute-start.8) | collective-permute-done | bytes 753696 | tf_op jit(solution)/shard_map/ppermute | solution.py:133
  118.2 2.2 %collective-permute-start.9 = (bf16[64,5888]{1,0:T(8,128)(2,1)}, bf16[64,5888]{1,0:T(8,128)(2,1)}, u32[]{:S(2)}, u32[]{:S(2)}) collective-permute-start(bf16[64,5888]{1,0:T(8,128)(2,1)} %collective-permute-done.8), channel_id=1, source_target_pairs={{5,6},{6,7},{1,0},{2,1},{13,14},{14,15},{9,8},{10,9},{21,22},{22,2... | collective-permute-start | bytes 2261000 | tf_op jit(solution)/shard_map/ppermute | solution.py:133
  120.4 5.3 %collective-permute-start.18 = (bf16[2304,128]{1,0:T(8,128)(2,1)S(1)}, bf16[2304,128]{1,0:T(8,128)(2,1)}, u32[]{:S(2)}, u32[]{:S(2)}) collective-permute-start(bf16[2304,128]{1,0:T(8,128)(2,1)S(1)} %slice_bitcast_fusion.refs_0_), channel_id=1, source_target_pairs={{1,2},{6,5},{9,10},{14,13},{17,18},{22,21},{25,26},{30,29},{33,34}... | collective-permute-start | bytes 1769480 | tf_op jit(solution)/shard_map/ppermute | solution.py:136
  125.7 1.1 broadcast_in_dim.60
  126.8 6.0 %all-to-all-start.1 = ((bf16[32,2,16,512]{3,2,1,0:T(8,128)(2,1)}), bf16[32,2,16,512]{3,2,1,0:T(8,128)(2,1)}, u32[]{:S(2)}, u32[]{:S(2)}) async-start(bf16[32,2,16,512]{3,2,1,0:T(8,128)(2,1)} %broadcast_in_dim.60), calls=%async_computation.1 | async-start | bytes 2097152 | tf_op jit(solution)/shard_map/all_to_all | solution.py:180
  132.8 2.7 %fusion.71 = f32[22,64,128]{2,1,0:T(8,128)} fusion(f32[22,64,128]{2,1,0:T(8,128)} %copy-done.2, s32[]{:T(128)S(6)} %select_n.79, bf16[64,5888]{1,0:T(8,128)(2,1)} %collective-permute-done.8, bf16[1,8192,128]{2,1,0:T(8,128)(2,1)} %param.8), kind=kOutput, calls=%fused_computation.41 | convolution fusion | flops 96468992 | bytes 2293764 | tf_op jit(solution)/shard_map/dot_general | solution.py:35
  135.5 1.5 collective-permute-start.21
  137.0 2.2 %collective-permute-start.10 = (bf16[64,5888]{1,0:T(8,128)(2,1)}, bf16[64,5888]{1,0:T(8,128)(2,1)}, u32[]{:S(2)}, u32[]{:S(2)}) collective-permute-start(bf16[64,5888]{1,0:T(8,128)(2,1)} %collective-permute-done.9), channel_id=1, source_target_pairs={{6,7},{1,0},{14,15},{9,8},{22,23},{17,16},{30,31},{25,24},{38,39},... | collective-permute-start | bytes 2261000 | tf_op jit(solution)/shard_map/ppermute | solution.py:133
  140.4 3.3 %shard_map.93 = (f32[512,128]{1,0:T(8,128)S(1)}, bf16[512,128]{1,0:T(8,128)(2,1)}, bf16[512,128]{1,0:T(8,128)(2,1)}) custom-call(s32[1]{0:T(128)} %bitcast.22.low, bf16[256,2304]{1,0:T(8,128)(2,1)S(1)} %constant_dynamic-update-slice_fusion.near, bf16[256,2304]{1,0:T(8,128)(2,1)S(1)} %collective-permute-done.20.far, ...), custom_call_target="tpu_custom_call" | custom-call | tf_op jit(solution)/shard_map/pallas_call | solution.py:66
  144.5 1.3 collective-permute-start.22
  145.8 1.3 collective-permute-start.24
  147.1 3.1 %all-to-all-done.1 = bf16[32,2,16,512]{3,2,1,0:T(8,128)(2,1)} async-done(((bf16[32,2,16,512]{3,2,1,0:T(8,128)(2,1)}), bf16[32,2,16,512]{3,2,1,0:T(8,128)(2,1)}, u32[]{:S(2)}, u32[]{:S(2)}) %all-to-all-start.1) | async-done | bytes 1048608 | tf_op jit(solution)/shard_map/all_to_all | solution.py:180
  150.1 2.0 %shard_map.94 = bf16[512,128]{1,0:T(8,128)(2,1)S(1)} custom-call(s32[1]{0:T(128)} %bitcast.22.low, bf16[256,2304]{1,0:T(8,128)(2,1)S(1)} %constant_dynamic-update-slice_fusion.near, bf16[256,2304]{1,0:T(8,128)(2,1)S(1)} %collective-permute-done.20.far, bf16[2304,128]{1,0:T(8,128)(2,1)} %collective-permute-done.21.refs_0_), custom_call_target="tpu_custom_call" | custom-call | tf_op jit(solution)/shard_map/pallas_call | solution.py:66
  152.1 1.3 collective-permute-start.23
  153.4 2.2 %fusion.77.rows = f32[22,64,128]{2,1,0:T(8,128)} fusion(f32[22,64,128]{2,1,0:T(8,128)} %fusion.71, s32[]{:T(128)S(6)} %select_n.81, bf16[64,5888]{1,0:T(8,128)(2,1)} %collective-permute-done.9, bf16[1,8192,128]{2,1,0:T(8,128)(2,1)S(1)} %copy-done.1), kind=kOutput, calls=%fused_computation.43 | convolution fusion | flops 96468992 | bytes 2293764 | tf_op jit(solution)/shard_map/dot_general | solution.py:35
  155.6 2.4 %copy.11 = bf16[32,2,16,512]{3,2,0,1:T(8,128)(2,1)} copy(bf16[32,2,16,512]{3,2,1,0:T(8,128)(2,1)} %all-to-all-done.1) | data formatting | bytes 2097152 | tf_op jit(solution)/shard_map/optimization_barrier | solution.py:183
  158.0 6.0 %collective-permute-done.23.back2 = bf16[512,128]{1,0:T(8,128)(2,1)S(1)} collective-permute-done((bf16[512,128]{1,0:T(8,128)(2,1)S(1)}, bf16[512,128]{1,0:T(8,128)(2,1)S(1)}, u32[]{:S(2)}, u32[]{:S(2)}) %collective-permute-start.23) | collective-permute-done | bytes 131104 | tf_op jit(solution)/shard_map/ppermute | solution.py:188
  164.0 2.3 %shard_map.95 = bf16[512,128]{1,0:T(8,128)(2,1)} custom-call(s32[1]{0:T(128)} %bitcast.me, bf16[8192,128]{1,0:T(8,128)(2,1)S(1)} %bitcast.155, bf16[64,5888]{1,0:T(8,128)(2,1)} %collective-permute-done.10.block, f32[22,64,128]{2,1,0:T(8,128)S(1)} %copy-done.3, f32[512,128]{1,0:T(8,128)S(1)} %copy-done.5, bf16[512,128]{1,0:T(8,128)(2,1)} %collective-permute-done.22.back1, ...), custom_call_target="tpu_custom_call" | custom-call | flops 96468992 | tf_op jit(solution)/shard_map/pallas_call | solution.py:90
  (69 shorter events, 8.0 us)
Async XLA Ops:
  0.6 2.4 %copy-start.7 = (bf16[64,8192]{1,0:T(8,128)(2,1)S(1)}, bf16[64,8192]{1,0:T(8,128)(2,1)}, u32[]{:S(2)}) copy-start(bf16[64,8192]{1,0:T(8,128)(2,1)} %param.6) | copy-start | bytes 3145732
  0.6 13.1 %copy-start.8 = (bf16[1,1,1024,512]{3,2,1,0:T(8,128)(2,1)S(1)}, bf16[1,1,1024,512]{3,2,1,0:T(8,128)(2,1)}, u32[]{:S(2)}) copy-start(bf16[1,1,1024,512]{3,2,1,0:T(8,128)(2,1)} %param.9) | copy-start | bytes 3145732
  4.2 20.8 %collective-permute-start.4 = (bf16[64,5888]{1,0:T(8,128)(2,1)}, bf16[64,5888]{1,0:T(8,128)(2,1)}, u32[]{:S(2)}, u32[]{:S(2)}) collective-permute-start(bf16[64,5888]{1,0:T(8,128)(2,1)} %multiply_convert_fusion), channel_id=1, source_target_pairs={{0,1},{1,2},{2,3},{3,4},{4,5},{5,6},{6,7},{8,9},{9,10},{10,11},{11... | collective-permute-start | bytes 2261000 | tf_op jit(solution)/shard_map/ppermute | solution.py:127
  8.0 21.7 %collective-permute-start = (bf16[64,5888]{1,0:T(8,128)(2,1)}, bf16[64,5888]{1,0:T(8,128)(2,1)}, u32[]{:S(2)}, u32[]{:S(2)}) collective-permute-start(bf16[64,5888]{1,0:T(8,128)(2,1)} %multiply_convert_fusion), channel_id=1, source_target_pairs={{1,0},{2,1},{3,2},{4,3},{5,4},{6,5},{7,6},{9,8},{10,9},{11,10},{12... | collective-permute-start | bytes 2261000 | tf_op jit(solution)/shard_map/ppermute | solution.py:128
  14.8 4.8 %copy-start = (bf16[1,8192,128]{2,1,0:T(8,128)(2,1)S(1)}, bf16[1,8192,128]{2,1,0:T(8,128)(2,1)}, u32[]{:S(2)}) copy-start(bf16[1,8192,128]{2,1,0:T(8,128)(2,1)} %param.8) | copy-start | bytes 6291460
  14.8 22.1 %all-to-all-start = ((bf16[32,2,16,512]{3,2,1,0:T(8,128)(2,1)}), bf16[32,2,16,512]{3,2,1,0:T(8,128)(2,1)}, u32[]{:S(2)}, u32[]{:S(2)}) async-start(bf16[32,2,16,512]{3,2,1,0:T(8,128)(2,1)} %copy.10), calls=%async_computation | async-start | bytes 2097152 | tf_op jit(solution)/shard_map/all_to_all | solution.py:108
  19.8 3.3 %copy-start.9 = (bf16[8192]{0:T(1024)(128)(2,1)S(1)}, bf16[8192]{0:T(1024)(128)(2,1)}, u32[]{:S(2)}) copy-start(bf16[8192]{0:T(1024)(128)(2,1)} %param.7) | copy-start | bytes 49156
  25.0 30.7 %collective-permute-start.5 = (bf16[64,5888]{1,0:T(8,128)(2,1)}, bf16[64,5888]{1,0:T(8,128)(2,1)}, u32[]{:S(2)}, u32[]{:S(2)}) collective-permute-start(bf16[64,5888]{1,0:T(8,128)(2,1)} %collective-permute-done.4), channel_id=1, source_target_pairs={{1,2},{2,3},{3,4},{4,5},{5,6},{6,7},{9,10},{10,11},{11,12},{12,13}... | collective-permute-start | bytes 2261000 | tf_op jit(solution)/shard_map/ppermute | solution.py:127
  29.7 26.8 %collective-permute-start.1 = (bf16[64,5888]{1,0:T(8,128)(2,1)}, bf16[64,5888]{1,0:T(8,128)(2,1)}, u32[]{:S(2)}, u32[]{:S(2)}) collective-permute-start(bf16[64,5888]{1,0:T(8,128)(2,1)} %collective-permute-done), channel_id=1, source_target_pairs={{1,0},{2,1},{3,2},{4,3},{5,4},{6,5},{9,8},{10,9},{11,10},{12,11},{... | collective-permute-start | bytes 2261000 | tf_op jit(solution)/shard_map/ppermute | solution.py:128
  36.9 27.3 %collective-permute-start.13 = (bf16[2304,128]{1,0:T(8,128)(2,1)S(1)}, bf16[2304,128]{1,0:T(8,128)(2,1)S(1)}, u32[]{:S(2)}, u32[]{:S(2)}) collective-permute-start(bf16[2304,128]{1,0:T(8,128)(2,1)S(1)} %slice_bitcast_fusion.refs_0_), channel_id=1, source_target_pairs={{0,1},{7,6},{8,9},{15,14},{16,17},{23,22},{24,25},{31,30},{32,33},... | collective-permute-start | bytes 1769480 | tf_op jit(solution)/shard_map/ppermute | solution.py:136
  38.2 26.0 %collective-permute-start.12 = (bf16[64,2304]{1,0:T(8,128)(2,1)}, bf16[64,2304]{1,0:T(8,128)(2,1)S(1)}, u32[]{:S(2)}, u32[]{:S(2)}) collective-permute-start(bf16[64,2304]{1,0:T(8,128)(2,1)} %multiply_convert_fusion.1), channel_id=1, source_target_pairs={{0,1},{7,6},{8,9},{15,14},{16,17},{23,22},{24,25},{31,30},{32,33},... | collective-permute-start | bytes 884744 | tf_op jit(solution)/shard_map/ppermute | solution.py:136
  40.9 23.3 %collective-permute-start.11 = (f32[16,512]{1,0:T(8,128)S(1)}, f32[16,512]{1,0:T(8,128)S(1)}, u32[]{:S(2)}, u32[]{:S(2)}) collective-permute-start(f32[16,512]{1,0:T(8,128)S(1)} %dynamic-slice_bitcast_fusion), channel_id=1, source_target_pairs={{0,256},{256,0},{1,257},{257,1},{2,258},{258,2},{3,259},{259,3},{4... | collective-permute-start | bytes 98312 | tf_op jit(solution)/shard_map/ppermute | solution.py:150
  55.7 27.0 %collective-permute-start.6 = (bf16[64,5888]{1,0:T(8,128)(2,1)}, bf16[64,5888]{1,0:T(8,128)(2,1)S(1)}, u32[]{:S(2)}, u32[]{:S(2)}) collective-permute-start(bf16[64,5888]{1,0:T(8,128)(2,1)} %collective-permute-done.5), channel_id=1, source_target_pairs={{2,3},{3,4},{4,5},{5,6},{6,7},{10,11},{11,12},{12,13},{13,14},{14,... | collective-permute-start | bytes 2261000 | tf_op jit(solution)/shard_map/ppermute | solution.py:127
  56.4 23.3 %collective-permute-start.2 = (bf16[64,5888]{1,0:T(8,128)(2,1)}, bf16[64,5888]{1,0:T(8,128)(2,1)S(1)}, u32[]{:S(2)}, u32[]{:S(2)}) collective-permute-start(bf16[64,5888]{1,0:T(8,128)(2,1)} %collective-permute-done.1), channel_id=1, source_target_pairs={{1,0},{2,1},{3,2},{4,3},{5,4},{9,8},{10,9},{11,10},{12,11},{13,12}... | collective-permute-start | bytes 2261000 | tf_op jit(solution)/shard_map/ppermute | solution.py:128
  62.6 1.6 copy-start.6
  62.6 3.0 %copy-start.10 = (f32[1,16,512]{2,1,0:T(8,128)S(1)}, f32[1,16,512]{2,1,0:T(8,128)}, u32[]{:S(2)}) copy-start(f32[1,16,512]{2,1,0:T(8,128)} %param.11) | copy-start | bytes 98308
  62.6 3.0 %copy-start.11 = (f32[1,16,512]{2,1,0:T(8,128)S(1)}, f32[1,16,512]{2,1,0:T(8,128)}, u32[]{:S(2)}) copy-start(f32[1,16,512]{2,1,0:T(8,128)} %param.10) | copy-start | bytes 98308
  64.3 20.0 %collective-permute-start.14 = (bf16[128,2304]{1,0:T(8,128)(2,1)S(1)}, bf16[128,2304]{1,0:T(8,128)(2,1)S(1)}, u32[]{:S(2)}, u32[]{:S(2)}) collective-permute-start(bf16[128,2304]{1,0:T(8,128)(2,1)S(1)} %pad_maximum_fusion.2), channel_id=1, source_target_pairs={{1,2},{6,5},{9,10},{14,13},{17,18},{22,21},{25,26},{30,29},{33,34}... | collective-permute-start | bytes 1769480 | tf_op jit(solution)/shard_map/ppermute | solution.py:136
  66.3 17.9 %collective-permute-start.15 = (bf16[16,512]{1,0:T(8,128)(2,1)S(1)}, bf16[16,512]{1,0:T(8,128)(2,1)S(1)}, u32[]{:S(2)}, u32[]{:S(2)}) collective-permute-start(bf16[16,512]{1,0:T(8,128)(2,1)S(1)} %get-tuple-element.64), channel_id=1, source_target_pairs={{0,256},{256,0},{1,257},{257,1},{2,258},{258,2},{3,259},{259,3},{4... | collective-permute-start | bytes 49160 | tf_op jit(solution)/shard_map/ppermute | solution.py:158
  79.8 19.6 %collective-permute-start.3 = (bf16[64,5888]{1,0:T(8,128)(2,1)S(1)}, bf16[64,5888]{1,0:T(8,128)(2,1)S(1)}, u32[]{:S(2)}, u32[]{:S(2)}) collective-permute-start(bf16[64,5888]{1,0:T(8,128)(2,1)S(1)} %collective-permute-done.2), channel_id=1, source_target_pairs={{1,0},{2,1},{3,2},{4,3},{9,8},{10,9},{11,10},{12,11},{17,16},{18,1... | collective-permute-start | bytes 2261000 | tf_op jit(solution)/shard_map/ppermute | solution.py:128
  82.7 16.7 %collective-permute-start.7 = (bf16[64,5888]{1,0:T(8,128)(2,1)S(1)}, bf16[64,5888]{1,0:T(8,128)(2,1)S(1)}, u32[]{:S(2)}, u32[]{:S(2)}) collective-permute-start(bf16[64,5888]{1,0:T(8,128)(2,1)S(1)} %collective-permute-done.6), channel_id=1, source_target_pairs={{3,4},{4,5},{5,6},{6,7},{11,12},{12,13},{13,14},{14,15},{19,20},{2... | collective-permute-start | bytes 2261000 | tf_op jit(solution)/shard_map/ppermute | solution.py:127
  84.3 20.7 %collective-permute-start.16 = (bf16[192,2304]{1,0:T(8,128)(2,1)S(1)}, bf16[192,2304]{1,0:T(8,128)(2,1)S(1)}, u32[]{:S(2)}, u32[]{:S(2)}) collective-permute-start(bf16[192,2304]{1,0:T(8,128)(2,1)S(1)} %pad_maximum_fusion.1), channel_id=1, source_target_pairs={{2,3},{5,4},{10,11},{13,12},{18,19},{21,20},{26,27},{29,28},{34,35... | collective-permute-start | bytes 2654216 | tf_op jit(solution)/shard_map/ppermute | solution.py:136
  85.0 20.0 %collective-permute-start.17 = (bf16[2304,128]{1,0:T(8,128)(2,1)S(1)}, bf16[2304,128]{1,0:T(8,128)(2,1)S(1)}, u32[]{:S(2)}, u32[]{:S(2)}) collective-permute-start(bf16[2304,128]{1,0:T(8,128)(2,1)S(1)} %collective-permute-done.13), channel_id=1, source_target_pairs={{1,2},{6,5},{9,10},{14,13},{17,18},{22,21},{25,26},{30,29},{33,34}... | collective-permute-start | bytes 1769480 | tf_op jit(solution)/shard_map/ppermute | solution.py:136
  99.5 18.6 %collective-permute-start.8 = (bf16[64,5888]{1,0:T(8,128)(2,1)S(1)}, bf16[64,5888]{1,0:T(8,128)(2,1)}, u32[]{:S(2)}, u32[]{:S(2)}) collective-permute-start(bf16[64,5888]{1,0:T(8,128)(2,1)S(1)} %broadcast_select_fusion), channel_id=1, source_target_pairs={{4,5},{5,6},{6,7},{1,0},{2,1},{3,2},{12,13},{13,14},{14,15},{9,8},... | collective-permute-start | bytes 2261000 | tf_op jit(solution)/shard_map/ppermute | solution.py:133
  102.4 2.7 %copy-start.2 = (f32[22,64,128]{2,1,0:T(8,128)}, f32[22,64,128]{2,1,0:T(8,128)S(1)}, u32[]{:S(2)}) copy-start(f32[22,64,128]{2,1,0:T(8,128)S(1)} %fusion.65) | copy-start | bytes 2162692
  105.2 30.4 %collective-permute-start.20 = (bf16[256,2304]{1,0:T(8,128)(2,1)S(1)}, bf16[256,2304]{1,0:T(8,128)(2,1)S(1)}, u32[]{:S(2)}, u32[]{:S(2)}) collective-permute-start(bf16[256,2304]{1,0:T(8,128)(2,1)S(1)} %constant_dynamic-update-slice_fusion.near), channel_id=1, source_target_pairs={{3,4},{4,3},{11,12},{12,11},{19,20},{20,19},{27,28},{28,27},{35,36... | collective-permute-start | bytes 3538952 | tf_op jit(solution)/shard_map/ppermute | solution.py:172
  107.0 28.5 %collective-permute-start.19 = (bf16[4608,128]{1,0:T(8,128)(2,1)}, bf16[4608,128]{1,0:T(8,128)(2,1)}, u32[]{:S(2)}, u32[]{:S(2)}) collective-permute-start(bf16[4608,128]{1,0:T(8,128)(2,1)} %pad_maximum_fusion), channel_id=1, source_target_pairs={{2,3},{5,4},{10,11},{13,12},{18,19},{21,20},{26,27},{29,28},{34,35... | collective-permute-start | bytes 3538952 | tf_op jit(solution)/shard_map/ppermute | solution.py:136
  118.2 18.9 %collective-permute-start.9 = (bf16[64,5888]{1,0:T(8,128)(2,1)}, bf16[64,5888]{1,0:T(8,128)(2,1)}, u32[]{:S(2)}, u32[]{:S(2)}) collective-permute-start(bf16[64,5888]{1,0:T(8,128)(2,1)} %collective-permute-done.8), channel_id=1, source_target_pairs={{5,6},{6,7},{1,0},{2,1},{13,14},{14,15},{9,8},{10,9},{21,22},{22,2... | collective-permute-start | bytes 2261000 | tf_op jit(solution)/shard_map/ppermute | solution.py:133
  120.4 15.2 %collective-permute-start.18 = (bf16[2304,128]{1,0:T(8,128)(2,1)S(1)}, bf16[2304,128]{1,0:T(8,128)(2,1)}, u32[]{:S(2)}, u32[]{:S(2)}) collective-permute-start(bf16[2304,128]{1,0:T(8,128)(2,1)S(1)} %slice_bitcast_fusion.refs_0_), channel_id=1, source_target_pairs={{1,2},{6,5},{9,10},{14,13},{17,18},{22,21},{25,26},{30,29},{33,34}... | collective-permute-start | bytes 1769480 | tf_op jit(solution)/shard_map/ppermute | solution.py:136
  126.8 23.4 %all-to-all-start.1 = ((bf16[32,2,16,512]{3,2,1,0:T(8,128)(2,1)}), bf16[32,2,16,512]{3,2,1,0:T(8,128)(2,1)}, u32[]{:S(2)}, u32[]{:S(2)}) async-start(bf16[32,2,16,512]{3,2,1,0:T(8,128)(2,1)} %broadcast_in_dim.60), calls=%async_computation.1 | async-start | bytes 2097152 | tf_op jit(solution)/shard_map/all_to_all | solution.py:180
  135.5 14.6 %collective-permute-start.21 = (bf16[2304,128]{1,0:T(8,128)(2,1)}, bf16[2304,128]{1,0:T(8,128)(2,1)}, u32[]{:S(2)}, u32[]{:S(2)}) collective-permute-start(bf16[2304,128]{1,0:T(8,128)(2,1)} %collective-permute-done.18), channel_id=1, source_target_pairs={{2,3},{5,4},{10,11},{13,12},{18,19},{21,20},{26,27},{29,28},{34,35... | collective-permute-start | bytes 1769480 | tf_op jit(solution)/shard_map/ppermute | solution.py:136
  137.0 27.0 %collective-permute-start.10 = (bf16[64,5888]{1,0:T(8,128)(2,1)}, bf16[64,5888]{1,0:T(8,128)(2,1)}, u32[]{:S(2)}, u32[]{:S(2)}) collective-permute-start(bf16[64,5888]{1,0:T(8,128)(2,1)} %collective-permute-done.9), channel_id=1, source_target_pairs={{6,7},{1,0},{14,15},{9,8},{22,23},{17,16},{30,31},{25,24},{38,39},... | collective-permute-start | bytes 2261000 | tf_op jit(solution)/shard_map/ppermute | solution.py:133
  143.7 0.7 copy-start.4
  144.5 13.5 %collective-permute-start.22 = (bf16[512,128]{1,0:T(8,128)(2,1)}, bf16[512,128]{1,0:T(8,128)(2,1)}, u32[]{:S(2)}, u32[]{:S(2)}) collective-permute-start(bf16[512,128]{1,0:T(8,128)(2,1)} %get-tuple-element.60), channel_id=1, source_target_pairs={{3,2},{4,5},{11,10},{12,13},{19,18},{20,21},{27,26},{28,29},{35,34... | collective-permute-start | bytes 393224 | tf_op jit(solution)/shard_map/ppermute | solution.py:188
  145.8 12.2 %collective-permute-start.24 = (bf16[512,128]{1,0:T(8,128)(2,1)}, bf16[512,128]{1,0:T(8,128)(2,1)}, u32[]{:S(2)}, u32[]{:S(2)}) collective-permute-start(bf16[512,128]{1,0:T(8,128)(2,1)} %get-tuple-element.62), channel_id=1, source_target_pairs={{3,0},{4,7},{11,8},{12,15},{19,16},{20,23},{27,24},{28,31},{35,32}... | collective-permute-start | bytes 393224 | tf_op jit(solution)/shard_map/ppermute | solution.py:188
  150.1 3.3 %copy-start.1 = (bf16[1,8192,128]{2,1,0:T(8,128)(2,1)S(1)}, bf16[1,8192,128]{2,1,0:T(8,128)(2,1)}, u32[]{:S(2)}) copy-start(bf16[1,8192,128]{2,1,0:T(8,128)(2,1)} %param.8) | copy-start | bytes 6291460
  152.1 11.9 %collective-permute-start.23 = (bf16[512,128]{1,0:T(8,128)(2,1)S(1)}, bf16[512,128]{1,0:T(8,128)(2,1)S(1)}, u32[]{:S(2)}, u32[]{:S(2)}) collective-permute-start(bf16[512,128]{1,0:T(8,128)(2,1)S(1)} %shard_map.94), channel_id=1, source_target_pairs={{3,1},{4,6},{11,9},{12,14},{19,17},{20,22},{27,25},{28,30},{35,33}... | collective-permute-start | bytes 393224 | tf_op jit(solution)/shard_map/ppermute | solution.py:188
  155.6 8.4 %copy-start.3 = (f32[22,64,128]{2,1,0:T(8,128)S(1)}, f32[22,64,128]{2,1,0:T(8,128)}, u32[]{:S(2)}) copy-start(f32[22,64,128]{2,1,0:T(8,128)} %fusion.77.rows) | copy-start | bytes 2162692
  155.6 8.4 %copy-start.5 = (f32[512,128]{1,0:T(8,128)S(1)}, f32[512,128]{1,0:T(8,128)}, u32[]{:S(2)}) copy-start(f32[512,128]{1,0:T(8,128)} %copy-done.4) | copy-start | bytes 786436
